TPU v7x, 32 devices: a whole 2x2x4 slice. The times are simulated.
32 devices in a mesh: dp: 4 (over y, x), tensor: 8 (over z, core).
Axes of the slice: x: 2, y: 2, z: 4, core: 2. Of those that a mesh axis runs over, the one named last changes fastest.
Arguments:
- hidden_in: bfloat16 [12, 1024, 2048], P('dp', 'tensor'), may hold values from -6 to 6
- out_grad: bfloat16 [12, 1024, 2048], P('dp', 'tensor'), may hold values from -6 to 6
- buckets: int32 [1024, 1024], replicated, may hold values from 0 to 31
- gain_attn: bfloat16 [2048], replicated, may hold values from 0.099609375 to 1.8984375
- gain_ffn: bfloat16 [2048], replicated, may hold values from 0.099609375 to 1.8984375
- w_query: bfloat16 [2048, 2048], P('dp', 'tensor'), may hold values from -0.03125 to 0.03125
- w_key: bfloat16 [2048, 2048], P('dp', 'tensor'), may hold values from -0.125 to 0.125
- w_value: bfloat16 [2048, 2048], P('dp', 'tensor'), may hold values from -0.125 to 0.125
- w_out: bfloat16 [2048, 2048], P('tensor', 'dp'), may hold values from -1 to 1
- w_gate: bfloat16 [2048, 5120], P('dp', 'tensor'), may hold values from -0.125 to 0.125
- w_up: bfloat16 [2048, 5120], P('dp', 'tensor'), may hold values from -0.125 to 0.125
- w_down: bfloat16 [5120, 2048], P('tensor', 'dp'), may hold values from -0.125 to 0.125
- bias_table: bfloat16 [32, 32], P('dp', 'tensor'), may hold values from -4 to 4
Outputs:
- output: bfloat16 [12, 1024, 2048], P('dp', 'tensor')
- grad_input: bfloat16 [12, 1024, 2048], P('dp', 'tensor')
- grad_gain_attn: float32 [2048], replicated
- grad_gain_ffn: float32 [2048], replicated
- grad_query: float32 [2048, 2048], P('dp', 'tensor')
- grad_key: float32 [2048, 2048], P('dp', 'tensor')
- grad_value: float32 [2048, 2048], P('dp', 'tensor')
- grad_out: float32 [2048, 2048], P('tensor', 'dp')
- grad_gate: float32 [2048, 5120], P('dp', 'tensor')
- grad_up: float32 [2048, 5120], P('dp', 'tensor')
- grad_down: float32 [5120, 2048], P('tensor', 'dp')
- grad_bias: float32 [32, 32], P('dp', 'tensor')
Inputs may be any that keep to these rules, and one draw needn't show every extreme that they name: `buckets`: the bucket of each pair of query and key positions, the same for every sequence and head.
All inputs are finite; a program needn't handle non-finite values.
Results may differ from a plain program's by a relative error of at most 0.018.
Values may be sent and summed in bfloat16 or wider, within the bound.
No kernel may reach another device: no remote copies, remote signals or barrier semaphores. Data moves between devices by JAX's collectives and lax.ppermute only.
A program may use at most 320 MiB of HBM per device.

v0:
```python
import jax
import jax.numpy as jnp
from jax import lax
from jax.sharding import PartitionSpec as P

HD = 64


norm_eps = 1e-06
FULL_PRECISION = lax.Precision.HIGHEST


def rms_parts(seq_rows, gain_vec):
    inv_rms = lax.rsqrt(jnp.mean(seq_rows * seq_rows, axis=-1, keepdims=True) + norm_eps)
    plain_rows = seq_rows * inv_rms
    return (plain_rows, inv_rms, (plain_rows * gain_vec).astype(jnp.bfloat16))


def rms_back(grad_norm, plain_rows, inv_rms, gain_vec):
    scaled_grad = grad_norm * gain_vec
    return inv_rms * (
        scaled_grad - plain_rows * jnp.mean(scaled_grad * plain_rows, axis=-1, keepdims=True)
    )


def gelu_gate(gate_pre, up_pre):
    return jax.nn.gelu(gate_pre, approximate=True) * up_pre


def contract_rows(left_mat, right_mat):
    return lax.dot_general(
        left_mat, right_mat, (((0,), (0,)), ((), ())), preferred_element_type=jnp.float32
    )


def times_transpose(left_mat, right_mat):
    return lax.dot_general(
        left_mat, right_mat, (((1,), (1,)), ((), ())), preferred_element_type=jnp.float32
    )


def gather_norm(normed):
    return lax.all_gather(normed, "tensor", axis=0, tiled=True)


def gather_grad(grad_rows):
    return lax.all_gather(grad_rows, "tensor", axis=0, tiled=True)


def branch_sum(left_mat, right_mat):
    return lax.psum_scatter(
        jnp.dot(left_mat, right_mat, preferred_element_type=jnp.float32),
        "tensor",
        scatter_dimension=0,
        tiled=True,
    )


def input_sum(left_mat, right_mat):
    return lax.psum_scatter(
        times_transpose(left_mat, right_mat), "tensor", scatter_dimension=0, tiled=True
    )


def expand_bias(buckets, bias_cols):
    length = buckets.shape[0]
    block_rows = min(64, length)
    bucket_ids = jnp.arange(bias_cols.shape[0], dtype=jnp.int32)[None, :, None]

    def expand_one_block(bucket_rows):
        onehot = (bucket_rows[:, None, :] == bucket_ids).astype(jnp.float32)
        return jnp.einsum("ibj,bh->ihj", onehot, bias_cols, precision=FULL_PRECISION)

    blocks = lax.map(expand_one_block, buckets.reshape(length // block_rows, block_rows, length))
    return blocks.reshape(length, bias_cols.shape[1], length)


def bias_grad(buckets, grad_accum, bucket_count):
    length = buckets.shape[0]
    local_heads = grad_accum.shape[1]
    block_rows = min(64, length)
    bucket_ids = jnp.arange(bucket_count, dtype=jnp.int32)[None, :, None]

    def bias_one_block(carried, block_pair):
        bucket_rows, grad_rows = block_pair
        onehot = (bucket_rows[:, None, :] == bucket_ids).astype(jnp.float32)
        return (
            carried + jnp.einsum("ibj,ihj->bh", onehot, grad_rows, precision=FULL_PRECISION),
            None,
        )

    stacked = (
        buckets.reshape(length // block_rows, block_rows, length),
        grad_accum.reshape(length // block_rows, block_rows, local_heads, length),
    )
    total, _ = lax.scan(
        bias_one_block, jnp.zeros((bucket_count, local_heads), jnp.float32), stacked
    )
    return total


def body(
    hidden_in,
    out_grad,
    buckets,
    gain_attn,
    gain_ffn,
    w_query,
    w_key,
    w_value,
    w_out,
    w_gate,
    w_up,
    w_down,
    bias_table,
):
    query_cols, key_cols, value_cols, out_rows, gate_cols, up_cols, down_rows, bias_cols = (
        lax.all_gather(w_query, "dp", axis=0, tiled=True),
        lax.all_gather(w_key, "dp", axis=0, tiled=True),
        lax.all_gather(w_value, "dp", axis=0, tiled=True),
        lax.all_gather(w_out, "dp", axis=1, tiled=True),
        lax.all_gather(w_gate, "dp", axis=0, tiled=True),
        lax.all_gather(w_up, "dp", axis=0, tiled=True),
        lax.all_gather(w_down, "dp", axis=1, tiled=True),
        lax.all_gather(bias_table, "dp", axis=0, tiled=True),
    )
    gain_one = gain_attn.astype(jnp.float32)
    gain_two = gain_ffn.astype(jnp.float32)
    w_qkv = jnp.concatenate([query_cols, key_cols, value_cols], axis=1)
    w_ffn = jnp.concatenate([gate_cols, up_cols], axis=1)
    local_inner = query_cols.shape[1]
    local_heads = local_inner // HD
    local_ff = gate_cols.shape[1]
    seq_len = buckets.shape[0]
    model_dim = hidden_in.shape[2]
    block_len = min(512, seq_len)
    block_starts = list(range(0, seq_len, block_len))
    bias_full = expand_bias(buckets, bias_cols.astype(jnp.float32))
    out_initial = jnp.zeros((local_inner, model_dim), jnp.float32)

    def block_scores(queries, key_rows, row_start):
        query_block = queries[row_start : row_start + block_len]
        scores = jnp.einsum(
            "ihd,jhd->ihj", query_block, key_rows, preferred_element_type=jnp.float32
        )
        return (query_block, scores + bias_full[row_start : row_start + block_len])

    def micro_step(carried, scan_pair):
        grad_qkv, grad_outw, grad_ffn, grad_downw, grad_gone, grad_gtwo, grad_table = carried
        seq_in, seq_cot = scan_pair
        seq_rows = seq_in.astype(jnp.float32)
        plain_one, inv_one, norm_one = rms_parts(seq_rows, gain_one)
        norm_full = gather_norm(norm_one)
        projected = jnp.dot(norm_full, w_qkv, preferred_element_type=jnp.float32).astype(
            jnp.bfloat16
        )
        queries = projected[:, :local_inner].reshape(seq_len, local_heads, HD)
        key_rows = projected[:, local_inner : 2 * local_inner].reshape(seq_len, local_heads, HD)
        value_rows = projected[:, 2 * local_inner :].reshape(seq_len, local_heads, HD)
        context_parts = []
        lse_parts = []
        for row_start in block_starts:
            query_block, scores = block_scores(queries, key_rows, row_start)
            top_score = jnp.max(scores, axis=-1, keepdims=True)
            shifted = jnp.exp(scores - top_score)
            totals = jnp.sum(shifted, axis=-1, keepdims=True)
            attn_probs = shifted / totals
            lse_parts.append(top_score + jnp.log(totals))
            context_parts.append(
                jnp.einsum(
                    "ihj,jhd->ihd",
                    attn_probs.astype(jnp.bfloat16),
                    value_rows,
                    preferred_element_type=jnp.float32,
                ).astype(jnp.bfloat16)
            )
        context = jnp.concatenate(context_parts, axis=0).reshape(seq_len, local_inner)
        attn_rows = branch_sum(context, out_rows)
        mid_rows = seq_rows + attn_rows
        plain_two, inv_two, norm_two = rms_parts(mid_rows, gain_two)
        norm_full_two = gather_norm(norm_two)
        pre_ffn = jnp.dot(norm_full_two, w_ffn, preferred_element_type=jnp.float32)
        gate_pre = pre_ffn[:, :local_ff]
        up_pre = pre_ffn[:, local_ff:]
        hidden = gelu_gate(gate_pre, up_pre).astype(jnp.bfloat16)
        ffn_rows = branch_sum(hidden, down_rows)
        seq_out = (mid_rows + ffn_rows).astype(jnp.bfloat16)
        cot_full = gather_grad(seq_cot)
        grad_downw = grad_downw + contract_rows(hidden, cot_full)
        grad_hidden = times_transpose(cot_full, down_rows)
        _, gelu_pull = jax.vjp(gelu_gate, gate_pre, up_pre)
        grad_gate_pre, grad_up_pre = gelu_pull(grad_hidden)
        grad_pre = jnp.concatenate([grad_gate_pre, grad_up_pre], axis=1).astype(jnp.bfloat16)
        grad_ffn = grad_ffn + contract_rows(norm_full_two, grad_pre)
        grad_norm_two = input_sum(grad_pre, w_ffn)
        grad_gtwo = grad_gtwo + jnp.sum(grad_norm_two * plain_two, axis=0)
        grad_mid = seq_cot.astype(jnp.float32) + rms_back(
            grad_norm_two, plain_two, inv_two, gain_two
        )
        grad_mid_low = grad_mid.astype(jnp.bfloat16)
        grad_full = gather_grad(grad_mid_low)
        grad_context = times_transpose(grad_full, out_rows).astype(jnp.bfloat16)
        grad_outw = grad_outw + contract_rows(context, grad_full)
        grad_context = grad_context.reshape(seq_len, local_heads, HD)
        grad_query_parts = []
        grad_keys = jnp.zeros((seq_len, local_heads, HD), jnp.float32)
        grad_values = jnp.zeros((seq_len, local_heads, HD), jnp.float32)
        for block_index, row_start in enumerate(block_starts):
            query_block, scores = block_scores(queries, key_rows, row_start)
            attn_probs = jnp.exp(scores - lse_parts[block_index])
            probs_low = attn_probs.astype(jnp.bfloat16)
            grad_block = grad_context[row_start : row_start + block_len]
            grad_probs = jnp.einsum(
                "ihd,jhd->ihj", grad_block, value_rows, preferred_element_type=jnp.float32
            )
            row_inner = jnp.sum(attn_probs * grad_probs, axis=-1, keepdims=True)
            grad_scores = (attn_probs * (grad_probs - row_inner)).astype(jnp.bfloat16)
            grad_table = grad_table.at[row_start : row_start + block_len].add(
                grad_scores.astype(jnp.float32)
            )
            grad_query_parts.append(
                jnp.einsum(
                    "ihj,jhd->ihd", grad_scores, key_rows, preferred_element_type=jnp.float32
                )
            )
            grad_keys = grad_keys + jnp.einsum(
                "ihj,ihd->jhd", grad_scores, query_block, preferred_element_type=jnp.float32
            )
            grad_values = grad_values + jnp.einsum(
                "ihj,ihd->jhd", probs_low, grad_block, preferred_element_type=jnp.float32
            )
        grad_queries = jnp.concatenate(grad_query_parts, axis=0)
        grad_proj = jnp.concatenate(
            [
                grad_queries.reshape(seq_len, local_inner),
                grad_keys.reshape(seq_len, local_inner),
                grad_values.reshape(seq_len, local_inner),
            ],
            axis=1,
        ).astype(jnp.bfloat16)
        grad_qkv = grad_qkv + contract_rows(norm_full, grad_proj)
        grad_norm_one = input_sum(grad_proj, w_qkv)
        grad_gone = grad_gone + jnp.sum(grad_norm_one * plain_one, axis=0)
        grad_in = (grad_mid + rms_back(grad_norm_one, plain_one, inv_one, gain_one)).astype(
            jnp.bfloat16
        )
        new_carry = (grad_qkv, grad_outw, grad_ffn, grad_downw, grad_gone, grad_gtwo, grad_table)
        return (new_carry, (seq_out, grad_in))

    initial = (
        jnp.zeros((model_dim, 3 * local_inner), jnp.float32),
        out_initial,
        jnp.zeros((model_dim, 2 * local_ff), jnp.float32),
        jnp.zeros((local_ff, model_dim), jnp.float32),
        jnp.zeros((model_dim,), jnp.float32),
        jnp.zeros((model_dim,), jnp.float32),
        jnp.zeros((seq_len, local_heads, seq_len), jnp.float32),
    )
    final_carry, (outputs_seq, grads_seq) = lax.scan(micro_step, initial, (hidden_in, out_grad))
    grad_qkv, grad_outw, grad_ffn, grad_downw, grad_gone, grad_gtwo, grad_table = final_carry
    table_grad = bias_grad(buckets, grad_table, bias_cols.shape[0])
    shards = (
        lax.psum_scatter(
            grad_qkv[:, :local_inner].astype(jnp.bfloat16), "dp", scatter_dimension=0, tiled=True
        ).astype(jnp.float32),
        lax.psum_scatter(
            grad_qkv[:, local_inner : 2 * local_inner].astype(jnp.bfloat16),
            "dp",
            scatter_dimension=0,
            tiled=True,
        ).astype(jnp.float32),
        lax.psum_scatter(
            grad_qkv[:, 2 * local_inner :].astype(jnp.bfloat16),
            "dp",
            scatter_dimension=0,
            tiled=True,
        ).astype(jnp.float32),
        lax.psum_scatter(
            grad_outw.astype(jnp.bfloat16), "dp", scatter_dimension=1, tiled=True
        ).astype(jnp.float32),
        lax.psum_scatter(
            grad_ffn[:, :local_ff].astype(jnp.bfloat16), "dp", scatter_dimension=0, tiled=True
        ).astype(jnp.float32),
        lax.psum_scatter(
            grad_ffn[:, local_ff:].astype(jnp.bfloat16), "dp", scatter_dimension=0, tiled=True
        ).astype(jnp.float32),
        lax.psum_scatter(
            grad_downw.astype(jnp.bfloat16), "dp", scatter_dimension=1, tiled=True
        ).astype(jnp.float32),
        lax.psum_scatter(
            table_grad.astype(jnp.bfloat16), "dp", scatter_dimension=0, tiled=True
        ).astype(jnp.float32),
    )
    gain_sums = lax.psum((grad_gone, grad_gtwo), ("dp", "tensor"))
    return (
        outputs_seq,
        grads_seq,
        gain_sums[0],
        gain_sums[1],
        shards[0],
        shards[1],
        shards[2],
        shards[3],
        shards[4],
        shards[5],
        shards[6],
        shards[7],
    )


def solution(mesh):
    in_specs = (
        P("dp", "tensor", None),
        P("dp", "tensor", None),
        P(),
        P(),
        P(),
        P("dp", "tensor"),
        P("dp", "tensor"),
        P("dp", "tensor"),
        P("tensor", "dp"),
        P("dp", "tensor"),
        P("dp", "tensor"),
        P("tensor", "dp"),
        P("dp", "tensor"),
    )
    out_specs = (
        P("dp", "tensor", None),
        P("dp", "tensor", None),
        P(),
        P(),
        P("dp", "tensor"),
        P("dp", "tensor"),
        P("dp", "tensor"),
        P("tensor", "dp"),
        P("dp", "tensor"),
        P("dp", "tensor"),
        P("tensor", "dp"),
        P("dp", "tensor"),
    )
    return jax.shard_map(body, mesh=mesh, in_specs=in_specs, out_specs=out_specs, check_vma=False)
```

profile of v0, /device:TPU:0, one launch (start us, length us, event | category | flops | bytes accessed | tf_op | source)
XLA Modules:
  0.0 2525.8 jit_solution(10109821729811257224)
XLA Ops:
  21.7 73.3 %while.53 = (s32[]{:T(128)}, f32[16,64,4,1024]{3,2,1,0:T(4,128)}, s32[16,64,1024]{2,1,0:T(8,128)}, f32[32,4]{0,1:T(4,128)S(1)}, s32[]{:T(128)}) while((s32[]{:T(128)}, f32[16,64,4,1024]{3,2,1,0:T(4,128)}, s32[16,64,1024]{2,1,0:T(8,128)}, f32[32,4]{0,1:T(4,128)S(1)}, s32[]{:T(128)}) %tuple.177), condition=%wide.region_1.2_spmd.clone, body=%wide.region_0.1_spmd.clone.sunk | while | flops 102760448 | bytes 1835597 | solution.py:74
  137.1 41.2 %all-gather.29.cloned.1.call-done = bf16[2048,640]{1,0:T(8,128)(2,1)} async-done(((bf16[512,640]{1,0:T(8,128)(2,1)}), bf16[2048,640]{1,0:T(8,128)(2,1)}) %all-gather.29.cloned.1.call-update) | async-done | bytes 2621456 | tf_op jit(solution)/shard_map/all_gather | solution.py:123
  183.6 22.7 all-gather.23.cloned.1.call-done
  206.4 41.2 %all-gather.25.cloned.1.call-done = bf16[640,2048]{1,0:T(8,128)(2,1)} async-done(((bf16[640,512]{1,0:T(8,128)(2,1)}), bf16[640,2048]{1,0:T(8,128)(2,1)}) %all-gather.25.cloned.1.call-update) | async-done | bytes 2621456 | tf_op jit(solution)/shard_map/all_gather | solution.py:124
  255.5 2008.2 %while.54 = (s32[]{:T(128)}, f32[2048,768]{1,0:T(8,128)}, f32[256,2048]{1,0:T(8,128)}, f32[2048,1280]{1,0:T(8,128)}, f32[640,2048]{1,0:T(8,128)}, /*index=5*/f32...) while((s32[]{:T(128)}, f32[2048,768]{1,0:T(8,128)}, ...), condition=%wide.region_19.20_spmd.clone, body=%wide.region_2.19_spmd.clone.sunk | while | flops 40408182784 | bytes 830275520 | solution.py:259
  258.9 47.0 %all-gather.31.cloned.1.call-done = bf16[1024,2048]{1,0:T(8,128)(2,1)} async-done(((bf16[128,2048]{1,0:T(8,128)(2,1)}), bf16[1024,2048]{1,0:T(8,128)(2,1)}) %all-gather.31.cloned.1.call-update) | async-done | bytes 4194320 | tf_op jit(solution)/shard_map/while/body/eval_jaxpr/all_gather | solution.py:43
  336.9 88.4 %reduce-scatter.27.cloned.1.call-done = f32[128,2048]{1,0:T(8,128)} async-done(((f32[1024,2048]{1,0:T(8,128)}), f32[128,2048]{1,0:T(8,128)}) %reduce-scatter.27.cloned.1.call-update) | async-done | bytes 1048592 | tf_op jit(solution)/shard_map/while/body/eval_jaxpr/reduce_scatter | solution.py:51
  429.9 43.5 %all-gather.33.cloned.1.call-done = bf16[1024,2048]{1,0:T(8,128)(2,1)} async-done(((bf16[128,2048]{1,0:T(8,128)(2,1)}), bf16[1024,2048]{1,0:T(8,128)(2,1)}) %all-gather.33.cloned.1.call-update) | async-done | bytes 4194320 | tf_op jit(solution)/shard_map/while/body/eval_jaxpr/all_gather | solution.py:43
  483.7 37.6 %all-gather.35.cloned.1.call-done = bf16[1,1024,2048]{2,1,0:T(8,128)(2,1)} async-done(((bf16[1,128,2048]{2,1,0:T(8,128)(2,1)}), bf16[1,1024,2048]{2,1,0:T(8,128)(2,1)}) %all-gather.35.cloned.1.call-update) | async-done | bytes 4194320 | tf_op jit(solution)/shard_map/while/body/eval_jaxpr/all_gather | solution.py:47
  543.5 88.5 %reduce-scatter.29.cloned.1.call-done = f32[128,2048]{1,0:T(8,128)} async-done(((f32[1024,2048]{1,0:T(8,128)}), f32[128,2048]{1,0:T(8,128)}) %reduce-scatter.29.cloned.1.call-update) | async-done | bytes 1048592 | tf_op jit(solution)/shard_map/while/body/eval_jaxpr/reduce_scatter | solution.py:60
  637.0 45.2 %all-gather.37.cloned.1.call-done = bf16[1024,2048]{1,0:T(8,128)(2,1)} async-done(((bf16[128,2048]{1,0:T(8,128)(2,1)}), bf16[1024,2048]{1,0:T(8,128)(2,1)}) %all-gather.37.cloned.1.call-update) | async-done | bytes 4194320 | tf_op jit(solution)/shard_map/while/body/eval_jaxpr/all_gather | solution.py:47
  776.3 53.9 %reduce-scatter.31.cloned.1.call-done = f32[128,2048]{1,0:T(8,128)} async-done(((f32[1024,2048]{1,0:T(8,128)}), f32[128,2048]{1,0:T(8,128)}) %reduce-scatter.31.cloned.1.call-update) | async-done | bytes 1048592 | tf_op jit(solution)/shard_map/while/body/eval_jaxpr/reduce_scatter | solution.py:60
  831.9 88.4 %reduce-scatter.33.cloned.1.call-done = f32[128,2048]{1,0:T(8,128)} async-done(((f32[1024,2048]{1,0:T(8,128)}), f32[128,2048]{1,0:T(8,128)}) %reduce-scatter.33.cloned.1.call-update) | async-done | bytes 1048592 | tf_op jit(solution)/shard_map/while/body/eval_jaxpr/reduce_scatter | solution.py:51
  927.3 45.4 %all-gather.31.cloned.1.call-done = bf16[1024,2048]{1,0:T(8,128)(2,1)} async-done(((bf16[128,2048]{1,0:T(8,128)(2,1)}), bf16[1024,2048]{1,0:T(8,128)(2,1)}) %all-gather.31.cloned.1.call-update) | async-done | bytes 4194320 | tf_op jit(solution)/shard_map/while/body/eval_jaxpr/all_gather | solution.py:43
  1003.7 88.4 %reduce-scatter.27.cloned.1.call-done = f32[128,2048]{1,0:T(8,128)} async-done(((f32[1024,2048]{1,0:T(8,128)}), f32[128,2048]{1,0:T(8,128)}) %reduce-scatter.27.cloned.1.call-update) | async-done | bytes 1048592 | tf_op jit(solution)/shard_map/while/body/eval_jaxpr/reduce_scatter | solution.py:51
  1096.8 43.5 %all-gather.33.cloned.1.call-done = bf16[1024,2048]{1,0:T(8,128)(2,1)} async-done(((bf16[128,2048]{1,0:T(8,128)(2,1)}), bf16[1024,2048]{1,0:T(8,128)(2,1)}) %all-gather.33.cloned.1.call-update) | async-done | bytes 4194320 | tf_op jit(solution)/shard_map/while/body/eval_jaxpr/all_gather | solution.py:43
  1150.6 37.6 %all-gather.35.cloned.1.call-done = bf16[1,1024,2048]{2,1,0:T(8,128)(2,1)} async-done(((bf16[1,128,2048]{2,1,0:T(8,128)(2,1)}), bf16[1,1024,2048]{2,1,0:T(8,128)(2,1)}) %all-gather.35.cloned.1.call-update) | async-done | bytes 4194320 | tf_op jit(solution)/shard_map/while/body/eval_jaxpr/all_gather | solution.py:47
  1210.4 88.4 %reduce-scatter.29.cloned.1.call-done = f32[128,2048]{1,0:T(8,128)} async-done(((f32[1024,2048]{1,0:T(8,128)}), f32[128,2048]{1,0:T(8,128)}) %reduce-scatter.29.cloned.1.call-update) | async-done | bytes 1048592 | tf_op jit(solution)/shard_map/while/body/eval_jaxpr/reduce_scatter | solution.py:60
  1303.8 45.2 %all-gather.37.cloned.1.call-done = bf16[1024,2048]{1,0:T(8,128)(2,1)} async-done(((bf16[128,2048]{1,0:T(8,128)(2,1)}), bf16[1024,2048]{1,0:T(8,128)(2,1)}) %all-gather.37.cloned.1.call-update) | async-done | bytes 4194320 | tf_op jit(solution)/shard_map/while/body/eval_jaxpr/all_gather | solution.py:47
  1449.5 47.5 %reduce-scatter.31.cloned.1.call-done = f32[128,2048]{1,0:T(8,128)} async-done(((f32[1024,2048]{1,0:T(8,128)}), f32[128,2048]{1,0:T(8,128)}) %reduce-scatter.31.cloned.1.call-update) | async-done | bytes 1048592 | tf_op jit(solution)/shard_map/while/body/eval_jaxpr/reduce_scatter | solution.py:60
  1498.8 88.5 %reduce-scatter.33.cloned.1.call-done = f32[128,2048]{1,0:T(8,128)} async-done(((f32[1024,2048]{1,0:T(8,128)}), f32[128,2048]{1,0:T(8,128)}) %reduce-scatter.33.cloned.1.call-update) | async-done | bytes 1048592 | tf_op jit(solution)/shard_map/while/body/eval_jaxpr/reduce_scatter | solution.py:51
  1594.3 45.4 %all-gather.31.cloned.1.call-done = bf16[1024,2048]{1,0:T(8,128)(2,1)} async-done(((bf16[128,2048]{1,0:T(8,128)(2,1)}), bf16[1024,2048]{1,0:T(8,128)(2,1)}) %all-gather.31.cloned.1.call-update) | async-done | bytes 4194320 | tf_op jit(solution)/shard_map/while/body/eval_jaxpr/all_gather | solution.py:43
  1670.8 88.4 %reduce-scatter.27.cloned.1.call-done = f32[128,2048]{1,0:T(8,128)} async-done(((f32[1024,2048]{1,0:T(8,128)}), f32[128,2048]{1,0:T(8,128)}) %reduce-scatter.27.cloned.1.call-update) | async-done | bytes 1048592 | tf_op jit(solution)/shard_map/while/body/eval_jaxpr/reduce_scatter | solution.py:51
  1763.8 43.5 %all-gather.33.cloned.1.call-done = bf16[1024,2048]{1,0:T(8,128)(2,1)} async-done(((bf16[128,2048]{1,0:T(8,128)(2,1)}), bf16[1024,2048]{1,0:T(8,128)(2,1)}) %all-gather.33.cloned.1.call-update) | async-done | bytes 4194320 | tf_op jit(solution)/shard_map/while/body/eval_jaxpr/all_gather | solution.py:43
  1817.6 37.4 %all-gather.35.cloned.1.call-done = bf16[1,1024,2048]{2,1,0:T(8,128)(2,1)} async-done(((bf16[1,128,2048]{2,1,0:T(8,128)(2,1)}), bf16[1,1024,2048]{2,1,0:T(8,128)(2,1)}) %all-gather.35.cloned.1.call-update) | async-done | bytes 4194320 | tf_op jit(solution)/shard_map/while/body/eval_jaxpr/all_gather | solution.py:47
  1877.3 88.4 %reduce-scatter.29.cloned.1.call-done = f32[128,2048]{1,0:T(8,128)} async-done(((f32[1024,2048]{1,0:T(8,128)}), f32[128,2048]{1,0:T(8,128)}) %reduce-scatter.29.cloned.1.call-update) | async-done | bytes 1048592 | tf_op jit(solution)/shard_map/while/body/eval_jaxpr/reduce_scatter | solution.py:60
  1970.7 45.2 %all-gather.37.cloned.1.call-done = bf16[1024,2048]{1,0:T(8,128)(2,1)} async-done(((bf16[128,2048]{1,0:T(8,128)(2,1)}), bf16[1024,2048]{1,0:T(8,128)(2,1)}) %all-gather.37.cloned.1.call-update) | async-done | bytes 4194320 | tf_op jit(solution)/shard_map/while/body/eval_jaxpr/all_gather | solution.py:47
  2116.3 47.5 %reduce-scatter.31.cloned.1.call-done = f32[128,2048]{1,0:T(8,128)} async-done(((f32[1024,2048]{1,0:T(8,128)}), f32[128,2048]{1,0:T(8,128)}) %reduce-scatter.31.cloned.1.call-update) | async-done | bytes 1048592 | tf_op jit(solution)/shard_map/while/body/eval_jaxpr/reduce_scatter | solution.py:60
  2165.6 88.6 %reduce-scatter.33.cloned.1.call-done = f32[128,2048]{1,0:T(8,128)} async-done(((f32[1024,2048]{1,0:T(8,128)}), f32[128,2048]{1,0:T(8,128)}) %reduce-scatter.33.cloned.1.call-update) | async-done | bytes 1048592 | tf_op jit(solution)/shard_map/while/body/eval_jaxpr/reduce_scatter | solution.py:51
  2306.5 104.5 %while.55 = (s32[]{:T(128)}, f32[32,4]{0,1:T(4,128)S(1)}, s32[16,64,1024]{2,1,0:T(8,128)}, f32[16,64,4,1024]{3,2,1,0:T(4,128)}, s32[]{:T(128)}, /*index=5*/s32[]{:T(128)}) while((s32[]{:T(128)}, f32[32,4]{0,1:T(4,128)S(1)}, s32[16,64,1024]{2,1,0:T(8,128)}, f32[16,64,4,1024]{3,2,1,0:T(4,128)}, s32[]{:T(128)}, ...), condition=%wide.region_30.31_spmd.clone, body=%wide.region_29.30_spmd.clone.sunk | while | flops 102760704 | bytes 1836127 | solution.py:96
  2420.8 37.9 %all-reduce.1 = (f32[2048]{0:T(1024)}, f32[2048]{0:T(1024)}) all-reduce(f32[2048]{0:T(1024)S(1)} %copy-done.26, f32[2048]{0:T(1024)S(1)} %copy-done.23), channel_id=1, replica_groups=mesh['dp'=4,'tensor'=8] {'dp','tensor'}, use_global_device_ids=true, to_apply=%region_20.21 | all-reduce | flops 4096 | bytes 32768 | tf_op jit(solution)/shard_map/psum | solution.py:294
  2476.4 40.4 %reduce-scatter.23.cloned.1.call-done = bf16[512,640]{1,0:T(8,128)(2,1)} async-done(((bf16[2048,640]{1,0:T(8,128)(2,1)}), bf16[512,640]{1,0:T(8,128)(2,1)}) %reduce-scatter.23.cloned.1.call-update) | async-done | bytes 655376 | tf_op jit(solution)/shard_map/reduce_scatter | solution.py:284
  (599 shorter events, 857.4 us)
Async XLA Ops:
  7.2 107.2 %all-gather.17.cloned.1.call-start = ((), (), s32[]{:S(2)}) async-start(), calls=%async_computation.11 | async-start | bytes 1310720 | tf_op jit(solution)/shard_map/all_gather | solution.py:118
  7.9 106.5 %all-gather.19.cloned.1.call-start = ((), (), s32[]{:S(2)}) async-start(), calls=%async_computation.12 | async-start | bytes 1310720 | tf_op jit(solution)/shard_map/all_gather | solution.py:119
  8.7 105.7 %all-gather.21.cloned.1.call-start = ((), (), s32[]{:S(2)}) async-start(), calls=%async_computation.13 | async-start | bytes 1310720 | tf_op jit(solution)/shard_map/all_gather | solution.py:120
  9.4 127.7 %all-gather.27.cloned.1.call-start = ((), (), s32[]{:S(2)}) async-start(), calls=%async_computation.16 | async-start | bytes 3276800 | tf_op jit(solution)/shard_map/all_gather | solution.py:122
  10.0 168.3 %all-gather.29.cloned.1.call-start = ((), (), s32[]{:S(2)}) async-start(), calls=%async_computation.17 | async-start | bytes 3276800 | tf_op jit(solution)/shard_map/all_gather | solution.py:123
  10.6 195.8 %all-gather.23.cloned.1.call-start = ((), (), s32[]{:S(2)}) async-start(), calls=%async_computation.14 | async-start | bytes 1310720 | tf_op jit(solution)/shard_map/all_gather | solution.py:121
  11.1 236.5 %all-gather.25.cloned.1.call-start = ((), (), s32[]{:S(2)}) async-start(), calls=%async_computation.15 | async-start | bytes 3276800 | tf_op jit(solution)/shard_map/all_gather | solution.py:124
  258.8 166.5 %reduce-scatter.27.cloned.1.call-start = ((), (), s32[]{:S(2)}) async-start(), calls=%async_computation.26 | async-start | bytes 9437184 | tf_op jit(solution)/shard_map/while/body/eval_jaxpr/reduce_scatter | solution.py:51
  336.8 136.5 %all-gather.33.cloned.1.call-start = ((), (), s32[]{:S(2)}) async-start(), calls=%async_computation.27 | async-start | bytes 4718592 | tf_op jit(solution)/shard_map/while/body/eval_jaxpr/all_gather | solution.py:43
  429.8 202.2 %reduce-scatter.29.cloned.1.call-start = ((), (), s32[]{:S(2)}) async-start(), calls=%async_computation.29 | async-start | bytes 9437184 | tf_op jit(solution)/shard_map/while/body/eval_jaxpr/reduce_scatter | solution.py:60
  543.5 138.7 %all-gather.37.cloned.1.call-start = ((), (), s32[]{:S(2)}) async-start(), calls=%async_computation.30 | async-start | bytes 4718592 | tf_op jit(solution)/shard_map/while/body/eval_jaxpr/all_gather | solution.py:47
  636.7 193.4 %reduce-scatter.31.cloned.1.call-start = ((), (), s32[]{:S(2)}) async-start(), calls=%async_computation.31 | async-start | bytes 9437184 | tf_op jit(solution)/shard_map/while/body/eval_jaxpr/reduce_scatter | solution.py:60
  741.6 178.7 %reduce-scatter.33.cloned.1.call-start = ((), (), s32[]{:S(2)}) async-start(), calls=%async_computation.32 | async-start | bytes 9437184 | tf_op jit(solution)/shard_map/while/body/eval_jaxpr/reduce_scatter | solution.py:51
  927.2 164.9 %reduce-scatter.27.cloned.1.call-start = ((), (), s32[]{:S(2)}) async-start(), calls=%async_computation.26 | async-start | bytes 9437184 | tf_op jit(solution)/shard_map/while/body/eval_jaxpr/reduce_scatter | solution.py:51
  1003.7 136.6 %all-gather.33.cloned.1.call-start = ((), (), s32[]{:S(2)}) async-start(), calls=%async_computation.27 | async-start | bytes 4718592 | tf_op jit(solution)/shard_map/while/body/eval_jaxpr/all_gather | solution.py:43
  1096.7 202.2 %reduce-scatter.29.cloned.1.call-start = ((), (), s32[]{:S(2)}) async-start(), calls=%async_computation.29 | async-start | bytes 9437184 | tf_op jit(solution)/shard_map/while/body/eval_jaxpr/reduce_scatter | solution.py:60
  1210.4 138.7 %all-gather.37.cloned.1.call-start = ((), (), s32[]{:S(2)}) async-start(), calls=%async_computation.30 | async-start | bytes 4718592 | tf_op jit(solution)/shard_map/while/body/eval_jaxpr/all_gather | solution.py:47
  1303.6 193.4 %reduce-scatter.31.cloned.1.call-start = ((), (), s32[]{:S(2)}) async-start(), calls=%async_computation.31 | async-start | bytes 9437184 | tf_op jit(solution)/shard_map/while/body/eval_jaxpr/reduce_scatter | solution.py:60
  1408.5 178.8 %reduce-scatter.33.cloned.1.call-start = ((), (), s32[]{:S(2)}) async-start(), calls=%async_computation.32 | async-start | bytes 9437184 | tf_op jit(solution)/shard_map/while/body/eval_jaxpr/reduce_scatter | solution.py:51
  1594.2 164.9 %reduce-scatter.27.cloned.1.call-start = ((), (), s32[]{:S(2)}) async-start(), calls=%async_computation.26 | async-start | bytes 9437184 | tf_op jit(solution)/shard_map/while/body/eval_jaxpr/reduce_scatter | solution.py:51
  1670.7 136.5 %all-gather.33.cloned.1.call-start = ((), (), s32[]{:S(2)}) async-start(), calls=%async_computation.27 | async-start | bytes 4718592 | tf_op jit(solution)/shard_map/while/body/eval_jaxpr/all_gather | solution.py:43
  1763.7 202.0 %reduce-scatter.29.cloned.1.call-start = ((), (), s32[]{:S(2)}) async-start(), calls=%async_computation.29 | async-start | bytes 9437184 | tf_op jit(solution)/shard_map/while/body/eval_jaxpr/reduce_scatter | solution.py:60
  1877.2 138.7 %all-gather.37.cloned.1.call-start = ((), (), s32[]{:S(2)}) async-start(), calls=%async_computation.30 | async-start | bytes 4718592 | tf_op jit(solution)/shard_map/while/body/eval_jaxpr/all_gather | solution.py:47
  1970.4 193.4 %reduce-scatter.31.cloned.1.call-start = ((), (), s32[]{:S(2)}) async-start(), calls=%async_computation.31 | async-start | bytes 9437184 | tf_op jit(solution)/shard_map/while/body/eval_jaxpr/reduce_scatter | solution.py:60
  2075.3 178.8 %reduce-scatter.33.cloned.1.call-start = ((), (), s32[]{:S(2)}) async-start(), calls=%async_computation.32 | async-start | bytes 9437184 | tf_op jit(solution)/shard_map/while/body/eval_jaxpr/reduce_scatter | solution.py:51
  2263.7 195.7 %reduce-scatter.19.cloned.1.call-start = ((), (), s32[]{:S(2)}) async-start(), calls=%async_computation.21 | async-start | bytes 1310720 | tf_op jit(solution)/shard_map/reduce_scatter | solution.py:278
  2266.5 194.7 %reduce-scatter.13.cloned.1.call-start = ((), (), s32[]{:S(2)}) async-start(), calls=%async_computation.18 | async-start | bytes 1310720 | tf_op jit(solution)/shard_map/reduce_scatter | solution.py:263
  2271.4 191.6 %reduce-scatter.15.cloned.1.call-start = ((), (), s32[]{:S(2)}) async-start(), calls=%async_computation.19 | async-start | bytes 1310720 | tf_op jit(solution)/shard_map/reduce_scatter | solution.py:266
  2272.1 192.6 %reduce-scatter.17.cloned.1.call-start = ((), (), s32[]{:S(2)}) async-start(), calls=%async_computation.20 | async-start | bytes 1310720 | tf_op jit(solution)/shard_map/reduce_scatter | solution.py:272
  2272.9 193.7 %reduce-scatter.25.cloned.1.call-start = ((), (), s32[]{:S(2)}) async-start(), calls=%async_computation.24 | async-start | bytes 3276800 | tf_op jit(solution)/shard_map/reduce_scatter | solution.py:287
  2277.4 196.8 %reduce-scatter.21.cloned.1.call-start = ((), (), s32[]{:S(2)}) async-start(), calls=%async_computation.22 | async-start | bytes 3276800 | tf_op jit(solution)/shard_map/reduce_scatter | solution.py:281
  2284.9 231.9 %reduce-scatter.23.cloned.1.call-start = ((), (), s32[]{:S(2)}) async-start(), calls=%async_computation.23 | async-start | bytes 3276800 | tf_op jit(solution)/shard_map/reduce_scatter | solution.py:284
  (134 other events, 4881.2 us)
Sparse Core Ops, SparseCore 0:
  9.8 29.2 all-gather.16
  97.5 39.4 all-gather.26
  138.8 39.4 all-gather.28
  208.2 39.3 all-gather.24
  258.9 46.8 all-gather.30
  337.0 88.3 reduce-scatter.26
  428.0 45.3 all-gather.32
  475.5 45.6 all-gather.34
  543.6 88.3 reduce-scatter.28
  636.9 45.3 all-gather.36
  741.7 88.3 reduce-scatter.30
  832.3 87.9 reduce-scatter.32
  927.3 45.3 all-gather.30
  1003.8 88.3 reduce-scatter.26
  1094.9 45.3 all-gather.32
  1142.4 45.6 all-gather.34
  1210.5 88.3 reduce-scatter.28
  1303.7 45.3 all-gather.36
  1408.6 88.3 reduce-scatter.30
  1499.3 87.9 reduce-scatter.32
  1594.4 45.3 all-gather.30
  1670.8 88.3 reduce-scatter.26
  1761.9 45.3 all-gather.32
  1809.3 45.6 all-gather.34
  1877.3 88.3 reduce-scatter.28
  1970.6 45.3 all-gather.36
  2075.5 88.3 reduce-scatter.30
  2166.1 88.0 reduce-scatter.32
  2328.6 27.9 reduce-scatter.14
  2390.9 40.1 reduce-scatter.24
  2433.9 40.2 reduce-scatter.20
  2477.2 39.5 reduce-scatter.22
  (6 shorter events, 161.3 us)
where the time goes:
time: 2530 us
  waiting for transfers between devices  1640 us (65%)
  matrix products  548 us (22%)
  other arithmetic  151 us (6%)
  local copies, waits for them, and re-layouts  105 us (4%)
  blocking collectives  57.4 us (2%)
    reduce_scatter x6, waiting for transfers between devices, branch_sum(): lax.psum_scatter(jnp.dot(left_mat, right_mat, preferred_element_type=jnp....  531 us
    reduce_scatter x6, waiting for transfers between devices, input_sum(): lax.psum_scatter(times_transpose(left_mat, right_mat), 'tensor', scatter_...  414 us
    all_gather x6, waiting for transfers between devices, gather_norm(): return lax.all_gather(normed, 'tensor', axis=0, tiled=True)  268 us
    all_gather x6, waiting for transfers between devices, gather_grad(): return lax.all_gather(grad_rows, 'tensor', axis=0, tiled=True)  248 us
    dot_general x12, matrix products, times_transpose(): lax.dot_general(left_mat, right_mat, (((1,), (1,)), ((), ())), preferred_...  96.6 us
    dot_general x16, matrix products, bias_one_block(): jnp.einsum('ibj,ihj->bh', onehot, grad_rows, precision=FULL_PRECISION)  88.6 us
    dot_general x12, matrix products, contract_rows(): lax.dot_general(left_mat, right_mat, (((0,), (0,)), ((), ())), preferred_...  84.3 us
    scatter-add x6, other arithmetic, micro_step(): grad_table.at[row_start:row_start + block_len]  58.8 us
  transfers between devices with their start and end apart: 38, of which 30 were waited for; matrix products, arithmetic and copies ran while one was open for 16% of the time, Pallas kernels for 0%

commit v1 on v0

v1 whole, which is shorter than its diff:
```python
import functools
import jax
import jax.numpy as jnp
from jax import lax
from jax.experimental import pallas as pl
from jax.experimental.pallas import tpu as pltpu
from jax.sharding import PartitionSpec as P

HD = 64
LANES = 128
norm_eps = 1e-06
VMEM_ROOM = 50 * 1024 * 1024


def nt_dot(left, right):
    return lax.dot_general(
        left, right, (((1,), (1,)), ((), ())), preferred_element_type=jnp.float32
    )


def nn_dot(left, right):
    return jnp.dot(left, right, preferred_element_type=jnp.float32)


def head_masks(rows):
    lane = lax.broadcasted_iota(jnp.int32, (rows, LANES), 1)
    return (lane < HD, lane >= HD)


def only_head(keep, pair_cols):
    return jnp.where(keep, pair_cols, jnp.zeros_like(pair_cols))


def expand_kernel(buckets_ref, table_ref, bias_ref):
    heads = table_ref.shape[0]
    rows, cols = buckets_ref.shape
    for col in range(0, cols, LANES):
        ids = buckets_ref[:, col : col + LANES]
        for head in range(heads):
            row = jnp.broadcast_to(table_ref[head : head + 1, :], (rows, LANES))
            bias_ref[head, :, col : col + LANES] = jnp.take_along_axis(
                row, ids, axis=1
            ).astype(jnp.bfloat16)


def expand_bias(buckets_t, table_rows):
    length = buckets_t.shape[0]
    heads = table_rows.shape[0]
    block = 64
    return pl.pallas_call(
        expand_kernel,
        grid=(length // block,),
        in_specs=[
            pl.BlockSpec((block, length), lambda i: (i, 0)),
            pl.BlockSpec((heads, LANES), lambda i: (0, 0)),
        ],
        out_specs=pl.BlockSpec((heads, block, length), lambda i: (0, i, 0)),
        out_shape=jax.ShapeDtypeStruct((heads, length, length), jnp.bfloat16),
        cost_estimate=pl.CostEstimate(
            flops=8 * heads * length * length,
            bytes_accessed=length * length * (4 + 2 * heads),
            transcendentals=0,
        ),
        name="expand_bias",
    )(buckets_t, table_rows)


def forward_kernel(block_cols, qkv_ref, bias_ref, context_ref, lse_ref):
    length = qkv_ref.shape[0]
    keys = qkv_ref[:, LANES : 2 * LANES]
    masks = head_masks(length)
    head_keys = [only_head(keep, keys) for keep in masks]
    values_t = qkv_ref[:, 2 * LANES :].T
    for start in range(0, length, block_cols):
        span = pl.ds(start, block_cols)
        queries = qkv_ref[span, :LANES]
        pieces = []
        for head in range(2):
            scores = nt_dot(head_keys[head], queries) + bias_ref[head, :, span].astype(
                jnp.float32
            )
            top = jnp.max(scores, axis=0, keepdims=True)
            shifted = jnp.exp(scores - top)
            total = jnp.sum(shifted, axis=0, keepdims=True)
            probs = (shifted * (1.0 / total)).astype(jnp.bfloat16)
            pieces.append(nn_dot(values_t[head * HD : (head + 1) * HD], probs))
            lse_ref[0, head : head + 1, span] = top + jnp.log(total)
        context_ref[span, :] = jnp.concatenate(pieces, axis=0).T.astype(jnp.bfloat16)


def attention_forward(qkv, bias_t):
    length = qkv.shape[0]
    pairs = qkv.shape[1] // (3 * LANES)
    heads = 2 * pairs
    return pl.pallas_call(
        functools.partial(forward_kernel, min(256, length)),
        grid=(pairs,),
        in_specs=[
            pl.BlockSpec((length, 3 * LANES), lambda p: (0, p)),
            pl.BlockSpec((2, length, length), lambda p: (p, 0, 0)),
        ],
        out_specs=[
            pl.BlockSpec((length, LANES), lambda p: (0, p)),
            pl.BlockSpec((1, 2, length), lambda p: (p, 0, 0)),
        ],
        out_shape=[
            jax.ShapeDtypeStruct((length, pairs * LANES), jnp.bfloat16),
            jax.ShapeDtypeStruct((pairs, 2, length), jnp.float32),
        ],
        compiler_params=pltpu.CompilerParams(vmem_limit_bytes=VMEM_ROOM),
        cost_estimate=pl.CostEstimate(
            flops=16 * heads * length * length * HD,
            bytes_accessed=2 * heads * length * length + 8 * heads * length * HD,
            transcendentals=heads * length * length,
        ),
        name="attention_forward",
    )(qkv, bias_t)


def backward_kernel(
    block_cols, qkv_ref, grad_ref, bias_ref, lse_ref, out_ref, grad_scores_ref, dk_acc, dv_acc
):
    length = qkv_ref.shape[0]
    keys = qkv_ref[:, LANES : 2 * LANES]
    values = qkv_ref[:, 2 * LANES :]
    masks = head_masks(length)
    small_masks = head_masks(block_cols)
    head_keys = [only_head(keep, keys) for keep in masks]
    head_values = [only_head(keep, values) for keep in masks]
    keys_t = keys.T
    for start in range(0, length, block_cols):
        span = pl.ds(start, block_cols)
        queries = qkv_ref[span, :LANES]
        grads = grad_ref[span, :]
        pieces = []
        for head in range(2):
            scores = nt_dot(head_keys[head], queries) + bias_ref[head, :, span].astype(
                jnp.float32
            )
            probs = jnp.exp(scores - lse_ref[0, head : head + 1, span])
            grad_probs = nt_dot(head_values[head], grads)
            inner = jnp.sum(probs * grad_probs, axis=0, keepdims=True)
            grad_scores = (probs * (grad_probs - inner)).astype(jnp.bfloat16)
            grad_scores_ref[head, :, span] = grad_scores
            value_part = nn_dot(
                probs.astype(jnp.bfloat16), only_head(small_masks[head], grads)
            )
            key_part = nn_dot(grad_scores, only_head(small_masks[head], queries))
            if start == 0 and head == 0:
                dv_acc[...] = value_part
                dk_acc[...] = key_part
            else:
                dv_acc[...] += value_part
                dk_acc[...] += key_part
            pieces.append(nn_dot(keys_t[head * HD : (head + 1) * HD], grad_scores))
        out_ref[span, :LANES] = jnp.concatenate(pieces, axis=0).T.astype(jnp.bfloat16)
    out_ref[:, LANES : 2 * LANES] = dk_acc[...].astype(jnp.bfloat16)
    out_ref[:, 2 * LANES :] = dv_acc[...].astype(jnp.bfloat16)


def attention_backward(qkv, grad_context, bias_t, lse):
    length = qkv.shape[0]
    pairs = qkv.shape[1] // (3 * LANES)
    heads = 2 * pairs
    return pl.pallas_call(
        functools.partial(backward_kernel, min(256, length)),
        grid=(pairs,),
        in_specs=[
            pl.BlockSpec((length, 3 * LANES), lambda p: (0, p)),
            pl.BlockSpec((length, LANES), lambda p: (0, p)),
            pl.BlockSpec((2, length, length), lambda p: (p, 0, 0)),
            pl.BlockSpec((1, 2, length), lambda p: (p, 0, 0)),
        ],
        out_specs=[
            pl.BlockSpec((length, 3 * LANES), lambda p: (0, p)),
            pl.BlockSpec((2, length, length), lambda p: (p, 0, 0)),
        ],
        out_shape=[
            jax.ShapeDtypeStruct((length, pairs * 3 * LANES), jnp.bfloat16),
            jax.ShapeDtypeStruct((heads, length, length), jnp.bfloat16),
        ],
        scratch_shapes=[
            pltpu.VMEM((length, LANES), jnp.float32),
            pltpu.VMEM((length, LANES), jnp.float32),
        ],
        compiler_params=pltpu.CompilerParams(vmem_limit_bytes=VMEM_ROOM),
        cost_estimate=pl.CostEstimate(
            flops=40 * heads * length * length * HD,
            bytes_accessed=4 * heads * length * length + 16 * heads * length * HD,
            transcendentals=heads * length * length,
        ),
        name="attention_backward",
    )(qkv, grad_context, bias_t, lse)


def histogram_kernel(bucket_count, group, buckets_ref, *refs):
    grads, (sums_ref, values) = refs[:-2], refs[-2:]
    heads, rows, cols = values.shape

    @pl.when(pl.program_id(0) == 0)
    def _():
        sums_ref[...] = jnp.zeros_like(sums_ref)

    total = grads[0][...].astype(jnp.float32)
    for other in grads[1:]:
        total = total + other[...].astype(jnp.float32)
    values[...] = total

    @pl.loop(0, bucket_count // group)
    def _(step):
        first = step * group
        acc = [[jnp.zeros((8, LANES), jnp.float32) for _ in range(heads)] for _ in range(group)]
        for row in range(0, rows, 8):
            for col in range(0, cols, LANES):
                ids = buckets_ref[row : row + 8, col : col + LANES]
                vals = [values[h, row : row + 8, col : col + LANES] for h in range(heads)]
                for j in range(group):
                    hit = ids == first + j
                    for h in range(heads):
                        acc[j][h] = acc[j][h] + jnp.where(hit, vals[h], 0.0)
        for j in range(group):
            for h in range(heads):
                sums_ref[h, first + j] += acc[j][h]


def bucket_sums(buckets_t, grad_scores, bucket_count):
    heads, length, _ = grad_scores[0].shape
    block = 32
    sums = pl.pallas_call(
        functools.partial(histogram_kernel, bucket_count, 4),
        grid=(length // block,),
        in_specs=[pl.BlockSpec((block, length), lambda i: (i, 0))]
        + [pl.BlockSpec((heads, block, length), lambda i: (0, i, 0))] * len(grad_scores),
        out_specs=pl.BlockSpec((heads, bucket_count, 8, LANES), lambda i: (0, 0, 0, 0)),
        out_shape=jax.ShapeDtypeStruct((heads, bucket_count, 8, LANES), jnp.float32),
        scratch_shapes=[pltpu.VMEM((heads, block, length), jnp.float32)],
        compiler_params=pltpu.CompilerParams(vmem_limit_bytes=VMEM_ROOM),
        cost_estimate=pl.CostEstimate(
            flops=60 * bucket_count * heads * length * length,
            bytes_accessed=length * length * (4 + 2 * heads * len(grad_scores)),
            transcendentals=0,
        ),
        name="bucket_sums",
    )(buckets_t, *grad_scores)
    return jnp.sum(sums, axis=(2, 3)).T


def xor_pairs(count, mask):
    return [(i, i ^ mask) for i in range(count)]


def reorder(blocks, place):
    blocks = list(blocks)
    bit = 1
    while bit < len(blocks):
        flag = (place & bit) != 0
        blocks = [jnp.where(flag, blocks[i ^ bit], blocks[i]) for i in range(len(blocks))]
        bit *= 2
    return blocks


def rms_parts(seq_rows, gain_vec):
    inv_rms = lax.rsqrt(jnp.mean(seq_rows * seq_rows, axis=-1, keepdims=True) + norm_eps)
    plain_rows = seq_rows * inv_rms
    return (plain_rows, inv_rms, (plain_rows * gain_vec).astype(jnp.bfloat16))


def rms_back(grad_norm, plain_rows, inv_rms, gain_vec):
    scaled_grad = grad_norm * gain_vec
    return inv_rms * (
        scaled_grad - plain_rows * jnp.mean(scaled_grad * plain_rows, axis=-1, keepdims=True)
    )


def gelu_gate(gate_pre, up_pre):
    return jax.nn.gelu(gate_pre, approximate=True) * up_pre


def tn_dot(left, right):
    return lax.dot_general(
        left, right, (((0,), (0,)), ((), ())), preferred_element_type=jnp.float32
    )


def make_body(dp_size, tensor_size):
    zs = tensor_size // 2
    z_groups = [[2 * z + core for z in range(zs)] for core in range(2)]
    core_pairs = xor_pairs(tensor_size, 1)

    def to_core(x):
        return lax.ppermute(x, "tensor", core_pairs)

    def to_dp(x, mask):
        return lax.ppermute(x, "dp", xor_pairs(dp_size, mask))

    def to_z(x, mask):
        return lax.ppermute(x, "tensor", xor_pairs(tensor_size, 2 * mask))

    def dp_relative(x):
        return [x] + [to_dp(x, k) for k in range(1, dp_size)]

    def dp_total(pick):
        own = pick(0).astype(jnp.float32)
        for k in range(1, dp_size):
            own = own + to_dp(pick(k).astype(jnp.bfloat16), k).astype(jnp.float32)
        return own

    def z_gather(x):
        return lax.all_gather(x, "tensor", axis=0, tiled=True, axis_index_groups=z_groups)

    def z_scatter(x):
        return lax.psum_scatter(
            x, "tensor", scatter_dimension=0, tiled=True, axis_index_groups=z_groups
        )

    def all_sum(x):
        bit = 1
        while bit < tensor_size:
            x = x + lax.ppermute(x, "tensor", xor_pairs(tensor_size, bit))
            bit *= 2
        bit = 1
        while bit < dp_size:
            x = x + to_dp(x, bit)
            bit *= 2
        return x

    def body(
        hidden_in,
        out_grad,
        buckets,
        gain_attn,
        gain_ffn,
        w_query,
        w_key,
        w_value,
        w_out,
        w_gate,
        w_up,
        w_down,
        bias_table,
    ):
        dp_at = lax.axis_index("dp")
        tensor_at = lax.axis_index("tensor")
        core_at = tensor_at % 2
        z_at = tensor_at // 2
        seqs, rows, width = hidden_in.shape
        tokens = seqs * rows
        length = buckets.shape[0]
        feats = w_query.shape[0]
        inner = w_query.shape[1]
        heads = inner // HD
        pairs = inner // LANES
        ff = w_gate.shape[1]
        part = ff // dp_size
        table_rows = bias_table.shape[0]
        bucket_count = table_rows * dp_size
        gain_one = gain_attn.astype(jnp.float32)
        gain_two = gain_ffn.astype(jnp.float32)

        qkv_local = jnp.concatenate(
            [
                w[:, p * LANES : (p + 1) * LANES]
                for p in range(pairs)
                for w in (w_query, w_key, w_value)
            ],
            axis=1,
        )
        pad_rows = -table_rows % 16
        table_pad = jnp.pad(bias_table, ((0, pad_rows), (0, 3 * inner - heads)))
        payload = reorder(
            dp_relative(jnp.concatenate([qkv_local, table_pad], axis=0)), dp_at
        )
        w_qkv = jnp.concatenate([p[:feats] for p in payload], axis=0)
        table = jnp.concatenate(
            [p[feats : feats + table_rows, :heads] for p in payload], axis=0
        )
        buckets_t = buckets.T
        bias_t = expand_bias(
            buckets_t,
            jnp.pad(table.astype(jnp.float32).T, ((0, 0), (0, LANES - bucket_count))),
        )

        x_rows = hidden_in.astype(jnp.float32)
        plain_one, inv_one, norm_one = rms_parts(x_rows, gain_one)
        norm_full = [
            lax.all_gather(norm_one[s], "tensor", axis=0, tiled=True) for s in range(seqs)
        ]

        out_z = z_gather(w_out)
        out_own = jnp.concatenate(reorder(dp_relative(out_z), dp_at), axis=1)
        out_other = to_core(out_own)

        ffn_local = jnp.stack([w_gate.T, w_up.T, w_down]).reshape(3, dp_size, part, feats)

        def ffn_block(k):
            return lax.dynamic_index_in_dim(ffn_local, dp_at ^ k, 1, keepdims=False)

        ffn_parts = [ffn_block(0)] + [to_dp(ffn_block(k), k) for k in range(1, dp_size)]
        ffn_rows = jnp.concatenate(reorder(ffn_parts, dp_at), axis=2).reshape(3 * part, width)
        ffn_all = z_gather(ffn_rows).reshape(zs, 3, part, width)
        ffn_all = jnp.transpose(ffn_all, (1, 0, 2, 3)).reshape(3 * ff, width)
        w_pre = ffn_all[: 2 * ff]
        w_post = ffn_all[2 * ff :]

        def context_to_tokens(context):
            blocks = context.reshape(zs, 2, rows, inner)
            own = lax.dynamic_index_in_dim(blocks, core_at, 1, keepdims=False)
            got = to_core(lax.dynamic_index_in_dim(blocks, 1 - core_at, 1, keepdims=False))
            both = jnp.concatenate([own, got], axis=-1)
            moved = [lax.dynamic_index_in_dim(both, z_at, 0, keepdims=False)]
            for k in range(1, zs):
                moved.append(
                    to_z(lax.dynamic_index_in_dim(both, z_at ^ k, 0, keepdims=False), k)
                )
            moved = reorder(moved, z_at)
            return (
                jnp.concatenate([m[:, :inner] for m in moved], axis=1),
                jnp.concatenate([m[:, inner:] for m in moved], axis=1),
            )

        def tokens_to_context(own, other):
            pair = jnp.stack(reorder([own, to_core(other)], core_at))

            def block(k):
                return lax.dynamic_slice_in_dim(pair, (z_at ^ k) * inner, inner, 2)

            moved = [block(0)] + [to_z(block(k), k) for k in range(1, zs)]
            return jnp.stack(reorder(moved, z_at)).reshape(length, inner)

        qkv_all, lse_all, ctx_own, ctx_other = [], [], [], []
        for s in range(seqs):
            qkv = nn_dot(norm_full[s], w_qkv).astype(jnp.bfloat16)
            context, lse = attention_forward(qkv, bias_t)
            own, other = context_to_tokens(context)
            qkv_all.append(qkv)
            lse_all.append(lse)
            ctx_own.append(own)
            ctx_other.append(other)
        ctx_own = jnp.concatenate(ctx_own, axis=0)
        ctx_other = jnp.concatenate(ctx_other, axis=0)
        attn_rows = nn_dot(ctx_own, out_own) + nn_dot(ctx_other, out_other)
        x_flat = x_rows.reshape(tokens, width)
        mid_rows = x_flat + attn_rows
        plain_two, inv_two, norm_two = rms_parts(mid_rows, gain_two)

        def group_rows(x):
            own = jnp.concatenate(dp_relative(x), axis=0)
            return (own, to_core(own))

        def group_total(own, other):
            own = own + to_core(other.astype(jnp.bfloat16)).astype(jnp.float32)
            return dp_total(lambda k: own[k * tokens : (k + 1) * tokens])

        cot_halves = group_rows(out_grad.reshape(tokens, width))
        norm_halves = group_rows(norm_two)
        out_parts, back_parts, hidden_halves, pre_halves = [], [], [], []
        for norm_half, cot_half in zip(norm_halves, cot_halves):
            pre = nt_dot(norm_half, w_pre)
            hidden, pull = jax.vjp(gelu_gate, pre[:, :ff], pre[:, ff:])
            hidden = hidden.astype(jnp.bfloat16)
            grad_gate, grad_up = pull(nt_dot(cot_half, w_post))
            grad_pre = jnp.concatenate([grad_gate, grad_up], axis=1).astype(jnp.bfloat16)
            out_parts.append(nn_dot(hidden, w_post))
            back_parts.append(nn_dot(grad_pre, w_pre))
            hidden_halves.append(hidden)
            pre_halves.append(grad_pre)
        grad_post = tn_dot(hidden_halves[0], cot_halves[0]) + tn_dot(
            hidden_halves[1], cot_halves[1]
        )
        grad_first = tn_dot(pre_halves[0], norm_halves[0]) + tn_dot(
            pre_halves[1], norm_halves[1]
        )
        grad_norm_two = group_total(*back_parts)
        post_z = z_scatter(grad_post.astype(jnp.bfloat16))
        first_z = z_scatter(
            jnp.transpose(
                grad_first.astype(jnp.bfloat16).reshape(2, zs, part, width), (1, 0, 2, 3)
            ).reshape(zs * 2 * part, width)
        )
        output = (mid_rows + group_total(*out_parts)).astype(jnp.bfloat16)

        grad_gain_two = jnp.sum(grad_norm_two * plain_two, axis=0)
        grad_mid = out_grad.reshape(tokens, width).astype(jnp.float32) + rms_back(
            grad_norm_two, plain_two, inv_two, gain_two
        )
        grad_mid_low = grad_mid.astype(jnp.bfloat16)
        back_own = nt_dot(grad_mid_low, out_own).astype(jnp.bfloat16)
        back_other = nt_dot(grad_mid_low, out_other).astype(jnp.bfloat16)
        grad_norm_one, grad_qkv, grad_scores = [], None, []
        for s in range(seqs):
            at = slice(s * rows, (s + 1) * rows)
            grad_context = tokens_to_context(back_own[at], back_other[at])
            grad_proj, grad_score = attention_backward(
                qkv_all[s], grad_context, bias_t, lse_all[s]
            )
            grad_scores.append(grad_score)
            grad_norm_one.append(
                lax.psum_scatter(
                    nt_dot(grad_proj, w_qkv).astype(jnp.bfloat16),
                    "tensor",
                    scatter_dimension=0,
                    tiled=True,
                ).astype(jnp.float32)
            )
            more = tn_dot(norm_full[s], grad_proj)
            grad_qkv = more if grad_qkv is None else grad_qkv + more

        grad_out_own = tn_dot(ctx_own, grad_mid_low)
        grad_out_other = tn_dot(ctx_other, grad_mid_low)
        grad_out_own = grad_out_own + to_core(grad_out_other.astype(jnp.bfloat16)).astype(
            jnp.float32
        )
        grad_out = z_scatter(
            dp_total(
                lambda k: lax.dynamic_slice_in_dim(grad_out_own, (dp_at ^ k) * feats, feats, 1)
            ).astype(jnp.bfloat16)
        ).astype(jnp.float32)

        def ffn_grad(z_rows, mats):
            def block(k):
                return lax.dynamic_slice_in_dim(z_rows, (dp_at ^ k) * feats, feats, 1)

            moved = [block(0)] + [to_dp(block(k), k) for k in range(1, dp_size)]
            moved = jnp.stack(reorder(moved, dp_at)).reshape(dp_size, mats, part, feats)
            return [moved[:, m].reshape(ff, feats).astype(jnp.float32) for m in range(mats)]

        (grad_down,) = ffn_grad(post_z, 1)
        grad_gate_t, grad_up_t = ffn_grad(first_z, 2)

        table_grad = bucket_sums(buckets_t, grad_scores, bucket_count)

        def qkv_block(k):
            at = dp_at ^ k
            return jnp.concatenate(
                [
                    lax.dynamic_slice_in_dim(grad_qkv, at * feats, feats, 0),
                    jnp.pad(
                        lax.dynamic_slice_in_dim(table_grad, at * table_rows, table_rows, 0),
                        ((0, pad_rows), (0, 3 * inner - heads)),
                    ),
                ],
                axis=0,
            )

        summed = dp_total(qkv_block)
        grad_table = summed[feats : feats + table_rows, :heads]

        def columns(which):
            return jnp.concatenate(
                [
                    summed[:feats, (3 * p + which) * LANES : (3 * p + which + 1) * LANES]
                    for p in range(pairs)
                ],
                axis=1,
            )

        grad_norm_one = jnp.stack(grad_norm_one)
        grad_gain_one = jnp.sum(grad_norm_one * plain_one, axis=(0, 1))
        grad_in = (
            grad_mid.reshape(seqs, rows, width)
            + rms_back(grad_norm_one, plain_one, inv_one, gain_one)
        ).astype(jnp.bfloat16)
        gains = all_sum(jnp.stack([grad_gain_one, grad_gain_two]))
        return (
            output.reshape(seqs, rows, width),
            grad_in,
            gains[0],
            gains[1],
            columns(0),
            columns(1),
            columns(2),
            grad_out,
            grad_gate_t.T,
            grad_up_t.T,
            grad_down,
            grad_table,
        )

    return body


def solution(mesh):
    in_specs = (
        P("dp", "tensor", None),
        P("dp", "tensor", None),
        P(),
        P(),
        P(),
        P("dp", "tensor"),
        P("dp", "tensor"),
        P("dp", "tensor"),
        P("tensor", "dp"),
        P("dp", "tensor"),
        P("dp", "tensor"),
        P("tensor", "dp"),
        P("dp", "tensor"),
    )
    out_specs = (
        P("dp", "tensor", None),
        P("dp", "tensor", None),
        P(),
        P(),
        P("dp", "tensor"),
        P("dp", "tensor"),
        P("dp", "tensor"),
        P("tensor", "dp"),
        P("dp", "tensor"),
        P("dp", "tensor"),
        P("tensor", "dp"),
        P("dp", "tensor"),
    )
    body = make_body(mesh.shape["dp"], mesh.shape["tensor"])
    return jax.shard_map(body, mesh=mesh, in_specs=in_specs, out_specs=out_specs, check_vma=False)
```

time: 2530 us -> 1110 us (0.44)
  waiting for transfers between devices: 1640 us -> 478 us
  matrix products: 548 us -> 209 us
  Pallas kernels: 0 us -> 178 us
  starting transfers between devices: 2.72 us -> 95.2 us
  other arithmetic: 151 us -> 67.9 us
  blocking collectives: 57.4 us -> 0 us
  local copies, waits for them, and re-layouts: 105 us -> 64.6 us
    reduce_scatter x19 -> x6, waiting for transfers between devices: 991 us -> 10.2 us  [the longest x3 10.1 us: z_scatter(): lax.psum_scatter(x, 'tensor', scatter_dimension=0, tiled=True, axis_index...]
    all_gather x19 -> x5, waiting for transfers between devices: 641 us -> 7.7 us  [the longest x3 7.7 us: body(): lax.all_gather(norm_one[s], 'tensor', axis=0, tiled=True)]
    ppermute x0 -> x68, waiting for transfers between devices: none -> 458 us  [the longest x35 369 us: to_dp(): return lax.ppermute(x, 'dp', xor_pairs(dp_size, mask))]
    dot_general x104 -> x27, matrix products: 548 us -> 209 us  [the longest x9 70.6 us: tn_dot(): lax.dot_general(left, right, (((0,), (0,)), ((), ())), preferred_element_...]
    pallas_call x0 -> x8, Pallas kernels: none -> 178 us  [the longest x3 57.3 us: attention_backward(): pl.pallas_call(functools.partial(backward_kernel, min(256, length)), grid...]
    ppermute x0 -> x68, starting transfers between devices: none -> 94.2 us  [the longest x35 46.1 us: to_dp(): return lax.ppermute(x, 'dp', xor_pairs(dp_size, mask))]
    scatter-add x6 -> x0, other arithmetic: 58.8 us -> none  [micro_step(): grad_table.at[row_start:row_start + block_len]]
    psum x1 -> x0, blocking collectives: 37.9 us -> none  [body(): gain_sums = lax.psum((grad_gone, grad_gtwo), ('dp', 'tensor'))]
  transfers between devices with their start and end apart: 38 -> 79, of which waited for: 30 -> 31; matrix products, arithmetic and copies ran while one was open for 16% -> 27% of each run, Pallas kernels for 0% -> 16%
where the time goes in v1:
time: 1110 us
  waiting for transfers between devices  478 us (43%)
  matrix products  209 us (19%)
  Pallas kernels  178 us (16%)
  starting transfers between devices  95.2 us (9%)
  other arithmetic  67.9 us (6%)
  local copies, waits for them, and re-layouts  64.6 us (6%)
  between operations  16.1 us (1%)
    ppermute x35, waiting for transfers between devices, to_dp(): return lax.ppermute(x, 'dp', xor_pairs(dp_size, mask))  369 us
    ppermute x18, waiting for transfers between devices, to_z(): return lax.ppermute(x, 'tensor', xor_pairs(tensor_size, 2 * mask))  83.6 us
    dot_general x9, matrix products, tn_dot(): lax.dot_general(left, right, (((0,), (0,)), ((), ())), preferred_element_...  70.6 us
    dot_general x9, matrix products, nt_dot(): lax.dot_general(left, right, (((1,), (1,)), ((), ())), preferred_element_...  69.6 us
    dot_general x9, matrix products, nn_dot(): return jnp.dot(left, right, preferred_element_type=jnp.float32)  68.6 us
    pallas_call x3, Pallas kernels, attention_backward(): pl.pallas_call(functools.partial(backward_kernel, min(256, length)), grid...  57.3 us
    pallas_call x1, Pallas kernels, bucket_sums(): pl.pallas_call(functools.partial(histogram_kernel, bucket_count, 4), grid...  55.6 us
    pallas_call x3, Pallas kernels, attention_forward(): pl.pallas_call(functools.partial(forward_kernel, min(256, length)), grid=...  51.5 us
  transfers between devices with their start and end apart: 79, of which 31 were waited for; matrix products, arithmetic and copies ran while one was open for 27% of the time, Pallas kernels for 16%

profile of v1, /device:TPU:0, one launch (start us, length us, event | category | flops | bytes accessed | tf_op | source)
XLA Modules:
  0.0 1109.0 jit_solution(8455990462784557306)
XLA Ops:
  30.0 21.7 %collective-permute-done.22 = bf16[3,160,512]{2,1,0:T(8,128)(2,1)S(1)} collective-permute-done((bf16[3,160,512]{2,1,0:T(8,128)(2,1)S(1)}, bf16[3,160,512]{2,1,0:T(8,128)(2,1)S(1)}, u32[]{:S(2)}, u32[]{:S(2)}) %collective-permute-start.22) | collective-permute-done | bytes 491552 | tf_op jit(solution)/shard_map/ppermute | solution.py:294
  88.5 14.0 %expand_bias.1.bias_ref = bf16[4,1024,1024]{2,1,0:T(8,128)(2,1)} custom-call(s32[1024,1024]{1,0:T(8,128)} %bitcast.228, f32[4,128]{1,0:T(4,128)} %pad_convert_fusion.table_ref), custom_call_target="tpu_custom_call" | custom-call | flops 33554432 | bytes 12582912 | tf_op jit(solution)/shard_map/expand_bias/pallas_call | solution.py:50
  102.5 21.3 %collective-permute-done.16 = bf16[1024,512]{1,0:T(8,128)(2,1)} collective-permute-done((bf16[1024,512]{1,0:T(8,128)(2,1)}, bf16[1024,512]{1,0:T(8,128)(2,1)}, u32[]{:S(2)}, u32[]{:S(2)}) %collective-permute-start.16) | collective-permute-done | bytes 1048608 | tf_op jit(solution)/shard_map/ppermute | solution.py:294
  134.2 17.0 %attention_forward.3 = (bf16[1024,256]{1,0:T(8,128)(2,1)S(1)}, f32[2,2,1024]{2,1,0:T(2,128)S(1)}) custom-call(bf16[1024,768]{1,0:T(8,128)(2,1)S(1)} %fusion.44.qkv_ref, bf16[4,1024,1024]{2,1,0:T(8,128)(2,1)} %expand_bias.1.bias_ref), custom_call_target="tpu_custom_call" | custom-call | flops 4294967296 | bytes 10485760 | tf_op jit(solution)/shard_map/attention_forward/pallas_call | solution.py:95
  158.6 16.8 %attention_forward.4 = (bf16[1024,256]{1,0:T(8,128)(2,1)S(1)}, f32[2,2,1024]{2,1,0:T(2,128)S(1)}) custom-call(bf16[1024,768]{1,0:T(8,128)(2,1)S(1)} %fusion.47.qkv_ref, bf16[4,1024,1024]{2,1,0:T(8,128)(2,1)} %expand_bias.1.bias_ref), custom_call_target="tpu_custom_call" | custom-call | flops 4294967296 | bytes 10485760 | tf_op jit(solution)/shard_map/attention_forward/pallas_call | solution.py:95
  190.9 17.7 %attention_forward.5 = (bf16[1024,256]{1,0:T(8,128)(2,1)S(1)}, f32[2,2,1024]{2,1,0:T(2,128)S(1)}) custom-call(bf16[1024,768]{1,0:T(8,128)(2,1)S(1)} %fusion.50.qkv_ref, bf16[4,1024,1024]{2,1,0:T(8,128)(2,1)} %expand_bias.1.bias_ref), custom_call_target="tpu_custom_call" | custom-call | flops 4294967296 | bytes 10485760 | tf_op jit(solution)/shard_map/attention_forward/pallas_call | solution.py:95
  223.3 13.4 %collective-permute-done.5 = bf16[128,512]{1,0:T(8,128)(2,1)S(1)} collective-permute-done((bf16[128,512]{1,0:T(8,128)(2,1)S(1)}, bf16[128,512]{1,0:T(8,128)(2,1)S(1)}, u32[]{:S(2)}, u32[]{:S(2)}) %collective-permute-start.5) | collective-permute-done | bytes 131104 | tf_op jit(solution)/shard_map/ppermute | solution.py:297
  244.7 12.3 %collective-permute-start.14 = (bf16[128,512]{1,0:T(8,128)(2,1)S(1)}, bf16[128,512]{1,0:T(8,128)(2,1)S(1)}, u32[]{:S(2)}, u32[]{:S(2)}) collective-permute-start(bf16[128,512]{1,0:T(8,128)(2,1)S(1)} %get-tuple-element.214), channel_id=1, source_target_pairs={{0,2},{1,3},{2,0},{3,1},{4,6},{5,7},{6,4},{7,5},{8,10},{9,11},{10,... | collective-permute-start | bytes 393224 | tf_op jit(solution)/shard_map/ppermute | solution.py:297
  265.5 20.7 %collective-permute-done.13 = bf16[128,512]{1,0:T(8,128)(2,1)S(1)} collective-permute-done((bf16[128,512]{1,0:T(8,128)(2,1)S(1)}, bf16[128,512]{1,0:T(8,128)(2,1)S(1)}, u32[]{:S(2)}, u32[]{:S(2)}) %collective-permute-start.13) | collective-permute-done | bytes 131104 | tf_op jit(solution)/shard_map/ppermute | solution.py:297
  298.6 30.8 %collective-permute-done.19 = bf16[384,2048]{1,0:T(8,128)(2,1)S(1)} collective-permute-done((bf16[384,2048]{1,0:T(8,128)(2,1)S(1)}, bf16[384,2048]{1,0:T(8,128)(2,1)S(1)}, u32[]{:S(2)}, u32[]{:S(2)}) %collective-permute-start.19) | collective-permute-done | bytes 1572896 | tf_op jit(solution)/shard_map/ppermute | solution.py:294
  331.9 32.8 %collective-permute-done.20 = bf16[384,2048]{1,0:T(8,128)(2,1)S(1)} collective-permute-done((bf16[384,2048]{1,0:T(8,128)(2,1)S(1)}, bf16[384,2048]{1,0:T(8,128)(2,1)S(1)}, u32[]{:S(2)}, u32[]{:S(2)}) %collective-permute-start.20) | collective-permute-done | bytes 1572896 | tf_op jit(solution)/shard_map/ppermute | solution.py:294
  368.5 28.4 %collective-permute-done.30 = bf16[384,2048]{1,0:T(8,128)(2,1)S(1)} collective-permute-done((bf16[384,2048]{1,0:T(8,128)(2,1)S(1)}, bf16[384,2048]{1,0:T(8,128)(2,1)S(1)}, u32[]{:S(2)}, u32[]{:S(2)}) %collective-permute-start.30) | collective-permute-done | bytes 1572896 | tf_op jit(solution)/shard_map/ppermute | solution.py:294
  396.9 34.0 %collective-permute-done.31 = bf16[384,2048]{1,0:T(8,128)(2,1)S(1)} collective-permute-done((bf16[384,2048]{1,0:T(8,128)(2,1)S(1)}, bf16[384,2048]{1,0:T(8,128)(2,1)S(1)}, u32[]{:S(2)}, u32[]{:S(2)}) %collective-permute-start.31) | collective-permute-done | bytes 1572896 | tf_op jit(solution)/shard_map/ppermute | solution.py:294
  443.9 12.6 %fusion.106 = f32[1536,1280]{0,1:T(8,128)} fusion(bf16[1280,2048]{1,0:T(8,128)(2,1)S(1)} %bitcast.239, bf16[384,2048]{1,0:T(8,128)(2,1)S(1)} %copy-done.33, bf16[384,2048]{1,0:T(8,128)(2,1)S(1)} %copy-done.30, bf16[384,2048]{1,0:T(8,128)(2,1)S(1)} %collective-permute-done.19, bf16[384,2048]{1,0:T(8,128)(2,1)S(1)} %multiply_convert_fusion.4), kind=kOutput, calls=%fused_computation.344 | convolution fusion | flops 8078229504 | bytes 19398656 | tf_op jit(solution)/shard_map/dot_general | solution.py:16
  456.5 12.5 %fusion.18 = (bf16[1536,640]{0,1:T(8,128)(2,1)}, bf16[1536,640]{0,1:T(8,128)(2,1)}, bf16[1536,640]{0,1:T(8,128)(2,1)S(1)}) fusion(f32[1536,1280]{0,1:T(8,128)} %fusion.106, bf16[1536,2048]{1,0:T(8,128)(2,1)} %pad_maximum_fusion.1, bf16[640,2048]{1,0:T(8,128)(2,1)S(1)} %bitcast.244), kind=kOutput, calls=%fused_computation.33 | convolution fusion | flops 4052090880 | bytes 22675456 | tf_op jit(solution)/shard_map/dot_general | solution.py:16
  469.1 13.2 %fusion.139 = f32[1536,1280]{0,1:T(8,128)} fusion(bf16[1536,2048]{1,0:T(8,128)(2,1)} %collective-permute-done.25, bf16[1280,2048]{1,0:T(8,128)(2,1)S(1)} %bitcast.240), kind=kOutput, calls=%fused_computation.370 | convolution fusion | flops 8053063680 | bytes 19398656 | tf_op jit(solution)/shard_map/dot_general | solution.py:16
  482.3 11.2 %fusion.25 = (bf16[1536,640]{0,1:T(8,128)(2,1)S(1)}, bf16[1536,640]{0,1:T(8,128)(2,1)S(1)}, bf16[1536,640]{0,1:T(8,128)(2,1)S(1)}) fusion(f32[1536,1280]{0,1:T(8,128)} %fusion.139, bf16[1536,2048]{1,0:T(8,128)(2,1)} %collective-permute-done.33, bf16[640,2048]{1,0:T(8,128)(2,1)S(1)} %bitcast.245), kind=kOutput, calls=%fused_computation.40 | convolution fusion | flops 4052090880 | bytes 22675456 | tf_op jit(solution)/shard_map/dot_general | solution.py:16
  528.7 13.4 %fusion.41 = f32[1280,2048]{1,0:T(8,128)} fusion(bf16[1536,2048]{1,0:T(8,128)(2,1)} %collective-permute-done.25, bf16[1536,640]{0,1:T(8,128)(2,1)S(1)} %copy-done.98, bf16[1536,640]{0,1:T(8,128)(2,1)S(1)} %copy-done.96), kind=kOutput, calls=%fused_computation.79 | convolution fusion | flops 8060928000 | bytes 20709376 | tf_op jit(solution)/shard_map/dot_general | solution.py:280
  542.1 13.8 %add_convert_fusion = bf16[1280,2048]{1,0:T(8,128)(2,1)} fusion(f32[1280,2048]{1,0:T(8,128)} %fusion.41, bf16[1536,640]{0,1:T(8,128)(2,1)} %get-tuple-element.106, bf16[1536,640]{0,1:T(8,128)(2,1)} %get-tuple-element.105, bf16[384,2048]{1,0:T(8,128)(2,1)S(1)} %copy-done.34, bf16[384,2048]{1,0:T(8,128)(2,1)S(1)} %copy-done.31, ...), kind=kOutput, calls=%fused_computation.2 | convolution fusion | flops 8091336704 | bytes 25952256 | tf_op jit(solution)/shard_map/dot_general | solution.py:280
  563.2 15.5 %fusion.138 = (bf16[1536,2048]{1,0:T(8,128)(2,1)S(1)}, f32[1536,2048]{1,0:T(8,128)}) fusion(bf16[1536,2048]{1,0:T(8,128)(2,1)} %collective-permute-done.34, bf16[1280,2048]{1,0:T(8,128)(2,1)} %bitcast.242, bf16[1536,640]{0,1:T(8,128)(2,1)} %get-tuple-element.106, bf16[1536,640]{0,1:T(8,128)(2,1)S(1)} %copy-done.99), kind=kOutput, calls=%fused_computation.369 | convolution fusion | flops 8070365184 | bytes 34340864 | tf_op jit(solution)/shard_map/dot_general | solution.py:22
  599.5 18.7 %collective-permute-done.35 = bf16[384,2048]{1,0:T(8,128)(2,1)} collective-permute-done((bf16[384,2048]{1,0:T(8,128)(2,1)S(1)}, bf16[384,2048]{1,0:T(8,128)(2,1)}, u32[]{:S(2)}, u32[]{:S(2)}) %collective-permute-start.35) | collective-permute-done | bytes 1572896 | tf_op jit(solution)/shard_map/ppermute | solution.py:294
  620.0 33.6 %collective-permute-done.36 = bf16[384,2048]{1,0:T(8,128)(2,1)} collective-permute-done((bf16[384,2048]{1,0:T(8,128)(2,1)}, bf16[384,2048]{1,0:T(8,128)(2,1)}, u32[]{:S(2)}, u32[]{:S(2)}) %collective-permute-start.36) | collective-permute-done | bytes 1572896 | tf_op jit(solution)/shard_map/ppermute | solution.py:294
  658.5 27.2 %collective-permute-done.27 = bf16[384,2048]{1,0:T(8,128)(2,1)} collective-permute-done((bf16[384,2048]{1,0:T(8,128)(2,1)}, bf16[384,2048]{1,0:T(8,128)(2,1)}, u32[]{:S(2)}, u32[]{:S(2)}) %collective-permute-start.27) | collective-permute-done | bytes 1572896 | tf_op jit(solution)/shard_map/ppermute | solution.py:294
  685.6 34.8 %collective-permute-done.28 = bf16[384,2048]{1,0:T(8,128)(2,1)} collective-permute-done((bf16[384,2048]{1,0:T(8,128)(2,1)}, bf16[384,2048]{1,0:T(8,128)(2,1)}, u32[]{:S(2)}, u32[]{:S(2)}) %collective-permute-start.28) | collective-permute-done | bytes 1572896 | tf_op jit(solution)/shard_map/ppermute | solution.py:294
  748.9 19.0 %attention_backward.3 = (bf16[1024,768]{1,0:T(8,128)(2,1)S(1)}, bf16[4,1024,1024]{2,1,0:T(8,128)(2,1)}) custom-call(bf16[1024,768]{1,0:T(8,128)(2,1)S(1)} %copy-done.5, bf16[1024,256]{1,0:T(8,128)(2,1)S(1)} %bitcast.226, bf16[4,1024,1024]{2,1,0:T(8,128)(2,1)} %expand_bias.1.bias_ref, f32[2,2,1024]{2,1,0:T(2,128)S(1)} %get-tuple-element.27.lse_ref), custom_call_target="tpu_custom_call" | custom-call | flops 10737418240 | bytes 20971520 | tf_op jit(solution)/shard_map/attention_backward/pallas_call | solution.py:165
  791.0 11.8 %collective-permute-done.44 = bf16[2,128,256]{2,1,0:T(8,128)(2,1)S(1)} collective-permute-done((bf16[2,128,256]{2,1,0:T(8,128)(2,1)S(1)}, bf16[2,128,256]{2,1,0:T(8,128)(2,1)S(1)}, u32[]{:S(2)}, u32[]{:S(2)}) %collective-permute-start.44) | collective-permute-done | bytes 131104 | tf_op jit(solution)/shard_map/ppermute | solution.py:297
  802.9 12.4 %collective-permute-done.48 = bf16[2,128,256]{2,1,0:T(8,128)(2,1)S(1)} collective-permute-done((bf16[2,128,256]{2,1,0:T(8,128)(2,1)S(1)}, bf16[2,128,256]{2,1,0:T(8,128)(2,1)S(1)}, u32[]{:S(2)}, u32[]{:S(2)}) %collective-permute-start.48) | collective-permute-done | bytes 131104 | tf_op jit(solution)/shard_map/ppermute | solution.py:297
  816.2 19.0 %attention_backward.4 = (bf16[1024,768]{1,0:T(8,128)(2,1)S(1)}, bf16[4,1024,1024]{2,1,0:T(8,128)(2,1)}) custom-call(bf16[1024,768]{1,0:T(8,128)(2,1)S(1)} %copy-done.3, bf16[1024,256]{1,0:T(8,128)(2,1)S(1)} %bitcast.227, bf16[4,1024,1024]{2,1,0:T(8,128)(2,1)} %expand_bias.1.bias_ref, f32[2,2,1024]{2,1,0:T(2,128)S(1)} %get-tuple-element.29.lse_ref), custom_call_target="tpu_custom_call" | custom-call | flops 10737418240 | bytes 20971520 | tf_op jit(solution)/shard_map/attention_backward/pallas_call | solution.py:165
  849.7 19.3 %attention_backward.5 = (bf16[1024,768]{1,0:T(8,128)(2,1)S(1)}, bf16[4,1024,1024]{2,1,0:T(8,128)(2,1)}) custom-call(bf16[1024,768]{1,0:T(8,128)(2,1)S(1)} %copy-done.1, bf16[1024,256]{1,0:T(8,128)(2,1)S(1)} %bitcast.225, bf16[4,1024,1024]{2,1,0:T(8,128)(2,1)} %expand_bias.1.bias_ref, f32[2,2,1024]{2,1,0:T(2,128)S(1)} %get-tuple-element.31.lse_ref), custom_call_target="tpu_custom_call" | custom-call | flops 10737418240 | bytes 20971520 | tf_op jit(solution)/shard_map/attention_backward/pallas_call | solution.py:165
  884.1 55.6 %bucket_sums.1 = f32[4,32,8,128]{3,2,1,0:T(8,128)S(1)} custom-call(s32[1024,1024]{1,0:T(8,128)} %bitcast.229, bf16[4,1024,1024]{2,1,0:T(8,128)(2,1)} %get-tuple-element.33.refs_0_, bf16[4,1024,1024]{2,1,0:T(8,128)(2,1)} %get-tuple-element.34.refs_1_, bf16[4,1024,1024]{2,1,0:T(8,128)(2,1)} %get-tuple-element.35.refs_2_), custom_call_target="tpu_custom_call" | custom-call | flops 8053063680 | bytes 29360128 | tf_op jit(solution)/shard_map/bucket_sums/pallas_call | solution.py:229
  982.8 25.6 %collective-permute-done.56 = bf16[528,768]{1,0:T(8,128)(2,1)} collective-permute-done((bf16[528,768]{1,0:T(8,128)(2,1)}, bf16[528,768]{1,0:T(8,128)(2,1)}, u32[]{:S(2)}, u32[]{:S(2)}) %collective-permute-start.56) | collective-permute-done | bytes 811040 | tf_op jit(solution)/shard_map/ppermute | solution.py:294
  1017.2 42.1 %collective-permute-done.63 = bf16[320,512]{1,0:T(8,128)(2,1)S(1)} collective-permute-done((bf16[320,512]{1,0:T(8,128)(2,1)S(1)}, bf16[320,512]{1,0:T(8,128)(2,1)S(1)}, u32[]{:S(2)}, u32[]{:S(2)}) %collective-permute-start.63) | collective-permute-done | bytes 327712 | tf_op jit(solution)/shard_map/ppermute | solution.py:294
  (511 shorter events, 400.7 us)
Async XLA Ops:
  7.2 54.4 %all-gather.9.cloned.1.call-start = ((), (), s32[]{:S(2)}) async-start(), calls=%async_computation.6 | async-start | bytes 1310720 | tf_op jit(solution)/shard_map/all_gather | solution.py:309
  7.9 119.7 %all-gather.13.cloned.1.call-start = ((), (), s32[]{:S(2)}) async-start(), calls=%async_computation.14 | async-start | bytes 4718592 | tf_op jit(solution)/shard_map/all_gather | solution.py:386
  13.6 138.4 %all-gather.15.cloned.1.call-start = ((), (), s32[]{:S(2)}) async-start(), calls=%async_computation.15 | async-start | bytes 4718592 | tf_op jit(solution)/shard_map/all_gather | solution.py:386
  14.3 170.1 %all-gather.17.cloned.1.call-start = ((), (), s32[]{:S(2)}) async-start(), calls=%async_computation.16 | async-start | bytes 4718592 | tf_op jit(solution)/shard_map/all_gather | solution.py:386
  14.9 419.9 %all-gather.11.cloned.1.call-start = ((), (), s32[]{:S(2)}) async-start(), calls=%async_computation.7 | async-start | bytes 9830400 | tf_op jit(solution)/shard_map/all_gather | solution.py:309
  64.2 59.6 %collective-permute-start.16 = (bf16[1024,512]{1,0:T(8,128)(2,1)}, bf16[1024,512]{1,0:T(8,128)(2,1)}, u32[]{:S(2)}, u32[]{:S(2)}) collective-permute-start(bf16[1024,512]{1,0:T(8,128)(2,1)} %all-gather.9.cloned.1.call-done), channel_id=1, source_target_pairs={{0,16},{8,24},{16,0},{24,8},{1,17},{9,25},{17,1},{25,9},{2,18},{10... | collective-permute-start | bytes 3145736 | tf_op jit(solution)/shard_map/ppermute | solution.py:294
  64.7 59.4 %collective-permute-start.17 = (bf16[1024,512]{1,0:T(8,128)(2,1)}, bf16[1024,512]{1,0:T(8,128)(2,1)}, u32[]{:S(2)}, u32[]{:S(2)}) collective-permute-start(bf16[1024,512]{1,0:T(8,128)(2,1)} %all-gather.9.cloned.1.call-done), channel_id=1, source_target_pairs={{0,8},{8,0},{16,24},{24,16},{1,9},{9,1},{17,25},{25,17},{2,10},{10... | collective-permute-start | bytes 3145736 | tf_op jit(solution)/shard_map/ppermute | solution.py:294
  68.0 773.9 %reduce-scatter.17.cloned.1.call-start = ((), (), s32[]{:S(2)}) async-start(), calls=%async_computation.13 | async-start | bytes 3276800 | tf_op jit(solution)/shard_map/reduce_scatter | solution.py:312
  152.0 58.0 %collective-permute-start.3 = (bf16[4,128,256]{2,1,0:T(8,128)(2,1)}, bf16[4,128,256]{2,1,0:T(8,128)(2,1)}, u32[]{:S(2)}, u32[]{:S(2)}) collective-permute-start(bf16[4,128,256]{2,1,0:T(8,128)(2,1)} %get-tuple-element.201), channel_id=1, source_target_pairs={{0,1},{1,0},{2,3},{3,2},{4,5},{5,4},{6,7},{7,6},{8,9},{9,8},{10,11... | collective-permute-start | bytes 786440 | tf_op jit(solution)/shard_map/ppermute | solution.py:291
  209.7 76.9 %collective-permute-start.18 = (bf16[1024,2048]{1,0:T(8,128)(2,1)S(1)}, bf16[1024,2048]{1,0:T(8,128)(2,1)S(1)}, u32[]{:S(2)}, u32[]{:S(2)}) collective-permute-start(bf16[1024,2048]{1,0:T(8,128)(2,1)S(1)} %pad_maximum_fusion.2), channel_id=1, source_target_pairs={{0,1},{1,0},{2,3},{3,2},{4,5},{5,4},{6,7},{7,6},{8,9},{9,8},{10,11... | collective-permute-start | bytes 12582920 | tf_op jit(solution)/shard_map/ppermute | solution.py:291
  293.7 71.0 %collective-permute-start.20 = (bf16[384,2048]{1,0:T(8,128)(2,1)S(1)}, bf16[384,2048]{1,0:T(8,128)(2,1)S(1)}, u32[]{:S(2)}, u32[]{:S(2)}) collective-permute-start(bf16[384,2048]{1,0:T(8,128)(2,1)S(1)} %multiply_convert_fusion.4), channel_id=1, source_target_pairs={{0,16},{8,24},{16,0},{24,8},{1,17},{9,25},{17,1},{25,9},{2,18},{10... | collective-permute-start | bytes 4718600 | tf_op jit(solution)/shard_map/ppermute | solution.py:294
  295.2 69.5 %collective-permute-start.21 = (bf16[384,2048]{1,0:T(8,128)(2,1)S(1)}, bf16[384,2048]{1,0:T(8,128)(2,1)S(1)}, u32[]{:S(2)}, u32[]{:S(2)}) collective-permute-start(bf16[384,2048]{1,0:T(8,128)(2,1)S(1)} %multiply_convert_fusion.4), channel_id=1, source_target_pairs={{0,24},{8,16},{16,8},{24,0},{1,25},{9,17},{17,9},{25,1},{2,26},{10... | collective-permute-start | bytes 4718600 | tf_op jit(solution)/shard_map/ppermute | solution.py:294
  295.7 101.2 %collective-permute-start.30 = (bf16[384,2048]{1,0:T(8,128)(2,1)S(1)}, bf16[384,2048]{1,0:T(8,128)(2,1)S(1)}, u32[]{:S(2)}, u32[]{:S(2)}) collective-permute-start(bf16[384,2048]{1,0:T(8,128)(2,1)S(1)} %bitcast.235), channel_id=1, source_target_pairs={{0,8},{8,0},{16,24},{24,16},{1,9},{9,1},{17,25},{25,17},{2,10},{10... | collective-permute-start | bytes 4718600 | tf_op jit(solution)/shard_map/ppermute | solution.py:294
  297.2 133.8 %collective-permute-start.31 = (bf16[384,2048]{1,0:T(8,128)(2,1)S(1)}, bf16[384,2048]{1,0:T(8,128)(2,1)S(1)}, u32[]{:S(2)}, u32[]{:S(2)}) collective-permute-start(bf16[384,2048]{1,0:T(8,128)(2,1)S(1)} %bitcast.236), channel_id=1, source_target_pairs={{0,16},{8,24},{16,0},{24,8},{1,17},{9,25},{17,1},{25,9},{2,18},{10... | collective-permute-start | bytes 4718600 | tf_op jit(solution)/shard_map/ppermute | solution.py:294
  329.5 101.5 %collective-permute-start.32 = (bf16[384,2048]{1,0:T(8,128)(2,1)S(1)}, bf16[384,2048]{1,0:T(8,128)(2,1)S(1)}, u32[]{:S(2)}, u32[]{:S(2)}) collective-permute-start(bf16[384,2048]{1,0:T(8,128)(2,1)S(1)} %bitcast.237), channel_id=1, source_target_pairs={{0,24},{8,16},{16,8},{24,0},{1,25},{9,17},{17,9},{25,1},{2,26},{10... | collective-permute-start | bytes 4718600 | tf_op jit(solution)/shard_map/ppermute | solution.py:294
  368.5 100.6 %collective-permute-start.25 = (bf16[1536,2048]{1,0:T(8,128)(2,1)}, bf16[1536,2048]{1,0:T(8,128)(2,1)}, u32[]{:S(2)}, u32[]{:S(2)}) collective-permute-start(bf16[1536,2048]{1,0:T(8,128)(2,1)} %pad_maximum_fusion), channel_id=1, source_target_pairs={{0,1},{1,0},{2,3},{3,2},{4,5},{5,4},{6,7},{7,6},{8,9},{9,8},{10,11... | collective-permute-start | bytes 18874376 | tf_op jit(solution)/shard_map/ppermute | solution.py:291
  504.0 57.7 %collective-permute-start.34 = (bf16[1536,2048]{1,0:T(8,128)(2,1)}, bf16[1536,2048]{1,0:T(8,128)(2,1)}, u32[]{:S(2)}, u32[]{:S(2)}) collective-permute-start(bf16[1536,2048]{1,0:T(8,128)(2,1)} %convolution_convert_fusion), channel_id=1, source_target_pairs={{0,1},{1,0},{2,3},{3,2},{4,5},{5,4},{6,7},{7,6},{8,9},{9,8},{10,11... | collective-permute-start | bytes 18874376 | tf_op jit(solution)/shard_map/ppermute | solution.py:291
  519.5 448.9 %reduce-scatter.15.cloned.1.call-start = ((), (), s32[]{:S(2)}) async-start(), calls=%async_computation.12 | async-start | bytes 6553600 | tf_op jit(solution)/shard_map/reduce_scatter | solution.py:312
  528.7 55.6 %collective-permute-start.26 = (bf16[1536,2048]{1,0:T(8,128)(2,1)}, bf16[1536,2048]{1,0:T(8,128)(2,1)}, u32[]{:S(2)}, u32[]{:S(2)}) collective-permute-start(bf16[1536,2048]{1,0:T(8,128)(2,1)} %convolution_convert_fusion.1), channel_id=1, source_target_pairs={{0,1},{1,0},{2,3},{3,2},{4,5},{5,4},{6,7},{7,6},{8,9},{9,8},{10,11... | collective-permute-start | bytes 18874376 | tf_op jit(solution)/shard_map/ppermute | solution.py:291
  561.6 503.5 %reduce-scatter.7.cloned.1.call-start = ((), (), s32[]{:S(2)}) async-start(), calls=%async_computation.8 | async-start | bytes 4718592 | tf_op jit(solution)/shard_map/reduce_scatter | solution.py:498
  582.3 71.3 %collective-permute-start.36 = (bf16[384,2048]{1,0:T(8,128)(2,1)}, bf16[384,2048]{1,0:T(8,128)(2,1)}, u32[]{:S(2)}, u32[]{:S(2)}) collective-permute-start(bf16[384,2048]{1,0:T(8,128)(2,1)} %get-tuple-element.119), channel_id=1, source_target_pairs={{0,16},{8,24},{16,0},{24,8},{1,17},{9,25},{17,1},{25,9},{2,18},{10... | collective-permute-start | bytes 4718600 | tf_op jit(solution)/shard_map/ppermute | solution.py:294
  583.2 70.4 %collective-permute-start.37 = (bf16[384,2048]{1,0:T(8,128)(2,1)}, bf16[384,2048]{1,0:T(8,128)(2,1)}, u32[]{:S(2)}, u32[]{:S(2)}) collective-permute-start(bf16[384,2048]{1,0:T(8,128)(2,1)} %get-tuple-element.118), channel_id=1, source_target_pairs={{0,24},{8,16},{16,8},{24,0},{1,25},{9,17},{17,9},{25,1},{2,26},{10... | collective-permute-start | bytes 4718600 | tf_op jit(solution)/shard_map/ppermute | solution.py:294
  596.8 88.8 %collective-permute-start.27 = (bf16[384,2048]{1,0:T(8,128)(2,1)}, bf16[384,2048]{1,0:T(8,128)(2,1)}, u32[]{:S(2)}, u32[]{:S(2)}) collective-permute-start(bf16[384,2048]{1,0:T(8,128)(2,1)} %get-tuple-element.120), channel_id=1, source_target_pairs={{0,8},{8,0},{16,24},{24,16},{1,9},{9,1},{17,25},{25,17},{2,10},{10... | collective-permute-start | bytes 4718600 | tf_op jit(solution)/shard_map/ppermute | solution.py:294
  598.3 122.1 %collective-permute-start.28 = (bf16[384,2048]{1,0:T(8,128)(2,1)}, bf16[384,2048]{1,0:T(8,128)(2,1)}, u32[]{:S(2)}, u32[]{:S(2)}) collective-permute-start(bf16[384,2048]{1,0:T(8,128)(2,1)} %get-tuple-element.122), channel_id=1, source_target_pairs={{0,16},{8,24},{16,0},{24,8},{1,17},{9,25},{17,1},{25,9},{2,18},{10... | collective-permute-start | bytes 4718600 | tf_op jit(solution)/shard_map/ppermute | solution.py:294
  618.2 102.2 %collective-permute-start.29 = (bf16[384,2048]{1,0:T(8,128)(2,1)}, bf16[384,2048]{1,0:T(8,128)(2,1)}, u32[]{:S(2)}, u32[]{:S(2)}) collective-permute-start(bf16[384,2048]{1,0:T(8,128)(2,1)} %get-tuple-element.121), channel_id=1, source_target_pairs={{0,24},{8,16},{16,8},{24,0},{1,25},{9,17},{17,9},{25,1},{2,26},{10... | collective-permute-start | bytes 4718600 | tf_op jit(solution)/shard_map/ppermute | solution.py:294
  773.5 291.6 %reduce-scatter.9.cloned.1.call-start = ((), (), s32[]{:S(2)}) async-start(), calls=%async_computation.9 | async-start | bytes 4718592 | tf_op jit(solution)/shard_map/reduce_scatter | solution.py:498
  841.8 223.3 %reduce-scatter.11.cloned.1.call-start = ((), (), s32[]{:S(2)}) async-start(), calls=%async_computation.10 | async-start | bytes 4718592 | tf_op jit(solution)/shard_map/reduce_scatter | solution.py:498
  875.6 214.5 %reduce-scatter.13.cloned.1.call-start = ((), (), s32[]{:S(2)}) async-start(), calls=%async_computation.11 | async-start | bytes 1310720 | tf_op jit(solution)/shard_map/reduce_scatter | solution.py:312
  884.1 87.8 %collective-permute-start.58 = (bf16[1024,2048]{1,0:T(8,128)(2,1)}, bf16[1024,2048]{1,0:T(8,128)(2,1)}, u32[]{:S(2)}, u32[]{:S(2)}) collective-permute-start(bf16[1024,2048]{1,0:T(8,128)(2,1)} %convolution_convert_fusion.2), channel_id=1, source_target_pairs={{0,1},{1,0},{2,3},{3,2},{4,5},{5,4},{6,7},{7,6},{8,9},{9,8},{10,11... | collective-permute-start | bytes 12582920 | tf_op jit(solution)/shard_map/ppermute | solution.py:291
  979.0 81.8 %collective-permute-start.59 = (bf16[1024,512]{1,0:T(8,128)(2,1)}, bf16[1024,512]{1,0:T(8,128)(2,1)}, u32[]{:S(2)}, u32[]{:S(2)}) collective-permute-start(bf16[1024,512]{1,0:T(8,128)(2,1)} %get-tuple-element.109), channel_id=1, source_target_pairs={{0,8},{8,0},{16,24},{24,16},{1,9},{9,1},{17,25},{25,17},{2,10},{10... | collective-permute-start | bytes 3145736 | tf_op jit(solution)/shard_map/ppermute | solution.py:294
  982.3 78.5 %collective-permute-start.60 = (bf16[1024,512]{1,0:T(8,128)(2,1)}, bf16[1024,512]{1,0:T(8,128)(2,1)}, u32[]{:S(2)}, u32[]{:S(2)}) collective-permute-start(bf16[1024,512]{1,0:T(8,128)(2,1)} %get-tuple-element.111), channel_id=1, source_target_pairs={{0,16},{8,24},{16,0},{24,8},{1,17},{9,25},{17,1},{25,9},{2,18},{10... | collective-permute-start | bytes 3145736 | tf_op jit(solution)/shard_map/ppermute | solution.py:294
  1008.3 52.5 %collective-permute-start.61 = (bf16[1024,512]{1,0:T(8,128)(2,1)}, bf16[1024,512]{1,0:T(8,128)(2,1)}, u32[]{:S(2)}, u32[]{:S(2)}) collective-permute-start(bf16[1024,512]{1,0:T(8,128)(2,1)} %get-tuple-element.110), channel_id=1, source_target_pairs={{0,24},{8,16},{16,8},{24,0},{1,25},{9,17},{17,9},{25,1},{2,26},{10... | collective-permute-start | bytes 3145736 | tf_op jit(solution)/shard_map/ppermute | solution.py:294
  (147 other events, 3167.0 us)
Sparse Core Ops, SparseCore 0:
  9.6 30.6 all-gather.8
  42.5 46.2 all-gather.12
  90.9 45.6 all-gather.14
  138.7 45.6 all-gather.16
  185.8 173.2 all-gather.10
  519.6 55.5 reduce-scatter.16
  577.5 93.3 reduce-scatter.14
  773.6 61.3 reduce-scatter.6
  841.9 48.4 reduce-scatter.8
  892.6 48.3 reduce-scatter.10
  1065.2 24.8 reduce-scatter.12

commit v2 on v1

--- a/solution.py
+++ b/solution.py
@@ -282,6 +282,10 @@
     )
 
 
+def after(x, *needed):
+    return lax.optimization_barrier((x, *needed))[0]
+
+
 def make_body(dp_size, tensor_size):
     zs = tensor_size // 2
     z_groups = [[2 * z + core for z in range(zs)] for core in range(2)]
@@ -299,10 +303,13 @@
     def dp_relative(x):
         return [x] + [to_dp(x, k) for k in range(1, dp_size)]
 
-    def dp_total(pick):
+    def exchange(send, pick, size):
+        return [pick(0)] + [send(pick(k), k) for k in range(1, size)]
+
+    def total_of(send, pick, size):
         own = pick(0).astype(jnp.float32)
-        for k in range(1, dp_size):
-            own = own + to_dp(pick(k).astype(jnp.bfloat16), k).astype(jnp.float32)
+        for k in range(1, size):
+            own = own + send(pick(k).astype(jnp.bfloat16), k).astype(jnp.float32)
         return own
 
     def z_gather(x):
@@ -344,7 +351,6 @@
         core_at = tensor_at % 2
         z_at = tensor_at // 2
         seqs, rows, width = hidden_in.shape
-        tokens = seqs * rows
         length = buckets.shape[0]
         feats = w_query.shape[0]
         inner = w_query.shape[1]
@@ -354,8 +360,19 @@
         part = ff // dp_size
         table_rows = bias_table.shape[0]
         bucket_count = table_rows * dp_size
+        pad_rows = -table_rows % 16
         gain_one = gain_attn.astype(jnp.float32)
         gain_two = gain_ffn.astype(jnp.float32)
+        every = range(seqs)
+
+        def feature_block(x, k):
+            return lax.dynamic_slice_in_dim(x, (dp_at ^ k) * feats, feats, 1)
+
+        x_rows = [hidden_in[s].astype(jnp.float32) for s in every]
+        first_norm = [rms_parts(x, gain_one) for x in x_rows]
+        norm_full = [
+            lax.all_gather(first_norm[s][2], "tensor", axis=0, tiled=True) for s in every
+        ]
 
         qkv_local = jnp.concatenate(
             [
@@ -365,11 +382,10 @@
             ],
             axis=1,
         )
-        pad_rows = -table_rows % 16
         table_pad = jnp.pad(bias_table, ((0, pad_rows), (0, 3 * inner - heads)))
-        payload = reorder(
-            dp_relative(jnp.concatenate([qkv_local, table_pad], axis=0)), dp_at
-        )
+        payload = dp_relative(jnp.concatenate([qkv_local, table_pad], axis=0))
+        arrived = payload[1:]
+        payload = reorder(payload, dp_at)
         w_qkv = jnp.concatenate([p[:feats] for p in payload], axis=0)
         table = jnp.concatenate(
             [p[feats : feats + table_rows, :heads] for p in payload], axis=0
@@ -380,192 +396,239 @@
             jnp.pad(table.astype(jnp.float32).T, ((0, 0), (0, LANES - bucket_count))),
         )
 
-        x_rows = hidden_in.astype(jnp.float32)
-        plain_one, inv_one, norm_one = rms_parts(x_rows, gain_one)
-        norm_full = [
-            lax.all_gather(norm_one[s], "tensor", axis=0, tiled=True) for s in range(seqs)
-        ]
-
-        out_z = z_gather(w_out)
-        out_own = jnp.concatenate(reorder(dp_relative(out_z), dp_at), axis=1)
-        out_other = to_core(out_own)
+        out_z = jnp.concatenate(reorder(exchange(to_z, lambda k: w_out, zs), z_at), axis=0)
 
         ffn_local = jnp.stack([w_gate.T, w_up.T, w_down]).reshape(3, dp_size, part, feats)
-
-        def ffn_block(k):
-            return lax.dynamic_index_in_dim(ffn_local, dp_at ^ k, 1, keepdims=False)
-
-        ffn_parts = [ffn_block(0)] + [to_dp(ffn_block(k), k) for k in range(1, dp_size)]
-        ffn_rows = jnp.concatenate(reorder(ffn_parts, dp_at), axis=2).reshape(3 * part, width)
-        ffn_all = z_gather(ffn_rows).reshape(zs, 3, part, width)
-        ffn_all = jnp.transpose(ffn_all, (1, 0, 2, 3)).reshape(3 * ff, width)
-        w_pre = ffn_all[: 2 * ff]
-        w_post = ffn_all[2 * ff :]
+        ffn_local = after(ffn_local, *arrived)
+        ffn_parts = exchange(
+            to_dp,
+            lambda k: lax.dynamic_index_in_dim(ffn_local, dp_at ^ k, 1, keepdims=False),
+            dp_size,
+        )
+        arrived = ffn_parts[1:]
+        ffn_parts = reorder(ffn_parts, dp_at)
+        pre_rows = jnp.concatenate([p[:2] for p in ffn_parts], axis=2)
+        post_rows = jnp.concatenate([p[2] for p in ffn_parts], axis=1)
+        pre_gathered = z_gather(pre_rows.reshape(2 * part, width))
+        post_gathered = z_gather(post_rows)
+
+        out_parts = dp_relative(after(out_z, *arrived))
+
+        def group_rows(x):
+            own = jnp.concatenate(dp_relative(x), axis=0)
+            return jnp.concatenate([own, to_core(own)], axis=0)
 
         def context_to_tokens(context):
             blocks = context.reshape(zs, 2, rows, inner)
             own = lax.dynamic_index_in_dim(blocks, core_at, 1, keepdims=False)
             got = to_core(lax.dynamic_index_in_dim(blocks, 1 - core_at, 1, keepdims=False))
             both = jnp.concatenate([own, got], axis=-1)
-            moved = [lax.dynamic_index_in_dim(both, z_at, 0, keepdims=False)]
-            for k in range(1, zs):
-                moved.append(
-                    to_z(lax.dynamic_index_in_dim(both, z_at ^ k, 0, keepdims=False), k)
-                )
+            swapped = got
+            moved = exchange(
+                to_z,
+                lambda k: lax.dynamic_index_in_dim(both, z_at ^ k, 0, keepdims=False),
+                zs,
+            )
             moved = reorder(moved, z_at)
             return (
                 jnp.concatenate([m[:, :inner] for m in moved], axis=1),
                 jnp.concatenate([m[:, inner:] for m in moved], axis=1),
+                swapped,
             )
 
         def tokens_to_context(own, other):
             pair = jnp.stack(reorder([own, to_core(other)], core_at))
-
-            def block(k):
-                return lax.dynamic_slice_in_dim(pair, (z_at ^ k) * inner, inner, 2)
-
-            moved = [block(0)] + [to_z(block(k), k) for k in range(1, zs)]
+            moved = exchange(
+                to_z,
+                lambda k: lax.dynamic_slice_in_dim(pair, (z_at ^ k) * inner, inner, 2),
+                zs,
+            )
             return jnp.stack(reorder(moved, z_at)).reshape(length, inner)
 
-        qkv_all, lse_all, ctx_own, ctx_other = [], [], [], []
-        for s in range(seqs):
-            qkv = nn_dot(norm_full[s], w_qkv).astype(jnp.bfloat16)
+        qkv_all, lse_all, ctx_own, ctx_other, swaps = [], [], [], [], []
+        mid_rows, second_norm, norm_two_full, cot_full = [], [], [], []
+
+        def feed_forward_input(s):
+            mid = x_rows[s] + (nn_dot(ctx_own[s], out_own) + nn_dot(ctx_other[s], out_other))
+            mid_rows.append(mid)
+            second_norm.append(rms_parts(mid, gain_two))
+            norm_two_full.append(group_rows(second_norm[s][2]))
+
+        for s in every:
+            source = norm_full[s]
+            if s > 0:
+                source = after(source, swaps[s - 1])
+            if s > 1:
+                source = after(source, second_norm[s - 2][2])
+            qkv = nn_dot(source, w_qkv).astype(jnp.bfloat16)
             context, lse = attention_forward(qkv, bias_t)
-            own, other = context_to_tokens(context)
+            if s == 0:
+                out_parts = after(tuple(out_parts), context)
+                out_own = jnp.concatenate(reorder(out_parts, dp_at), axis=1)
+                out_other = to_core(out_own)
+            own, other, swapped = context_to_tokens(context)
             qkv_all.append(qkv)
             lse_all.append(lse)
             ctx_own.append(own)
             ctx_other.append(other)
-        ctx_own = jnp.concatenate(ctx_own, axis=0)
-        ctx_other = jnp.concatenate(ctx_other, axis=0)
-        attn_rows = nn_dot(ctx_own, out_own) + nn_dot(ctx_other, out_other)
-        x_flat = x_rows.reshape(tokens, width)
-        mid_rows = x_flat + attn_rows
-        plain_two, inv_two, norm_two = rms_parts(mid_rows, gain_two)
-
-        def group_rows(x):
-            own = jnp.concatenate(dp_relative(x), axis=0)
-            return (own, to_core(own))
-
-        def group_total(own, other):
+            swaps.append(swapped)
+            cot_full.append(group_rows(after(out_grad[s], context)))
+            if s > 0:
+                feed_forward_input(s - 1)
+        feed_forward_input(seqs - 1)
+
+        pre_gathered, w_post = after((pre_gathered, post_gathered), norm_two_full[-1])
+        w_pre = jnp.transpose(
+            pre_gathered.reshape(zs, 2, part, width), (1, 0, 2, 3)
+        ).reshape(2 * ff, width)
+        half = dp_size * rows
+
+        def group_total(partial, count):
+            own = partial[: dp_size * count]
+            other = partial[dp_size * count :]
             own = own + to_core(other.astype(jnp.bfloat16)).astype(jnp.float32)
-            return dp_total(lambda k: own[k * tokens : (k + 1) * tokens])
-
-        cot_halves = group_rows(out_grad.reshape(tokens, width))
-        norm_halves = group_rows(norm_two)
-        out_parts, back_parts, hidden_halves, pre_halves = [], [], [], []
-        for norm_half, cot_half in zip(norm_halves, cot_halves):
-            pre = nt_dot(norm_half, w_pre)
-            hidden, pull = jax.vjp(gelu_gate, pre[:, :ff], pre[:, ff:])
-            hidden = hidden.astype(jnp.bfloat16)
-            grad_gate, grad_up = pull(nt_dot(cot_half, w_post))
+            return total_of(to_dp, lambda k: own[k * count : (k + 1) * count], dp_size)
+
+        first_parts, hidden_all = [], []
+        grad_post = None
+        for s in every:
+            pre = nt_dot(norm_two_full[s], w_pre)
+            hidden = gelu_gate(pre[:, :ff], pre[:, ff:]).astype(jnp.bfloat16)
+            first_parts.append(pre)
+            hidden_all.append(hidden)
+            more = tn_dot(hidden, cot_full[s])
+            grad_post = more if grad_post is None else grad_post + more
+        grad_post = grad_post.astype(jnp.bfloat16)
+        pre_all, grad_norm_two = [], []
+        ready = grad_post
+        for s in every:
+            pre = first_parts[s]
+            _, pull = jax.vjp(gelu_gate, pre[:, :ff], pre[:, ff:])
+            grad_gate, grad_up = pull(nt_dot(after(cot_full[s], ready), w_post))
             grad_pre = jnp.concatenate([grad_gate, grad_up], axis=1).astype(jnp.bfloat16)
-            out_parts.append(nn_dot(hidden, w_post))
-            back_parts.append(nn_dot(grad_pre, w_pre))
-            hidden_halves.append(hidden)
-            pre_halves.append(grad_pre)
-        grad_post = tn_dot(hidden_halves[0], cot_halves[0]) + tn_dot(
-            hidden_halves[1], cot_halves[1]
-        )
-        grad_first = tn_dot(pre_halves[0], norm_halves[0]) + tn_dot(
-            pre_halves[1], norm_halves[1]
-        )
-        grad_norm_two = group_total(*back_parts)
-        post_z = z_scatter(grad_post.astype(jnp.bfloat16))
-        first_z = z_scatter(
+            ready = nn_dot(grad_pre, w_pre)
+            grad_norm_two.append(group_total(ready, rows))
+            pre_all.append(grad_pre)
+        grad_pre_w = None
+        for s in every:
+            more = tn_dot(after(pre_all[s], ready), norm_two_full[s])
+            grad_pre_w = more if grad_pre_w is None else grad_pre_w + more
+        grad_pre_w = grad_pre_w.astype(jnp.bfloat16)
+        post_z = z_scatter(grad_post)
+        pre_z = z_scatter(
             jnp.transpose(
-                grad_first.astype(jnp.bfloat16).reshape(2, zs, part, width), (1, 0, 2, 3)
+                grad_pre_w.reshape(2, zs, part, width), (1, 0, 2, 3)
             ).reshape(zs * 2 * part, width)
         )
-        output = (mid_rows + group_total(*out_parts)).astype(jnp.bfloat16)
-
-        grad_gain_two = jnp.sum(grad_norm_two * plain_two, axis=0)
-        grad_mid = out_grad.reshape(tokens, width).astype(jnp.float32) + rms_back(
-            grad_norm_two, plain_two, inv_two, gain_two
-        )
-        grad_mid_low = grad_mid.astype(jnp.bfloat16)
-        back_own = nt_dot(grad_mid_low, out_own).astype(jnp.bfloat16)
-        back_other = nt_dot(grad_mid_low, out_other).astype(jnp.bfloat16)
-        grad_norm_one, grad_qkv, grad_scores = [], None, []
-        for s in range(seqs):
-            at = slice(s * rows, (s + 1) * rows)
-            grad_context = tokens_to_context(back_own[at], back_other[at])
+
+        grad_mid, grad_mid_low, gain_two_sum = [], [], None
+        for s in every:
+            plain, inv, _ = second_norm[s]
+            more = jnp.sum(grad_norm_two[s] * plain, axis=0)
+            gain_two_sum = more if gain_two_sum is None else gain_two_sum + more
+            grad = out_grad[s].astype(jnp.float32) + rms_back(
+                grad_norm_two[s], plain, inv, gain_two
+            )
+            grad_mid.append(grad)
+            grad_mid_low.append(grad.astype(jnp.bfloat16))
+
+        grad_normed, grad_qkv, grad_scores = [], None, []
+        for s in every:
+            back_own = nt_dot(grad_mid_low[s], out_own).astype(jnp.bfloat16)
+            back_other = nt_dot(grad_mid_low[s], out_other).astype(jnp.bfloat16)
+            grad_context = tokens_to_context(back_own, back_other)
+            if s == 0:
+                grad_context = after(grad_context, grad_pre_w)
             grad_proj, grad_score = attention_backward(
                 qkv_all[s], grad_context, bias_t, lse_all[s]
             )
             grad_scores.append(grad_score)
-            grad_norm_one.append(
+            normed_part = nt_dot(grad_proj, w_qkv).astype(jnp.bfloat16)
+            grad_normed.append(
                 lax.psum_scatter(
-                    nt_dot(grad_proj, w_qkv).astype(jnp.bfloat16),
-                    "tensor",
-                    scatter_dimension=0,
-                    tiled=True,
+                    normed_part, "tensor", scatter_dimension=0, tiled=True
                 ).astype(jnp.float32)
             )
-            more = tn_dot(norm_full[s], grad_proj)
+            more = tn_dot(norm_full[s], after(grad_proj, normed_part))
             grad_qkv = more if grad_qkv is None else grad_qkv + more
 
-        grad_out_own = tn_dot(ctx_own, grad_mid_low)
-        grad_out_other = tn_dot(ctx_other, grad_mid_low)
-        grad_out_own = grad_out_own + to_core(grad_out_other.astype(jnp.bfloat16)).astype(
+        mid_low = after(jnp.concatenate(grad_mid_low, axis=0), grad_qkv)
+        grad_out_own = tn_dot(jnp.concatenate(ctx_own, axis=0), mid_low)
+        grad_out_other = tn_dot(jnp.concatenate(ctx_other, axis=0), mid_low)
+        grad_out_sum = grad_out_own + to_core(grad_out_other.astype(jnp.bfloat16)).astype(
             jnp.float32
         )
-        grad_out = z_scatter(
-            dp_total(
-                lambda k: lax.dynamic_slice_in_dim(grad_out_own, (dp_at ^ k) * feats, feats, 1)
-            ).astype(jnp.bfloat16)
-        ).astype(jnp.float32)
+        grad_out_z = total_of(to_dp, lambda k: feature_block(grad_out_sum, k), dp_size)
+        grad_out = total_of(
+            to_z,
+            lambda k: lax.dynamic_slice_in_dim(grad_out_z, (z_at ^ k) * inner, inner, 0),
+            zs,
+        )
+
+        hidden_own = jnp.concatenate([h[:half] for h in hidden_all], axis=0)
+        hidden_other = jnp.concatenate([h[half:] for h in hidden_all], axis=0)
+        hidden_own, hidden_other = (
+            after(hidden_own, grad_out_other, grad_out_own),
+            after(hidden_other, grad_out_other),
+        )
+        sent = to_core(nn_dot(hidden_other, w_post).astype(jnp.bfloat16))
+        own = (nn_dot(hidden_own, w_post) + sent.astype(jnp.float32)).reshape(
+            seqs, dp_size, rows, width
+        )
+        ffn_out = total_of(to_dp, lambda k: own[:, k], dp_size)
+        output = jnp.stack(
+            [(mid_rows[s] + ffn_out[s]).astype(jnp.bfloat16) for s in every]
+        )
 
         def ffn_grad(z_rows, mats):
-            def block(k):
-                return lax.dynamic_slice_in_dim(z_rows, (dp_at ^ k) * feats, feats, 1)
-
-            moved = [block(0)] + [to_dp(block(k), k) for k in range(1, dp_size)]
+            moved = exchange(to_dp, lambda k: feature_block(z_rows, k), dp_size)
             moved = jnp.stack(reorder(moved, dp_at)).reshape(dp_size, mats, part, feats)
             return [moved[:, m].reshape(ff, feats).astype(jnp.float32) for m in range(mats)]
 
         (grad_down,) = ffn_grad(post_z, 1)
-        grad_gate_t, grad_up_t = ffn_grad(first_z, 2)
-
-        table_grad = bucket_sums(buckets_t, grad_scores, bucket_count)
-
-        def qkv_block(k):
-            at = dp_at ^ k
-            return jnp.concatenate(
-                [
-                    lax.dynamic_slice_in_dim(grad_qkv, at * feats, feats, 0),
-                    jnp.pad(
-                        lax.dynamic_slice_in_dim(table_grad, at * table_rows, table_rows, 0),
-                        ((0, pad_rows), (0, 3 * inner - heads)),
-                    ),
-                ],
-                axis=0,
-            )
-
-        summed = dp_total(qkv_block)
-        grad_table = summed[feats : feats + table_rows, :heads]
+        grad_gate_t, grad_up_t = ffn_grad(pre_z, 2)
+
+        summed = total_of(
+            to_dp,
+            lambda k: lax.dynamic_slice_in_dim(grad_qkv, (dp_at ^ k) * feats, feats, 0),
+            dp_size,
+        )
 
         def columns(which):
             return jnp.concatenate(
                 [
-                    summed[:feats, (3 * p + which) * LANES : (3 * p + which + 1) * LANES]
+                    summed[:, (3 * p + which) * LANES : (3 * p + which + 1) * LANES]
                     for p in range(pairs)
                 ],
                 axis=1,
             )
 
-        grad_norm_one = jnp.stack(grad_norm_one)
-        grad_gain_one = jnp.sum(grad_norm_one * plain_one, axis=(0, 1))
-        grad_in = (
-            grad_mid.reshape(seqs, rows, width)
-            + rms_back(grad_norm_one, plain_one, inv_one, gain_one)
-        ).astype(jnp.bfloat16)
-        gains = all_sum(jnp.stack([grad_gain_one, grad_gain_two]))
+        table_grad = bucket_sums(after(buckets_t, own), grad_scores, bucket_count)
+        grad_table = total_of(
+            to_dp,
+            lambda k: lax.dynamic_slice_in_dim(
+                table_grad, (dp_at ^ k) * table_rows, table_rows, 0
+            ),
+            dp_size,
+        )
+
+        grad_in, gain_one_sum = [], None
+        for s in every:
+            plain, inv, _ = first_norm[s]
+            more = jnp.sum(grad_normed[s] * plain, axis=0)
+            gain_one_sum = more if gain_one_sum is None else gain_one_sum + more
+            grad_in.append(
+                (grad_mid[s] + rms_back(grad_normed[s], plain, inv, gain_one)).astype(
+                    jnp.bfloat16
+                )
+            )
+        gain_two_sum = all_sum(gain_two_sum)
+        gain_one_sum = all_sum(gain_one_sum)
         return (
-            output.reshape(seqs, rows, width),
-            grad_in,
-            gains[0],
-            gains[1],
+            output,
+            jnp.stack(grad_in),
+            gain_one_sum,
+            gain_two_sum,
             columns(0),
             columns(1),
             columns(2),

time: 1110 us -> 1200 us (1.081)
  local copies, waits for them, and re-layouts: 64.6 us -> 107 us
  waiting for transfers between devices: 478 us -> 446 us
  starting transfers between devices: 95.2 us -> 119 us
  matrix products: 209 us -> 231 us
  other arithmetic: 67.9 us -> 87.8 us
    ppermute x35 -> x58, waiting for transfers between devices: 369 us -> 311 us  [to_dp(): return lax.ppermute(x, 'dp', xor_pairs(dp_size, mask))]
    ppermute x18 -> x24, waiting for transfers between devices: 83.6 us -> 112 us  [to_z(): return lax.ppermute(x, 'tensor', xor_pairs(tensor_size, 2 * mask))]
    unnamed x221 -> x436, local copies, waits for them, and re-layouts: 27.5 us -> 52.5 us
    ppermute x35 -> x58, starting transfers between devices: 46.1 us -> 69.9 us  [to_dp(): return lax.ppermute(x, 'dp', xor_pairs(dp_size, mask))]
    dot_general x9 -> x15, matrix products: 69.6 us -> 88.1 us  [nt_dot(): lax.dot_general(left, right, (((1,), (1,)), ((), ())), preferred_element_...]
    another operation x1 -> x8, other arithmetic: 0.02 us -> 18.2 us  [body(): gains = all_sum(jnp.stack([grad_gain_one, grad_gain_two]))]
    ppermute x3 -> x6, waiting for transfers between devices: 5.97 us -> 19.3 us  [all_sum(): x = x + lax.ppermute(x, 'tensor', xor_pairs(tensor_size, bit))]
    convert_element_type x4, other arithmetic: 16.4 us -> 3.69 us  [the longest x3 2.74 us: body(): hidden = gelu_gate(pre[:, :ff], pre[:, ff:]).astype(jnp.bfloat16)]
  transfers between devices with their start and end apart: 79 -> 116, of which waited for: 31 -> 50; matrix products, arithmetic and copies ran while one was open for 27% -> 31% of each run, Pallas kernels for 16% -> 15%
where the time goes in v2:
time: 1200 us; the launch traced here: 1190 us
  waiting for transfers between devices  446 us (37%)
  matrix products  231 us (19%)
  Pallas kernels  179 us (15%)
  starting transfers between devices  119 us (10%)
  local copies, waits for them, and re-layouts  107 us (9%)
  other arithmetic  87.8 us (7%)
  between operations  18 us (2%)
    ppermute x58, waiting for transfers between devices, to_dp(): return lax.ppermute(x, 'dp', xor_pairs(dp_size, mask))  311 us
    ppermute x24, waiting for transfers between devices, to_z(): return lax.ppermute(x, 'tensor', xor_pairs(tensor_size, 2 * mask))  112 us
    dot_general x15, matrix products, nt_dot(): lax.dot_general(left, right, (((1,), (1,)), ((), ())), preferred_element_...  88.1 us
    dot_general x14, matrix products, nn_dot(): return jnp.dot(left, right, preferred_element_type=jnp.float32)  74.1 us
    ppermute x58, starting transfers between devices, to_dp(): return lax.ppermute(x, 'dp', xor_pairs(dp_size, mask))  69.9 us
    dot_general x11, matrix products, tn_dot(): lax.dot_general(left, right, (((0,), (0,)), ((), ())), preferred_element_...  68.7 us
    pallas_call x3, Pallas kernels, attention_backward(): pl.pallas_call(functools.partial(backward_kernel, min(256, length)), grid...  58.1 us
    pallas_call x1, Pallas kernels, bucket_sums(): pl.pallas_call(functools.partial(histogram_kernel, bucket_count, 4), grid...  55.6 us
  transfers between devices with their start and end apart: 116, of which 50 were waited for; matrix products, arithmetic and copies ran while one was open for 31% of the time, Pallas kernels for 15%

profile of v2, /device:TPU:0, one launch (start us, length us, event | category | flops | bytes accessed | tf_op | source)
XLA Modules:
  0.0 1187.7 jit_solution(13826275479545064681)
XLA Ops:
  26.1 12.7 %collective-permute-done.2 = bf16[528,768]{1,0:T(8,128)(2,1)} collective-permute-done((bf16[528,768]{1,0:T(8,128)(2,1)}, bf16[528,768]{1,0:T(8,128)(2,1)}, u32[]{:S(2)}, u32[]{:S(2)}) %collective-permute-start.2) | collective-permute-done | bytes 811040 | tf_op jit(solution)/shard_map/ppermute | solution.py:298
  38.8 18.0 %collective-permute-done.1 = bf16[528,768]{1,0:T(8,128)(2,1)} collective-permute-done((bf16[528,768]{1,0:T(8,128)(2,1)}, bf16[528,768]{1,0:T(8,128)(2,1)}, u32[]{:S(2)}, u32[]{:S(2)}) %collective-permute-start.1) | collective-permute-done | bytes 811040 | tf_op jit(solution)/shard_map/ppermute | solution.py:298
  61.5 11.8 collective-permute-done.12
  96.9 23.1 %collective-permute-done.8 = bf16[256,512]{1,0:T(8,128)(2,1)} collective-permute-done((bf16[256,512]{1,0:T(8,128)(2,1)S(1)}, bf16[256,512]{1,0:T(8,128)(2,1)}, u32[]{:S(2)}, u32[]{:S(2)}) %collective-permute-start.8) | collective-permute-done | bytes 262176 | tf_op jit(solution)/shard_map/ppermute | solution.py:301
  136.2 14.2 %expand_bias.1.bias_ref = bf16[4,1024,1024]{2,1,0:T(8,128)(2,1)} custom-call(s32[1024,1024]{1,0:T(8,128)} %bitcast.332, f32[4,128]{1,0:T(4,128)} %pad_convert_fusion.table_ref), custom_call_target="tpu_custom_call" | custom-call | flops 33554432 | bytes 12582912 | tf_op jit(solution)/shard_map/expand_bias/pallas_call | solution.py:50
  161.8 16.9 %attention_forward.3 = (bf16[1024,256]{1,0:T(8,128)(2,1)S(1)}, f32[2,2,1024]{2,1,0:T(2,128)S(1)}) custom-call(bf16[1024,768]{1,0:T(8,128)(2,1)S(1)} %convolution_convert_fusion.6.qkv_ref, bf16[4,1024,1024]{2,1,0:T(8,128)(2,1)} %expand_bias.1.bias_ref), custom_call_target="tpu_custom_call" | custom-call | flops 4294967296 | bytes 10485760 | tf_op jit(solution)/shard_map/attention_forward/pallas_call | solution.py:95
  181.6 18.8 %collective-permute-done.14 = bf16[1024,512]{1,0:T(8,128)(2,1)} collective-permute-done((bf16[1024,512]{1,0:T(8,128)(2,1)}, bf16[1024,512]{1,0:T(8,128)(2,1)}, u32[]{:S(2)}, u32[]{:S(2)}) %collective-permute-start.14) | collective-permute-done | bytes 1048608 | tf_op jit(solution)/shard_map/ppermute | solution.py:298
  206.2 9.5 collective-permute-start.6
  223.9 17.1 %attention_forward.4 = (bf16[1024,256]{1,0:T(8,128)(2,1)S(1)}, f32[2,2,1024]{2,1,0:T(2,128)S(1)}) custom-call(bf16[1024,768]{1,0:T(8,128)(2,1)S(1)} %convolution_convert_fusion.5.qkv_ref, bf16[4,1024,1024]{2,1,0:T(8,128)(2,1)} %expand_bias.1.bias_ref), custom_call_target="tpu_custom_call" | custom-call | flops 4294967296 | bytes 10485760 | tf_op jit(solution)/shard_map/attention_forward/pallas_call | solution.py:95
  278.4 15.1 %collective-permute-done.31 = bf16[128,512]{1,0:T(8,128)(2,1)} collective-permute-done((bf16[128,512]{1,0:T(8,128)(2,1)}, bf16[128,512]{1,0:T(8,128)(2,1)}, u32[]{:S(2)}, u32[]{:S(2)}) %collective-permute-start.31) | collective-permute-done | bytes 131104 | tf_op jit(solution)/shard_map/ppermute | solution.py:301
  316.2 17.0 %attention_forward.5 = (bf16[1024,256]{1,0:T(8,128)(2,1)S(1)}, f32[2,2,1024]{2,1,0:T(2,128)S(1)}) custom-call(bf16[1024,768]{1,0:T(8,128)(2,1)S(1)} %convolution_convert_fusion.4.qkv_ref, bf16[4,1024,1024]{2,1,0:T(8,128)(2,1)} %expand_bias.1.bias_ref), custom_call_target="tpu_custom_call" | custom-call | flops 4294967296 | bytes 10485760 | tf_op jit(solution)/shard_map/attention_forward/pallas_call | solution.py:95
  352.0 10.2 collective-permute-done.24
  386.8 20.8 %collective-permute-done.28 = bf16[128,2048]{1,0:T(8,128)(2,1)S(1)} collective-permute-done((bf16[128,2048]{1,0:T(8,128)(2,1)S(1)}, bf16[128,2048]{1,0:T(8,128)(2,1)S(1)}, u32[]{:S(2)}, u32[]{:S(2)}) %collective-permute-start.28) | collective-permute-done | bytes 524320 | tf_op jit(solution)/shard_map/ppermute | solution.py:298
  409.0 18.5 %collective-permute-done.27 = bf16[128,2048]{1,0:T(8,128)(2,1)S(1)} collective-permute-done((bf16[128,2048]{1,0:T(8,128)(2,1)S(1)}, bf16[128,2048]{1,0:T(8,128)(2,1)S(1)}, u32[]{:S(2)}, u32[]{:S(2)}) %collective-permute-start.27) | collective-permute-done | bytes 524320 | tf_op jit(solution)/shard_map/ppermute | solution.py:298
  444.6 9.6 fusion.273
  490.8 9.5 fusion.9
  509.9 10.5 fusion.16
  565.2 11.4 add_convert_fusion
  602.4 10.7 collective-permute-done.52
  625.0 10.7 collective-permute-done.56
  637.7 9.6 collective-permute-done.58
  647.3 9.9 collective-permute-done.60
  692.2 19.3 %attention_backward.3 = (bf16[1024,768]{1,0:T(8,128)(2,1)S(1)}, bf16[4,1024,1024]{2,1,0:T(8,128)(2,1)}) custom-call(bf16[1024,768]{1,0:T(8,128)(2,1)S(1)} %copy-done.3, bf16[1024,256]{1,0:T(8,128)(2,1)S(1)} %bitcast.330, bf16[4,1024,1024]{2,1,0:T(8,128)(2,1)} %expand_bias.1.bias_ref, f32[2,2,1024]{2,1,0:T(2,128)S(1)} %get-tuple-element.76.lse_ref), custom_call_target="tpu_custom_call" | custom-call | flops 10737418240 | bytes 20971520 | tf_op jit(solution)/shard_map/attention_backward/pallas_call | solution.py:165
  769.6 12.0 %collective-permute-done.67 = bf16[2,128,256]{2,1,0:T(8,128)(2,1)S(1)} collective-permute-done((bf16[2,128,256]{2,1,0:T(8,128)(2,1)S(1)}, bf16[2,128,256]{2,1,0:T(8,128)(2,1)S(1)}, u32[]{:S(2)}, u32[]{:S(2)}) %collective-permute-start.67) | collective-permute-done | bytes 131104 | tf_op jit(solution)/shard_map/ppermute | solution.py:301
  781.9 19.7 %attention_backward.4 = (bf16[1024,768]{1,0:T(8,128)(2,1)S(1)}, bf16[4,1024,1024]{2,1,0:T(8,128)(2,1)}) custom-call(bf16[1024,768]{1,0:T(8,128)(2,1)S(1)} %copy-done.1, bf16[1024,256]{1,0:T(8,128)(2,1)S(1)} %bitcast.331, bf16[4,1024,1024]{2,1,0:T(8,128)(2,1)} %expand_bias.1.bias_ref, f32[2,2,1024]{2,1,0:T(2,128)S(1)} %get-tuple-element.79.lse_ref), custom_call_target="tpu_custom_call" | custom-call | flops 10737418240 | bytes 20971520 | tf_op jit(solution)/shard_map/attention_backward/pallas_call | solution.py:165
  809.5 19.1 %attention_backward.5 = (bf16[1024,768]{1,0:T(8,128)(2,1)S(1)}, bf16[4,1024,1024]{2,1,0:T(8,128)(2,1)}) custom-call(bf16[1024,768]{1,0:T(8,128)(2,1)S(1)} %copy-done.5, bf16[1024,256]{1,0:T(8,128)(2,1)S(1)} %bitcast.329, bf16[4,1024,1024]{2,1,0:T(8,128)(2,1)} %expand_bias.1.bias_ref, f32[2,2,1024]{2,1,0:T(2,128)S(1)} %get-tuple-element.82.lse_ref), custom_call_target="tpu_custom_call" | custom-call | flops 10737418240 | bytes 20971520 | tf_op jit(solution)/shard_map/attention_backward/pallas_call | solution.py:165
  861.0 10.1 collective-permute-done.82
  913.5 16.3 %collective-permute-done.89 = bf16[512,768]{0,1:T(8,128)(2,1)} collective-permute-done((bf16[512,768]{0,1:T(8,128)(2,1)}, bf16[512,768]{0,1:T(8,128)(2,1)}, u32[]{:S(2)}, u32[]{:S(2)}) %collective-permute-start.89) | collective-permute-done | bytes 786464 | tf_op jit(solution)/shard_map/ppermute | solution.py:298
  935.9 41.0 %collective-permute-done.101 = bf16[160,512]{1,0:T(8,128)(2,1)S(1)} collective-permute-done((bf16[160,512]{1,0:T(8,128)(2,1)S(1)}, bf16[160,512]{1,0:T(8,128)(2,1)S(1)}, u32[]{:S(2)}, u32[]{:S(2)}) %collective-permute-start.101) | collective-permute-done | bytes 163872 | tf_op jit(solution)/shard_map/ppermute | solution.py:298
  992.7 9.9 convert_add_fusion
  1002.6 55.6 %bucket_sums.1 = f32[4,32,8,128]{3,2,1,0:T(8,128)S(1)} custom-call(s32[1024,1024]{1,0:T(8,128)} %bitcast.333, bf16[4,1024,1024]{2,1,0:T(8,128)(2,1)} %get-tuple-element.89.refs_0_, bf16[4,1024,1024]{2,1,0:T(8,128)(2,1)} %get-tuple-element.90.refs_1_, bf16[4,1024,1024]{2,1,0:T(8,128)(2,1)} %get-tuple-element.91.refs_2_), custom_call_target="tpu_custom_call" | custom-call | flops 8053063680 | bytes 29360128 | tf_op jit(solution)/shard_map/bucket_sums/pallas_call | solution.py:229
  1085.6 60.2 %collective-permute-done.98 = bf16[320,512]{1,0:T(8,128)(2,1)S(1)} collective-permute-done((bf16[320,512]{1,0:T(8,128)(2,1)S(1)}, bf16[320,512]{1,0:T(8,128)(2,1)S(1)}, u32[]{:S(2)}, u32[]{:S(2)}) %collective-permute-start.98) | collective-permute-done | bytes 327712 | tf_op jit(solution)/shard_map/ppermute | solution.py:298
  (867 shorter events, 600.9 us)
Async XLA Ops:
  7.2 148.2 %all-gather.6.cloned.1.call-start = ((), (), s32[]{:S(2)}) async-start(), calls=%async_computation.5 | async-start | bytes 4718592 | tf_op jit(solution)/shard_map/all_gather | solution.py:374
  11.9 194.3 %all-gather.14.cloned.1.call-start = ((), (), s32[]{:S(2)}) async-start(), calls=%async_computation.9 | async-start | bytes 4718592 | tf_op jit(solution)/shard_map/all_gather | solution.py:374
  12.7 265.7 %all-gather.12.cloned.1.call-start = ((), (), s32[]{:S(2)}) async-start(), calls=%async_computation.8 | async-start | bytes 4718592 | tf_op jit(solution)/shard_map/all_gather | solution.py:374
  13.4 428.3 %all-gather.10.cloned.1.call-start = ((), (), s32[]{:S(2)}) async-start(), calls=%async_computation.7 | async-start | bytes 3276800 | tf_op jit(solution)/shard_map/all_gather | solution.py:316
  85.4 356.3 %all-gather.8.cloned.1.call-start = ((), (), s32[]{:S(2)}) async-start(), calls=%async_computation.6 | async-start | bytes 6553600 | tf_op jit(solution)/shard_map/all_gather | solution.py:316
  152.7 47.6 %collective-permute-start.14 = (bf16[1024,512]{1,0:T(8,128)(2,1)}, bf16[1024,512]{1,0:T(8,128)(2,1)}, u32[]{:S(2)}, u32[]{:S(2)}) collective-permute-start(bf16[1024,512]{1,0:T(8,128)(2,1)} %pad_maximum_fusion.19), channel_id=1, source_target_pairs={{0,16},{8,24},{16,0},{24,8},{1,17},{9,25},{17,1},{25,9},{2,18},{10... | collective-permute-start | bytes 3145736 | tf_op jit(solution)/shard_map/ppermute | solution.py:298
  155.3 739.6 %reduce-scatter.14.cloned.1.call-start = ((), (), s32[]{:S(2)}) async-start(), calls=%async_computation.14 | async-start | bytes 3276800 | tf_op jit(solution)/shard_map/reduce_scatter | solution.py:319
  178.7 81.6 %collective-permute-start.39 = (bf16[128,2048]{1,0:T(8,128)(2,1)S(1)}, bf16[128,2048]{1,0:T(8,128)(2,1)}, u32[]{:S(2)}, u32[]{:S(2)}) collective-permute-start(bf16[128,2048]{1,0:T(8,128)(2,1)S(1)} %copy-done.42), channel_id=1, source_target_pairs={{0,24},{8,16},{16,8},{24,0},{1,25},{9,17},{17,9},{25,1},{2,26},{10... | collective-permute-start | bytes 1572872 | tf_op jit(solution)/shard_map/ppermute | solution.py:298
  181.0 81.9 %collective-permute-start.38 = (bf16[128,2048]{1,0:T(8,128)(2,1)S(1)}, bf16[128,2048]{1,0:T(8,128)(2,1)}, u32[]{:S(2)}, u32[]{:S(2)}) collective-permute-start(bf16[128,2048]{1,0:T(8,128)(2,1)S(1)} %copy-done.42), channel_id=1, source_target_pairs={{0,16},{8,24},{16,0},{24,8},{1,17},{9,25},{17,1},{25,9},{2,18},{10... | collective-permute-start | bytes 1572872 | tf_op jit(solution)/shard_map/ppermute | solution.py:298
  243.4 60.5 %collective-permute-start.16 = (bf16[1024,2048]{1,0:T(8,128)(2,1)}, bf16[1024,2048]{1,0:T(8,128)(2,1)}, u32[]{:S(2)}, u32[]{:S(2)}) collective-permute-start(bf16[1024,2048]{1,0:T(8,128)(2,1)} %pad_maximum_fusion), channel_id=1, source_target_pairs={{0,1},{1,0},{2,3},{3,2},{4,5},{5,4},{6,7},{7,6},{8,9},{9,8},{10,11... | collective-permute-start | bytes 12582920 | tf_op jit(solution)/shard_map/ppermute | solution.py:295
  309.8 63.0 %collective-permute-start.19 = (bf16[128,2048]{1,0:T(8,128)(2,1)S(1)}, bf16[128,2048]{1,0:T(8,128)(2,1)S(1)}, u32[]{:S(2)}, u32[]{:S(2)}) collective-permute-start(bf16[128,2048]{1,0:T(8,128)(2,1)S(1)} %get-tuple-element.175), channel_id=1, source_target_pairs={{0,24},{8,16},{16,8},{24,0},{1,25},{9,17},{17,9},{25,1},{2,26},{10... | collective-permute-start | bytes 1572872 | tf_op jit(solution)/shard_map/ppermute | solution.py:298
  312.2 62.3 %collective-permute-start.18 = (bf16[128,2048]{1,0:T(8,128)(2,1)S(1)}, bf16[128,2048]{1,0:T(8,128)(2,1)S(1)}, u32[]{:S(2)}, u32[]{:S(2)}) collective-permute-start(bf16[128,2048]{1,0:T(8,128)(2,1)S(1)} %get-tuple-element.175), channel_id=1, source_target_pairs={{0,16},{8,24},{16,0},{24,8},{1,17},{9,25},{17,1},{25,9},{2,18},{10... | collective-permute-start | bytes 1572872 | tf_op jit(solution)/shard_map/ppermute | solution.py:298
  372.8 57.4 %collective-permute-start.35 = (bf16[128,2048]{1,0:T(8,128)(2,1)S(1)}, bf16[128,2048]{1,0:T(8,128)(2,1)S(1)}, u32[]{:S(2)}, u32[]{:S(2)}) collective-permute-start(bf16[128,2048]{1,0:T(8,128)(2,1)S(1)} %get-tuple-element.177), channel_id=1, source_target_pairs={{0,24},{8,16},{16,8},{24,0},{1,25},{9,17},{17,9},{25,1},{2,26},{10... | collective-permute-start | bytes 1572872 | tf_op jit(solution)/shard_map/ppermute | solution.py:298
  374.4 55.9 %collective-permute-start.34 = (bf16[128,2048]{1,0:T(8,128)(2,1)S(1)}, bf16[128,2048]{1,0:T(8,128)(2,1)S(1)}, u32[]{:S(2)}, u32[]{:S(2)}) collective-permute-start(bf16[128,2048]{1,0:T(8,128)(2,1)S(1)} %get-tuple-element.177), channel_id=1, source_target_pairs={{0,16},{8,24},{16,0},{24,8},{1,17},{9,25},{17,1},{25,9},{2,18},{10... | collective-permute-start | bytes 1572872 | tf_op jit(solution)/shard_map/ppermute | solution.py:298
  490.7 574.0 %reduce-scatter.12.cloned.1.call-start = ((), (), s32[]{:S(2)}) async-start(), calls=%async_computation.13 | async-start | bytes 6553600 | tf_op jit(solution)/shard_map/reduce_scatter | solution.py:319
  527.7 55.2 %collective-permute-start.49 = (bf16[512,2048]{1,0:T(8,128)(2,1)}, bf16[512,2048]{1,0:T(8,128)(2,1)}, u32[]{:S(2)}, u32[]{:S(2)}) collective-permute-start(bf16[512,2048]{1,0:T(8,128)(2,1)} %slice.633), channel_id=1, source_target_pairs={{0,1},{1,0},{2,3},{3,2},{4,5},{5,4},{6,7},{7,6},{8,9},{9,8},{10,11... | collective-permute-start | bytes 6291464 | tf_op jit(solution)/shard_map/ppermute | solution.py:295
  538.0 52.9 %collective-permute-start.53 = (bf16[512,2048]{1,0:T(8,128)(2,1)}, bf16[512,2048]{1,0:T(8,128)(2,1)}, u32[]{:S(2)}, u32[]{:S(2)}) collective-permute-start(bf16[512,2048]{1,0:T(8,128)(2,1)} %slice.632), channel_id=1, source_target_pairs={{0,1},{1,0},{2,3},{3,2},{4,5},{5,4},{6,7},{7,6},{8,9},{9,8},{10,11... | collective-permute-start | bytes 6291464 | tf_op jit(solution)/shard_map/ppermute | solution.py:295
  579.4 577.5 %reduce-scatter.6.cloned.1.call-start = ((), (), s32[]{:S(2)}) async-start(), calls=%async_computation.10 | async-start | bytes 4718592 | tf_op jit(solution)/shard_map/reduce_scatter | solution.py:548
  718.2 438.8 %reduce-scatter.8.cloned.1.call-start = ((), (), s32[]{:S(2)}) async-start(), calls=%async_computation.11 | async-start | bytes 4718592 | tf_op jit(solution)/shard_map/reduce_scatter | solution.py:548
  808.1 348.9 %reduce-scatter.10.cloned.1.call-start = ((), (), s32[]{:S(2)}) async-start(), calls=%async_computation.12 | async-start | bytes 4718592 | tf_op jit(solution)/shard_map/reduce_scatter | solution.py:548
  860.5 132.2 %collective-permute-start.73 = (bf16[1536,2048]{1,0:T(8,128)(2,1)}, bf16[1536,2048]{1,0:T(8,128)(2,1)}, u32[]{:S(2)}, u32[]{:S(2)}) collective-permute-start(bf16[1536,2048]{1,0:T(8,128)(2,1)} %convolution_convert_fusion), channel_id=1, source_target_pairs={{0,1},{1,0},{2,3},{3,2},{4,5},{5,4},{6,7},{7,6},{8,9},{9,8},{10,11... | collective-permute-start | bytes 18874376 | tf_op jit(solution)/shard_map/ppermute | solution.py:295
  912.0 72.5 %collective-permute-start.91 = (bf16[1024,512]{1,0:T(8,128)(2,1)}, bf16[1024,512]{1,0:T(8,128)(2,1)}, u32[]{:S(2)}, u32[]{:S(2)}) collective-permute-start(bf16[1024,512]{1,0:T(8,128)(2,1)} %get-tuple-element.186), channel_id=1, source_target_pairs={{0,8},{8,0},{16,24},{24,16},{1,9},{9,1},{17,25},{25,17},{2,10},{10... | collective-permute-start | bytes 3145736 | tf_op jit(solution)/shard_map/ppermute | solution.py:298
  929.8 54.8 %collective-permute-start.93 = (bf16[1024,512]{1,0:T(8,128)(2,1)}, bf16[1024,512]{1,0:T(8,128)(2,1)}, u32[]{:S(2)}, u32[]{:S(2)}) collective-permute-start(bf16[1024,512]{1,0:T(8,128)(2,1)} %get-tuple-element.187), channel_id=1, source_target_pairs={{0,24},{8,16},{16,8},{24,0},{1,25},{9,17},{17,9},{25,1},{2,26},{10... | collective-permute-start | bytes 3145736 | tf_op jit(solution)/shard_map/ppermute | solution.py:298
  931.4 53.2 %collective-permute-start.92 = (bf16[1024,512]{1,0:T(8,128)(2,1)S(1)}, bf16[1024,512]{1,0:T(8,128)(2,1)}, u32[]{:S(2)}, u32[]{:S(2)}) collective-permute-start(bf16[1024,512]{1,0:T(8,128)(2,1)S(1)} %get-tuple-element.188), channel_id=1, source_target_pairs={{0,16},{8,24},{16,0},{24,8},{1,17},{9,25},{17,1},{25,9},{2,18},{10... | collective-permute-start | bytes 3145736 | tf_op jit(solution)/shard_map/ppermute | solution.py:298
  988.7 79.4 %collective-permute-start.94 = (bf16[256,512]{1,0:T(8,128)(2,1)}, bf16[256,512]{1,0:T(8,128)(2,1)}, u32[]{:S(2)}, u32[]{:S(2)}) collective-permute-start(bf16[256,512]{1,0:T(8,128)(2,1)} %get-tuple-element.220), channel_id=1, source_target_pairs={{0,2},{1,3},{2,0},{3,1},{4,6},{5,7},{6,4},{7,5},{8,10},{9,11},{10,... | collective-permute-start | bytes 786440 | tf_op jit(solution)/shard_map/ppermute | solution.py:301
  990.0 79.7 %collective-permute-start.96 = (bf16[256,512]{1,0:T(8,128)(2,1)}, bf16[256,512]{1,0:T(8,128)(2,1)}, u32[]{:S(2)}, u32[]{:S(2)}) collective-permute-start(bf16[256,512]{1,0:T(8,128)(2,1)} %get-tuple-element.221), channel_id=1, source_target_pairs={{0,6},{1,7},{2,4},{3,5},{4,2},{5,3},{6,0},{7,1},{8,14},{9,15},{10,... | collective-permute-start | bytes 786440 | tf_op jit(solution)/shard_map/ppermute | solution.py:301
  992.4 78.4 %collective-permute-start.95 = (bf16[256,512]{1,0:T(8,128)(2,1)S(1)}, bf16[256,512]{1,0:T(8,128)(2,1)}, u32[]{:S(2)}, u32[]{:S(2)}) collective-permute-start(bf16[256,512]{1,0:T(8,128)(2,1)S(1)} %get-tuple-element.222), channel_id=1, source_target_pairs={{0,4},{1,5},{2,6},{3,7},{4,0},{5,1},{6,2},{7,3},{8,12},{9,13},{10,... | collective-permute-start | bytes 786440 | tf_op jit(solution)/shard_map/ppermute | solution.py:301
  1070.7 80.0 %collective-permute-start.74 = (bf16[3,128,2048]{2,1,0:T(8,128)(2,1)}, bf16[3,128,2048]{2,1,0:T(8,128)(2,1)}, u32[]{:S(2)}, u32[]{:S(2)}) collective-permute-start(bf16[3,128,2048]{2,1,0:T(8,128)(2,1)} %get-tuple-element.198), channel_id=1, source_target_pairs={{0,8},{8,0},{16,24},{24,16},{1,9},{9,1},{17,25},{25,17},{2,10},{10... | collective-permute-start | bytes 4718600 | tf_op jit(solution)/shard_map/ppermute | solution.py:298
  1076.7 74.1 %collective-permute-start.76 = (bf16[3,128,2048]{2,1,0:T(8,128)(2,1)}, bf16[3,128,2048]{2,1,0:T(8,128)(2,1)}, u32[]{:S(2)}, u32[]{:S(2)}) collective-permute-start(bf16[3,128,2048]{2,1,0:T(8,128)(2,1)} %get-tuple-element.199), channel_id=1, source_target_pairs={{0,24},{8,16},{16,8},{24,0},{1,25},{9,17},{17,9},{25,1},{2,26},{10... | collective-permute-start | bytes 4718600 | tf_op jit(solution)/shard_map/ppermute | solution.py:298
  1078.3 72.5 %collective-permute-start.75 = (bf16[3,128,2048]{2,1,0:T(8,128)(2,1)}, bf16[3,128,2048]{2,1,0:T(8,128)(2,1)}, u32[]{:S(2)}, u32[]{:S(2)}) collective-permute-start(bf16[3,128,2048]{2,1,0:T(8,128)(2,1)} %get-tuple-element.200), channel_id=1, source_target_pairs={{0,16},{8,24},{16,0},{24,8},{1,17},{9,25},{17,1},{25,9},{2,18},{10... | collective-permute-start | bytes 4718600 | tf_op jit(solution)/shard_map/ppermute | solution.py:298
  1080.5 65.2 %collective-permute-start.98 = (bf16[320,512]{1,0:T(8,128)(2,1)S(1)}, bf16[320,512]{1,0:T(8,128)(2,1)S(1)}, u32[]{:S(2)}, u32[]{:S(2)}) collective-permute-start(bf16[320,512]{1,0:T(8,128)(2,1)S(1)} %get-tuple-element.253), channel_id=1, source_target_pairs={{0,16},{8,24},{16,0},{24,8},{1,17},{9,25},{17,1},{25,9},{2,18},{10... | collective-permute-start | bytes 983048 | tf_op jit(solution)/shard_map/ppermute | solution.py:298
  1081.6 64.2 %collective-permute-start.97 = (bf16[320,512]{1,0:T(8,128)(2,1)S(1)}, bf16[320,512]{1,0:T(8,128)(2,1)S(1)}, u32[]{:S(2)}, u32[]{:S(2)}) collective-permute-start(bf16[320,512]{1,0:T(8,128)(2,1)S(1)} %get-tuple-element.254), channel_id=1, source_target_pairs={{0,24},{8,16},{16,8},{24,0},{1,25},{9,17},{17,9},{25,1},{2,26},{10... | collective-permute-start | bytes 983048 | tf_op jit(solution)/shard_map/ppermute | solution.py:298
  (282 other events, 3892.1 us)
Sparse Core Ops, SparseCore 0:
  12.0 49.5 all-gather.5
  63.8 66.3 all-gather.13
  132.4 45.5 all-gather.11
  179.5 64.6 all-gather.9
  246.2 119.0 all-gather.7
  490.8 52.1 reduce-scatter.13
  579.6 93.8 reduce-scatter.11
  718.3 66.9 reduce-scatter.5
  808.2 51.0 reduce-scatter.7
  887.3 51.0 reduce-scatter.9

commit v3 on v2

--- a/solution.py
+++ b/solution.py
@@ -236,7 +236,7 @@
         scratch_shapes=[pltpu.VMEM((heads, block, length), jnp.float32)],
         compiler_params=pltpu.CompilerParams(vmem_limit_bytes=VMEM_ROOM),
         cost_estimate=pl.CostEstimate(
-            flops=60 * bucket_count * heads * length * length,
+            flops=2 * heads * length * length,
             bytes_accessed=length * length * (4 + 2 * heads * len(grad_scores)),
             transcendentals=0,
         ),
@@ -360,7 +360,6 @@
         part = ff // dp_size
         table_rows = bias_table.shape[0]
         bucket_count = table_rows * dp_size
-        pad_rows = -table_rows % 16
         gain_one = gain_attn.astype(jnp.float32)
         gain_two = gain_ffn.astype(jnp.float32)
         every = range(seqs)
@@ -382,21 +381,19 @@
             ],
             axis=1,
         )
-        table_pad = jnp.pad(bias_table, ((0, pad_rows), (0, 3 * inner - heads)))
-        payload = dp_relative(jnp.concatenate([qkv_local, table_pad], axis=0))
-        arrived = payload[1:]
-        payload = reorder(payload, dp_at)
-        w_qkv = jnp.concatenate([p[:feats] for p in payload], axis=0)
-        table = jnp.concatenate(
-            [p[feats : feats + table_rows, :heads] for p in payload], axis=0
-        )
+        table = jnp.concatenate(reorder(dp_relative(bias_table), dp_at), axis=0)
         buckets_t = buckets.T
         bias_t = expand_bias(
             buckets_t,
             jnp.pad(table.astype(jnp.float32).T, ((0, 0), (0, LANES - bucket_count))),
         )
-
-        out_z = jnp.concatenate(reorder(exchange(to_z, lambda k: w_out, zs), z_at), axis=0)
+        payload = dp_relative(after(qkv_local, table))
+        arrived = payload[1:]
+        payload = after(tuple(payload), bias_t)
+        w_qkv = jnp.concatenate(reorder(payload, dp_at), axis=0)
+
+        out_z = after(tuple(exchange(to_z, lambda k: w_out, zs)), w_qkv)
+        out_z = jnp.concatenate(reorder(out_z, z_at), axis=0)
 
         ffn_local = jnp.stack([w_gate.T, w_up.T, w_down]).reshape(3, dp_size, part, feats)
         ffn_local = after(ffn_local, *arrived)
@@ -406,11 +403,10 @@
             dp_size,
         )
         arrived = ffn_parts[1:]
-        ffn_parts = reorder(ffn_parts, dp_at)
+        ffn_parts = reorder(after(tuple(ffn_parts), w_qkv), dp_at)
         pre_rows = jnp.concatenate([p[:2] for p in ffn_parts], axis=2)
         post_rows = jnp.concatenate([p[2] for p in ffn_parts], axis=1)
         pre_gathered = z_gather(pre_rows.reshape(2 * part, width))
-        post_gathered = z_gather(post_rows)
 
         out_parts = dp_relative(after(out_z, *arrived))
 
@@ -436,13 +432,17 @@
                 swapped,
             )
 
-        def tokens_to_context(own, other):
-            pair = jnp.stack(reorder([own, to_core(other)], core_at))
+        def send_tokens(own, other):
+            got = to_core(other)
+            pair = jnp.stack(reorder([own, got], core_at))
             moved = exchange(
                 to_z,
                 lambda k: lax.dynamic_slice_in_dim(pair, (z_at ^ k) * inner, inner, 2),
                 zs,
             )
+            return tuple(moved), got
+
+        def take_tokens(moved):
             return jnp.stack(reorder(moved, z_at)).reshape(length, inner)
 
         qkv_all, lse_all, ctx_own, ctx_other, swaps = [], [], [], [], []
@@ -463,16 +463,21 @@
             qkv = nn_dot(source, w_qkv).astype(jnp.bfloat16)
             context, lse = attention_forward(qkv, bias_t)
             if s == 0:
+                post_gathered = z_gather(after(post_rows, context))
                 out_parts = after(tuple(out_parts), context)
                 out_own = jnp.concatenate(reorder(out_parts, dp_at), axis=1)
                 out_other = to_core(out_own)
+                cot_parts = dp_relative(after(out_grad, *out_parts[1:]))
+            if s == seqs - 1:
+                cot_parts = after(tuple(cot_parts), context)
+                cot_own = jnp.concatenate([c[i] for i in every for c in cot_parts], axis=0)
+                cot_other = to_core(cot_own)
             own, other, swapped = context_to_tokens(context)
             qkv_all.append(qkv)
             lse_all.append(lse)
             ctx_own.append(own)
             ctx_other.append(other)
             swaps.append(swapped)
-            cot_full.append(group_rows(after(out_grad[s], context)))
             if s > 0:
                 feed_forward_input(s - 1)
         feed_forward_input(seqs - 1)
@@ -482,12 +487,13 @@
             pre_gathered.reshape(zs, 2, part, width), (1, 0, 2, 3)
         ).reshape(2 * ff, width)
         half = dp_size * rows
-
-        def group_total(partial, count):
-            own = partial[: dp_size * count]
-            other = partial[dp_size * count :]
-            own = own + to_core(other.astype(jnp.bfloat16)).astype(jnp.float32)
-            return total_of(to_dp, lambda k: own[k * count : (k + 1) * count], dp_size)
+        cot_full = [
+            jnp.concatenate(
+                [cot_own[s * half : (s + 1) * half], cot_other[s * half : (s + 1) * half]],
+                axis=0,
+            )
+            for s in every
+        ]
 
         first_parts, hidden_all = [], []
         grad_post = None
@@ -499,27 +505,60 @@
             more = tn_dot(hidden, cot_full[s])
             grad_post = more if grad_post is None else grad_post + more
         grad_post = grad_post.astype(jnp.bfloat16)
-        pre_all, grad_norm_two = [], []
+        pre_all, grad_norm_two, sums = [], [], []
         ready = grad_post
         for s in every:
             pre = first_parts[s]
             _, pull = jax.vjp(gelu_gate, pre[:, :ff], pre[:, ff:])
-            grad_gate, grad_up = pull(nt_dot(after(cot_full[s], ready), w_post))
+            cot = after(cot_full[s], ready)
+            if s > 1:
+                cot = after(cot, sums[s - 2])
+            grad_gate, grad_up = pull(nt_dot(cot, w_post))
             grad_pre = jnp.concatenate([grad_gate, grad_up], axis=1).astype(jnp.bfloat16)
             ready = nn_dot(grad_pre, w_pre)
-            grad_norm_two.append(group_total(ready, rows))
+            got = to_core(ready[half:].astype(jnp.bfloat16))
+            own = ready[:half] + got.astype(jnp.float32)
+            own = (own[:rows], own[rows:].astype(jnp.bfloat16))
+            grad_norm_two.append(
+                own[0]
+                + sum(
+                    to_dp(own[1][(k - 1) * rows : k * rows], k).astype(jnp.float32)
+                    for k in range(1, dp_size)
+                )
+            )
+            sums.append(got)
             pre_all.append(grad_pre)
+        post_z = z_scatter(grad_post)
         grad_pre_w = None
         for s in every:
-            more = tn_dot(after(pre_all[s], ready), norm_two_full[s])
+            grad_pre = after(pre_all[s], ready, sums[-1])
+            if s > 0:
+                grad_pre = after(grad_pre, grad_norm_two[s - 1])
+            if s == seqs - 1:
+                grad_pre = after(grad_pre, post_z)
+            more = tn_dot(grad_pre, norm_two_full[s])
             grad_pre_w = more if grad_pre_w is None else grad_pre_w + more
         grad_pre_w = grad_pre_w.astype(jnp.bfloat16)
-        post_z = z_scatter(grad_post)
         pre_z = z_scatter(
             jnp.transpose(
                 grad_pre_w.reshape(2, zs, part, width), (1, 0, 2, 3)
             ).reshape(zs * 2 * part, width)
         )
+
+        hidden_own = jnp.concatenate([h[:half] for h in hidden_all], axis=0)
+        hidden_other = jnp.concatenate([h[half:] for h in hidden_all], axis=0)
+        hidden_own, hidden_other = (
+            after(hidden_own, grad_pre_w),
+            after(hidden_other, grad_pre_w),
+        )
+        sent = to_core(nn_dot(hidden_other, w_post).astype(jnp.bfloat16))
+        own = (nn_dot(after(hidden_own, grad_norm_two[-1]), w_post) + sent.astype(jnp.float32)).reshape(
+            seqs, dp_size, rows, width
+        )
+        out_sent = [
+            to_dp(own[:, k].astype(jnp.bfloat16), k) for k in range(1, dp_size)
+        ]
+        ffn_own = own[:, 0]
 
         grad_mid, grad_mid_low, gain_two_sum = [], [], None
         for s in every:
@@ -532,61 +571,84 @@
             grad_mid.append(grad)
             grad_mid_low.append(grad.astype(jnp.bfloat16))
 
-        grad_normed, grad_qkv, grad_scores = [], None, []
+        moves, swapped_in = [], []
         for s in every:
             back_own = nt_dot(grad_mid_low[s], out_own).astype(jnp.bfloat16)
             back_other = nt_dot(grad_mid_low[s], out_other).astype(jnp.bfloat16)
-            grad_context = tokens_to_context(back_own, back_other)
-            if s == 0:
-                grad_context = after(grad_context, grad_pre_w)
+            moved, got = send_tokens(back_own, back_other)
+            moves.append(moved)
+            swapped_in.append(got)
+
+        def ffn_send(z_rows):
+            return tuple(exchange(to_dp, lambda k: feature_block(z_rows, k), dp_size))
+
+        def ffn_take(moved, mats):
+            moved = jnp.stack(reorder(moved, dp_at)).reshape(dp_size, mats, part, feats)
+            return [moved[:, m].reshape(ff, feats).astype(jnp.float32) for m in range(mats)]
+
+        post_moved = ffn_send(post_z)
+        grad_normed, grad_scores, normed_parts, qkv_grads = [], [], [], []
+        grad_qkv = None
+        gate = (grad_pre_w,)
+        for s in every:
+            moved = after(moves[s], *gate)
+            if s < seqs - 1:
+                moved = after(moved, swapped_in[s + 1])
+            if s == seqs - 1:
+                moved = after(moved, pre_z, *post_moved[1:])
             grad_proj, grad_score = attention_backward(
-                qkv_all[s], grad_context, bias_t, lse_all[s]
+                qkv_all[s], take_tokens(moved), bias_t, lse_all[s]
             )
             grad_scores.append(grad_score)
+            qkv_grads.append(grad_proj)
             normed_part = nt_dot(grad_proj, w_qkv).astype(jnp.bfloat16)
+            normed_parts.append(normed_part)
+            gate = (normed_part,)
             grad_normed.append(
                 lax.psum_scatter(
                     normed_part, "tensor", scatter_dimension=0, tiled=True
                 ).astype(jnp.float32)
             )
-            more = tn_dot(norm_full[s], after(grad_proj, normed_part))
-            grad_qkv = more if grad_qkv is None else grad_qkv + more
-
-        mid_low = after(jnp.concatenate(grad_mid_low, axis=0), grad_qkv)
-        grad_out_own = tn_dot(jnp.concatenate(ctx_own, axis=0), mid_low)
-        grad_out_other = tn_dot(jnp.concatenate(ctx_other, axis=0), mid_low)
-        grad_out_sum = grad_out_own + to_core(grad_out_other.astype(jnp.bfloat16)).astype(
-            jnp.float32
-        )
-        grad_out_z = total_of(to_dp, lambda k: feature_block(grad_out_sum, k), dp_size)
+            if s == 0:
+                mid_low = after(jnp.concatenate(grad_mid_low, axis=0), normed_part)
+                out_give = tn_dot(jnp.concatenate(ctx_other, axis=0), mid_low).astype(
+                    jnp.bfloat16
+                )
+                out_got = to_core(out_give)
+                out_keep = tn_dot(jnp.concatenate(ctx_own, axis=0), mid_low)
+                gate = gate + (out_give, out_keep)
+            else:
+                for t in [0, 1] if s == 1 else [s]:
+                    more = tn_dot(norm_full[t], after(qkv_grads[t], normed_part))
+                    grad_qkv = more if grad_qkv is None else grad_qkv + more
+                gate = gate + (grad_qkv,)
+            if s == 1:
+                out_sum = out_keep + after(out_got, normed_part).astype(jnp.float32)
+                out_moved = tuple(
+                    exchange(
+                        to_dp,
+                        lambda k: feature_block(out_sum, k)
+                        if k == 0
+                        else feature_block(out_sum, k).astype(jnp.bfloat16),
+                        dp_size,
+                    )
+                )
+        pre_moved = ffn_send(pre_z)
+        out_moved = after(out_moved, normed_parts[-1])
+        grad_out_z = sum(m.astype(jnp.float32) for m in out_moved)
         grad_out = total_of(
             to_z,
             lambda k: lax.dynamic_slice_in_dim(grad_out_z, (z_at ^ k) * inner, inner, 0),
             zs,
         )
-
-        hidden_own = jnp.concatenate([h[:half] for h in hidden_all], axis=0)
-        hidden_other = jnp.concatenate([h[half:] for h in hidden_all], axis=0)
-        hidden_own, hidden_other = (
-            after(hidden_own, grad_out_other, grad_out_own),
-            after(hidden_other, grad_out_other),
-        )
-        sent = to_core(nn_dot(hidden_other, w_post).astype(jnp.bfloat16))
-        own = (nn_dot(hidden_own, w_post) + sent.astype(jnp.float32)).reshape(
-            seqs, dp_size, rows, width
-        )
-        ffn_out = total_of(to_dp, lambda k: own[:, k], dp_size)
+        out_sent = after(tuple(out_sent), normed_parts[-1])
+        ffn_out = ffn_own + sum(m.astype(jnp.float32) for m in out_sent)
         output = jnp.stack(
             [(mid_rows[s] + ffn_out[s]).astype(jnp.bfloat16) for s in every]
         )
 
-        def ffn_grad(z_rows, mats):
-            moved = exchange(to_dp, lambda k: feature_block(z_rows, k), dp_size)
-            moved = jnp.stack(reorder(moved, dp_at)).reshape(dp_size, mats, part, feats)
-            return [moved[:, m].reshape(ff, feats).astype(jnp.float32) for m in range(mats)]
-
-        (grad_down,) = ffn_grad(post_z, 1)
-        grad_gate_t, grad_up_t = ffn_grad(pre_z, 2)
+        (grad_down,) = ffn_take(post_moved, 1)
+        grad_gate_t, grad_up_t = ffn_take(pre_moved, 2)
 
         summed = total_of(
             to_dp,
@@ -603,7 +665,9 @@
                 axis=1,
             )
 
-        table_grad = bucket_sums(after(buckets_t, own), grad_scores, bucket_count)
+        table_grad = bucket_sums(
+            after(buckets_t, grad_qkv, grad_normed[0]), grad_scores, bucket_count
+        )
         grad_table = total_of(
             to_dp,
             lambda k: lax.dynamic_slice_in_dim(
@@ -622,13 +686,12 @@
                     jnp.bfloat16
                 )
             )
-        gain_two_sum = all_sum(gain_two_sum)
-        gain_one_sum = all_sum(gain_one_sum)
+        gains = all_sum(jnp.stack([gain_one_sum, gain_two_sum]))
         return (
             output,
             jnp.stack(grad_in),
-            gain_one_sum,
-            gain_two_sum,
+            gains[0],
+            gains[1],
             columns(0),
             columns(1),
             columns(2),

time: 1200 us -> 1070 us (0.89)
  waiting for transfers between devices: 446 us -> 309 us
  starting transfers between devices: 119 us -> 132 us
    ppermute x58 -> x53, waiting for transfers between devices: 311 us -> 204 us  [to_dp(): return lax.ppermute(x, 'dp', xor_pairs(dp_size, mask))]
    ppermute x24, waiting for transfers between devices: 112 us -> 88.5 us  [to_z(): return lax.ppermute(x, 'tensor', xor_pairs(tensor_size, 2 * mask))]
    ppermute x24, starting transfers between devices: 37.8 us -> 54.6 us  [to_z(): return lax.ppermute(x, 'tensor', xor_pairs(tensor_size, 2 * mask))]
    ppermute x6 -> x3, waiting for transfers between devices: 19.3 us -> 3.98 us  [all_sum(): x = x + lax.ppermute(x, 'tensor', xor_pairs(tensor_size, bit))]
    add x0 -> x3, other arithmetic: none -> 14.4 us  [the longest x1 6.07 us: body(): ffn_out = ffn_own + sum((m.astype(jnp.float32) for m in out_sent))]
    unnamed x436 -> x396, local copies, waits for them, and re-layouts: 52.5 us -> 55 us
    ppermute x58 -> x53, starting transfers between devices: 69.9 us -> 67.9 us  [to_dp(): return lax.ppermute(x, 'dp', xor_pairs(dp_size, mask))]
  transfers between devices with their start and end apart: 116 -> 106, of which waited for: 50 -> 38; matrix products, arithmetic and copies ran while one was open for 31% -> 32% of each run, Pallas kernels for 15% -> 17%
where the time goes in v3:
time: 1070 us; the launch traced here: 1060 us
  waiting for transfers between devices  309 us (29%)
  matrix products  234 us (22%)
  Pallas kernels  179 us (17%)
  starting transfers between devices  132 us (12%)
  local copies, waits for them, and re-layouts  97.4 us (9%)
  other arithmetic  93.5 us (9%)
  between operations  18.1 us (2%)
    ppermute x53, waiting for transfers between devices, to_dp(): return lax.ppermute(x, 'dp', xor_pairs(dp_size, mask))  204 us
    ppermute x24, waiting for transfers between devices, to_z(): return lax.ppermute(x, 'tensor', xor_pairs(tensor_size, 2 * mask))  88.5 us
    dot_general x15, matrix products, nt_dot(): lax.dot_general(left, right, (((1,), (1,)), ((), ())), preferred_element_...  88.4 us
    dot_general x11, matrix products, tn_dot(): lax.dot_general(left, right, (((0,), (0,)), ((), ())), preferred_element_...  75.7 us
    dot_general x14, matrix products, nn_dot(): return jnp.dot(left, right, preferred_element_type=jnp.float32)  69.9 us
    ppermute x53, starting transfers between devices, to_dp(): return lax.ppermute(x, 'dp', xor_pairs(dp_size, mask))  67.9 us
    pallas_call x3, Pallas kernels, attention_backward(): pl.pallas_call(functools.partial(backward_kernel, min(256, length)), grid...  58.3 us
    pallas_call x1, Pallas kernels, bucket_sums(): pl.pallas_call(functools.partial(histogram_kernel, bucket_count, 4), grid...  55.8 us
  transfers between devices with their start and end apart: 106, of which 38 were waited for; matrix products, arithmetic and copies ran while one was open for 32% of the time, Pallas kernels for 17%

profile of v3, /device:TPU:0, one launch (start us, length us, event | category | flops | bytes accessed | tf_op | source)
XLA Modules:
  0.0 1062.3 jit_solution(1561146066567394206)
XLA Ops:
  35.4 14.0 %expand_bias.1.bias_ref = bf16[4,1024,1024]{2,1,0:T(8,128)(2,1)} custom-call(s32[1024,1024]{1,0:T(8,128)} %bitcast.355, f32[4,128]{1,0:T(4,128)} %pad_convert_fusion.table_ref), custom_call_target="tpu_custom_call" | custom-call | flops 33554432 | bytes 12582912 | tf_op jit(solution)/shard_map/expand_bias/pallas_call | solution.py:50
  49.3 9.5 collective-permute-done.4
  74.6 8.7 collective-permute-done.14
  90.3 19.7 %collective-permute-done.10 = bf16[256,512]{1,0:T(8,128)(2,1)S(1)} collective-permute-done((bf16[256,512]{1,0:T(8,128)(2,1)S(1)}, bf16[256,512]{1,0:T(8,128)(2,1)S(1)}, u32[]{:S(2)}, u32[]{:S(2)}) %collective-permute-start.10) | collective-permute-done | bytes 262176 | tf_op jit(solution)/shard_map/ppermute | solution.py:301
  110.0 10.8 %collective-permute-done.11 = bf16[256,512]{1,0:T(8,128)(2,1)S(1)} collective-permute-done((bf16[256,512]{1,0:T(8,128)(2,1)S(1)}, bf16[256,512]{1,0:T(8,128)(2,1)S(1)}, u32[]{:S(2)}, u32[]{:S(2)}) %collective-permute-start.11) | collective-permute-done | bytes 262176 | tf_op jit(solution)/shard_map/ppermute | solution.py:301
  136.9 17.2 %attention_forward.3 = (bf16[1024,256]{1,0:T(8,128)(2,1)S(1)}, f32[2,2,1024]{2,1,0:T(2,128)S(1)}) custom-call(bf16[1024,768]{1,0:T(8,128)(2,1)S(1)} %convolution_convert_fusion.7.qkv_ref, bf16[4,1024,1024]{2,1,0:T(8,128)(2,1)} %expand_bias.1.bias_ref), custom_call_target="tpu_custom_call" | custom-call | flops 4294967296 | bytes 10485760 | tf_op jit(solution)/shard_map/attention_forward/pallas_call | solution.py:95
  154.1 14.0 %collective-permute-done.17 = bf16[1024,512]{1,0:T(8,128)(2,1)} collective-permute-done((bf16[1024,512]{1,0:T(8,128)(2,1)S(1)}, bf16[1024,512]{1,0:T(8,128)(2,1)}, u32[]{:S(2)}, u32[]{:S(2)}) %collective-permute-start.17) | collective-permute-done | bytes 1048608 | tf_op jit(solution)/shard_map/ppermute | solution.py:298
  179.4 10.5 collective-permute-start.8
  196.4 16.7 %attention_forward.4 = (bf16[1024,256]{1,0:T(8,128)(2,1)S(1)}, f32[2,2,1024]{2,1,0:T(2,128)S(1)}) custom-call(bf16[1024,768]{1,0:T(8,128)(2,1)S(1)} %convolution_convert_fusion.6.qkv_ref, bf16[4,1024,1024]{2,1,0:T(8,128)(2,1)} %expand_bias.1.bias_ref), custom_call_target="tpu_custom_call" | custom-call | flops 4294967296 | bytes 10485760 | tf_op jit(solution)/shard_map/attention_forward/pallas_call | solution.py:95
  232.2 15.3 %collective-permute-done.34 = bf16[128,512]{1,0:T(8,128)(2,1)} collective-permute-done((bf16[128,512]{1,0:T(8,128)(2,1)}, bf16[128,512]{1,0:T(8,128)(2,1)}, u32[]{:S(2)}, u32[]{:S(2)}) %collective-permute-start.34) | collective-permute-done | bytes 131104 | tf_op jit(solution)/shard_map/ppermute | solution.py:301
  260.9 16.8 %attention_forward.5 = (bf16[1024,256]{1,0:T(8,128)(2,1)S(1)}, f32[2,2,1024]{2,1,0:T(2,128)S(1)}) custom-call(bf16[1024,768]{1,0:T(8,128)(2,1)S(1)} %convolution_convert_fusion.5.qkv_ref, bf16[4,1024,1024]{2,1,0:T(8,128)(2,1)} %expand_bias.1.bias_ref), custom_call_target="tpu_custom_call" | custom-call | flops 4294967296 | bytes 10485760 | tf_op jit(solution)/shard_map/attention_forward/pallas_call | solution.py:95
  277.7 24.7 %collective-permute-done.41 = bf16[3,128,2048]{2,1,0:T(8,128)(2,1)S(1)} collective-permute-done((bf16[3,128,2048]{2,1,0:T(8,128)(2,1)S(1)}, bf16[3,128,2048]{2,1,0:T(8,128)(2,1)S(1)}, u32[]{:S(2)}, u32[]{:S(2)}) %collective-permute-start.41) | collective-permute-done | bytes 1572896 | tf_op jit(solution)/shard_map/ppermute | solution.py:298
  327.5 20.2 %collective-permute-done.27 = bf16[128,512]{1,0:T(8,128)(2,1)S(1)} collective-permute-done((bf16[128,512]{1,0:T(8,128)(2,1)S(1)}, bf16[128,512]{1,0:T(8,128)(2,1)S(1)}, u32[]{:S(2)}, u32[]{:S(2)}) %collective-permute-start.27) | collective-permute-done | bytes 131104 | tf_op jit(solution)/shard_map/ppermute | solution.py:301
  380.3 33.2 %collective-permute-done.30 = bf16[128,2048]{1,0:T(8,128)(2,1)S(1)} collective-permute-done((bf16[128,2048]{1,0:T(8,128)(2,1)S(1)}, bf16[128,2048]{1,0:T(8,128)(2,1)S(1)}, u32[]{:S(2)}, u32[]{:S(2)}) %collective-permute-start.30) | collective-permute-done | bytes 524320 | tf_op jit(solution)/shard_map/ppermute | solution.py:298
  456.1 7.9 fusion.255
  488.0 9.5 fusion.7
  567.5 10.3 collective-permute-done.47
  579.8 8.0 collective-permute-done.50
  590.2 10.6 %fusion.258 = f32[1280,2048]{1,0:T(8,128)} fusion(bf16[1024,1280]{1,0:T(8,128)(2,1)S(1)} %copy-done.39, bf16[1024,2048]{1,0:T(8,128)(2,1)} %copy-done.128), kind=kOutput, calls=%fused_computation.621 | convolution fusion | flops 5368709120 | bytes 17301504 | tf_op jit(solution)/shard_map/dot_general | solution.py:280
  600.8 9.6 collective-permute-done.53
  610.4 11.5 %collective-permute-done.54 = bf16[128,2048]{1,0:T(8,128)(2,1)S(1)} collective-permute-done((bf16[128,2048]{1,0:T(8,128)(2,1)S(1)}, bf16[128,2048]{1,0:T(8,128)(2,1)S(1)}, u32[]{:S(2)}, u32[]{:S(2)}) %collective-permute-start.54) | collective-permute-done | bytes 524320 | tf_op jit(solution)/shard_map/ppermute | solution.py:298
  624.9 10.4 fusion.259
  635.3 13.2 %add_convert_fusion = bf16[1280,2048]{1,0:T(8,128)(2,1)S(1)} fusion(f32[1280,2048]{1,0:T(8,128)} %fusion.258, f32[1280,2048]{1,0:T(8,128)} %fusion.259, bf16[1024,1280]{1,0:T(8,128)(2,1)} %pad_maximum_fusion.4, bf16[1024,2048]{1,0:T(8,128)(2,1)} %constant_dynamic-update-slice_fusion.5), kind=kOutput, calls=%fused_computation.1 | convolution fusion | flops 5376573440 | bytes 33030144 | tf_op jit(solution)/shard_map/dot_general | solution.py:280
  692.5 19.6 %attention_backward.3 = (bf16[1024,768]{1,0:T(8,128)(2,1)S(1)}, bf16[4,1024,1024]{2,1,0:T(8,128)(2,1)}) custom-call(bf16[1024,768]{1,0:T(8,128)(2,1)S(1)} %copy-done.3, bf16[1024,256]{1,0:T(8,128)(2,1)S(1)} %bitcast.353, bf16[4,1024,1024]{2,1,0:T(8,128)(2,1)} %expand_bias.1.bias_ref, f32[2,2,1024]{2,1,0:T(2,128)S(1)} %get-tuple-element.158.lse_ref), custom_call_target="tpu_custom_call" | custom-call | flops 10737418240 | bytes 20971520 | tf_op jit(solution)/shard_map/attention_backward/pallas_call | solution.py:165
  732.7 19.0 %attention_backward.4 = (bf16[1024,768]{1,0:T(8,128)(2,1)S(1)}, bf16[4,1024,1024]{2,1,0:T(8,128)(2,1)}) custom-call(bf16[1024,768]{1,0:T(8,128)(2,1)S(1)} %copy-done.5, bf16[1024,256]{1,0:T(8,128)(2,1)S(1)} %bitcast.354, bf16[4,1024,1024]{2,1,0:T(8,128)(2,1)} %expand_bias.1.bias_ref, f32[2,2,1024]{2,1,0:T(2,128)S(1)} %get-tuple-element.169.lse_ref), custom_call_target="tpu_custom_call" | custom-call | flops 10737418240 | bytes 20971520 | tf_op jit(solution)/shard_map/attention_backward/pallas_call | solution.py:165
  770.4 7.9 collective-permute-start.61
  811.3 19.6 %attention_backward.5 = (bf16[1024,768]{1,0:T(8,128)(2,1)S(1)}, bf16[4,1024,1024]{2,1,0:T(8,128)(2,1)}) custom-call(bf16[1024,768]{1,0:T(8,128)(2,1)S(1)} %copy-done.1, bf16[1024,256]{1,0:T(8,128)(2,1)S(1)} %bitcast.352, bf16[4,1024,1024]{2,1,0:T(8,128)(2,1)} %expand_bias.1.bias_ref, f32[2,2,1024]{2,1,0:T(2,128)S(1)} %get-tuple-element.181.lse_ref), custom_call_target="tpu_custom_call" | custom-call | flops 10737418240 | bytes 20971520 | tf_op jit(solution)/shard_map/attention_backward/pallas_call | solution.py:165
  862.5 10.4 collective-permute-done.84
  880.6 55.8 %bucket_sums.1 = f32[4,32,8,128]{3,2,1,0:T(8,128)S(1)} custom-call(s32[1024,1024]{1,0:T(8,128)} %bitcast.356, bf16[4,1024,1024]{2,1,0:T(8,128)(2,1)} %get-tuple-element.193.refs_0_, bf16[4,1024,1024]{2,1,0:T(8,128)(2,1)} %get-tuple-element.194.refs_1_, bf16[4,1024,1024]{2,1,0:T(8,128)(2,1)} %get-tuple-element.195.refs_2_), custom_call_target="tpu_custom_call" | custom-call | flops 8388608 | bytes 29360128 | tf_op jit(solution)/shard_map/bucket_sums/pallas_call | solution.py:229
  946.7 14.2 %collective-permute-done.58 = bf16[3,128,2048]{2,1,0:T(8,128)(2,1)} collective-permute-done((bf16[3,128,2048]{2,1,0:T(8,128)(2,1)}, bf16[3,128,2048]{2,1,0:T(8,128)(2,1)}, u32[]{:S(2)}, u32[]{:S(2)}) %collective-permute-start.58) | collective-permute-done | bytes 1572896 | tf_op jit(solution)/shard_map/ppermute | solution.py:298
  1000.4 12.2 %collective-permute-done.80 = bf16[512,768]{0,1:T(8,128)(2,1)} collective-permute-done((bf16[512,768]{0,1:T(8,128)(2,1)}, bf16[512,768]{0,1:T(8,128)(2,1)}, u32[]{:S(2)}, u32[]{:S(2)}) %collective-permute-start.80) | collective-permute-done | bytes 786464 | tf_op jit(solution)/shard_map/ppermute | solution.py:298
  1013.1 8.9 collective-permute-done.82
  (782 shorter events, 554.2 us)
Async XLA Ops:
  7.2 123.2 %all-gather.6.cloned.1.call-start = ((), (), s32[]{:S(2)}) async-start(), calls=%async_computation.5 | async-start | bytes 4718592 | tf_op jit(solution)/shard_map/all_gather | solution.py:373
  11.3 178.6 %all-gather.14.cloned.1.call-start = ((), (), s32[]{:S(2)}) async-start(), calls=%async_computation.9 | async-start | bytes 4718592 | tf_op jit(solution)/shard_map/all_gather | solution.py:373
  12.1 216.5 %all-gather.12.cloned.1.call-start = ((), (), s32[]{:S(2)}) async-start(), calls=%async_computation.8 | async-start | bytes 4718592 | tf_op jit(solution)/shard_map/all_gather | solution.py:373
  12.8 418.5 %all-gather.8.cloned.1.call-start = ((), (), s32[]{:S(2)}) async-start(), calls=%async_computation.6 | async-start | bytes 6553600 | tf_op jit(solution)/shard_map/all_gather | solution.py:316
  85.6 345.7 %all-gather.10.cloned.1.call-start = ((), (), s32[]{:S(2)}) async-start(), calls=%async_computation.7 | async-start | bytes 3276800 | tf_op jit(solution)/shard_map/all_gather | solution.py:316
  124.7 43.5 %collective-permute-start.17 = (bf16[1024,512]{1,0:T(8,128)(2,1)S(1)}, bf16[1024,512]{1,0:T(8,128)(2,1)}, u32[]{:S(2)}, u32[]{:S(2)}) collective-permute-start(bf16[1024,512]{1,0:T(8,128)(2,1)S(1)} %pad_maximum_fusion.16), channel_id=1, source_target_pairs={{0,16},{8,24},{16,0},{24,8},{1,17},{9,25},{17,1},{25,9},{2,18},{10... | collective-permute-start | bytes 3145736 | tf_op jit(solution)/shard_map/ppermute | solution.py:298
  173.5 77.5 %collective-permute-start.19 = (bf16[1024,2048]{1,0:T(8,128)(2,1)}, bf16[1024,2048]{1,0:T(8,128)(2,1)}, u32[]{:S(2)}, u32[]{:S(2)}) collective-permute-start(bf16[1024,2048]{1,0:T(8,128)(2,1)} %pad_maximum_fusion), channel_id=1, source_target_pairs={{0,1},{1,0},{2,3},{3,2},{4,5},{5,4},{6,7},{7,6},{8,9},{9,8},{10,11... | collective-permute-start | bytes 12582920 | tf_op jit(solution)/shard_map/ppermute | solution.py:295
  174.9 102.8 %collective-permute-start.40 = (bf16[3,128,2048]{2,1,0:T(8,128)(2,1)S(1)}, bf16[3,128,2048]{2,1,0:T(8,128)(2,1)}, u32[]{:S(2)}, u32[]{:S(2)}) collective-permute-start(bf16[3,128,2048]{2,1,0:T(8,128)(2,1)S(1)} %copy-done.17), channel_id=1, source_target_pairs={{0,8},{8,0},{16,24},{24,16},{1,9},{9,1},{17,25},{25,17},{2,10},{10... | collective-permute-start | bytes 4718600 | tf_op jit(solution)/shard_map/ppermute | solution.py:298
  176.4 458.9 %reduce-scatter.6.cloned.1.call-start = ((), (), s32[]{:S(2)}) async-start(), calls=%async_computation.10 | async-start | bytes 3276800 | tf_op jit(solution)/shard_map/reduce_scatter | solution.py:319
  231.5 71.0 %collective-permute-start.41 = (bf16[3,128,2048]{2,1,0:T(8,128)(2,1)S(1)}, bf16[3,128,2048]{2,1,0:T(8,128)(2,1)S(1)}, u32[]{:S(2)}, u32[]{:S(2)}) collective-permute-start(bf16[3,128,2048]{2,1,0:T(8,128)(2,1)S(1)} %copy-done.17), channel_id=1, source_target_pairs={{0,16},{8,24},{16,0},{24,8},{1,17},{9,25},{17,1},{25,9},{2,18},{10... | collective-permute-start | bytes 4718600 | tf_op jit(solution)/shard_map/ppermute | solution.py:298
  247.5 54.9 %collective-permute-start.42 = (bf16[3,128,2048]{2,1,0:T(8,128)(2,1)S(1)}, bf16[3,128,2048]{2,1,0:T(8,128)(2,1)S(1)}, u32[]{:S(2)}, u32[]{:S(2)}) collective-permute-start(bf16[3,128,2048]{2,1,0:T(8,128)(2,1)S(1)} %copy-done.17), channel_id=1, source_target_pairs={{0,24},{8,16},{16,8},{24,0},{1,25},{9,17},{17,9},{25,1},{2,26},{10... | collective-permute-start | bytes 4718600 | tf_op jit(solution)/shard_map/ppermute | solution.py:298
  255.7 110.5 %collective-permute-start.20 = (bf16[128,2048]{1,0:T(8,128)(2,1)S(1)}, bf16[128,2048]{1,0:T(8,128)(2,1)S(1)}, u32[]{:S(2)}, u32[]{:S(2)}) collective-permute-start(bf16[128,2048]{1,0:T(8,128)(2,1)S(1)} %get-tuple-element.261), channel_id=1, source_target_pairs={{0,8},{8,0},{16,24},{24,16},{1,9},{9,1},{17,25},{25,17},{2,10},{10... | collective-permute-start | bytes 1572872 | tf_op jit(solution)/shard_map/ppermute | solution.py:298
  256.2 111.3 %collective-permute-start.21 = (bf16[128,2048]{1,0:T(8,128)(2,1)S(1)}, bf16[128,2048]{1,0:T(8,128)(2,1)S(1)}, u32[]{:S(2)}, u32[]{:S(2)}) collective-permute-start(bf16[128,2048]{1,0:T(8,128)(2,1)S(1)} %get-tuple-element.261), channel_id=1, source_target_pairs={{0,16},{8,24},{16,0},{24,8},{1,17},{9,25},{17,1},{25,9},{2,18},{10... | collective-permute-start | bytes 1572872 | tf_op jit(solution)/shard_map/ppermute | solution.py:298
  365.4 48.7 %collective-permute-start.36 = (bf16[128,2048]{1,0:T(8,128)(2,1)S(1)}, bf16[128,2048]{1,0:T(8,128)(2,1)S(1)}, u32[]{:S(2)}, u32[]{:S(2)}) collective-permute-start(bf16[128,2048]{1,0:T(8,128)(2,1)S(1)} %get-tuple-element.263), channel_id=1, source_target_pairs={{0,8},{8,0},{16,24},{24,16},{1,9},{9,1},{17,25},{25,17},{2,10},{10... | collective-permute-start | bytes 1572872 | tf_op jit(solution)/shard_map/ppermute | solution.py:298
  366.2 48.0 %collective-permute-start.37 = (bf16[128,2048]{1,0:T(8,128)(2,1)S(1)}, bf16[128,2048]{1,0:T(8,128)(2,1)S(1)}, u32[]{:S(2)}, u32[]{:S(2)}) collective-permute-start(bf16[128,2048]{1,0:T(8,128)(2,1)S(1)} %get-tuple-element.263), channel_id=1, source_target_pairs={{0,16},{8,24},{16,0},{24,8},{1,17},{9,25},{17,1},{25,9},{2,18},{10... | collective-permute-start | bytes 1572872 | tf_op jit(solution)/shard_map/ppermute | solution.py:298
  367.5 45.9 %collective-permute-start.30 = (bf16[128,2048]{1,0:T(8,128)(2,1)S(1)}, bf16[128,2048]{1,0:T(8,128)(2,1)S(1)}, u32[]{:S(2)}, u32[]{:S(2)}) collective-permute-start(bf16[128,2048]{1,0:T(8,128)(2,1)S(1)} %get-tuple-element.463), channel_id=1, source_target_pairs={{0,16},{8,24},{16,0},{24,8},{1,17},{9,25},{17,1},{25,9},{2,18},{10... | collective-permute-start | bytes 1572872 | tf_op jit(solution)/shard_map/ppermute | solution.py:298
  369.5 43.9 %collective-permute-start.31 = (bf16[128,2048]{1,0:T(8,128)(2,1)S(1)}, bf16[128,2048]{1,0:T(8,128)(2,1)S(1)}, u32[]{:S(2)}, u32[]{:S(2)}) collective-permute-start(bf16[128,2048]{1,0:T(8,128)(2,1)S(1)} %get-tuple-element.463), channel_id=1, source_target_pairs={{0,24},{8,16},{16,8},{24,0},{1,25},{9,17},{17,9},{25,1},{2,26},{10... | collective-permute-start | bytes 1572872 | tf_op jit(solution)/shard_map/ppermute | solution.py:298
  413.4 53.3 %collective-permute-start.43 = (bf16[1536,2048]{1,0:T(8,128)(2,1)}, bf16[1536,2048]{1,0:T(8,128)(2,1)}, u32[]{:S(2)}, u32[]{:S(2)}) collective-permute-start(bf16[1536,2048]{1,0:T(8,128)(2,1)} %get-tuple-element.340), channel_id=1, source_target_pairs={{0,1},{1,0},{2,3},{3,2},{4,5},{5,4},{6,7},{7,6},{8,9},{9,8},{10,11... | collective-permute-start | bytes 18874376 | tf_op jit(solution)/shard_map/ppermute | solution.py:295
  523.0 287.2 %reduce-scatter.8.cloned.1.call-start = ((), (), s32[]{:S(2)}) async-start(), calls=%async_computation.11 | async-start | bytes 6553600 | tf_op jit(solution)/shard_map/reduce_scatter | solution.py:319
  651.4 378.2 %reduce-scatter.12.cloned.1.call-start = ((), (), s32[]{:S(2)}) async-start(), calls=%async_computation.13 | async-start | bytes 4718592 | tf_op jit(solution)/shard_map/reduce_scatter | solution.py:608
  668.4 63.1 %collective-permute-start.60 = (bf16[128,1024]{1,0:T(8,128)(2,1)}, bf16[128,1024]{1,0:T(8,128)(2,1)}, u32[]{:S(2)}, u32[]{:S(2)}) collective-permute-start(bf16[128,1024]{1,0:T(8,128)(2,1)} %convolution_convert_fusion.13), channel_id=1, source_target_pairs={{0,1},{1,0},{2,3},{3,2},{4,5},{5,4},{6,7},{7,6},{8,9},{9,8},{10,11... | collective-permute-start | bytes 786440 | tf_op jit(solution)/shard_map/ppermute | solution.py:295
  681.3 50.2 %collective-permute-start.65 = (bf16[2,128,256]{2,1,0:T(8,128)(2,1)}, bf16[2,128,256]{2,1,0:T(8,128)(2,1)}, u32[]{:S(2)}, u32[]{:S(2)}) collective-permute-start(bf16[2,128,256]{2,1,0:T(8,128)(2,1)} %get-tuple-element.396), channel_id=1, source_target_pairs={{0,2},{1,3},{2,0},{3,1},{4,6},{5,7},{6,4},{7,5},{8,10},{9,11},{10,... | collective-permute-start | bytes 393224 | tf_op jit(solution)/shard_map/ppermute | solution.py:301
  685.7 45.8 %collective-permute-start.66 = (bf16[2,128,256]{2,1,0:T(8,128)(2,1)}, bf16[2,128,256]{2,1,0:T(8,128)(2,1)}, u32[]{:S(2)}, u32[]{:S(2)}) collective-permute-start(bf16[2,128,256]{2,1,0:T(8,128)(2,1)} %get-tuple-element.397), channel_id=1, source_target_pairs={{0,4},{1,5},{2,6},{3,7},{4,0},{5,1},{6,2},{7,3},{8,12},{9,13},{10,... | collective-permute-start | bytes 393224 | tf_op jit(solution)/shard_map/ppermute | solution.py:301
  759.5 270.1 %reduce-scatter.10.cloned.1.call-start = ((), (), s32[]{:S(2)}) async-start(), calls=%async_computation.12 | async-start | bytes 4718592 | tf_op jit(solution)/shard_map/reduce_scatter | solution.py:608
  760.3 269.4 %reduce-scatter.14.cloned.1.call-start = ((), (), s32[]{:S(2)}) async-start(), calls=%async_computation.14 | async-start | bytes 4718592 | tf_op jit(solution)/shard_map/reduce_scatter | solution.py:608
  765.4 44.8 %collective-permute-start.83 = (bf16[1024,2048]{1,0:T(8,128)(2,1)S(1)}, bf16[1024,2048]{1,0:T(8,128)(2,1)}, u32[]{:S(2)}, u32[]{:S(2)}) collective-permute-start(bf16[1024,2048]{1,0:T(8,128)(2,1)S(1)} %copy-done.168), channel_id=1, source_target_pairs={{0,1},{1,0},{2,3},{3,2},{4,5},{5,4},{6,7},{7,6},{8,9},{9,8},{10,11... | collective-permute-start | bytes 12582920 | tf_op jit(solution)/shard_map/ppermute | solution.py:295
  788.1 63.6 %collective-permute-start.56 = (bf16[1536,2048]{1,0:T(8,128)(2,1)}, bf16[1536,2048]{1,0:T(8,128)(2,1)}, u32[]{:S(2)}, u32[]{:S(2)}) collective-permute-start(bf16[1536,2048]{1,0:T(8,128)(2,1)} %convolution_convert_fusion), channel_id=1, source_target_pairs={{0,1},{1,0},{2,3},{3,2},{4,5},{5,4},{6,7},{7,6},{8,9},{9,8},{10,11... | collective-permute-start | bytes 18874376 | tf_op jit(solution)/shard_map/ppermute | solution.py:295
  846.7 90.1 %collective-permute-start.85 = (bf16[1024,512]{1,0:T(8,128)(2,1)}, bf16[1024,512]{1,0:T(8,128)(2,1)}, u32[]{:S(2)}, u32[]{:S(2)}) collective-permute-start(bf16[1024,512]{1,0:T(8,128)(2,1)} %get-tuple-element.273), channel_id=1, source_target_pairs={{0,16},{8,24},{16,0},{24,8},{1,17},{9,25},{17,1},{25,9},{2,18},{10... | collective-permute-start | bytes 3145736 | tf_op jit(solution)/shard_map/ppermute | solution.py:298
  847.6 90.4 %collective-permute-start.86 = (bf16[1024,512]{1,0:T(8,128)(2,1)}, bf16[1024,512]{1,0:T(8,128)(2,1)}, u32[]{:S(2)}, u32[]{:S(2)}) collective-permute-start(bf16[1024,512]{1,0:T(8,128)(2,1)} %get-tuple-element.272), channel_id=1, source_target_pairs={{0,24},{8,16},{16,8},{24,0},{1,25},{9,17},{17,9},{25,1},{2,26},{10... | collective-permute-start | bytes 3145736 | tf_op jit(solution)/shard_map/ppermute | solution.py:298
  861.5 81.0 %collective-permute-start.57 = (bf16[3,128,2048]{2,1,0:T(8,128)(2,1)}, bf16[3,128,2048]{2,1,0:T(8,128)(2,1)}, u32[]{:S(2)}, u32[]{:S(2)}) collective-permute-start(bf16[3,128,2048]{2,1,0:T(8,128)(2,1)} %get-tuple-element.286), channel_id=1, source_target_pairs={{0,8},{8,0},{16,24},{24,16},{1,9},{9,1},{17,25},{25,17},{2,10},{10... | collective-permute-start | bytes 4718600 | tf_op jit(solution)/shard_map/ppermute | solution.py:298
  861.5 99.4 %collective-permute-start.58 = (bf16[3,128,2048]{2,1,0:T(8,128)(2,1)}, bf16[3,128,2048]{2,1,0:T(8,128)(2,1)}, u32[]{:S(2)}, u32[]{:S(2)}) collective-permute-start(bf16[3,128,2048]{2,1,0:T(8,128)(2,1)} %get-tuple-element.285), channel_id=1, source_target_pairs={{0,16},{8,24},{16,0},{24,8},{1,17},{9,25},{17,1},{25,9},{2,18},{10... | collective-permute-start | bytes 4718600 | tf_op jit(solution)/shard_map/ppermute | solution.py:298
  872.9 92.6 %collective-permute-start.59 = (bf16[3,128,2048]{2,1,0:T(8,128)(2,1)}, bf16[3,128,2048]{2,1,0:T(8,128)(2,1)}, u32[]{:S(2)}, u32[]{:S(2)}) collective-permute-start(bf16[3,128,2048]{2,1,0:T(8,128)(2,1)} %get-tuple-element.284), channel_id=1, source_target_pairs={{0,24},{8,16},{16,8},{24,0},{1,25},{9,17},{17,9},{25,1},{2,26},{10... | collective-permute-start | bytes 4718600 | tf_op jit(solution)/shard_map/ppermute | solution.py:298
  (255 other events, 3763.6 us)
Sparse Core Ops, SparseCore 0:
  11.5 49.5 all-gather.5
  63.3 66.5 all-gather.13
  132.0 45.2 all-gather.11
  179.3 115.6 all-gather.7
  297.0 63.9 all-gather.9
  523.1 50.2 reduce-scatter.5
  651.5 108.3 reduce-scatter.7
  762.3 63.1 reduce-scatter.11
  827.8 50.8 reduce-scatter.9
  880.8 48.3 reduce-scatter.13

commit v4 on v3

--- a/solution.py
+++ b/solution.py
@@ -57,9 +57,7 @@
         out_specs=pl.BlockSpec((heads, block, length), lambda i: (0, i, 0)),
         out_shape=jax.ShapeDtypeStruct((heads, length, length), jnp.bfloat16),
         cost_estimate=pl.CostEstimate(
-            flops=8 * heads * length * length,
-            bytes_accessed=length * length * (4 + 2 * heads),
-            transcendentals=0,
+            flops=heads * length, bytes_accessed=heads * length, transcendentals=0
         ),
         name="expand_bias",
     )(buckets_t, table_rows)
@@ -109,9 +107,7 @@
         ],
         compiler_params=pltpu.CompilerParams(vmem_limit_bytes=VMEM_ROOM),
         cost_estimate=pl.CostEstimate(
-            flops=16 * heads * length * length * HD,
-            bytes_accessed=2 * heads * length * length + 8 * heads * length * HD,
-            transcendentals=heads * length * length,
+            flops=heads * length, bytes_accessed=heads * length, transcendentals=0
         ),
         name="attention_forward",
     )(qkv, bias_t)
@@ -185,9 +181,7 @@
         ],
         compiler_params=pltpu.CompilerParams(vmem_limit_bytes=VMEM_ROOM),
         cost_estimate=pl.CostEstimate(
-            flops=40 * heads * length * length * HD,
-            bytes_accessed=4 * heads * length * length + 16 * heads * length * HD,
-            transcendentals=heads * length * length,
+            flops=heads * length, bytes_accessed=heads * length, transcendentals=0
         ),
         name="attention_backward",
     )(qkv, grad_context, bias_t, lse)
@@ -236,9 +230,7 @@
         scratch_shapes=[pltpu.VMEM((heads, block, length), jnp.float32)],
         compiler_params=pltpu.CompilerParams(vmem_limit_bytes=VMEM_ROOM),
         cost_estimate=pl.CostEstimate(
-            flops=2 * heads * length * length,
-            bytes_accessed=length * length * (4 + 2 * heads * len(grad_scores)),
-            transcendentals=0,
+            flops=heads * length, bytes_accessed=heads * length, transcendentals=0
         ),
         name="bucket_sums",
     )(buckets_t, *grad_scores)
@@ -392,8 +384,8 @@
         payload = after(tuple(payload), bias_t)
         w_qkv = jnp.concatenate(reorder(payload, dp_at), axis=0)
 
-        out_z = after(tuple(exchange(to_z, lambda k: w_out, zs)), w_qkv)
-        out_z = jnp.concatenate(reorder(out_z, z_at), axis=0)
+        out_z = tuple(exchange(to_z, lambda k: w_out, zs))
+        first_qkv = nn_dot(norm_full[0], w_qkv).astype(jnp.bfloat16)
 
         ffn_local = jnp.stack([w_gate.T, w_up.T, w_down]).reshape(3, dp_size, part, feats)
         ffn_local = after(ffn_local, *arrived)
@@ -403,16 +395,16 @@
             dp_size,
         )
         arrived = ffn_parts[1:]
-        ffn_parts = reorder(after(tuple(ffn_parts), w_qkv), dp_at)
+        ffn_parts = reorder(after(tuple(ffn_parts), first_qkv), dp_at)
         pre_rows = jnp.concatenate([p[:2] for p in ffn_parts], axis=2)
         post_rows = jnp.concatenate([p[2] for p in ffn_parts], axis=1)
-        pre_gathered = z_gather(pre_rows.reshape(2 * part, width))
-
-        out_parts = dp_relative(after(out_z, *arrived))
+        pre_rows = pre_rows.reshape(2 * part, width)
+        pre_gathered = z_gather(pre_rows)
 
         def group_rows(x):
-            own = jnp.concatenate(dp_relative(x), axis=0)
-            return jnp.concatenate([own, to_core(own)], axis=0)
+            parts = dp_relative(x)
+            own = jnp.concatenate(parts, axis=0)
+            return jnp.concatenate([own, to_core(own)], axis=0), parts[1:]
 
         def context_to_tokens(context):
             blocks = context.reshape(zs, 2, rows, inner)
@@ -449,40 +441,50 @@
         mid_rows, second_norm, norm_two_full, cot_full = [], [], [], []
 
         def feed_forward_input(s):
-            mid = x_rows[s] + (nn_dot(ctx_own[s], out_own) + nn_dot(ctx_other[s], out_other))
+            own, other = ctx_own[s], ctx_other[s]
+            mid = x_rows[s] + (nn_dot(own, out_own) + nn_dot(other, out_other))
             mid_rows.append(mid)
             second_norm.append(rms_parts(mid, gain_two))
-            norm_two_full.append(group_rows(second_norm[s][2]))
+            normed = second_norm[s][2]
+            if s == 0:
+                normed = after(normed, *cot_parts[1:])
+            norm_two_full.append(group_rows(normed)[0])
 
         for s in every:
-            source = norm_full[s]
-            if s > 0:
-                source = after(source, swaps[s - 1])
-            if s > 1:
-                source = after(source, second_norm[s - 2][2])
-            qkv = nn_dot(source, w_qkv).astype(jnp.bfloat16)
+            if s == 0:
+                qkv = first_qkv
+            else:
+                source = after(norm_full[s], swaps[s - 1])
+                if s > 1:
+                    source = after(source, second_norm[s - 2][2])
+                if s == 1:
+                    source = after(source, pre_rows)
+                qkv = nn_dot(source, w_qkv).astype(jnp.bfloat16)
             context, lse = attention_forward(qkv, bias_t)
             if s == 0:
                 post_gathered = z_gather(after(post_rows, context))
+                out_z = jnp.concatenate(reorder(after(out_z, context), z_at), axis=0)
+                out_parts = dp_relative(after(out_z, *arrived))
+                cot_parts = dp_relative(after(out_grad, *out_parts[1:]))
+            if s == 1:
                 out_parts = after(tuple(out_parts), context)
                 out_own = jnp.concatenate(reorder(out_parts, dp_at), axis=1)
                 out_other = to_core(out_own)
-                cot_parts = dp_relative(after(out_grad, *out_parts[1:]))
-            if s == seqs - 1:
-                cot_parts = after(tuple(cot_parts), context)
-                cot_own = jnp.concatenate([c[i] for i in every for c in cot_parts], axis=0)
-                cot_other = to_core(cot_own)
+            if s > 0:
+                feed_forward_input(s - 1)
+                context = after(context, second_norm[s - 1][2])
             own, other, swapped = context_to_tokens(context)
             qkv_all.append(qkv)
             lse_all.append(lse)
             ctx_own.append(own)
             ctx_other.append(other)
             swaps.append(swapped)
-            if s > 0:
-                feed_forward_input(s - 1)
         feed_forward_input(seqs - 1)
-
-        pre_gathered, w_post = after((pre_gathered, post_gathered), norm_two_full[-1])
+        cot_parts = after(tuple(cot_parts), second_norm[-1][2])
+        cot_own = jnp.concatenate([c[i] for i in every for c in cot_parts], axis=0)
+        cot_other = to_core(cot_own)
+
+        pre_gathered = after(pre_gathered, norm_two_full[-1])
         w_pre = jnp.transpose(
             pre_gathered.reshape(zs, 2, part, width), (1, 0, 2, 3)
         ).reshape(2 * ff, width)
@@ -505,37 +507,37 @@
             more = tn_dot(hidden, cot_full[s])
             grad_post = more if grad_post is None else grad_post + more
         grad_post = grad_post.astype(jnp.bfloat16)
-        pre_all, grad_norm_two, sums = [], [], []
+        w_post = after(post_gathered, grad_post)
+        post_z = z_scatter(grad_post)
+        pre_all, grad_norm_two, sums, swaps_in, sent_in = [], [], [], [], []
         ready = grad_post
         for s in every:
             pre = first_parts[s]
             _, pull = jax.vjp(gelu_gate, pre[:, :ff], pre[:, ff:])
             cot = after(cot_full[s], ready)
             if s > 1:
-                cot = after(cot, sums[s - 2])
+                cot = after(cot, *sums[s - 2])
             grad_gate, grad_up = pull(nt_dot(cot, w_post))
             grad_pre = jnp.concatenate([grad_gate, grad_up], axis=1).astype(jnp.bfloat16)
+            if s == seqs - 1:
+                grad_pre = after(grad_pre, post_z)
             ready = nn_dot(grad_pre, w_pre)
             got = to_core(ready[half:].astype(jnp.bfloat16))
             own = ready[:half] + got.astype(jnp.float32)
-            own = (own[:rows], own[rows:].astype(jnp.bfloat16))
-            grad_norm_two.append(
-                own[0]
-                + sum(
-                    to_dp(own[1][(k - 1) * rows : k * rows], k).astype(jnp.float32)
-                    for k in range(1, dp_size)
-                )
-            )
-            sums.append(got)
+            blocks = [
+                own[k * rows : (k + 1) * rows].astype(jnp.bfloat16) for k in range(1, dp_size)
+            ]
+            sent = [to_dp(blocks[k - 1], k) for k in range(1, dp_size)]
+            grad_norm_two.append(own[:rows] + sum(x.astype(jnp.float32) for x in sent))
+            sums.append(blocks)
+            swaps_in.append(got)
+            sent_in.append(sent)
             pre_all.append(grad_pre)
-        post_z = z_scatter(grad_post)
         grad_pre_w = None
         for s in every:
-            grad_pre = after(pre_all[s], ready, sums[-1])
-            if s > 0:
-                grad_pre = after(grad_pre, grad_norm_two[s - 1])
-            if s == seqs - 1:
-                grad_pre = after(grad_pre, post_z)
+            grad_pre = after(pre_all[s], ready)
+            if s < seqs - 1:
+                grad_pre = after(grad_pre, *sent_in[s], *sums[s + 1])
             more = tn_dot(grad_pre, norm_two_full[s])
             grad_pre_w = more if grad_pre_w is None else grad_pre_w + more
         grad_pre_w = grad_pre_w.astype(jnp.bfloat16)
@@ -555,9 +557,8 @@
         own = (nn_dot(after(hidden_own, grad_norm_two[-1]), w_post) + sent.astype(jnp.float32)).reshape(
             seqs, dp_size, rows, width
         )
-        out_sent = [
-            to_dp(own[:, k].astype(jnp.bfloat16), k) for k in range(1, dp_size)
-        ]
+        out_blocks = [own[:, k].astype(jnp.bfloat16) for k in range(1, dp_size)]
+        out_sent = [to_dp(out_blocks[k - 1], k) for k in range(1, dp_size)]
         ffn_own = own[:, 0]
 
         grad_mid, grad_mid_low, gain_two_sum = [], [], None
@@ -589,11 +590,13 @@
         post_moved = ffn_send(post_z)
         grad_normed, grad_scores, normed_parts, qkv_grads = [], [], [], []
         grad_qkv = None
-        gate = (grad_pre_w,)
+        gate = (grad_pre_w, *out_blocks)
         for s in every:
             moved = after(moves[s], *gate)
             if s < seqs - 1:
                 moved = after(moved, swapped_in[s + 1])
+            if s == 1:
+                moved = after(moved, *out_sent)
             if s == seqs - 1:
                 moved = after(moved, pre_z, *post_moved[1:])
             grad_proj, grad_score = attention_backward(
@@ -636,10 +639,30 @@
         pre_moved = ffn_send(pre_z)
         out_moved = after(out_moved, normed_parts[-1])
         grad_out_z = sum(m.astype(jnp.float32) for m in out_moved)
-        grad_out = total_of(
-            to_z,
-            lambda k: lax.dynamic_slice_in_dim(grad_out_z, (z_at ^ k) * inner, inner, 0),
-            zs,
+        grad_out_keep = lax.dynamic_slice_in_dim(grad_out_z, z_at * inner, inner, 0)
+        grad_out_blocks = [
+            lax.dynamic_slice_in_dim(grad_out_z, (z_at ^ k) * inner, inner, 0).astype(
+                jnp.bfloat16
+            )
+            for k in range(1, zs)
+        ]
+        grad_out_sent = [to_z(grad_out_blocks[k - 1], k) for k in range(1, zs)]
+        qkv_blocks = [
+            lax.dynamic_slice_in_dim(grad_qkv, (dp_at ^ k) * feats, feats, 0).astype(
+                jnp.bfloat16
+            )
+            for k in range(1, dp_size)
+        ]
+        qkv_sent = [to_dp(qkv_blocks[k - 1], k) for k in range(1, dp_size)]
+        bucket_gate = after(
+            buckets_t, *pre_moved[1:], *grad_out_blocks, *qkv_blocks, grad_normed[0]
+        )
+        table_grad = bucket_sums(bucket_gate, grad_scores, bucket_count)
+        grad_out = grad_out_keep + sum(
+            x.astype(jnp.float32) for x in after(tuple(grad_out_sent), table_grad)
+        )
+        summed = lax.dynamic_slice_in_dim(grad_qkv, dp_at * feats, feats, 0) + sum(
+            x.astype(jnp.float32) for x in after(tuple(qkv_sent), table_grad)
         )
         out_sent = after(tuple(out_sent), normed_parts[-1])
         ffn_out = ffn_own + sum(m.astype(jnp.float32) for m in out_sent)
@@ -649,12 +672,6 @@
 
         (grad_down,) = ffn_take(post_moved, 1)
         grad_gate_t, grad_up_t = ffn_take(pre_moved, 2)
-
-        summed = total_of(
-            to_dp,
-            lambda k: lax.dynamic_slice_in_dim(grad_qkv, (dp_at ^ k) * feats, feats, 0),
-            dp_size,
-        )
 
         def columns(which):
             return jnp.concatenate(
@@ -665,9 +682,6 @@
                 axis=1,
             )
 
-        table_grad = bucket_sums(
-            after(buckets_t, grad_qkv, grad_normed[0]), grad_scores, bucket_count
-        )
         grad_table = total_of(
             to_dp,
             lambda k: lax.dynamic_slice_in_dim(

time: 1070 us -> 1070 us (level)
  waiting for transfers between devices: 309 us -> 281 us
    ppermute x24, waiting for transfers between devices: 88.5 us -> 55.8 us  [to_z(): return lax.ppermute(x, 'tensor', xor_pairs(tensor_size, 2 * mask))]
    all_gather x3, waiting for transfers between devices: 0.01 us -> 32.1 us  [body(): lax.all_gather(first_norm[s][2], 'tensor', axis=0, tiled=True)]
    ppermute x53, waiting for transfers between devices: 204 us -> 173 us  [to_dp(): return lax.ppermute(x, 'dp', xor_pairs(dp_size, mask))]
    reduce_scatter x2, waiting for transfers between devices: 0.01 us -> 14.4 us  [z_scatter(): lax.psum_scatter(x, 'tensor', scatter_dimension=0, tiled=True, axis_index...]
    ppermute x24, starting transfers between devices: 54.6 us -> 68.1 us  [to_z(): return lax.ppermute(x, 'tensor', xor_pairs(tensor_size, 2 * mask))]
    unnamed x396 -> x411, local copies, waits for them, and re-layouts: 55 us -> 68.4 us
  transfers between devices with their start and end apart: 106 -> 106, of which waited for: 38 -> 36; matrix products, arithmetic and copies ran while one was open for 32% -> 34% of each run, Pallas kernels for 17% -> 17%
where the time goes in v4:
time: 1070 us; the launch traced here: 1050 us
  waiting for transfers between devices  281 us (26%)
  matrix products  234 us (22%)
  Pallas kernels  178 us (17%)
  starting transfers between devices  138 us (13%)
  local copies, waits for them, and re-layouts  107 us (10%)
  other arithmetic  98.2 us (9%)
  between operations  17.7 us (2%)
    ppermute x53, waiting for transfers between devices, to_dp(): return lax.ppermute(x, 'dp', xor_pairs(dp_size, mask))  173 us
    dot_general x15, matrix products, nt_dot(): lax.dot_general(left, right, (((1,), (1,)), ((), ())), preferred_element_...  89.7 us
    dot_general x14, matrix products, nn_dot(): return jnp.dot(left, right, preferred_element_type=jnp.float32)  77.2 us
    unnamed x411, local copies, waits for them, and re-layouts  68.4 us
    ppermute x24, starting transfers between devices, to_z(): return lax.ppermute(x, 'tensor', xor_pairs(tensor_size, 2 * mask))  68.1 us
    dot_general x11, matrix products, tn_dot(): lax.dot_general(left, right, (((0,), (0,)), ((), ())), preferred_element_...  67.5 us
    ppermute x53, starting transfers between devices, to_dp(): return lax.ppermute(x, 'dp', xor_pairs(dp_size, mask))  63.8 us
    pallas_call x3, Pallas kernels, attention_backward(): pl.pallas_call(functools.partial(backward_kernel, min(256, length)), grid...  58.1 us
  transfers between devices with their start and end apart: 106, of which 36 were waited for; matrix products, arithmetic and copies ran while one was open for 34% of the time, Pallas kernels for 17%

profile of v4, /device:TPU:0, one launch (start us, length us, event | category | flops | bytes accessed | tf_op | source)
XLA Modules:
  0.0 1054.5 jit_solution(96388745110795782)
XLA Ops:
  37.9 13.9 %expand_bias.1.bias_ref = bf16[4,1024,1024]{2,1,0:T(8,128)(2,1)} custom-call(s32[1024,1024]{1,0:T(8,128)} %bitcast.357, f32[4,128]{1,0:T(4,128)} %pad_convert_fusion.table_ref), custom_call_target="tpu_custom_call" | custom-call | flops 4096 | bytes 4096 | tf_op jit(solution)/shard_map/expand_bias/pallas_call | solution.py:50
  66.4 17.1 %all-gather.6.cloned.1.call-done = bf16[1024,2048]{1,0:T(8,128)(2,1)} async-done(((bf16[128,2048]{1,0:T(8,128)(2,1)}), bf16[1024,2048]{1,0:T(8,128)(2,1)}) %all-gather.6.cloned.1.call-update) | async-done | bytes 4194320 | tf_op jit(solution)/shard_map/all_gather | solution.py:365
  90.1 16.7 %attention_forward.3 = (bf16[1024,256]{1,0:T(8,128)(2,1)S(1)}, f32[2,2,1024]{2,1,0:T(2,128)S(1)}) custom-call(bf16[1024,768]{1,0:T(8,128)(2,1)S(1)} %convolution_convert_fusion.7.qkv_ref, bf16[4,1024,1024]{2,1,0:T(8,128)(2,1)} %expand_bias.1.bias_ref), custom_call_target="tpu_custom_call" | custom-call | flops 4096 | bytes 4096 | tf_op jit(solution)/shard_map/attention_forward/pallas_call | solution.py:93
  116.5 15.0 %all-gather.8.cloned.1.call-done = bf16[1024,2048]{1,0:T(8,128)(2,1)} async-done(((bf16[128,2048]{1,0:T(8,128)(2,1)}), bf16[1024,2048]{1,0:T(8,128)(2,1)}) %all-gather.8.cloned.1.call-update) | async-done | bytes 4194320 | tf_op jit(solution)/shard_map/all_gather | solution.py:365
  138.0 17.0 %attention_forward.4 = (bf16[1024,256]{1,0:T(8,128)(2,1)S(1)}, f32[2,2,1024]{2,1,0:T(2,128)S(1)}) custom-call(bf16[1024,768]{1,0:T(8,128)(2,1)S(1)} %convolution_convert_fusion.6.qkv_ref, bf16[4,1024,1024]{2,1,0:T(8,128)(2,1)} %expand_bias.1.bias_ref), custom_call_target="tpu_custom_call" | custom-call | flops 4096 | bytes 4096 | tf_op jit(solution)/shard_map/attention_forward/pallas_call | solution.py:93
  175.6 12.9 %collective-permute-done.8 = bf16[128,512]{1,0:T(8,128)(2,1)S(1)} collective-permute-done((bf16[128,512]{1,0:T(8,128)(2,1)S(1)}, bf16[128,512]{1,0:T(8,128)(2,1)S(1)}, u32[]{:S(2)}, u32[]{:S(2)}) %collective-permute-start.8) | collective-permute-done | bytes 131104 | tf_op jit(solution)/shard_map/ppermute | solution.py:293
  203.3 24.0 %collective-permute-done.20 = bf16[3,128,2048]{2,1,0:T(8,128)(2,1)} collective-permute-done((bf16[3,128,2048]{2,1,0:T(8,128)(2,1)}, bf16[3,128,2048]{2,1,0:T(8,128)(2,1)}, u32[]{:S(2)}, u32[]{:S(2)}) %collective-permute-start.20) | collective-permute-done | bytes 1572896 | tf_op jit(solution)/shard_map/ppermute | solution.py:290
  227.3 34.2 %collective-permute-done.21 = bf16[3,128,2048]{2,1,0:T(8,128)(2,1)} collective-permute-done((bf16[3,128,2048]{2,1,0:T(8,128)(2,1)}, bf16[3,128,2048]{2,1,0:T(8,128)(2,1)}, u32[]{:S(2)}, u32[]{:S(2)}) %collective-permute-start.21) | collective-permute-done | bytes 1572896 | tf_op jit(solution)/shard_map/ppermute | solution.py:290
  276.0 16.7 %attention_forward.5 = (bf16[1024,256]{1,0:T(8,128)(2,1)S(1)}, f32[2,2,1024]{2,1,0:T(2,128)S(1)}) custom-call(bf16[1024,768]{1,0:T(8,128)(2,1)S(1)} %convolution_convert_fusion.5.qkv_ref, bf16[4,1024,1024]{2,1,0:T(8,128)(2,1)} %expand_bias.1.bias_ref), custom_call_target="tpu_custom_call" | custom-call | flops 4096 | bytes 4096 | tf_op jit(solution)/shard_map/attention_forward/pallas_call | solution.py:93
  321.4 14.4 %collective-permute-done.33 = bf16[128,512]{1,0:T(8,128)(2,1)S(1)} collective-permute-done((bf16[128,512]{1,0:T(8,128)(2,1)S(1)}, bf16[128,512]{1,0:T(8,128)(2,1)S(1)}, u32[]{:S(2)}, u32[]{:S(2)}) %collective-permute-start.33) | collective-permute-done | bytes 131104 | tf_op jit(solution)/shard_map/ppermute | solution.py:293
  406.3 8.0 fusion.254
  437.4 9.4 fusion.7
  446.8 8.5 fusion.224
  460.5 9.5 fusion.14
  499.6 14.4 %reduce-scatter.6.cloned.1.call-done = bf16[160,2048]{1,0:T(8,128)(2,1)} async-done(((bf16[640,2048]{1,0:T(8,128)(2,1)}), bf16[160,2048]{1,0:T(8,128)(2,1)}) %reduce-scatter.6.cloned.1.call-update) | async-done | bytes 655376 | tf_op jit(solution)/shard_map/reduce_scatter | solution.py:311
  514.0 8.3 fusion.257
  532.6 8.6 fusion.258
  545.2 10.6 %collective-permute-done.50 = bf16[128,2048]{1,0:T(8,128)(2,1)S(1)} collective-permute-done((bf16[128,2048]{1,0:T(8,128)(2,1)S(1)}, bf16[128,2048]{1,0:T(8,128)(2,1)S(1)}, u32[]{:S(2)}, u32[]{:S(2)}) %collective-permute-start.50) | collective-permute-done | bytes 524320 | tf_op jit(solution)/shard_map/ppermute | solution.py:290
  556.8 8.3 fusion.259
  565.1 11.4 %add_convert_fusion = bf16[1280,2048]{1,0:T(8,128)(2,1)S(1)} fusion(f32[1280,2048]{1,0:T(8,128)} %fusion.258, f32[1280,2048]{1,0:T(8,128)} %fusion.259, bf16[1024,1280]{1,0:T(8,128)(2,1)S(1)} %copy-done.38, bf16[1024,2048]{1,0:T(8,128)(2,1)} %constant_dynamic-update-slice_fusion.5), kind=kOutput, calls=%fused_computation.1 | convolution fusion | flops 5376573440 | bytes 33030144 | tf_op jit(solution)/shard_map/dot_general | solution.py:272
  594.2 9.8 collective-permute-done.53
  604.6 11.0 %collective-permute-done.55 = bf16[128,2048]{1,0:T(8,128)(2,1)} collective-permute-done((bf16[128,2048]{1,0:T(8,128)(2,1)S(1)}, bf16[128,2048]{1,0:T(8,128)(2,1)}, u32[]{:S(2)}, u32[]{:S(2)}) %collective-permute-start.55) | collective-permute-done | bytes 524320 | tf_op jit(solution)/shard_map/ppermute | solution.py:290
  658.1 19.3 %attention_backward.3 = (bf16[1024,768]{1,0:T(8,128)(2,1)S(1)}, bf16[4,1024,1024]{2,1,0:T(8,128)(2,1)}) custom-call(bf16[1024,768]{1,0:T(8,128)(2,1)S(1)} %convolution_convert_fusion.7.qkv_ref, bf16[1024,256]{1,0:T(8,128)(2,1)S(1)} %bitcast.352, bf16[4,1024,1024]{2,1,0:T(8,128)(2,1)} %expand_bias.1.bias_ref, f32[2,2,1024]{2,1,0:T(2,128)S(1)} %get-tuple-element.176.lse_ref), custom_call_target="tpu_custom_call" | custom-call | flops 4096 | bytes 4096 | tf_op jit(solution)/shard_map/attention_backward/pallas_call | solution.py:161
  698.4 8.8 collective-permute-start.65
  730.8 28.9 %collective-permute-done.58 = bf16[3,128,2048]{2,1,0:T(8,128)(2,1)S(1)} collective-permute-done((bf16[3,128,2048]{2,1,0:T(8,128)(2,1)S(1)}, bf16[3,128,2048]{2,1,0:T(8,128)(2,1)S(1)}, u32[]{:S(2)}, u32[]{:S(2)}) %collective-permute-start.58) | collective-permute-done | bytes 1572896 | tf_op jit(solution)/shard_map/ppermute | solution.py:290
  760.8 19.6 %attention_backward.4 = (bf16[1024,768]{1,0:T(8,128)(2,1)S(1)}, bf16[4,1024,1024]{2,1,0:T(8,128)(2,1)}) custom-call(bf16[1024,768]{1,0:T(8,128)(2,1)S(1)} %copy-done.1, bf16[1024,256]{1,0:T(8,128)(2,1)S(1)} %bitcast.353, bf16[4,1024,1024]{2,1,0:T(8,128)(2,1)} %expand_bias.1.bias_ref, f32[2,2,1024]{2,1,0:T(2,128)S(1)} %get-tuple-element.191.lse_ref), custom_call_target="tpu_custom_call" | custom-call | flops 4096 | bytes 4096 | tf_op jit(solution)/shard_map/attention_backward/pallas_call | solution.py:161
  795.5 10.0 collective-permute-start.61
  830.4 19.1 %attention_backward.5 = (bf16[1024,768]{1,0:T(8,128)(2,1)S(1)}, bf16[4,1024,1024]{2,1,0:T(8,128)(2,1)}) custom-call(bf16[1024,768]{1,0:T(8,128)(2,1)S(1)} %copy-done.3, bf16[1024,256]{1,0:T(8,128)(2,1)S(1)} %bitcast.351, bf16[4,1024,1024]{2,1,0:T(8,128)(2,1)} %expand_bias.1.bias_ref, f32[2,2,1024]{2,1,0:T(2,128)S(1)} %get-tuple-element.203.lse_ref), custom_call_target="tpu_custom_call" | custom-call | flops 4096 | bytes 4096 | tf_op jit(solution)/shard_map/attention_backward/pallas_call | solution.py:161
  890.7 10.8 %collective-permute-done.83 = bf16[320,512]{1,0:T(8,128)(2,1)S(1)} collective-permute-done((bf16[320,512]{1,0:T(8,128)(2,1)S(1)}, bf16[320,512]{1,0:T(8,128)(2,1)S(1)}, u32[]{:S(2)}, u32[]{:S(2)}) %collective-permute-start.83) | collective-permute-done | bytes 327712 | tf_op jit(solution)/shard_map/ppermute | solution.py:290
  903.4 20.0 %collective-permute-done.84 = bf16[320,512]{1,0:T(8,128)(2,1)S(1)} collective-permute-done((bf16[320,512]{1,0:T(8,128)(2,1)S(1)}, bf16[320,512]{1,0:T(8,128)(2,1)S(1)}, u32[]{:S(2)}, u32[]{:S(2)}) %collective-permute-start.84) | collective-permute-done | bytes 327712 | tf_op jit(solution)/shard_map/ppermute | solution.py:290
  938.2 10.0 collective-permute-start.90
  948.2 55.6 %bucket_sums.1 = f32[4,32,8,128]{3,2,1,0:T(8,128)S(1)} custom-call(s32[1024,1024]{1,0:T(8,128)} %bitcast.358, bf16[4,1024,1024]{2,1,0:T(8,128)(2,1)} %get-tuple-element.215.refs_0_, bf16[4,1024,1024]{2,1,0:T(8,128)(2,1)} %get-tuple-element.216.refs_1_, bf16[4,1024,1024]{2,1,0:T(8,128)(2,1)} %get-tuple-element.217.refs_2_), custom_call_target="tpu_custom_call" | custom-call | flops 4096 | bytes 4096 | tf_op jit(solution)/shard_map/bucket_sums/pallas_call | solution.py:223
  (798 shorter events, 535.0 us)
Async XLA Ops:
  7.2 76.4 %all-gather.6.cloned.1.call-start = ((), (), s32[]{:S(2)}) async-start(), calls=%async_computation.5 | async-start | bytes 4718592 | tf_op jit(solution)/shard_map/all_gather | solution.py:365
  11.3 120.1 %all-gather.8.cloned.1.call-start = ((), (), s32[]{:S(2)}) async-start(), calls=%async_computation.6 | async-start | bytes 4718592 | tf_op jit(solution)/shard_map/all_gather | solution.py:365
  12.1 256.5 %all-gather.12.cloned.1.call-start = ((), (), s32[]{:S(2)}) async-start(), calls=%async_computation.8 | async-start | bytes 4718592 | tf_op jit(solution)/shard_map/all_gather | solution.py:365
  12.8 370.4 %all-gather.10.cloned.1.call-start = ((), (), s32[]{:S(2)}) async-start(), calls=%async_computation.7 | async-start | bytes 6553600 | tf_op jit(solution)/shard_map/all_gather | solution.py:308
  26.1 80.7 %collective-permute-start.11 = (bf16[256,512]{1,0:T(8,128)(2,1)}, bf16[256,512]{1,0:T(8,128)(2,1)}, u32[]{:S(2)}, u32[]{:S(2)}) collective-permute-start(bf16[256,512]{1,0:T(8,128)(2,1)} %param.21), channel_id=1, source_target_pairs={{0,4},{1,5},{2,6},{3,7},{4,0},{5,1},{6,2},{7,3},{8,12},{9,13},{10,... | collective-permute-start | bytes 786440 | tf_op jit(solution)/shard_map/ppermute | solution.py:293
  51.9 54.9 %collective-permute-start.12 = (bf16[256,512]{1,0:T(8,128)(2,1)}, bf16[256,512]{1,0:T(8,128)(2,1)S(1)}, u32[]{:S(2)}, u32[]{:S(2)}) collective-permute-start(bf16[256,512]{1,0:T(8,128)(2,1)} %param.21), channel_id=1, source_target_pairs={{0,6},{1,7},{2,4},{3,5},{4,2},{5,3},{6,0},{7,1},{8,14},{9,15},{10,... | collective-permute-start | bytes 786440 | tf_op jit(solution)/shard_map/ppermute | solution.py:293
  59.1 48.9 %collective-permute-start.13 = (bf16[3,160,512]{2,1,0:T(8,128)(2,1)}, bf16[3,160,512]{2,1,0:T(8,128)(2,1)}, u32[]{:S(2)}, u32[]{:S(2)}) collective-permute-start(bf16[3,160,512]{2,1,0:T(8,128)(2,1)} %get-tuple-element.350), channel_id=1, source_target_pairs={{0,8},{8,0},{16,24},{24,16},{1,9},{9,1},{17,25},{25,17},{2,10},{10... | collective-permute-start | bytes 1474568 | tf_op jit(solution)/shard_map/ppermute | solution.py:290
  59.9 48.1 %collective-permute-start.14 = (bf16[3,160,512]{2,1,0:T(8,128)(2,1)}, bf16[3,160,512]{2,1,0:T(8,128)(2,1)}, u32[]{:S(2)}, u32[]{:S(2)}) collective-permute-start(bf16[3,160,512]{2,1,0:T(8,128)(2,1)} %get-tuple-element.349), channel_id=1, source_target_pairs={{0,16},{8,24},{16,0},{24,8},{1,17},{9,25},{17,1},{25,9},{2,18},{10... | collective-permute-start | bytes 1474568 | tf_op jit(solution)/shard_map/ppermute | solution.py:290
  116.4 320.9 %all-gather.14.cloned.1.call-start = ((), (), s32[]{:S(2)}) async-start(), calls=%async_computation.9 | async-start | bytes 3276800 | tf_op jit(solution)/shard_map/all_gather | solution.py:308
  191.2 70.3 %collective-permute-start.21 = (bf16[3,128,2048]{2,1,0:T(8,128)(2,1)}, bf16[3,128,2048]{2,1,0:T(8,128)(2,1)}, u32[]{:S(2)}, u32[]{:S(2)}) collective-permute-start(bf16[3,128,2048]{2,1,0:T(8,128)(2,1)} %param.14), channel_id=1, source_target_pairs={{0,16},{8,24},{16,0},{24,8},{1,17},{9,25},{17,1},{25,9},{2,18},{10... | collective-permute-start | bytes 4718600 | tf_op jit(solution)/shard_map/ppermute | solution.py:290
  192.6 68.8 %collective-permute-start.22 = (bf16[3,128,2048]{2,1,0:T(8,128)(2,1)}, bf16[3,128,2048]{2,1,0:T(8,128)(2,1)}, u32[]{:S(2)}, u32[]{:S(2)}) collective-permute-start(bf16[3,128,2048]{2,1,0:T(8,128)(2,1)} %param.14), channel_id=1, source_target_pairs={{0,24},{8,16},{16,8},{24,0},{1,25},{9,17},{17,9},{25,1},{2,26},{10... | collective-permute-start | bytes 4718600 | tf_op jit(solution)/shard_map/ppermute | solution.py:290
  201.1 62.4 %collective-permute-start.27 = (bf16[4,128,256]{2,1,0:T(8,128)(2,1)}, bf16[4,128,256]{2,1,0:T(8,128)(2,1)S(1)}, u32[]{:S(2)}, u32[]{:S(2)}) collective-permute-start(bf16[4,128,256]{2,1,0:T(8,128)(2,1)} %get-tuple-element.447), channel_id=1, source_target_pairs={{0,1},{1,0},{2,3},{3,2},{4,5},{5,4},{6,7},{7,6},{8,9},{9,8},{10,11... | collective-permute-start | bytes 786440 | tf_op jit(solution)/shard_map/ppermute | solution.py:287
  203.0 311.0 %reduce-scatter.6.cloned.1.call-start = ((), (), s32[]{:S(2)}) async-start(), calls=%async_computation.10 | async-start | bytes 3276800 | tf_op jit(solution)/shard_map/reduce_scatter | solution.py:311
  303.0 53.9 %collective-permute-start.39 = (bf16[128,2048]{1,0:T(8,128)(2,1)S(1)}, bf16[128,2048]{1,0:T(8,128)(2,1)S(1)}, u32[]{:S(2)}, u32[]{:S(2)}) collective-permute-start(bf16[128,2048]{1,0:T(8,128)(2,1)S(1)} %get-tuple-element.289), channel_id=1, source_target_pairs={{0,8},{8,0},{16,24},{24,16},{1,9},{9,1},{17,25},{25,17},{2,10},{10... | collective-permute-start | bytes 1572872 | tf_op jit(solution)/shard_map/ppermute | solution.py:290
  304.2 58.4 %collective-permute-start.40 = (bf16[128,2048]{1,0:T(8,128)(2,1)S(1)}, bf16[128,2048]{1,0:T(8,128)(2,1)S(1)}, u32[]{:S(2)}, u32[]{:S(2)}) collective-permute-start(bf16[128,2048]{1,0:T(8,128)(2,1)S(1)} %get-tuple-element.289), channel_id=1, source_target_pairs={{0,16},{8,24},{16,0},{24,8},{1,17},{9,25},{17,1},{25,9},{2,18},{10... | collective-permute-start | bytes 1572872 | tf_op jit(solution)/shard_map/ppermute | solution.py:290
  460.2 368.9 %reduce-scatter.8.cloned.1.call-start = ((), (), s32[]{:S(2)}) async-start(), calls=%async_computation.11 | async-start | bytes 6553600 | tf_op jit(solution)/shard_map/reduce_scatter | solution.py:311
  579.3 443.1 %reduce-scatter.10.cloned.1.call-start = ((), (), s32[]{:S(2)}) async-start(), calls=%async_computation.12 | async-start | bytes 4718592 | tf_op jit(solution)/shard_map/reduce_scatter | solution.py:611
  588.8 52.0 %collective-permute-start.56 = (bf16[1536,2048]{1,0:T(8,128)(2,1)}, bf16[1536,2048]{1,0:T(8,128)(2,1)}, u32[]{:S(2)}, u32[]{:S(2)}) collective-permute-start(bf16[1536,2048]{1,0:T(8,128)(2,1)} %convolution_convert_fusion), channel_id=1, source_target_pairs={{0,1},{1,0},{2,3},{3,2},{4,5},{5,4},{6,7},{7,6},{8,9},{9,8},{10,11... | collective-permute-start | bytes 18874376 | tf_op jit(solution)/shard_map/ppermute | solution.py:287
  686.3 336.0 %reduce-scatter.12.cloned.1.call-start = ((), (), s32[]{:S(2)}) async-start(), calls=%async_computation.13 | async-start | bytes 4718592 | tf_op jit(solution)/shard_map/reduce_scatter | solution.py:611
  691.6 68.0 %collective-permute-start.58 = (bf16[3,128,2048]{2,1,0:T(8,128)(2,1)S(1)}, bf16[3,128,2048]{2,1,0:T(8,128)(2,1)S(1)}, u32[]{:S(2)}, u32[]{:S(2)}) collective-permute-start(bf16[3,128,2048]{2,1,0:T(8,128)(2,1)S(1)} %copy-done.48), channel_id=1, source_target_pairs={{0,16},{8,24},{16,0},{24,8},{1,17},{9,25},{17,1},{25,9},{2,18},{10... | collective-permute-start | bytes 4718600 | tf_op jit(solution)/shard_map/ppermute | solution.py:290
  693.1 67.5 %collective-permute-start.59 = (bf16[3,128,2048]{2,1,0:T(8,128)(2,1)S(1)}, bf16[3,128,2048]{2,1,0:T(8,128)(2,1)S(1)}, u32[]{:S(2)}, u32[]{:S(2)}) collective-permute-start(bf16[3,128,2048]{2,1,0:T(8,128)(2,1)S(1)} %copy-done.47), channel_id=1, source_target_pairs={{0,24},{8,16},{16,8},{24,0},{1,25},{9,17},{17,9},{25,1},{2,26},{10... | collective-permute-start | bytes 4718600 | tf_op jit(solution)/shard_map/ppermute | solution.py:290
  788.0 234.3 %reduce-scatter.14.cloned.1.call-start = ((), (), s32[]{:S(2)}) async-start(), calls=%async_computation.14 | async-start | bytes 4718592 | tf_op jit(solution)/shard_map/reduce_scatter | solution.py:611
  807.6 53.2 %collective-permute-start.86 = (bf16[1024,2048]{1,0:T(8,128)(2,1)}, bf16[1024,2048]{1,0:T(8,128)(2,1)}, u32[]{:S(2)}, u32[]{:S(2)}) collective-permute-start(bf16[1024,2048]{1,0:T(8,128)(2,1)} %convolution_convert_fusion.1), channel_id=1, source_target_pairs={{0,1},{1,0},{2,3},{3,2},{4,5},{5,4},{6,7},{7,6},{8,9},{9,8},{10,11... | collective-permute-start | bytes 12582920 | tf_op jit(solution)/shard_map/ppermute | solution.py:287
  868.5 61.8 %collective-permute-start.87 = (bf16[1024,512]{1,0:T(8,128)(2,1)S(1)}, bf16[1024,512]{1,0:T(8,128)(2,1)S(1)}, u32[]{:S(2)}, u32[]{:S(2)}) collective-permute-start(bf16[1024,512]{1,0:T(8,128)(2,1)S(1)} %get-tuple-element.300), channel_id=1, source_target_pairs={{0,8},{8,0},{16,24},{24,16},{1,9},{9,1},{17,25},{25,17},{2,10},{10... | collective-permute-start | bytes 3145736 | tf_op jit(solution)/shard_map/ppermute | solution.py:290
  870.5 63.9 %collective-permute-start.88 = (bf16[1024,512]{1,0:T(8,128)(2,1)}, bf16[1024,512]{1,0:T(8,128)(2,1)}, u32[]{:S(2)}, u32[]{:S(2)}) collective-permute-start(bf16[1024,512]{1,0:T(8,128)(2,1)} %get-tuple-element.299), channel_id=1, source_target_pairs={{0,16},{8,24},{16,0},{24,8},{1,17},{9,25},{17,1},{25,9},{2,18},{10... | collective-permute-start | bytes 3145736 | tf_op jit(solution)/shard_map/ppermute | solution.py:290
  873.6 49.8 %collective-permute-start.84 = (bf16[320,512]{1,0:T(8,128)(2,1)S(1)}, bf16[320,512]{1,0:T(8,128)(2,1)S(1)}, u32[]{:S(2)}, u32[]{:S(2)}) collective-permute-start(bf16[320,512]{1,0:T(8,128)(2,1)S(1)} %get-tuple-element.382), channel_id=1, source_target_pairs={{0,16},{8,24},{16,0},{24,8},{1,17},{9,25},{17,1},{25,9},{2,18},{10... | collective-permute-start | bytes 983048 | tf_op jit(solution)/shard_map/ppermute | solution.py:290
  874.4 52.1 %collective-permute-start.85 = (bf16[320,512]{1,0:T(8,128)(2,1)S(1)}, bf16[320,512]{1,0:T(8,128)(2,1)S(1)}, u32[]{:S(2)}, u32[]{:S(2)}) collective-permute-start(bf16[320,512]{1,0:T(8,128)(2,1)S(1)} %get-tuple-element.381), channel_id=1, source_target_pairs={{0,24},{8,16},{16,8},{24,0},{1,25},{9,17},{17,9},{25,1},{2,26},{10... | collective-permute-start | bytes 983048 | tf_op jit(solution)/shard_map/ppermute | solution.py:290
  923.4 80.9 %collective-permute-start.80 = (bf16[512,768]{0,1:T(8,128)(2,1)}, bf16[512,768]{0,1:T(8,128)(2,1)}, u32[]{:S(2)}, u32[]{:S(2)}) collective-permute-start(bf16[512,768]{0,1:T(8,128)(2,1)} %get-tuple-element.309), channel_id=1, source_target_pairs={{0,8},{8,0},{16,24},{24,16},{1,9},{9,1},{17,25},{25,17},{2,10},{10... | collective-permute-start | bytes 2359304 | tf_op jit(solution)/shard_map/ppermute | solution.py:290
  926.5 80.1 %collective-permute-start.81 = (bf16[512,768]{0,1:T(8,128)(2,1)}, bf16[512,768]{0,1:T(8,128)(2,1)}, u32[]{:S(2)}, u32[]{:S(2)}) collective-permute-start(bf16[512,768]{0,1:T(8,128)(2,1)} %get-tuple-element.308), channel_id=1, source_target_pairs={{0,16},{8,24},{16,0},{24,8},{1,17},{9,25},{17,1},{25,9},{2,18},{10... | collective-permute-start | bytes 2359304 | tf_op jit(solution)/shard_map/ppermute | solution.py:290
  930.3 76.9 %collective-permute-start.82 = (bf16[512,768]{0,1:T(8,128)(2,1)}, bf16[512,768]{0,1:T(8,128)(2,1)}, u32[]{:S(2)}, u32[]{:S(2)}) collective-permute-start(bf16[512,768]{0,1:T(8,128)(2,1)} %get-tuple-element.307), channel_id=1, source_target_pairs={{0,24},{8,16},{16,8},{24,0},{1,25},{9,17},{17,9},{25,1},{2,26},{10... | collective-permute-start | bytes 2359304 | tf_op jit(solution)/shard_map/ppermute | solution.py:290
  938.2 81.9 %collective-permute-start.90 = (bf16[256,512]{1,0:T(8,128)(2,1)}, bf16[256,512]{1,0:T(8,128)(2,1)}, u32[]{:S(2)}, u32[]{:S(2)}) collective-permute-start(bf16[256,512]{1,0:T(8,128)(2,1)} %get-tuple-element.333), channel_id=1, source_target_pairs={{0,2},{1,3},{2,0},{3,1},{4,6},{5,7},{6,4},{7,5},{8,10},{9,11},{10,... | collective-permute-start | bytes 786440 | tf_op jit(solution)/shard_map/ppermute | solution.py:293
  948.2 72.0 %collective-permute-start.91 = (bf16[256,512]{1,0:T(8,128)(2,1)}, bf16[256,512]{1,0:T(8,128)(2,1)}, u32[]{:S(2)}, u32[]{:S(2)}) collective-permute-start(bf16[256,512]{1,0:T(8,128)(2,1)} %get-tuple-element.332), channel_id=1, source_target_pairs={{0,4},{1,5},{2,6},{3,7},{4,0},{5,1},{6,2},{7,3},{8,12},{9,13},{10,... | collective-permute-start | bytes 786440 | tf_op jit(solution)/shard_map/ppermute | solution.py:293
  (262 other events, 3624.0 us)
Sparse Core Ops, SparseCore 0:
  11.5 72.0 all-gather.5
  85.7 45.6 all-gather.7
  133.7 56.8 all-gather.11
  192.6 107.7 all-gather.9
  302.4 63.3 all-gather.13
  460.3 53.6 reduce-scatter.5
  579.4 100.8 reduce-scatter.7
  686.4 66.7 reduce-scatter.9
  788.2 67.6 reduce-scatter.11
  858.0 51.7 reduce-scatter.13

commit v5 on v4

--- a/solution.py
+++ b/solution.py
@@ -401,10 +401,9 @@
         pre_rows = pre_rows.reshape(2 * part, width)
         pre_gathered = z_gather(pre_rows)
 
-        def group_rows(x):
-            parts = dp_relative(x)
-            own = jnp.concatenate(parts, axis=0)
-            return jnp.concatenate([own, to_core(own)], axis=0), parts[1:]
+        def both_cores(blocks):
+            own = jnp.concatenate(blocks, axis=0)
+            return jnp.concatenate([own, to_core(own)], axis=0)
 
         def context_to_tokens(context):
             blocks = context.reshape(zs, 2, rows, inner)
@@ -438,17 +437,29 @@
             return jnp.stack(reorder(moved, z_at)).reshape(length, inner)
 
         qkv_all, lse_all, ctx_own, ctx_other, swaps = [], [], [], [], []
-        mid_rows, second_norm, norm_two_full, cot_full = [], [], [], []
+        mid_rows, second_norm, norm_two_full = [], [], []
+
+        early = dp_relative(
+            after(jnp.concatenate([out_grad[0], out_grad[1]], axis=0), *arrived)
+        )
+        recent = [early[1:]]
+        cot_full = []
 
         def feed_forward_input(s):
             own, other = ctx_own[s], ctx_other[s]
+            if s == 1:
+                own = after(own, *recent[-1])
             mid = x_rows[s] + (nn_dot(own, out_own) + nn_dot(other, out_other))
             mid_rows.append(mid)
             second_norm.append(rms_parts(mid, gain_two))
             normed = second_norm[s][2]
-            if s == 0:
-                normed = after(normed, *cot_parts[1:])
-            norm_two_full.append(group_rows(normed)[0])
+            normed = after(normed, *recent[-1])
+            riders = [out_grad[t] for t in every if 1 <= s == t - 1]
+            parts = dp_relative(jnp.concatenate([normed, *riders], axis=0))
+            recent.append(parts[1:])
+            norm_two_full.append(both_cores([x[:rows] for x in parts]))
+            for i in range(1, len(riders) + 1):
+                cot_full.append(both_cores([x[i * rows : (i + 1) * rows] for x in parts]))
 
         for s in every:
             if s == 0:
@@ -465,11 +476,14 @@
                 post_gathered = z_gather(after(post_rows, context))
                 out_z = jnp.concatenate(reorder(after(out_z, context), z_at), axis=0)
                 out_parts = dp_relative(after(out_z, *arrived))
-                cot_parts = dp_relative(after(out_grad, *out_parts[1:]))
             if s == 1:
                 out_parts = after(tuple(out_parts), context)
                 out_own = jnp.concatenate(reorder(out_parts, dp_at), axis=1)
                 out_other = to_core(out_own)
+            if s == 1:
+                taken = after(tuple(early), context)
+                cot_full.append(both_cores([x[:rows] for x in taken]))
+                cot_full.append(both_cores([x[rows:] for x in taken]))
             if s > 0:
                 feed_forward_input(s - 1)
                 context = after(context, second_norm[s - 1][2])
@@ -480,23 +494,11 @@
             ctx_other.append(other)
             swaps.append(swapped)
         feed_forward_input(seqs - 1)
-        cot_parts = after(tuple(cot_parts), second_norm[-1][2])
-        cot_own = jnp.concatenate([c[i] for i in every for c in cot_parts], axis=0)
-        cot_other = to_core(cot_own)
-
         pre_gathered = after(pre_gathered, norm_two_full[-1])
         w_pre = jnp.transpose(
             pre_gathered.reshape(zs, 2, part, width), (1, 0, 2, 3)
         ).reshape(2 * ff, width)
         half = dp_size * rows
-        cot_full = [
-            jnp.concatenate(
-                [cot_own[s * half : (s + 1) * half], cot_other[s * half : (s + 1) * half]],
-                axis=0,
-            )
-            for s in every
-        ]
-
         first_parts, hidden_all = [], []
         grad_post = None
         for s in every:
@@ -519,8 +521,6 @@
                 cot = after(cot, *sums[s - 2])
             grad_gate, grad_up = pull(nt_dot(cot, w_post))
             grad_pre = jnp.concatenate([grad_gate, grad_up], axis=1).astype(jnp.bfloat16)
-            if s == seqs - 1:
-                grad_pre = after(grad_pre, post_z)
             ready = nn_dot(grad_pre, w_pre)
             got = to_core(ready[half:].astype(jnp.bfloat16))
             own = ready[:half] + got.astype(jnp.float32)
@@ -533,11 +533,32 @@
             swaps_in.append(got)
             sent_in.append(sent)
             pre_all.append(grad_pre)
+        grad_mid, grad_mid_low, gain_two_sum = [], [], None
+        for s in every:
+            plain, inv, _ = second_norm[s]
+            more = jnp.sum(grad_norm_two[s] * plain, axis=0)
+            gain_two_sum = more if gain_two_sum is None else gain_two_sum + more
+            grad = out_grad[s].astype(jnp.float32) + rms_back(
+                grad_norm_two[s], plain, inv, gain_two
+            )
+            grad_mid.append(grad)
+            grad_mid_low.append(grad.astype(jnp.bfloat16))
+
+        moves, swapped_in = [], []
+        for s in every:
+            back_own = nt_dot(grad_mid_low[s], out_own).astype(jnp.bfloat16)
+            back_other = nt_dot(grad_mid_low[s], out_other).astype(jnp.bfloat16)
+            moved, got = send_tokens(back_own, back_other)
+            moves.append(moved)
+            swapped_in.append(got)
+
         grad_pre_w = None
         for s in every:
             grad_pre = after(pre_all[s], ready)
-            if s < seqs - 1:
-                grad_pre = after(grad_pre, *sent_in[s], *sums[s + 1])
+            if s == 0:
+                grad_pre = after(grad_pre, *sums[1], post_z)
+            else:
+                grad_pre = after(grad_pre, swapped_in[s - 1])
             more = tn_dot(grad_pre, norm_two_full[s])
             grad_pre_w = more if grad_pre_w is None else grad_pre_w + more
         grad_pre_w = grad_pre_w.astype(jnp.bfloat16)
@@ -561,25 +582,6 @@
         out_sent = [to_dp(out_blocks[k - 1], k) for k in range(1, dp_size)]
         ffn_own = own[:, 0]
 
-        grad_mid, grad_mid_low, gain_two_sum = [], [], None
-        for s in every:
-            plain, inv, _ = second_norm[s]
-            more = jnp.sum(grad_norm_two[s] * plain, axis=0)
-            gain_two_sum = more if gain_two_sum is None else gain_two_sum + more
-            grad = out_grad[s].astype(jnp.float32) + rms_back(
-                grad_norm_two[s], plain, inv, gain_two
-            )
-            grad_mid.append(grad)
-            grad_mid_low.append(grad.astype(jnp.bfloat16))
-
-        moves, swapped_in = [], []
-        for s in every:
-            back_own = nt_dot(grad_mid_low[s], out_own).astype(jnp.bfloat16)
-            back_other = nt_dot(grad_mid_low[s], out_other).astype(jnp.bfloat16)
-            moved, got = send_tokens(back_own, back_other)
-            moves.append(moved)
-            swapped_in.append(got)
-
         def ffn_send(z_rows):
             return tuple(exchange(to_dp, lambda k: feature_block(z_rows, k), dp_size))
 
@@ -588,23 +590,29 @@
             return [moved[:, m].reshape(ff, feats).astype(jnp.float32) for m in range(mats)]
 
         post_moved = ffn_send(post_z)
+        pre_moved = ffn_send(pre_z)
         grad_normed, grad_scores, normed_parts, qkv_grads = [], [], [], []
         grad_qkv = None
-        gate = (grad_pre_w, *out_blocks)
+        gate = (grad_pre_w,)
         for s in every:
             moved = after(moves[s], *gate)
             if s < seqs - 1:
                 moved = after(moved, swapped_in[s + 1])
             if s == 1:
-                moved = after(moved, *out_sent)
+                moved = after(moved, *out_blocks)
             if s == seqs - 1:
-                moved = after(moved, pre_z, *post_moved[1:])
+                moved = after(moved, *post_moved[1:], *pre_moved[1:], *out_give_dp)
             grad_proj, grad_score = attention_backward(
                 qkv_all[s], take_tokens(moved), bias_t, lse_all[s]
             )
             grad_scores.append(grad_score)
             qkv_grads.append(grad_proj)
-            normed_part = nt_dot(grad_proj, w_qkv).astype(jnp.bfloat16)
+            ordered = grad_proj
+            if s == 1:
+                ordered = after(ordered, *out_sent)
+            if s == seqs - 1:
+                ordered = after(ordered, *out_moved[1:])
+            normed_part = nt_dot(ordered, w_qkv).astype(jnp.bfloat16)
             normed_parts.append(normed_part)
             gate = (normed_part,)
             grad_normed.append(
@@ -627,16 +635,13 @@
                 gate = gate + (grad_qkv,)
             if s == 1:
                 out_sum = out_keep + after(out_got, normed_part).astype(jnp.float32)
-                out_moved = tuple(
-                    exchange(
-                        to_dp,
-                        lambda k: feature_block(out_sum, k)
-                        if k == 0
-                        else feature_block(out_sum, k).astype(jnp.bfloat16),
-                        dp_size,
-                    )
+                out_give_dp = [
+                    feature_block(out_sum, k).astype(jnp.bfloat16) for k in range(1, dp_size)
+                ]
+                out_moved = (
+                    feature_block(out_sum, 0),
+                    *[to_dp(out_give_dp[k - 1], k) for k in range(1, dp_size)],
                 )
-        pre_moved = ffn_send(pre_z)
         out_moved = after(out_moved, normed_parts[-1])
         grad_out_z = sum(m.astype(jnp.float32) for m in out_moved)
         grad_out_keep = lax.dynamic_slice_in_dim(grad_out_z, z_at * inner, inner, 0)
@@ -655,7 +660,7 @@
         ]
         qkv_sent = [to_dp(qkv_blocks[k - 1], k) for k in range(1, dp_size)]
         bucket_gate = after(
-            buckets_t, *pre_moved[1:], *grad_out_blocks, *qkv_blocks, grad_normed[0]
+            buckets_t, *grad_out_blocks, *qkv_blocks, grad_normed[0]
         )
         table_grad = bucket_sums(bucket_gate, grad_scores, bucket_count)
         grad_out = grad_out_keep + sum(
@@ -664,8 +669,9 @@
         summed = lax.dynamic_slice_in_dim(grad_qkv, dp_at * feats, feats, 0) + sum(
             x.astype(jnp.float32) for x in after(tuple(qkv_sent), table_grad)
         )
-        out_sent = after(tuple(out_sent), normed_parts[-1])
-        ffn_out = ffn_own + sum(m.astype(jnp.float32) for m in out_sent)
+        ffn_out = ffn_own + sum(
+            m.astype(jnp.float32) for m in after(tuple(out_sent), normed_parts[-1])
+        )
         output = jnp.stack(
             [(mid_rows[s] + ffn_out[s]).astype(jnp.bfloat16) for s in every]
         )

time: 1070 us -> 1050 us (0.981); the launches traced: 1050 us -> 1050 us
  waiting for transfers between devices: 281 us -> 305 us
  matrix products: 234 us -> 212 us
  starting transfers between devices: 138 us -> 127 us
    ppermute x53, waiting for transfers between devices: 173 us -> 221 us  [to_dp(): return lax.ppermute(x, 'dp', xor_pairs(dp_size, mask))]
    all_gather x3, waiting for transfers between devices: 32.1 us -> 0.01 us  [body(): lax.all_gather(first_norm[s][2], 'tensor', axis=0, tiled=True)]
    ppermute x24, waiting for transfers between devices: 55.8 us -> 78.3 us  [to_z(): return lax.ppermute(x, 'tensor', xor_pairs(tensor_size, 2 * mask))]
    reduce_scatter x2, waiting for transfers between devices: 14.4 us -> 0.01 us  [z_scatter(): lax.psum_scatter(x, 'tensor', scatter_dimension=0, tiled=True, axis_index...]
    ppermute x24, starting transfers between devices: 68.1 us -> 54 us  [to_z(): return lax.ppermute(x, 'tensor', xor_pairs(tensor_size, 2 * mask))]
    dot_general x14, matrix products: 77.2 us -> 63.2 us  [nn_dot(): return jnp.dot(left, right, preferred_element_type=jnp.float32)]
    unnamed x411 -> x473, local copies, waits for them, and re-layouts: 68.4 us -> 66.3 us
  transfers between devices with their start and end apart: 106 -> 108, of which waited for: 36 -> 31; matrix products, arithmetic and copies ran while one was open for 34% -> 31% of each run, Pallas kernels for 17% -> 17%
where the time goes in v5:
time: 1050 us
  waiting for transfers between devices  305 us (29%)
  matrix products  212 us (20%)
  Pallas kernels  177 us (17%)
  starting transfers between devices  127 us (12%)
  local copies, waits for them, and re-layouts  111 us (11%)
  other arithmetic  96.5 us (9%)
  between operations  18 us (2%)
    ppermute x53, waiting for transfers between devices, to_dp(): return lax.ppermute(x, 'dp', xor_pairs(dp_size, mask))  221 us
    dot_general x15, matrix products, nt_dot(): lax.dot_general(left, right, (((1,), (1,)), ((), ())), preferred_element_...  79.8 us
    ppermute x24, waiting for transfers between devices, to_z(): return lax.ppermute(x, 'tensor', xor_pairs(tensor_size, 2 * mask))  78.3 us
    dot_general x11, matrix products, tn_dot(): lax.dot_general(left, right, (((0,), (0,)), ((), ())), preferred_element_...  68.6 us
    unnamed x473, local copies, waits for them, and re-layouts  66.3 us
    dot_general x14, matrix products, nn_dot(): return jnp.dot(left, right, preferred_element_type=jnp.float32)  63.2 us
    ppermute x53, starting transfers between devices, to_dp(): return lax.ppermute(x, 'dp', xor_pairs(dp_size, mask))  62.7 us
    pallas_call x3, Pallas kernels, attention_backward(): pl.pallas_call(functools.partial(backward_kernel, min(256, length)), grid...  57.6 us
  transfers between devices with their start and end apart: 108, of which 31 were waited for; matrix products, arithmetic and copies ran while one was open for 31% of the time, Pallas kernels for 17%

profile of v5, /device:TPU:0, one launch (start us, length us, event | category | flops | bytes accessed | tf_op | source)
XLA Modules:
  0.0 1046.4 jit_solution(1804403074223823)
XLA Ops:
  34.3 14.0 %expand_bias.1.bias_ref = bf16[4,1024,1024]{2,1,0:T(8,128)(2,1)} custom-call(s32[1024,1024]{1,0:T(8,128)} %bitcast.326, f32[4,128]{1,0:T(4,128)} %pad_convert_fusion.table_ref), custom_call_target="tpu_custom_call" | custom-call | flops 4096 | bytes 4096 | tf_op jit(solution)/shard_map/expand_bias/pallas_call | solution.py:50
  48.3 11.9 %collective-permute-done.4 = bf16[512,768]{1,0:T(8,128)(2,1)} collective-permute-done((bf16[512,768]{1,0:T(8,128)(2,1)}, bf16[512,768]{1,0:T(8,128)(2,1)}, u32[]{:S(2)}, u32[]{:S(2)}) %collective-permute-start.4) | collective-permute-done | bytes 786464 | tf_op jit(solution)/shard_map/ppermute | solution.py:290
  76.0 8.7 collective-permute-done.14
  98.1 16.3 %attention_forward.3 = (bf16[1024,256]{1,0:T(8,128)(2,1)S(1)}, f32[2,2,1024]{2,1,0:T(2,128)S(1)}) custom-call(bf16[1024,768]{1,0:T(8,128)(2,1)S(1)} %convolution_convert_fusion.7.qkv_ref, bf16[4,1024,1024]{2,1,0:T(8,128)(2,1)} %expand_bias.1.bias_ref), custom_call_target="tpu_custom_call" | custom-call | flops 4096 | bytes 4096 | tf_op jit(solution)/shard_map/attention_forward/pallas_call | solution.py:93
  144.5 16.4 %attention_forward.4 = (bf16[1024,256]{1,0:T(8,128)(2,1)S(1)}, f32[2,2,1024]{2,1,0:T(2,128)S(1)}) custom-call(bf16[1024,768]{1,0:T(8,128)(2,1)S(1)} %convolution_convert_fusion.6.qkv_ref, bf16[4,1024,1024]{2,1,0:T(8,128)(2,1)} %expand_bias.1.bias_ref), custom_call_target="tpu_custom_call" | custom-call | flops 4096 | bytes 4096 | tf_op jit(solution)/shard_map/attention_forward/pallas_call | solution.py:93
  164.2 21.2 %collective-permute-done.17 = bf16[1024,512]{1,0:T(8,128)(2,1)} collective-permute-done((bf16[1024,512]{1,0:T(8,128)(2,1)}, bf16[1024,512]{1,0:T(8,128)(2,1)}, u32[]{:S(2)}, u32[]{:S(2)}) %collective-permute-start.17) | collective-permute-done | bytes 1048608 | tf_op jit(solution)/shard_map/ppermute | solution.py:290
  205.5 19.4 %collective-permute-done.8 = bf16[128,512]{1,0:T(8,128)(2,1)S(1)} collective-permute-done((bf16[128,512]{1,0:T(8,128)(2,1)S(1)}, bf16[128,512]{1,0:T(8,128)(2,1)S(1)}, u32[]{:S(2)}, u32[]{:S(2)}) %collective-permute-start.8) | collective-permute-done | bytes 131104 | tf_op jit(solution)/shard_map/ppermute | solution.py:293
  247.7 16.9 %attention_forward.5 = (bf16[1024,256]{1,0:T(8,128)(2,1)S(1)}, f32[2,2,1024]{2,1,0:T(2,128)S(1)}) custom-call(bf16[1024,768]{1,0:T(8,128)(2,1)S(1)} %convolution_convert_fusion.5.qkv_ref, bf16[4,1024,1024]{2,1,0:T(8,128)(2,1)} %expand_bias.1.bias_ref), custom_call_target="tpu_custom_call" | custom-call | flops 4096 | bytes 4096 | tf_op jit(solution)/shard_map/attention_forward/pallas_call | solution.py:93
  269.2 9.5 collective-permute-done.25
  307.8 19.7 %collective-permute-done.36 = bf16[256,2048]{1,0:T(8,128)(2,1)S(1)} collective-permute-done((bf16[256,2048]{1,0:T(8,128)(2,1)S(1)}, bf16[256,2048]{1,0:T(8,128)(2,1)S(1)}, u32[]{:S(2)}, u32[]{:S(2)}) %collective-permute-start.36) | collective-permute-done | bytes 1048608 | tf_op jit(solution)/shard_map/ppermute | solution.py:290
  332.3 9.9 collective-permute-done.38
  342.3 9.5 collective-permute-done.39
  407.2 9.5 fusion.7
  416.8 8.9 fusion.217
  484.6 12.2 %collective-permute-done.52 = bf16[128,2048]{1,0:T(8,128)(2,1)S(1)} collective-permute-done((bf16[128,2048]{1,0:T(8,128)(2,1)S(1)}, bf16[128,2048]{1,0:T(8,128)(2,1)S(1)}, u32[]{:S(2)}, u32[]{:S(2)}) %collective-permute-start.52) | collective-permute-done | bytes 524320 | tf_op jit(solution)/shard_map/ppermute | solution.py:290
  497.9 20.6 %collective-permute-done.53 = bf16[128,2048]{1,0:T(8,128)(2,1)S(1)} collective-permute-done((bf16[128,2048]{1,0:T(8,128)(2,1)S(1)}, bf16[128,2048]{1,0:T(8,128)(2,1)S(1)}, u32[]{:S(2)}, u32[]{:S(2)}) %collective-permute-start.53) | collective-permute-done | bytes 524320 | tf_op jit(solution)/shard_map/ppermute | solution.py:290
  524.3 9.1 collective-permute-done.57
  564.6 10.9 %fusion.257 = f32[1280,2048]{1,0:T(8,128)} fusion(bf16[1024,1280]{1,0:T(8,128)(2,1)} %pad_maximum_fusion.2, bf16[1024,2048]{1,0:T(8,128)(2,1)} %copy-done.185), kind=kOutput, calls=%fused_computation.617 | convolution fusion | flops 5368709120 | bytes 17301504 | tf_op jit(solution)/shard_map/dot_general | solution.py:272
  575.5 11.4 %add_convert_fusion = bf16[1280,2048]{1,0:T(8,128)(2,1)S(1)} fusion(f32[1280,2048]{1,0:T(8,128)} %fusion.257, f32[1280,2048]{1,0:T(8,128)} %fusion.258, bf16[1024,1280]{1,0:T(8,128)(2,1)S(1)} %copy-done.54, bf16[1024,2048]{1,0:T(8,128)(2,1)} %constant_dynamic-update-slice_fusion.5), kind=kOutput, calls=%fused_computation.1 | convolution fusion | flops 5376573440 | bytes 33030144 | tf_op jit(solution)/shard_map/dot_general | solution.py:272
  612.9 8.9 collective-permute-done.71
  621.8 10.9 %collective-permute-done.72 = bf16[2,128,256]{2,1,0:T(8,128)(2,1)S(1)} collective-permute-done((bf16[2,128,256]{2,1,0:T(8,128)(2,1)S(1)}, bf16[2,128,256]{2,1,0:T(8,128)(2,1)S(1)}, u32[]{:S(2)}, u32[]{:S(2)}) %collective-permute-start.72) | collective-permute-done | bytes 131104 | tf_op jit(solution)/shard_map/ppermute | solution.py:293
  632.9 19.0 %attention_backward.3 = (bf16[1024,768]{1,0:T(8,128)(2,1)S(1)}, bf16[4,1024,1024]{2,1,0:T(8,128)(2,1)}) custom-call(bf16[1024,768]{1,0:T(8,128)(2,1)S(1)} %convolution_convert_fusion.7.qkv_ref, bf16[1024,256]{1,0:T(8,128)(2,1)S(1)} %bitcast.321, bf16[4,1024,1024]{2,1,0:T(8,128)(2,1)} %expand_bias.1.bias_ref, f32[2,2,1024]{2,1,0:T(2,128)S(1)} %get-tuple-element.184.lse_ref), custom_call_target="tpu_custom_call" | custom-call | flops 4096 | bytes 4096 | tf_op jit(solution)/shard_map/attention_backward/pallas_call | solution.py:161
  680.9 9.6 collective-permute-start.68
  706.2 19.6 %attention_backward.4 = (bf16[1024,768]{1,0:T(8,128)(2,1)S(1)}, bf16[4,1024,1024]{2,1,0:T(8,128)(2,1)}) custom-call(bf16[1024,768]{1,0:T(8,128)(2,1)S(1)} %convolution_convert_fusion.6.qkv_ref, bf16[1024,256]{1,0:T(8,128)(2,1)S(1)} %bitcast.322, bf16[4,1024,1024]{2,1,0:T(8,128)(2,1)} %expand_bias.1.bias_ref, f32[2,2,1024]{2,1,0:T(2,128)S(1)} %get-tuple-element.199.lse_ref), custom_call_target="tpu_custom_call" | custom-call | flops 4096 | bytes 4096 | tf_op jit(solution)/shard_map/attention_backward/pallas_call | solution.py:161
  725.8 14.0 %collective-permute-done.62 = bf16[3,128,2048]{2,1,0:T(8,128)(2,1)} collective-permute-done((bf16[3,128,2048]{2,1,0:T(8,128)(2,1)S(1)}, bf16[3,128,2048]{2,1,0:T(8,128)(2,1)}, u32[]{:S(2)}, u32[]{:S(2)}) %collective-permute-start.62) | collective-permute-done | bytes 1572896 | tf_op jit(solution)/shard_map/ppermute | solution.py:290
  753.3 13.7 %collective-permute-start.65 = (bf16[2,128,256]{2,1,0:T(8,128)(2,1)S(1)}, bf16[2,128,256]{2,1,0:T(8,128)(2,1)S(1)}, u32[]{:S(2)}, u32[]{:S(2)}) collective-permute-start(bf16[2,128,256]{2,1,0:T(8,128)(2,1)S(1)} %get-tuple-element.446), channel_id=1, source_target_pairs={{0,2},{1,3},{2,0},{3,1},{4,6},{5,7},{6,4},{7,5},{8,10},{9,11},{10,... | collective-permute-start | bytes 393224 | tf_op jit(solution)/shard_map/ppermute | solution.py:293
  771.4 10.1 convert_add_fusion.1
  808.5 47.9 %collective-permute-done.78 = bf16[320,512]{1,0:T(8,128)(2,1)S(1)} collective-permute-done((bf16[320,512]{1,0:T(8,128)(2,1)S(1)}, bf16[320,512]{1,0:T(8,128)(2,1)S(1)}, u32[]{:S(2)}, u32[]{:S(2)}) %collective-permute-start.78) | collective-permute-done | bytes 327712 | tf_op jit(solution)/shard_map/ppermute | solution.py:290
  857.2 18.9 %attention_backward.5 = (bf16[1024,768]{1,0:T(8,128)(2,1)S(1)}, bf16[4,1024,1024]{2,1,0:T(8,128)(2,1)}) custom-call(bf16[1024,768]{1,0:T(8,128)(2,1)S(1)} %copy-done.1, bf16[1024,256]{1,0:T(8,128)(2,1)S(1)} %bitcast.320, bf16[4,1024,1024]{2,1,0:T(8,128)(2,1)} %expand_bias.1.bias_ref, f32[2,2,1024]{2,1,0:T(2,128)S(1)} %get-tuple-element.213.lse_ref), custom_call_target="tpu_custom_call" | custom-call | flops 4096 | bytes 4096 | tf_op jit(solution)/shard_map/attention_backward/pallas_call | solution.py:161
  904.6 55.7 %bucket_sums.1 = f32[4,32,8,128]{3,2,1,0:T(8,128)S(1)} custom-call(s32[1024,1024]{1,0:T(8,128)} %bitcast.327, bf16[4,1024,1024]{2,1,0:T(8,128)(2,1)} %get-tuple-element.225.refs_0_, bf16[4,1024,1024]{2,1,0:T(8,128)(2,1)} %get-tuple-element.226.refs_1_, bf16[4,1024,1024]{2,1,0:T(8,128)(2,1)} %get-tuple-element.227.refs_2_), custom_call_target="tpu_custom_call" | custom-call | flops 4096 | bytes 4096 | tf_op jit(solution)/shard_map/bucket_sums/pallas_call | solution.py:223
  974.0 12.5 %collective-permute-done.97 = bf16[8,4]{0,1:T(4,128)(2,1)S(1)} collective-permute-done((bf16[8,4]{0,1:T(4,128)(2,1)S(1)}, bf16[8,4]{0,1:T(4,128)(2,1)S(1)}, u32[]{:S(2)}, u32[]{:S(2)}) %collective-permute-start.97) | collective-permute-done | bytes 96 | tf_op jit(solution)/shard_map/ppermute | solution.py:290
  993.8 8.7 collective-permute-done.93
  (881 shorter events, 522.9 us)
Async XLA Ops:
  7.2 61.1 %all-gather.6.cloned.1.call-start = ((), (), s32[]{:S(2)}) async-start(), calls=%async_computation.5 | async-start | bytes 4718592 | tf_op jit(solution)/shard_map/all_gather | solution.py:365
  11.8 123.6 %all-gather.8.cloned.1.call-start = ((), (), s32[]{:S(2)}) async-start(), calls=%async_computation.6 | async-start | bytes 4718592 | tf_op jit(solution)/shard_map/all_gather | solution.py:365
  12.6 226.3 %all-gather.12.cloned.1.call-start = ((), (), s32[]{:S(2)}) async-start(), calls=%async_computation.8 | async-start | bytes 4718592 | tf_op jit(solution)/shard_map/all_gather | solution.py:365
  13.3 349.7 %all-gather.10.cloned.1.call-start = ((), (), s32[]{:S(2)}) async-start(), calls=%async_computation.7 | async-start | bytes 6553600 | tf_op jit(solution)/shard_map/all_gather | solution.py:308
  88.7 318.5 %all-gather.14.cloned.1.call-start = ((), (), s32[]{:S(2)}) async-start(), calls=%async_computation.9 | async-start | bytes 3276800 | tf_op jit(solution)/shard_map/all_gather | solution.py:308
  96.9 64.0 %collective-permute-start.21 = (bf16[256,2048]{1,0:T(8,128)(2,1)}, bf16[256,2048]{1,0:T(8,128)(2,1)}, u32[]{:S(2)}, u32[]{:S(2)}) collective-permute-start(bf16[256,2048]{1,0:T(8,128)(2,1)} %pad_maximum_fusion.20), channel_id=1, source_target_pairs={{0,16},{8,24},{16,0},{24,8},{1,17},{9,25},{17,1},{25,9},{2,18},{10... | collective-permute-start | bytes 3145736 | tf_op jit(solution)/shard_map/ppermute | solution.py:290
  115.1 45.8 %collective-permute-start.22 = (bf16[256,2048]{1,0:T(8,128)(2,1)}, bf16[256,2048]{1,0:T(8,128)(2,1)}, u32[]{:S(2)}, u32[]{:S(2)}) collective-permute-start(bf16[256,2048]{1,0:T(8,128)(2,1)} %pad_maximum_fusion.20), channel_id=1, source_target_pairs={{0,24},{8,16},{16,8},{24,0},{1,25},{9,17},{17,9},{25,1},{2,26},{10... | collective-permute-start | bytes 3145736 | tf_op jit(solution)/shard_map/ppermute | solution.py:290
  134.0 51.5 %collective-permute-start.17 = (bf16[1024,512]{1,0:T(8,128)(2,1)}, bf16[1024,512]{1,0:T(8,128)(2,1)}, u32[]{:S(2)}, u32[]{:S(2)}) collective-permute-start(bf16[1024,512]{1,0:T(8,128)(2,1)} %pad_maximum_fusion.19), channel_id=1, source_target_pairs={{0,16},{8,24},{16,0},{24,8},{1,17},{9,25},{17,1},{25,9},{2,18},{10... | collective-permute-start | bytes 3145736 | tf_op jit(solution)/shard_map/ppermute | solution.py:290
  136.4 49.0 %collective-permute-start.18 = (bf16[1024,512]{1,0:T(8,128)(2,1)}, bf16[1024,512]{1,0:T(8,128)(2,1)}, u32[]{:S(2)}, u32[]{:S(2)}) collective-permute-start(bf16[1024,512]{1,0:T(8,128)(2,1)} %pad_maximum_fusion.19), channel_id=1, source_target_pairs={{0,24},{8,16},{16,8},{24,0},{1,25},{9,17},{17,9},{25,1},{2,26},{10... | collective-permute-start | bytes 3145736 | tf_op jit(solution)/shard_map/ppermute | solution.py:290
  144.0 420.6 %reduce-scatter.6.cloned.1.call-start = ((), (), s32[]{:S(2)}) async-start(), calls=%async_computation.10 | async-start | bytes 3276800 | tf_op jit(solution)/shard_map/reduce_scatter | solution.py:311
  281.9 45.5 %collective-permute-start.36 = (bf16[256,2048]{1,0:T(8,128)(2,1)S(1)}, bf16[256,2048]{1,0:T(8,128)(2,1)S(1)}, u32[]{:S(2)}, u32[]{:S(2)}) collective-permute-start(bf16[256,2048]{1,0:T(8,128)(2,1)S(1)} %pad_maximum_fusion.21), channel_id=1, source_target_pairs={{0,16},{8,24},{16,0},{24,8},{1,17},{9,25},{17,1},{25,9},{2,18},{10... | collective-permute-start | bytes 3145736 | tf_op jit(solution)/shard_map/ppermute | solution.py:290
  305.3 51.4 %collective-permute-start.26 = (bf16[512,2048]{1,0:T(8,128)(2,1)S(1)}, bf16[512,2048]{1,0:T(8,128)(2,1)S(1)}, u32[]{:S(2)}, u32[]{:S(2)}) collective-permute-start(bf16[512,2048]{1,0:T(8,128)(2,1)S(1)} %pad_maximum_fusion.5), channel_id=1, source_target_pairs={{0,1},{1,0},{2,3},{3,2},{4,5},{5,4},{6,7},{7,6},{8,9},{9,8},{10,11... | collective-permute-start | bytes 6291464 | tf_op jit(solution)/shard_map/ppermute | solution.py:287
  470.4 311.0 %reduce-scatter.8.cloned.1.call-start = ((), (), s32[]{:S(2)}) async-start(), calls=%async_computation.11 | async-start | bytes 6553600 | tf_op jit(solution)/shard_map/reduce_scatter | solution.py:311
  470.4 50.2 %collective-permute-start.48 = (bf16[128,2048]{1,0:T(8,128)(2,1)}, bf16[128,2048]{1,0:T(8,128)(2,1)S(1)}, u32[]{:S(2)}, u32[]{:S(2)}) collective-permute-start(bf16[128,2048]{1,0:T(8,128)(2,1)} %get-tuple-element.345), channel_id=1, source_target_pairs={{0,8},{8,0},{16,24},{24,16},{1,9},{9,1},{17,25},{25,17},{2,10},{10... | collective-permute-start | bytes 1572872 | tf_op jit(solution)/shard_map/ppermute | solution.py:290
  470.8 53.5 %collective-permute-start.49 = (bf16[128,2048]{1,0:T(8,128)(2,1)}, bf16[128,2048]{1,0:T(8,128)(2,1)S(1)}, u32[]{:S(2)}, u32[]{:S(2)}) collective-permute-start(bf16[128,2048]{1,0:T(8,128)(2,1)} %get-tuple-element.344), channel_id=1, source_target_pairs={{0,16},{8,24},{16,0},{24,8},{1,17},{9,25},{17,1},{25,9},{2,18},{10... | collective-permute-start | bytes 1572872 | tf_op jit(solution)/shard_map/ppermute | solution.py:290
  478.7 41.9 %collective-permute-start.54 = (bf16[128,2048]{1,0:T(8,128)(2,1)S(1)}, bf16[128,2048]{1,0:T(8,128)(2,1)S(1)}, u32[]{:S(2)}, u32[]{:S(2)}) collective-permute-start(bf16[128,2048]{1,0:T(8,128)(2,1)S(1)} %get-tuple-element.341), channel_id=1, source_target_pairs={{0,24},{8,16},{16,8},{24,0},{1,25},{9,17},{17,9},{25,1},{2,26},{10... | collective-permute-start | bytes 1572872 | tf_op jit(solution)/shard_map/ppermute | solution.py:290
  589.7 422.4 %reduce-scatter.10.cloned.1.call-start = ((), (), s32[]{:S(2)}) async-start(), calls=%async_computation.12 | async-start | bytes 4718592 | tf_op jit(solution)/shard_map/reduce_scatter | solution.py:619
  603.9 62.8 %collective-permute-start.60 = (bf16[1536,2048]{1,0:T(8,128)(2,1)}, bf16[1536,2048]{1,0:T(8,128)(2,1)}, u32[]{:S(2)}, u32[]{:S(2)}) collective-permute-start(bf16[1536,2048]{1,0:T(8,128)(2,1)} %convolution_convert_fusion), channel_id=1, source_target_pairs={{0,1},{1,0},{2,3},{3,2},{4,5},{5,4},{6,7},{7,6},{8,9},{9,8},{10,11... | collective-permute-start | bytes 18874376 | tf_op jit(solution)/shard_map/ppermute | solution.py:287
  660.9 351.2 %reduce-scatter.12.cloned.1.call-start = ((), (), s32[]{:S(2)}) async-start(), calls=%async_computation.13 | async-start | bytes 4718592 | tf_op jit(solution)/shard_map/reduce_scatter | solution.py:619
  674.7 51.1 %collective-permute-start.61 = (bf16[3,128,2048]{2,1,0:T(8,128)(2,1)S(1)}, bf16[3,128,2048]{2,1,0:T(8,128)(2,1)}, u32[]{:S(2)}, u32[]{:S(2)}) collective-permute-start(bf16[3,128,2048]{2,1,0:T(8,128)(2,1)S(1)} %get-tuple-element.318), channel_id=1, source_target_pairs={{0,8},{8,0},{16,24},{24,16},{1,9},{9,1},{17,25},{25,17},{2,10},{10... | collective-permute-start | bytes 4718600 | tf_op jit(solution)/shard_map/ppermute | solution.py:290
  675.9 63.9 %collective-permute-start.62 = (bf16[3,128,2048]{2,1,0:T(8,128)(2,1)S(1)}, bf16[3,128,2048]{2,1,0:T(8,128)(2,1)}, u32[]{:S(2)}, u32[]{:S(2)}) collective-permute-start(bf16[3,128,2048]{2,1,0:T(8,128)(2,1)S(1)} %get-tuple-element.317), channel_id=1, source_target_pairs={{0,16},{8,24},{16,0},{24,8},{1,17},{9,25},{17,1},{25,9},{2,18},{10... | collective-permute-start | bytes 4718600 | tf_op jit(solution)/shard_map/ppermute | solution.py:290
  677.6 63.1 %collective-permute-start.63 = (bf16[3,128,2048]{2,1,0:T(8,128)(2,1)S(1)}, bf16[3,128,2048]{2,1,0:T(8,128)(2,1)}, u32[]{:S(2)}, u32[]{:S(2)}) collective-permute-start(bf16[3,128,2048]{2,1,0:T(8,128)(2,1)S(1)} %get-tuple-element.316), channel_id=1, source_target_pairs={{0,24},{8,16},{16,8},{24,0},{1,25},{9,17},{17,9},{25,1},{2,26},{10... | collective-permute-start | bytes 4718600 | tf_op jit(solution)/shard_map/ppermute | solution.py:290
  706.0 65.3 %collective-permute-start.80 = (bf16[1024,2048]{1,0:T(8,128)(2,1)}, bf16[1024,2048]{1,0:T(8,128)(2,1)}, u32[]{:S(2)}, u32[]{:S(2)}) collective-permute-start(bf16[1024,2048]{1,0:T(8,128)(2,1)} %convolution_convert_fusion.1), channel_id=1, source_target_pairs={{0,1},{1,0},{2,3},{3,2},{4,5},{5,4},{6,7},{7,6},{8,9},{9,8},{10,11... | collective-permute-start | bytes 12582920 | tf_op jit(solution)/shard_map/ppermute | solution.py:287
  748.4 263.7 %reduce-scatter.14.cloned.1.call-start = ((), (), s32[]{:S(2)}) async-start(), calls=%async_computation.14 | async-start | bytes 4718592 | tf_op jit(solution)/shard_map/reduce_scatter | solution.py:619
  796.5 79.6 %collective-permute-start.81 = (bf16[1024,512]{1,0:T(8,128)(2,1)S(1)}, bf16[1024,512]{1,0:T(8,128)(2,1)S(1)}, u32[]{:S(2)}, u32[]{:S(2)}) collective-permute-start(bf16[1024,512]{1,0:T(8,128)(2,1)S(1)} %get-tuple-element.306), channel_id=1, source_target_pairs={{0,8},{8,0},{16,24},{24,16},{1,9},{9,1},{17,25},{25,17},{2,10},{10... | collective-permute-start | bytes 3145736 | tf_op jit(solution)/shard_map/ppermute | solution.py:290
  797.1 79.0 %collective-permute-start.82 = (bf16[1024,512]{1,0:T(8,128)(2,1)S(1)}, bf16[1024,512]{1,0:T(8,128)(2,1)}, u32[]{:S(2)}, u32[]{:S(2)}) collective-permute-start(bf16[1024,512]{1,0:T(8,128)(2,1)S(1)} %get-tuple-element.305), channel_id=1, source_target_pairs={{0,16},{8,24},{16,0},{24,8},{1,17},{9,25},{17,1},{25,9},{2,18},{10... | collective-permute-start | bytes 3145736 | tf_op jit(solution)/shard_map/ppermute | solution.py:290
  798.3 77.8 %collective-permute-start.83 = (bf16[1024,512]{1,0:T(8,128)(2,1)S(1)}, bf16[1024,512]{1,0:T(8,128)(2,1)}, u32[]{:S(2)}, u32[]{:S(2)}) collective-permute-start(bf16[1024,512]{1,0:T(8,128)(2,1)S(1)} %get-tuple-element.304), channel_id=1, source_target_pairs={{0,24},{8,16},{16,8},{24,0},{1,25},{9,17},{17,9},{25,1},{2,26},{10... | collective-permute-start | bytes 3145736 | tf_op jit(solution)/shard_map/ppermute | solution.py:290
  800.7 55.6 %collective-permute-start.78 = (bf16[320,512]{1,0:T(8,128)(2,1)S(1)}, bf16[320,512]{1,0:T(8,128)(2,1)S(1)}, u32[]{:S(2)}, u32[]{:S(2)}) collective-permute-start(bf16[320,512]{1,0:T(8,128)(2,1)S(1)} %get-tuple-element.372), channel_id=1, source_target_pairs={{0,16},{8,24},{16,0},{24,8},{1,17},{9,25},{17,1},{25,9},{2,18},{10... | collective-permute-start | bytes 983048 | tf_op jit(solution)/shard_map/ppermute | solution.py:290
  801.3 55.1 %collective-permute-start.79 = (bf16[320,512]{1,0:T(8,128)(2,1)S(1)}, bf16[320,512]{1,0:T(8,128)(2,1)S(1)}, u32[]{:S(2)}, u32[]{:S(2)}) collective-permute-start(bf16[320,512]{1,0:T(8,128)(2,1)S(1)} %get-tuple-element.371), channel_id=1, source_target_pairs={{0,24},{8,16},{16,8},{24,0},{1,25},{9,17},{17,9},{25,1},{2,26},{10... | collective-permute-start | bytes 983048 | tf_op jit(solution)/shard_map/ppermute | solution.py:290
  893.9 93.8 %collective-permute-start.92 = (bf16[256,512]{1,0:T(8,128)(2,1)S(1)}, bf16[256,512]{1,0:T(8,128)(2,1)S(1)}, u32[]{:S(2)}, u32[]{:S(2)}) collective-permute-start(bf16[256,512]{1,0:T(8,128)(2,1)S(1)} %get-tuple-element.336), channel_id=1, source_target_pairs={{0,2},{1,3},{2,0},{3,1},{4,6},{5,7},{6,4},{7,5},{8,10},{9,11},{10,... | collective-permute-start | bytes 786440 | tf_op jit(solution)/shard_map/ppermute | solution.py:293
  902.9 101.6 %collective-permute-start.89 = (bf16[512,768]{0,1:T(8,128)(2,1)}, bf16[512,768]{0,1:T(8,128)(2,1)}, u32[]{:S(2)}, u32[]{:S(2)}) collective-permute-start(bf16[512,768]{0,1:T(8,128)(2,1)} %get-tuple-element.315), channel_id=1, source_target_pairs={{0,8},{8,0},{16,24},{24,16},{1,9},{9,1},{17,25},{25,17},{2,10},{10... | collective-permute-start | bytes 2359304 | tf_op jit(solution)/shard_map/ppermute | solution.py:290
  903.4 101.2 %collective-permute-start.90 = (bf16[512,768]{0,1:T(8,128)(2,1)}, bf16[512,768]{0,1:T(8,128)(2,1)}, u32[]{:S(2)}, u32[]{:S(2)}) collective-permute-start(bf16[512,768]{0,1:T(8,128)(2,1)} %get-tuple-element.314), channel_id=1, source_target_pairs={{0,16},{8,24},{16,0},{24,8},{1,17},{9,25},{17,1},{25,9},{2,18},{10... | collective-permute-start | bytes 2359304 | tf_op jit(solution)/shard_map/ppermute | solution.py:290
  (301 other events, 4211.9 us)
Sparse Core Ops, SparseCore 0:
  12.0 49.5 all-gather.5
  63.8 65.0 all-gather.7
  131.1 45.2 all-gather.11
  178.3 130.2 all-gather.9
  310.6 52.9 all-gather.13
  470.5 50.0 reduce-scatter.5
  589.9 101.1 reduce-scatter.7
  693.3 54.5 reduce-scatter.9
  750.2 63.7 reduce-scatter.11
  884.2 53.2 reduce-scatter.13

commit v6 on v5

--- a/solution.py
+++ b/solution.py
@@ -312,16 +312,10 @@
             x, "tensor", scatter_dimension=0, tiled=True, axis_index_groups=z_groups
         )
 
-    def all_sum(x):
-        bit = 1
-        while bit < tensor_size:
-            x = x + lax.ppermute(x, "tensor", xor_pairs(tensor_size, bit))
-            bit *= 2
-        bit = 1
-        while bit < dp_size:
-            x = x + to_dp(x, bit)
-            bit *= 2
-        return x
+    def all_sum(x, dp_at, z_at, core_at):
+        x = sum(reorder([x, to_core(x)], core_at))
+        x = sum(reorder(exchange(to_z, lambda k: x, zs), z_at))
+        return sum(reorder(dp_relative(x), dp_at))
 
     def body(
         hidden_in,
@@ -385,7 +379,7 @@
         w_qkv = jnp.concatenate(reorder(payload, dp_at), axis=0)
 
         out_z = tuple(exchange(to_z, lambda k: w_out, zs))
-        first_qkv = nn_dot(norm_full[0], w_qkv).astype(jnp.bfloat16)
+        first_qkv = nn_dot(after(norm_full[0], *out_z[1:]), w_qkv).astype(jnp.bfloat16)
 
         ffn_local = jnp.stack([w_gate.T, w_up.T, w_down]).reshape(3, dp_size, part, feats)
         ffn_local = after(ffn_local, *arrived)
@@ -400,6 +394,8 @@
         post_rows = jnp.concatenate([p[2] for p in ffn_parts], axis=1)
         pre_rows = pre_rows.reshape(2 * part, width)
         pre_gathered = z_gather(pre_rows)
+
+        out_rows = after(jnp.concatenate(reorder(out_z, z_at), axis=0), *arrived)
 
         def both_cores(blocks):
             own = jnp.concatenate(blocks, axis=0)
@@ -439,10 +435,7 @@
         qkv_all, lse_all, ctx_own, ctx_other, swaps = [], [], [], [], []
         mid_rows, second_norm, norm_two_full = [], [], []
 
-        early = dp_relative(
-            after(jnp.concatenate([out_grad[0], out_grad[1]], axis=0), *arrived)
-        )
-        recent = [early[1:]]
+        recent = []
         cot_full = []
 
         def feed_forward_input(s):
@@ -474,8 +467,11 @@
             context, lse = attention_forward(qkv, bias_t)
             if s == 0:
                 post_gathered = z_gather(after(post_rows, context))
-                out_z = jnp.concatenate(reorder(after(out_z, context), z_at), axis=0)
-                out_parts = dp_relative(after(out_z, *arrived))
+                out_parts = dp_relative(out_rows)
+                early = dp_relative(
+                    after(jnp.concatenate([out_grad[0], out_grad[1]], axis=0), context, *out_parts[1:])
+                )
+                recent.append(early[1:])
             if s == 1:
                 out_parts = after(tuple(out_parts), context)
                 out_own = jnp.concatenate(reorder(out_parts, dp_at), axis=1)
@@ -511,7 +507,7 @@
         grad_post = grad_post.astype(jnp.bfloat16)
         w_post = after(post_gathered, grad_post)
         post_z = z_scatter(grad_post)
-        pre_all, grad_norm_two, sums, swaps_in, sent_in = [], [], [], [], []
+        pre_all, kept, sums, swaps_in, sent_in = [], [], [], [], []
         ready = grad_post
         for s in every:
             pre = first_parts[s]
@@ -528,40 +524,41 @@
                 own[k * rows : (k + 1) * rows].astype(jnp.bfloat16) for k in range(1, dp_size)
             ]
             sent = [to_dp(blocks[k - 1], k) for k in range(1, dp_size)]
-            grad_norm_two.append(own[:rows] + sum(x.astype(jnp.float32) for x in sent))
+            kept.append(own[:rows])
             sums.append(blocks)
             swaps_in.append(got)
             sent_in.append(sent)
             pre_all.append(grad_pre)
         grad_mid, grad_mid_low, gain_two_sum = [], [], None
+        moves, swapped_in, received = [], [], []
+        grad_pre_w = None
         for s in every:
+            grad_pre = after(pre_all[s], ready)
+            if s == 0:
+                grad_pre = after(grad_pre, *sums[1])
+            else:
+                grad_pre = after(grad_pre, swapped_in[s - 1], *sums[-1])
+            if s == seqs - 1:
+                grad_pre = after(grad_pre, post_z)
+            more = tn_dot(grad_pre, norm_two_full[s])
+            grad_pre_w = more if grad_pre_w is None else grad_pre_w + more
+            if s == seqs - 1:
+                grad_pre_w = grad_pre_w.astype(jnp.bfloat16)
+                more = grad_pre_w
+            sent = after(tuple(sent_in[s]), more)
+            received.append(sent)
+            grad_norm = kept[s] + sum(x.astype(jnp.float32) for x in sent)
             plain, inv, _ = second_norm[s]
-            more = jnp.sum(grad_norm_two[s] * plain, axis=0)
+            more = jnp.sum(grad_norm * plain, axis=0)
             gain_two_sum = more if gain_two_sum is None else gain_two_sum + more
-            grad = out_grad[s].astype(jnp.float32) + rms_back(
-                grad_norm_two[s], plain, inv, gain_two
-            )
+            grad = out_grad[s].astype(jnp.float32) + rms_back(grad_norm, plain, inv, gain_two)
             grad_mid.append(grad)
             grad_mid_low.append(grad.astype(jnp.bfloat16))
-
-        moves, swapped_in = [], []
-        for s in every:
             back_own = nt_dot(grad_mid_low[s], out_own).astype(jnp.bfloat16)
             back_other = nt_dot(grad_mid_low[s], out_other).astype(jnp.bfloat16)
             moved, got = send_tokens(back_own, back_other)
             moves.append(moved)
             swapped_in.append(got)
-
-        grad_pre_w = None
-        for s in every:
-            grad_pre = after(pre_all[s], ready)
-            if s == 0:
-                grad_pre = after(grad_pre, *sums[1], post_z)
-            else:
-                grad_pre = after(grad_pre, swapped_in[s - 1])
-            more = tn_dot(grad_pre, norm_two_full[s])
-            grad_pre_w = more if grad_pre_w is None else grad_pre_w + more
-        grad_pre_w = grad_pre_w.astype(jnp.bfloat16)
         pre_z = z_scatter(
             jnp.transpose(
                 grad_pre_w.reshape(2, zs, part, width), (1, 0, 2, 3)
@@ -575,9 +572,8 @@
             after(hidden_other, grad_pre_w),
         )
         sent = to_core(nn_dot(hidden_other, w_post).astype(jnp.bfloat16))
-        own = (nn_dot(after(hidden_own, grad_norm_two[-1]), w_post) + sent.astype(jnp.float32)).reshape(
-            seqs, dp_size, rows, width
-        )
+        own = nn_dot(after(hidden_own, *sent_in[-1]), w_post) + sent.astype(jnp.float32)
+        own = own.reshape(seqs, dp_size, rows, width)
         out_blocks = [own[:, k].astype(jnp.bfloat16) for k in range(1, dp_size)]
         out_sent = [to_dp(out_blocks[k - 1], k) for k in range(1, dp_size)]
         ffn_own = own[:, 0]
@@ -601,13 +597,15 @@
             if s == 1:
                 moved = after(moved, *out_blocks)
             if s == seqs - 1:
-                moved = after(moved, *post_moved[1:], *pre_moved[1:], *out_give_dp)
+                moved = after(moved, *post_moved[1:], *out_give_dp)
             grad_proj, grad_score = attention_backward(
                 qkv_all[s], take_tokens(moved), bias_t, lse_all[s]
             )
             grad_scores.append(grad_score)
             qkv_grads.append(grad_proj)
             ordered = grad_proj
+            if s == 0:
+                ordered = after(ordered, *sent_in[-1])
             if s == 1:
                 ordered = after(ordered, *out_sent)
             if s == seqs - 1:
@@ -660,7 +658,7 @@
         ]
         qkv_sent = [to_dp(qkv_blocks[k - 1], k) for k in range(1, dp_size)]
         bucket_gate = after(
-            buckets_t, *grad_out_blocks, *qkv_blocks, grad_normed[0]
+            buckets_t, *pre_moved[1:], *grad_out_blocks, *qkv_blocks, grad_normed[0]
         )
         table_grad = bucket_sums(bucket_gate, grad_scores, bucket_count)
         grad_out = grad_out_keep + sum(
@@ -706,7 +704,7 @@
                     jnp.bfloat16
                 )
             )
-        gains = all_sum(jnp.stack([gain_one_sum, gain_two_sum]))
+        gains = all_sum(jnp.stack([gain_one_sum, gain_two_sum]), dp_at, z_at, core_at)
         return (
             output,
             jnp.stack(grad_in),

time: 1050 us -> 953 us (0.908)
  waiting for transfers between devices: 305 us -> 193 us
  matrix products: 212 us -> 242 us
  starting transfers between devices: 127 us -> 109 us
    ppermute x53 -> x54, waiting for transfers between devices: 221 us -> 125 us  [to_dp(): return lax.ppermute(x, 'dp', xor_pairs(dp_size, mask))]
    ppermute x24 -> x27, waiting for transfers between devices: 78.3 us -> 49 us  [to_z(): return lax.ppermute(x, 'tensor', xor_pairs(tensor_size, 2 * mask))]
    all_gather x3, waiting for transfers between devices: 0.01 us -> 16.2 us  [body(): lax.all_gather(first_norm[s][2], 'tensor', axis=0, tiled=True)]
    ppermute x24 -> x27, starting transfers between devices: 54 us -> 39.6 us  [to_z(): return lax.ppermute(x, 'tensor', xor_pairs(tensor_size, 2 * mask))]
    dot_general x15, matrix products: 79.8 us -> 90.6 us  [nt_dot(): lax.dot_general(left, right, (((1,), (1,)), ((), ())), preferred_element_...]
    unnamed x473 -> x495, local copies, waits for them, and re-layouts: 66.3 us -> 57.3 us
    ppermute x53 -> x54, starting transfers between devices: 62.7 us -> 65.4 us  [to_dp(): return lax.ppermute(x, 'dp', xor_pairs(dp_size, mask))]
  transfers between devices with their start and end apart: 108 -> 110, of which waited for: 31 -> 25; matrix products, arithmetic and copies ran while one was open for 31% -> 39% of each run, Pallas kernels for 17% -> 19%
where the time goes in v6:
time: 953 us; the launch traced here: 945 us
  matrix products  242 us (25%)
  waiting for transfers between devices  193 us (20%)
  Pallas kernels  177 us (19%)
  local copies, waits for them, and re-layouts  112 us (12%)
  starting transfers between devices  109 us (11%)
  other arithmetic  94.8 us (10%)
  between operations  18.3 us (2%)
    ppermute x54, waiting for transfers between devices, to_dp(): return lax.ppermute(x, 'dp', xor_pairs(dp_size, mask))  125 us
    dot_general x15, matrix products, nt_dot(): lax.dot_general(left, right, (((1,), (1,)), ((), ())), preferred_element_...  90.6 us
    dot_general x11, matrix products, tn_dot(): lax.dot_general(left, right, (((0,), (0,)), ((), ())), preferred_element_...  77.8 us
    dot_general x14, matrix products, nn_dot(): return jnp.dot(left, right, preferred_element_type=jnp.float32)  73.4 us
    ppermute x54, starting transfers between devices, to_dp(): return lax.ppermute(x, 'dp', xor_pairs(dp_size, mask))  65.4 us
    pallas_call x3, Pallas kernels, attention_backward(): pl.pallas_call(functools.partial(backward_kernel, min(256, length)), grid...  57.5 us
    unnamed x495, local copies, waits for them, and re-layouts  57.3 us
    pallas_call x1, Pallas kernels, bucket_sums(): pl.pallas_call(functools.partial(histogram_kernel, bucket_count, 4), grid...  55.4 us
  transfers between devices with their start and end apart: 110, of which 25 were waited for; matrix products, arithmetic and copies ran while one was open for 39% of the time, Pallas kernels for 19%

profile of v6, /device:TPU:0, one launch (start us, length us, event | category | flops | bytes accessed | tf_op | source)
XLA Modules:
  0.0 945.1 jit_solution(7560415211725935066)
XLA Ops:
  37.7 14.0 %expand_bias.1.bias_ref = bf16[4,1024,1024]{2,1,0:T(8,128)(2,1)} custom-call(s32[1024,1024]{1,0:T(8,128)} %bitcast.326, f32[4,128]{1,0:T(4,128)} %pad_convert_fusion.table_ref), custom_call_target="tpu_custom_call" | custom-call | flops 4096 | bytes 4096 | tf_op jit(solution)/shard_map/expand_bias/pallas_call | solution.py:50
  67.4 16.2 %all-gather.6.cloned.1.call-done = bf16[1024,2048]{1,0:T(8,128)(2,1)} async-done(((bf16[128,2048]{1,0:T(8,128)(2,1)}), bf16[1024,2048]{1,0:T(8,128)(2,1)}) %all-gather.6.cloned.1.call-update) | async-done | bytes 4194320 | tf_op jit(solution)/shard_map/all_gather | solution.py:359
  102.1 16.4 %attention_forward.3 = (bf16[1024,256]{1,0:T(8,128)(2,1)S(1)}, f32[2,2,1024]{2,1,0:T(2,128)S(1)}) custom-call(bf16[1024,768]{1,0:T(8,128)(2,1)S(1)} %convolution_convert_fusion.7.qkv_ref, bf16[4,1024,1024]{2,1,0:T(8,128)(2,1)} %expand_bias.1.bias_ref), custom_call_target="tpu_custom_call" | custom-call | flops 4096 | bytes 4096 | tf_op jit(solution)/shard_map/attention_forward/pallas_call | solution.py:93
  121.8 22.9 %collective-permute-done.17 = bf16[1024,512]{1,0:T(8,128)(2,1)S(1)} collective-permute-done((bf16[1024,512]{1,0:T(8,128)(2,1)S(1)}, bf16[1024,512]{1,0:T(8,128)(2,1)S(1)}, u32[]{:S(2)}, u32[]{:S(2)}) %collective-permute-start.17) | collective-permute-done | bytes 1048608 | tf_op jit(solution)/shard_map/ppermute | solution.py:290
  161.0 17.0 %attention_forward.4 = (bf16[1024,256]{1,0:T(8,128)(2,1)S(1)}, f32[2,2,1024]{2,1,0:T(2,128)S(1)}) custom-call(bf16[1024,768]{1,0:T(8,128)(2,1)S(1)} %convolution_convert_fusion.6.qkv_ref, bf16[4,1024,1024]{2,1,0:T(8,128)(2,1)} %expand_bias.1.bias_ref), custom_call_target="tpu_custom_call" | custom-call | flops 4096 | bytes 4096 | tf_op jit(solution)/shard_map/attention_forward/pallas_call | solution.py:93
  183.3 9.4 collective-permute-done.21
  236.2 16.5 %attention_forward.5 = (bf16[1024,256]{1,0:T(8,128)(2,1)S(1)}, f32[2,2,1024]{2,1,0:T(2,128)S(1)}) custom-call(bf16[1024,768]{1,0:T(8,128)(2,1)S(1)} %convolution_convert_fusion.5.qkv_ref, bf16[4,1024,1024]{2,1,0:T(8,128)(2,1)} %expand_bias.1.bias_ref), custom_call_target="tpu_custom_call" | custom-call | flops 4096 | bytes 4096 | tf_op jit(solution)/shard_map/attention_forward/pallas_call | solution.py:93
  287.4 11.0 %collective-permute-done.33 = bf16[128,512]{1,0:T(8,128)(2,1)S(1)} collective-permute-done((bf16[128,512]{1,0:T(8,128)(2,1)S(1)}, bf16[128,512]{1,0:T(8,128)(2,1)S(1)}, u32[]{:S(2)}, u32[]{:S(2)}) %collective-permute-start.33) | collective-permute-done | bytes 131104 | tf_op jit(solution)/shard_map/ppermute | solution.py:293
  305.3 11.5 %collective-permute-done.36 = bf16[256,2048]{1,0:T(8,128)(2,1)S(1)} collective-permute-done((bf16[256,2048]{1,0:T(8,128)(2,1)S(1)}, bf16[256,2048]{1,0:T(8,128)(2,1)S(1)}, u32[]{:S(2)}, u32[]{:S(2)}) %collective-permute-start.36) | collective-permute-done | bytes 1048608 | tf_op jit(solution)/shard_map/ppermute | solution.py:290
  321.7 9.9 %collective-permute-done.38 = bf16[128,2048]{1,0:T(8,128)(2,1)S(1)} collective-permute-done((bf16[128,2048]{1,0:T(8,128)(2,1)S(1)}, bf16[128,2048]{1,0:T(8,128)(2,1)S(1)}, u32[]{:S(2)}, u32[]{:S(2)}) %collective-permute-start.38) | collective-permute-done | bytes 524320 | tf_op jit(solution)/shard_map/ppermute | solution.py:290
  332.7 7.2 collective-permute-done.40
  371.3 7.9 fusion.253
  396.3 9.5 %fusion.7 = (bf16[1024,640]{1,0:T(8,128)(2,1)S(1)}, bf16[1024,640]{1,0:T(8,128)(2,1)S(1)}) fusion(f32[1024,1280]{1,0:T(8,128)} %copy-done.38, bf16[1024,2048]{1,0:T(8,128)(2,1)} %constant_dynamic-update-slice_fusion.15, bf16[640,2048]{1,0:T(8,128)(2,1)} %all-gather.14.cloned.1.call-done), kind=kOutput, calls=%fused_computation.33 | convolution fusion | flops 2700083200 | bytes 14680064 | tf_op jit(solution)/shard_map/dot_general | solution.py:16
  406.8 7.9 fusion.216
  416.9 10.1 %fusion.14 = (bf16[1024,640]{1,0:T(8,128)(2,1)S(1)}, bf16[1024,640]{1,0:T(8,128)(2,1)S(1)}) fusion(f32[1024,1280]{1,0:T(8,128)S(1)} %bitcast.343, bf16[1024,2048]{1,0:T(8,128)(2,1)} %constant_dynamic-update-slice_fusion.20, bf16[640,2048]{1,0:T(8,128)(2,1)S(1)} %copy-done.222), kind=kOutput, calls=%fused_computation.40 | convolution fusion | flops 2700083200 | bytes 14680064 | tf_op jit(solution)/shard_map/dot_general | solution.py:16
  458.8 7.5 fusion.214
  472.4 10.6 %fusion.256 = f32[1280,2048]{1,0:T(8,128)} fusion(bf16[1024,1280]{1,0:T(8,128)(2,1)S(1)} %copy-done.51, bf16[1024,2048]{1,0:T(8,128)(2,1)} %copy-done.191), kind=kOutput, calls=%fused_computation.619 | convolution fusion | flops 5368709120 | bytes 17301504 | tf_op jit(solution)/shard_map/dot_general | solution.py:272
  501.0 8.3 fusion.257
  518.8 13.3 %add_convert_fusion = bf16[1280,2048]{1,0:T(8,128)(2,1)S(1)} fusion(f32[1280,2048]{1,0:T(8,128)} %fusion.256, f32[1280,2048]{1,0:T(8,128)} %fusion.257, bf16[1024,1280]{1,0:T(8,128)(2,1)} %pad_maximum_fusion.4, bf16[1024,2048]{1,0:T(8,128)(2,1)} %constant_dynamic-update-slice_fusion.5), kind=kOutput, calls=%fused_computation.1 | convolution fusion | flops 5376573440 | bytes 33030144 | tf_op jit(solution)/shard_map/dot_general | solution.py:272
  541.0 7.3 convolution_convert_fusion
  559.9 9.9 %collective-permute-done.71 = bf16[2,128,256]{2,1,0:T(8,128)(2,1)S(1)} collective-permute-done((bf16[2,128,256]{2,1,0:T(8,128)(2,1)S(1)}, bf16[2,128,256]{2,1,0:T(8,128)(2,1)S(1)}, u32[]{:S(2)}, u32[]{:S(2)}) %collective-permute-start.71) | collective-permute-done | bytes 131104 | tf_op jit(solution)/shard_map/ppermute | solution.py:293
  577.0 9.7 %collective-permute-done.73 = bf16[2,128,256]{2,1,0:T(8,128)(2,1)S(1)} collective-permute-done((bf16[2,128,256]{2,1,0:T(8,128)(2,1)S(1)}, bf16[2,128,256]{2,1,0:T(8,128)(2,1)S(1)}, u32[]{:S(2)}, u32[]{:S(2)}) %collective-permute-start.73) | collective-permute-done | bytes 131104 | tf_op jit(solution)/shard_map/ppermute | solution.py:293
  586.8 19.0 %attention_backward.3 = (bf16[1024,768]{1,0:T(8,128)(2,1)S(1)}, bf16[4,1024,1024]{2,1,0:T(8,128)(2,1)}) custom-call(bf16[1024,768]{1,0:T(8,128)(2,1)S(1)} %convolution_convert_fusion.7.qkv_ref, bf16[1024,256]{1,0:T(8,128)(2,1)S(1)} %bitcast.321, bf16[4,1024,1024]{2,1,0:T(8,128)(2,1)} %expand_bias.1.bias_ref, f32[2,2,1024]{2,1,0:T(2,128)S(1)} %get-tuple-element.199.lse_ref), custom_call_target="tpu_custom_call" | custom-call | flops 4096 | bytes 4096 | tf_op jit(solution)/shard_map/attention_backward/pallas_call | solution.py:161
  607.5 7.8 convolution_convert_fusion.4
  662.0 19.5 %attention_backward.4 = (bf16[1024,768]{1,0:T(8,128)(2,1)S(1)}, bf16[4,1024,1024]{2,1,0:T(8,128)(2,1)}) custom-call(bf16[1024,768]{1,0:T(8,128)(2,1)S(1)} %copy-done.1, bf16[1024,256]{1,0:T(8,128)(2,1)S(1)} %bitcast.322, bf16[4,1024,1024]{2,1,0:T(8,128)(2,1)} %expand_bias.1.bias_ref, f32[2,2,1024]{2,1,0:T(2,128)S(1)} %get-tuple-element.215.lse_ref), custom_call_target="tpu_custom_call" | custom-call | flops 4096 | bytes 4096 | tf_op jit(solution)/shard_map/attention_backward/pallas_call | solution.py:161
  681.5 28.0 %collective-permute-done.62 = bf16[3,128,2048]{2,1,0:T(8,128)(2,1)S(1)} collective-permute-done((bf16[3,128,2048]{2,1,0:T(8,128)(2,1)S(1)}, bf16[3,128,2048]{2,1,0:T(8,128)(2,1)S(1)}, u32[]{:S(2)}, u32[]{:S(2)}) %collective-permute-start.62) | collective-permute-done | bytes 1572896 | tf_op jit(solution)/shard_map/ppermute | solution.py:290
  748.6 7.4 convolution_add_fusion.1
  757.9 19.0 %attention_backward.5 = (bf16[1024,768]{1,0:T(8,128)(2,1)S(1)}, bf16[4,1024,1024]{2,1,0:T(8,128)(2,1)}) custom-call(bf16[1024,768]{1,0:T(8,128)(2,1)S(1)} %copy-done.3, bf16[1024,256]{1,0:T(8,128)(2,1)S(1)} %bitcast.320, bf16[4,1024,1024]{2,1,0:T(8,128)(2,1)} %expand_bias.1.bias_ref, f32[2,2,1024]{2,1,0:T(2,128)S(1)} %get-tuple-element.229.lse_ref), custom_call_target="tpu_custom_call" | custom-call | flops 4096 | bytes 4096 | tf_op jit(solution)/shard_map/attention_backward/pallas_call | solution.py:161
  776.9 14.7 %collective-permute-done.80 = bf16[1024,512]{1,0:T(8,128)(2,1)} collective-permute-done((bf16[1024,512]{1,0:T(8,128)(2,1)S(1)}, bf16[1024,512]{1,0:T(8,128)(2,1)}, u32[]{:S(2)}, u32[]{:S(2)}) %collective-permute-start.80) | collective-permute-done | bytes 1048608 | tf_op jit(solution)/shard_map/ppermute | solution.py:290
  791.6 7.6 convolution_convert_fusion.2
  811.1 7.7 convolution_add_fusion
  838.2 55.4 %bucket_sums.1 = f32[4,32,8,128]{3,2,1,0:T(8,128)S(1)} custom-call(s32[1024,1024]{1,0:T(8,128)} %bitcast.327, bf16[4,1024,1024]{2,1,0:T(8,128)(2,1)} %get-tuple-element.241.refs_0_, bf16[4,1024,1024]{2,1,0:T(8,128)(2,1)} %get-tuple-element.242.refs_1_, bf16[4,1024,1024]{2,1,0:T(8,128)(2,1)} %get-tuple-element.243.refs_2_), custom_call_target="tpu_custom_call" | custom-call | flops 4096 | bytes 4096 | tf_op jit(solution)/shard_map/bucket_sums/pallas_call | solution.py:223
  (911 shorter events, 486.6 us)
Async XLA Ops:
  7.2 76.4 %all-gather.6.cloned.1.call-start = ((), (), s32[]{:S(2)}) async-start(), calls=%async_computation.5 | async-start | bytes 4718592 | tf_op jit(solution)/shard_map/all_gather | solution.py:359
  11.4 141.8 %all-gather.8.cloned.1.call-start = ((), (), s32[]{:S(2)}) async-start(), calls=%async_computation.6 | async-start | bytes 4718592 | tf_op jit(solution)/shard_map/all_gather | solution.py:359
  12.1 216.6 %all-gather.12.cloned.1.call-start = ((), (), s32[]{:S(2)}) async-start(), calls=%async_computation.8 | async-start | bytes 4718592 | tf_op jit(solution)/shard_map/all_gather | solution.py:359
  12.9 337.1 %all-gather.10.cloned.1.call-start = ((), (), s32[]{:S(2)}) async-start(), calls=%async_computation.7 | async-start | bytes 6553600 | tf_op jit(solution)/shard_map/all_gather | solution.py:308
  25.1 40.4 %collective-permute-start = (bf16[256,512]{1,0:T(8,128)(2,1)}, bf16[256,512]{1,0:T(8,128)(2,1)S(1)}, u32[]{:S(2)}, u32[]{:S(2)}) collective-permute-start(bf16[256,512]{1,0:T(8,128)(2,1)} %param.21), channel_id=1, source_target_pairs={{0,2},{1,3},{2,0},{3,1},{4,6},{5,7},{6,4},{7,5},{8,10},{9,11},{10,... | collective-permute-start | bytes 786440 | tf_op jit(solution)/shard_map/ppermute | solution.py:293
  27.1 39.9 %collective-permute-start.1 = (bf16[256,512]{1,0:T(8,128)(2,1)}, bf16[256,512]{1,0:T(8,128)(2,1)}, u32[]{:S(2)}, u32[]{:S(2)}) collective-permute-start(bf16[256,512]{1,0:T(8,128)(2,1)} %param.21), channel_id=1, source_target_pairs={{0,4},{1,5},{2,6},{3,7},{4,0},{5,1},{6,2},{7,3},{8,12},{9,13},{10,... | collective-permute-start | bytes 786440 | tf_op jit(solution)/shard_map/ppermute | solution.py:293
  93.9 302.4 %all-gather.14.cloned.1.call-start = ((), (), s32[]{:S(2)}) async-start(), calls=%async_computation.9 | async-start | bytes 3276800 | tf_op jit(solution)/shard_map/all_gather | solution.py:308
  97.2 47.5 %collective-permute-start.17 = (bf16[1024,512]{1,0:T(8,128)(2,1)S(1)}, bf16[1024,512]{1,0:T(8,128)(2,1)S(1)}, u32[]{:S(2)}, u32[]{:S(2)}) collective-permute-start(bf16[1024,512]{1,0:T(8,128)(2,1)S(1)} %pad_maximum_fusion.19), channel_id=1, source_target_pairs={{0,16},{8,24},{16,0},{24,8},{1,17},{9,25},{17,1},{25,9},{2,18},{10... | collective-permute-start | bytes 3145736 | tf_op jit(solution)/shard_map/ppermute | solution.py:290
  98.6 46.0 %collective-permute-start.18 = (bf16[1024,512]{1,0:T(8,128)(2,1)S(1)}, bf16[1024,512]{1,0:T(8,128)(2,1)S(1)}, u32[]{:S(2)}, u32[]{:S(2)}) collective-permute-start(bf16[1024,512]{1,0:T(8,128)(2,1)S(1)} %pad_maximum_fusion.19), channel_id=1, source_target_pairs={{0,24},{8,16},{16,8},{24,0},{1,25},{9,17},{17,9},{25,1},{2,26},{10... | collective-permute-start | bytes 3145736 | tf_op jit(solution)/shard_map/ppermute | solution.py:290
  145.8 46.8 %collective-permute-start.21 = (bf16[256,2048]{1,0:T(8,128)(2,1)}, bf16[256,2048]{1,0:T(8,128)(2,1)S(1)}, u32[]{:S(2)}, u32[]{:S(2)}) collective-permute-start(bf16[256,2048]{1,0:T(8,128)(2,1)} %pad_maximum_fusion.20), channel_id=1, source_target_pairs={{0,16},{8,24},{16,0},{24,8},{1,17},{9,25},{17,1},{25,9},{2,18},{10... | collective-permute-start | bytes 3145736 | tf_op jit(solution)/shard_map/ppermute | solution.py:290
  146.7 46.9 %collective-permute-start.22 = (bf16[256,2048]{1,0:T(8,128)(2,1)}, bf16[256,2048]{1,0:T(8,128)(2,1)}, u32[]{:S(2)}, u32[]{:S(2)}) collective-permute-start(bf16[256,2048]{1,0:T(8,128)(2,1)} %pad_maximum_fusion.20), channel_id=1, source_target_pairs={{0,24},{8,16},{16,8},{24,0},{1,25},{9,17},{17,9},{25,1},{2,26},{10... | collective-permute-start | bytes 3145736 | tf_op jit(solution)/shard_map/ppermute | solution.py:290
  205.0 313.8 %reduce-scatter.6.cloned.1.call-start = ((), (), s32[]{:S(2)}) async-start(), calls=%async_computation.10 | async-start | bytes 3276800 | tf_op jit(solution)/shard_map/reduce_scatter | solution.py:311
  220.7 38.7 %collective-permute-start.23 = (bf16[128,2048]{1,0:T(8,128)(2,1)S(1)}, bf16[128,2048]{1,0:T(8,128)(2,1)S(1)}, u32[]{:S(2)}, u32[]{:S(2)}) collective-permute-start(bf16[128,2048]{1,0:T(8,128)(2,1)S(1)} %multiply_convert_fusion.8), channel_id=1, source_target_pairs={{0,8},{8,0},{16,24},{24,16},{1,9},{9,1},{17,25},{25,17},{2,10},{10... | collective-permute-start | bytes 1572872 | tf_op jit(solution)/shard_map/ppermute | solution.py:290
  271.5 45.3 %collective-permute-start.36 = (bf16[256,2048]{1,0:T(8,128)(2,1)S(1)}, bf16[256,2048]{1,0:T(8,128)(2,1)S(1)}, u32[]{:S(2)}, u32[]{:S(2)}) collective-permute-start(bf16[256,2048]{1,0:T(8,128)(2,1)S(1)} %pad_maximum_fusion.21), channel_id=1, source_target_pairs={{0,16},{8,24},{16,0},{24,8},{1,17},{9,25},{17,1},{25,9},{2,18},{10... | collective-permute-start | bytes 3145736 | tf_op jit(solution)/shard_map/ppermute | solution.py:290
  298.3 45.4 %collective-permute-start.26 = (bf16[512,2048]{1,0:T(8,128)(2,1)S(1)}, bf16[512,2048]{1,0:T(8,128)(2,1)S(1)}, u32[]{:S(2)}, u32[]{:S(2)}) collective-permute-start(bf16[512,2048]{1,0:T(8,128)(2,1)S(1)} %pad_maximum_fusion.5), channel_id=1, source_target_pairs={{0,1},{1,0},{2,3},{3,2},{4,5},{5,4},{6,7},{7,6},{8,9},{9,8},{10,11... | collective-permute-start | bytes 6291464 | tf_op jit(solution)/shard_map/ppermute | solution.py:287
  437.7 381.1 %reduce-scatter.14.cloned.1.call-start = ((), (), s32[]{:S(2)}) async-start(), calls=%async_computation.14 | async-start | bytes 6553600 | tf_op jit(solution)/shard_map/reduce_scatter | solution.py:311
  534.9 380.6 %reduce-scatter.8.cloned.1.call-start = ((), (), s32[]{:S(2)}) async-start(), calls=%async_computation.11 | async-start | bytes 4718592 | tf_op jit(solution)/shard_map/reduce_scatter | solution.py:617
  548.3 82.6 %collective-permute-start.60 = (bf16[1536,2048]{1,0:T(8,128)(2,1)}, bf16[1536,2048]{1,0:T(8,128)(2,1)}, u32[]{:S(2)}, u32[]{:S(2)}) collective-permute-start(bf16[1536,2048]{1,0:T(8,128)(2,1)} %convolution_convert_fusion), channel_id=1, source_target_pairs={{0,1},{1,0},{2,3},{3,2},{4,5},{5,4},{6,7},{7,6},{8,9},{9,8},{10,11... | collective-permute-start | bytes 18874376 | tf_op jit(solution)/shard_map/ppermute | solution.py:287
  557.8 48.1 %collective-permute-start.57 = (bf16[128,2048]{1,0:T(8,128)(2,1)S(1)}, bf16[128,2048]{1,0:T(8,128)(2,1)S(1)}, u32[]{:S(2)}, u32[]{:S(2)}) collective-permute-start(bf16[128,2048]{1,0:T(8,128)(2,1)S(1)} %copy-done.109), channel_id=1, source_target_pairs={{0,8},{8,0},{16,24},{24,16},{1,9},{9,1},{17,25},{25,17},{2,10},{10... | collective-permute-start | bytes 1572872 | tf_op jit(solution)/shard_map/ppermute | solution.py:290
  558.8 47.1 %collective-permute-start.58 = (bf16[128,2048]{1,0:T(8,128)(2,1)S(1)}, bf16[128,2048]{1,0:T(8,128)(2,1)S(1)}, u32[]{:S(2)}, u32[]{:S(2)}) collective-permute-start(bf16[128,2048]{1,0:T(8,128)(2,1)S(1)} %copy-done.108), channel_id=1, source_target_pairs={{0,16},{8,24},{16,0},{24,8},{1,17},{9,25},{17,1},{25,9},{2,18},{10... | collective-permute-start | bytes 1572872 | tf_op jit(solution)/shard_map/ppermute | solution.py:290
  615.4 300.1 %reduce-scatter.10.cloned.1.call-start = ((), (), s32[]{:S(2)}) async-start(), calls=%async_computation.12 | async-start | bytes 4718592 | tf_op jit(solution)/shard_map/reduce_scatter | solution.py:617
  640.3 41.1 %collective-permute-start.61 = (bf16[3,128,2048]{2,1,0:T(8,128)(2,1)S(1)}, bf16[3,128,2048]{2,1,0:T(8,128)(2,1)S(1)}, u32[]{:S(2)}, u32[]{:S(2)}) collective-permute-start(bf16[3,128,2048]{2,1,0:T(8,128)(2,1)S(1)} %get-tuple-element.334), channel_id=1, source_target_pairs={{0,8},{8,0},{16,24},{24,16},{1,9},{9,1},{17,25},{25,17},{2,10},{10... | collective-permute-start | bytes 4718600 | tf_op jit(solution)/shard_map/ppermute | solution.py:290
  641.9 67.6 %collective-permute-start.62 = (bf16[3,128,2048]{2,1,0:T(8,128)(2,1)S(1)}, bf16[3,128,2048]{2,1,0:T(8,128)(2,1)S(1)}, u32[]{:S(2)}, u32[]{:S(2)}) collective-permute-start(bf16[3,128,2048]{2,1,0:T(8,128)(2,1)S(1)} %get-tuple-element.333), channel_id=1, source_target_pairs={{0,16},{8,24},{16,0},{24,8},{1,17},{9,25},{17,1},{25,9},{2,18},{10... | collective-permute-start | bytes 4718600 | tf_op jit(solution)/shard_map/ppermute | solution.py:290
  643.1 67.8 %collective-permute-start.63 = (bf16[3,128,2048]{2,1,0:T(8,128)(2,1)S(1)}, bf16[3,128,2048]{2,1,0:T(8,128)(2,1)}, u32[]{:S(2)}, u32[]{:S(2)}) collective-permute-start(bf16[3,128,2048]{2,1,0:T(8,128)(2,1)S(1)} %get-tuple-element.332), channel_id=1, source_target_pairs={{0,24},{8,16},{16,8},{24,0},{1,25},{9,17},{17,9},{25,1},{2,26},{10... | collective-permute-start | bytes 4718600 | tf_op jit(solution)/shard_map/ppermute | solution.py:290
  661.2 67.9 %collective-permute-start.77 = (bf16[1024,2048]{1,0:T(8,128)(2,1)}, bf16[1024,2048]{1,0:T(8,128)(2,1)}, u32[]{:S(2)}, u32[]{:S(2)}) collective-permute-start(bf16[1024,2048]{1,0:T(8,128)(2,1)} %convolution_convert_fusion.1), channel_id=1, source_target_pairs={{0,1},{1,0},{2,3},{3,2},{4,5},{5,4},{6,7},{7,6},{8,9},{9,8},{10,11... | collective-permute-start | bytes 12582920 | tf_op jit(solution)/shard_map/ppermute | solution.py:287
  717.6 197.9 %reduce-scatter.12.cloned.1.call-start = ((), (), s32[]{:S(2)}) async-start(), calls=%async_computation.13 | async-start | bytes 4718592 | tf_op jit(solution)/shard_map/reduce_scatter | solution.py:617
  748.2 43.4 %collective-permute-start.80 = (bf16[1024,512]{1,0:T(8,128)(2,1)S(1)}, bf16[1024,512]{1,0:T(8,128)(2,1)}, u32[]{:S(2)}, u32[]{:S(2)}) collective-permute-start(bf16[1024,512]{1,0:T(8,128)(2,1)S(1)} %get-tuple-element.320), channel_id=1, source_target_pairs={{0,24},{8,16},{16,8},{24,0},{1,25},{9,17},{17,9},{25,1},{2,26},{10... | collective-permute-start | bytes 3145736 | tf_op jit(solution)/shard_map/ppermute | solution.py:290
  809.5 85.9 %collective-permute-start.94 = (bf16[256,512]{1,0:T(8,128)(2,1)}, bf16[256,512]{1,0:T(8,128)(2,1)}, u32[]{:S(2)}, u32[]{:S(2)}) collective-permute-start(bf16[256,512]{1,0:T(8,128)(2,1)} %get-tuple-element.352), channel_id=1, source_target_pairs={{0,2},{1,3},{2,0},{3,1},{4,6},{5,7},{6,4},{7,5},{8,10},{9,11},{10,... | collective-permute-start | bytes 786440 | tf_op jit(solution)/shard_map/ppermute | solution.py:293
  809.7 90.4 %collective-permute-start.95 = (bf16[256,512]{1,0:T(8,128)(2,1)}, bf16[256,512]{1,0:T(8,128)(2,1)}, u32[]{:S(2)}, u32[]{:S(2)}) collective-permute-start(bf16[256,512]{1,0:T(8,128)(2,1)} %get-tuple-element.351), channel_id=1, source_target_pairs={{0,4},{1,5},{2,6},{3,7},{4,0},{5,1},{6,2},{7,3},{8,12},{9,13},{10,... | collective-permute-start | bytes 786440 | tf_op jit(solution)/shard_map/ppermute | solution.py:293
  832.8 72.0 %collective-permute-start.88 = (bf16[512,768]{0,1:T(8,128)(2,1)}, bf16[512,768]{0,1:T(8,128)(2,1)}, u32[]{:S(2)}, u32[]{:S(2)}) collective-permute-start(bf16[512,768]{0,1:T(8,128)(2,1)} %get-tuple-element.331), channel_id=1, source_target_pairs={{0,8},{8,0},{16,24},{24,16},{1,9},{9,1},{17,25},{25,17},{2,10},{10... | collective-permute-start | bytes 2359304 | tf_op jit(solution)/shard_map/ppermute | solution.py:290
  834.7 72.0 %collective-permute-start.89 = (bf16[512,768]{0,1:T(8,128)(2,1)}, bf16[512,768]{0,1:T(8,128)(2,1)}, u32[]{:S(2)}, u32[]{:S(2)}) collective-permute-start(bf16[512,768]{0,1:T(8,128)(2,1)} %get-tuple-element.330), channel_id=1, source_target_pairs={{0,16},{8,24},{16,0},{24,8},{1,17},{9,25},{17,1},{25,9},{2,18},{10... | collective-permute-start | bytes 2359304 | tf_op jit(solution)/shard_map/ppermute | solution.py:290
  835.2 71.5 %collective-permute-start.90 = (bf16[512,768]{0,1:T(8,128)(2,1)}, bf16[512,768]{0,1:T(8,128)(2,1)}, u32[]{:S(2)}, u32[]{:S(2)}) collective-permute-start(bf16[512,768]{0,1:T(8,128)(2,1)} %get-tuple-element.329), channel_id=1, source_target_pairs={{0,24},{8,16},{16,8},{24,0},{1,25},{9,17},{17,9},{25,1},{2,26},{10... | collective-permute-start | bytes 2359304 | tf_op jit(solution)/shard_map/ppermute | solution.py:290
  (314 other events, 3206.5 us)
Sparse Core Ops, SparseCore 0:
  11.5 72.0 all-gather.5
  85.8 45.5 all-gather.7
  133.5 45.6 all-gather.11
  181.2 121.2 all-gather.9
  304.5 52.6 all-gather.13
  437.8 54.0 reduce-scatter.5
  535.0 109.2 reduce-scatter.13
  646.5 53.0 reduce-scatter.7
  717.7 57.3 reduce-scatter.9
  799.3 56.6 reduce-scatter.11

commit v7 on v6

--- a/solution.py
+++ b/solution.py
@@ -435,61 +435,39 @@
         qkv_all, lse_all, ctx_own, ctx_other, swaps = [], [], [], [], []
         mid_rows, second_norm, norm_two_full = [], [], []
 
-        recent = []
-        cot_full = []
-
-        def feed_forward_input(s):
-            own, other = ctx_own[s], ctx_other[s]
-            if s == 1:
-                own = after(own, *recent[-1])
-            mid = x_rows[s] + (nn_dot(own, out_own) + nn_dot(other, out_other))
-            mid_rows.append(mid)
-            second_norm.append(rms_parts(mid, gain_two))
-            normed = second_norm[s][2]
-            normed = after(normed, *recent[-1])
-            riders = [out_grad[t] for t in every if 1 <= s == t - 1]
-            parts = dp_relative(jnp.concatenate([normed, *riders], axis=0))
-            recent.append(parts[1:])
-            norm_two_full.append(both_cores([x[:rows] for x in parts]))
-            for i in range(1, len(riders) + 1):
-                cot_full.append(both_cores([x[i * rows : (i + 1) * rows] for x in parts]))
-
+        early = dp_relative(after(out_grad.reshape(seqs * rows, width), *arrived))
         for s in every:
             if s == 0:
                 qkv = first_qkv
             else:
                 source = after(norm_full[s], swaps[s - 1])
-                if s > 1:
-                    source = after(source, second_norm[s - 2][2])
                 if s == 1:
                     source = after(source, pre_rows)
                 qkv = nn_dot(source, w_qkv).astype(jnp.bfloat16)
             context, lse = attention_forward(qkv, bias_t)
             if s == 0:
                 post_gathered = z_gather(after(post_rows, context))
-                out_parts = dp_relative(out_rows)
-                early = dp_relative(
-                    after(jnp.concatenate([out_grad[0], out_grad[1]], axis=0), context, *out_parts[1:])
-                )
-                recent.append(early[1:])
-            if s == 1:
-                out_parts = after(tuple(out_parts), context)
-                out_own = jnp.concatenate(reorder(out_parts, dp_at), axis=1)
-                out_other = to_core(out_own)
-            if s == 1:
-                taken = after(tuple(early), context)
-                cot_full.append(both_cores([x[:rows] for x in taken]))
-                cot_full.append(both_cores([x[rows:] for x in taken]))
-            if s > 0:
-                feed_forward_input(s - 1)
-                context = after(context, second_norm[s - 1][2])
+            if s == min(1, seqs - 1):
+                out_parts = dp_relative(after(out_rows, context, *early[1:]))
             own, other, swapped = context_to_tokens(context)
             qkv_all.append(qkv)
             lse_all.append(lse)
             ctx_own.append(own)
             ctx_other.append(other)
             swaps.append(swapped)
-        feed_forward_input(seqs - 1)
+        out_parts = after(tuple(out_parts), context)
+        out_own = jnp.concatenate(reorder(out_parts, dp_at), axis=1)
+        out_other = to_core(out_own)
+        for s in every:
+            own, other = ctx_own[s], ctx_other[s]
+            mid = x_rows[s] + (nn_dot(own, out_own) + nn_dot(other, out_other))
+            mid_rows.append(mid)
+            second_norm.append(rms_parts(mid, gain_two))
+            norm_two_full.append(both_cores(dp_relative(second_norm[s][2])))
+        taken = after(tuple(early), second_norm[-1][2])
+        cot_full = [
+            both_cores([x[s * rows : (s + 1) * rows] for x in taken]) for s in every
+        ]
         pre_gathered = after(pre_gathered, norm_two_full[-1])
         w_pre = jnp.transpose(
             pre_gathered.reshape(zs, 2, part, width), (1, 0, 2, 3)
@@ -539,7 +517,7 @@
             else:
                 grad_pre = after(grad_pre, swapped_in[s - 1], *sums[-1])
             if s == seqs - 1:
-                grad_pre = after(grad_pre, post_z)
+                grad_pre = after(grad_pre, post_z, *moves[0][1:])
             more = tn_dot(grad_pre, norm_two_full[s])
             grad_pre_w = more if grad_pre_w is None else grad_pre_w + more
             if s == seqs - 1:

time: 953 us -> 959 us (level)
  waiting for transfers between devices: 193 us -> 227 us
  matrix products: 242 us -> 215 us
  local copies, waits for them, and re-layouts: 112 us -> 102 us
    ppermute x54, waiting for transfers between devices: 125 us -> 149 us  [to_dp(): return lax.ppermute(x, 'dp', xor_pairs(dp_size, mask))]
    dot_general x14, matrix products: 73.4 us -> 59.4 us  [nn_dot(): return jnp.dot(left, right, preferred_element_type=jnp.float32)]
    all_gather x3, waiting for transfers between devices: 16.2 us -> 25.9 us  [body(): lax.all_gather(first_norm[s][2], 'tensor', axis=0, tiled=True)]
    unnamed x495 -> x446, local copies, waits for them, and re-layouts: 57.3 us -> 49.6 us
  transfers between devices with their start and end apart: 110 -> 110, of which waited for: 25 -> 27; matrix products, arithmetic and copies ran while one was open for 39% -> 35% of each run, Pallas kernels for 19% -> 19%
where the time goes in v7:
time: 959 us; the launch traced here: 951 us
  waiting for transfers between devices  227 us (24%)
  matrix products  215 us (22%)
  Pallas kernels  177 us (18%)
  starting transfers between devices  110 us (11%)
  local copies, waits for them, and re-layouts  102 us (11%)
  other arithmetic  102 us (11%)
  between operations  18.3 us (2%)
    ppermute x54, waiting for transfers between devices, to_dp(): return lax.ppermute(x, 'dp', xor_pairs(dp_size, mask))  149 us
    dot_general x15, matrix products, nt_dot(): lax.dot_general(left, right, (((1,), (1,)), ((), ())), preferred_element_...  81.6 us
    dot_general x11, matrix products, tn_dot(): lax.dot_general(left, right, (((0,), (0,)), ((), ())), preferred_element_...  73.9 us
    ppermute x54, starting transfers between devices, to_dp(): return lax.ppermute(x, 'dp', xor_pairs(dp_size, mask))  61.5 us
    dot_general x14, matrix products, nn_dot(): return jnp.dot(left, right, preferred_element_type=jnp.float32)  59.4 us
    pallas_call x3, Pallas kernels, attention_backward(): pl.pallas_call(functools.partial(backward_kernel, min(256, length)), grid...  57.5 us
    pallas_call x1, Pallas kernels, bucket_sums(): pl.pallas_call(functools.partial(histogram_kernel, bucket_count, 4), grid...  55.4 us
    pallas_call x3, Pallas kernels, attention_forward(): pl.pallas_call(functools.partial(forward_kernel, min(256, length)), grid=...  50 us
  transfers between devices with their start and end apart: 110, of which 27 were waited for; matrix products, arithmetic and copies ran while one was open for 35% of the time, Pallas kernels for 19%

profile of v7, /device:TPU:0, one launch (start us, length us, event | category | flops | bytes accessed | tf_op | source)
XLA Modules:
  0.0 951.3 jit_solution(346268014682877080)
XLA Ops:
  39.9 14.0 %expand_bias.1.bias_ref = bf16[4,1024,1024]{2,1,0:T(8,128)(2,1)} custom-call(s32[1024,1024]{1,0:T(8,128)} %bitcast.321, f32[4,128]{1,0:T(4,128)} %pad_convert_fusion.table_ref), custom_call_target="tpu_custom_call" | custom-call | flops 4096 | bytes 4096 | tf_op jit(solution)/shard_map/expand_bias/pallas_call | solution.py:50
  69.4 14.2 %all-gather.6.cloned.1.call-done = bf16[1024,2048]{1,0:T(8,128)(2,1)} async-done(((bf16[128,2048]{1,0:T(8,128)(2,1)}), bf16[1024,2048]{1,0:T(8,128)(2,1)}) %all-gather.6.cloned.1.call-update) | async-done | bytes 4194320 | tf_op jit(solution)/shard_map/all_gather | solution.py:359
  95.9 16.3 %attention_forward.3 = (bf16[1024,256]{1,0:T(8,128)(2,1)S(1)}, f32[2,2,1024]{2,1,0:T(2,128)S(1)}) custom-call(bf16[1024,768]{1,0:T(8,128)(2,1)S(1)} %convolution_convert_fusion.7.qkv_ref, bf16[4,1024,1024]{2,1,0:T(8,128)(2,1)} %expand_bias.1.bias_ref), custom_call_target="tpu_custom_call" | custom-call | flops 4096 | bytes 4096 | tf_op jit(solution)/shard_map/attention_forward/pallas_call | solution.py:93
  119.6 11.7 %all-gather.8.cloned.1.call-done = bf16[1024,2048]{1,0:T(8,128)(2,1)} async-done(((bf16[128,2048]{1,0:T(8,128)(2,1)}), bf16[1024,2048]{1,0:T(8,128)(2,1)}) %all-gather.8.cloned.1.call-update) | async-done | bytes 4194320 | tf_op jit(solution)/shard_map/all_gather | solution.py:359
  139.4 16.9 %attention_forward.4 = (bf16[1024,256]{1,0:T(8,128)(2,1)S(1)}, f32[2,2,1024]{2,1,0:T(2,128)S(1)}) custom-call(bf16[1024,768]{1,0:T(8,128)(2,1)S(1)} %convolution_convert_fusion.6.qkv_ref, bf16[4,1024,1024]{2,1,0:T(8,128)(2,1)} %expand_bias.1.bias_ref), custom_call_target="tpu_custom_call" | custom-call | flops 4096 | bytes 4096 | tf_op jit(solution)/shard_map/attention_forward/pallas_call | solution.py:93
  159.6 26.5 %collective-permute-done.17 = bf16[384,2048]{1,0:T(8,128)(2,1)} collective-permute-done((bf16[384,2048]{1,0:T(8,128)(2,1)}, bf16[384,2048]{1,0:T(8,128)(2,1)}, u32[]{:S(2)}, u32[]{:S(2)}) %collective-permute-start.17) | collective-permute-done | bytes 1572896 | tf_op jit(solution)/shard_map/ppermute | solution.py:290
  201.3 16.8 %attention_forward.5 = (bf16[1024,256]{1,0:T(8,128)(2,1)S(1)}, f32[2,2,1024]{2,1,0:T(2,128)S(1)}) custom-call(bf16[1024,768]{1,0:T(8,128)(2,1)S(1)} %convolution_convert_fusion.5.qkv_ref, bf16[4,1024,1024]{2,1,0:T(8,128)(2,1)} %expand_bias.1.bias_ref), custom_call_target="tpu_custom_call" | custom-call | flops 4096 | bytes 4096 | tf_op jit(solution)/shard_map/attention_forward/pallas_call | solution.py:93
  218.1 15.0 %collective-permute-done.20 = bf16[1024,512]{1,0:T(8,128)(2,1)} collective-permute-done((bf16[1024,512]{1,0:T(8,128)(2,1)}, bf16[1024,512]{1,0:T(8,128)(2,1)}, u32[]{:S(2)}, u32[]{:S(2)}) %collective-permute-start.20) | collective-permute-done | bytes 1048608 | tf_op jit(solution)/shard_map/ppermute | solution.py:290
  251.0 8.5 collective-permute-start.30
  259.5 14.6 %collective-permute-done.37 = bf16[128,512]{1,0:T(8,128)(2,1)S(1)} collective-permute-done((bf16[128,512]{1,0:T(8,128)(2,1)S(1)}, bf16[128,512]{1,0:T(8,128)(2,1)S(1)}, u32[]{:S(2)}, u32[]{:S(2)}) %collective-permute-start.37) | collective-permute-done | bytes 131104 | tf_op jit(solution)/shard_map/ppermute | solution.py:293
  275.1 20.5 %collective-permute-done.30 = bf16[128,512]{1,0:T(8,128)(2,1)S(1)} collective-permute-done((bf16[128,512]{1,0:T(8,128)(2,1)S(1)}, bf16[128,512]{1,0:T(8,128)(2,1)S(1)}, u32[]{:S(2)}, u32[]{:S(2)}) %collective-permute-start.30) | collective-permute-done | bytes 131104 | tf_op jit(solution)/shard_map/ppermute | solution.py:293
  315.1 14.2 %collective-permute-done.32 = bf16[128,2048]{1,0:T(8,128)(2,1)S(1)} collective-permute-done((bf16[128,2048]{1,0:T(8,128)(2,1)S(1)}, bf16[128,2048]{1,0:T(8,128)(2,1)S(1)}, u32[]{:S(2)}, u32[]{:S(2)}) %collective-permute-start.32) | collective-permute-done | bytes 524320 | tf_op jit(solution)/shard_map/ppermute | solution.py:290
  329.2 18.2 %collective-permute-done.33 = bf16[128,2048]{1,0:T(8,128)(2,1)S(1)} collective-permute-done((bf16[128,2048]{1,0:T(8,128)(2,1)S(1)}, bf16[128,2048]{1,0:T(8,128)(2,1)S(1)}, u32[]{:S(2)}, u32[]{:S(2)}) %collective-permute-start.33) | collective-permute-done | bytes 524320 | tf_op jit(solution)/shard_map/ppermute | solution.py:290
  354.6 7.6 collective-permute-done.24
  363.9 11.9 %collective-permute-done.25 = bf16[128,2048]{1,0:T(8,128)(2,1)S(1)} collective-permute-done((bf16[128,2048]{1,0:T(8,128)(2,1)S(1)}, bf16[128,2048]{1,0:T(8,128)(2,1)S(1)}, u32[]{:S(2)}, u32[]{:S(2)}) %collective-permute-start.25) | collective-permute-done | bytes 524320 | tf_op jit(solution)/shard_map/ppermute | solution.py:290
  417.8 8.3 fusion.258
  440.8 9.4 fusion.7
  450.2 8.8 fusion.224
  459.1 8.9 fusion.14
  508.3 8.6 fusion.261
  540.2 11.0 %fusion.262 = f32[1280,2048]{1,0:T(8,128)} fusion(bf16[1024,1280]{1,0:T(8,128)(2,1)S(1)} %pad_maximum_fusion.3, bf16[1024,2048]{1,0:T(8,128)(2,1)} %copy-done.173), kind=kOutput, calls=%fused_computation.619 | convolution fusion | flops 5368709120 | bytes 17301504 | tf_op jit(solution)/shard_map/dot_general | solution.py:272
  558.2 13.2 %add_convert_fusion = bf16[1280,2048]{1,0:T(8,128)(2,1)S(1)} fusion(f32[1280,2048]{1,0:T(8,128)} %fusion.261, f32[1280,2048]{1,0:T(8,128)} %fusion.262, bf16[1024,1280]{1,0:T(8,128)(2,1)} %pad_maximum_fusion.4, bf16[1024,2048]{1,0:T(8,128)(2,1)} %constant_dynamic-update-slice_fusion.5), kind=kOutput, calls=%fused_computation.1 | convolution fusion | flops 5376573440 | bytes 33030144 | tf_op jit(solution)/shard_map/dot_general | solution.py:272
  592.0 19.0 %attention_backward.3 = (bf16[1024,768]{1,0:T(8,128)(2,1)S(1)}, bf16[4,1024,1024]{2,1,0:T(8,128)(2,1)}) custom-call(bf16[1024,768]{1,0:T(8,128)(2,1)S(1)} %convolution_convert_fusion.7.qkv_ref, bf16[1024,256]{1,0:T(8,128)(2,1)S(1)} %bitcast.316, bf16[4,1024,1024]{2,1,0:T(8,128)(2,1)} %expand_bias.1.bias_ref, f32[2,2,1024]{2,1,0:T(2,128)S(1)} %get-tuple-element.187.lse_ref), custom_call_target="tpu_custom_call" | custom-call | flops 4096 | bytes 4096 | tf_op jit(solution)/shard_map/attention_backward/pallas_call | solution.py:161
  614.5 7.9 convolution_convert_fusion.4
  639.7 7.4 convert_add_fusion
  669.0 19.5 %attention_backward.4 = (bf16[1024,768]{1,0:T(8,128)(2,1)S(1)}, bf16[4,1024,1024]{2,1,0:T(8,128)(2,1)}) custom-call(bf16[1024,768]{1,0:T(8,128)(2,1)S(1)} %copy-done.3, bf16[1024,256]{1,0:T(8,128)(2,1)S(1)} %bitcast.317, bf16[4,1024,1024]{2,1,0:T(8,128)(2,1)} %expand_bias.1.bias_ref, f32[2,2,1024]{2,1,0:T(2,128)S(1)} %get-tuple-element.203.lse_ref), custom_call_target="tpu_custom_call" | custom-call | flops 4096 | bytes 4096 | tf_op jit(solution)/shard_map/attention_backward/pallas_call | solution.py:161
  688.5 28.5 %collective-permute-done.65 = bf16[3,128,2048]{2,1,0:T(8,128)(2,1)} collective-permute-done((bf16[3,128,2048]{2,1,0:T(8,128)(2,1)S(1)}, bf16[3,128,2048]{2,1,0:T(8,128)(2,1)}, u32[]{:S(2)}, u32[]{:S(2)}) %collective-permute-start.65) | collective-permute-done | bytes 1572896 | tf_op jit(solution)/shard_map/ppermute | solution.py:290
  763.2 19.0 %attention_backward.5 = (bf16[1024,768]{1,0:T(8,128)(2,1)S(1)}, bf16[4,1024,1024]{2,1,0:T(8,128)(2,1)}) custom-call(bf16[1024,768]{1,0:T(8,128)(2,1)S(1)} %copy-done.1, bf16[1024,256]{1,0:T(8,128)(2,1)S(1)} %bitcast.315, bf16[4,1024,1024]{2,1,0:T(8,128)(2,1)} %expand_bias.1.bias_ref, f32[2,2,1024]{2,1,0:T(2,128)S(1)} %get-tuple-element.217.lse_ref), custom_call_target="tpu_custom_call" | custom-call | flops 4096 | bytes 4096 | tf_op jit(solution)/shard_map/attention_backward/pallas_call | solution.py:161
  782.2 15.1 %collective-permute-done.80 = bf16[1024,512]{1,0:T(8,128)(2,1)} collective-permute-done((bf16[1024,512]{1,0:T(8,128)(2,1)S(1)}, bf16[1024,512]{1,0:T(8,128)(2,1)}, u32[]{:S(2)}, u32[]{:S(2)}) %collective-permute-start.80) | collective-permute-done | bytes 1048608 | tf_op jit(solution)/shard_map/ppermute | solution.py:290
  797.3 7.6 convolution_convert_fusion.2
  815.5 7.6 convolution_add_fusion
  842.7 55.4 %bucket_sums.1 = f32[4,32,8,128]{3,2,1,0:T(8,128)S(1)} custom-call(s32[1024,1024]{1,0:T(8,128)} %bitcast.322, bf16[4,1024,1024]{2,1,0:T(8,128)(2,1)} %get-tuple-element.229.refs_0_, bf16[4,1024,1024]{2,1,0:T(8,128)(2,1)} %get-tuple-element.230.refs_1_, bf16[4,1024,1024]{2,1,0:T(8,128)(2,1)} %get-tuple-element.231.refs_2_), custom_call_target="tpu_custom_call" | custom-call | flops 4096 | bytes 4096 | tf_op jit(solution)/shard_map/bucket_sums/pallas_call | solution.py:223
  (847 shorter events, 451.0 us)
Async XLA Ops:
  7.2 76.4 %all-gather.6.cloned.1.call-start = ((), (), s32[]{:S(2)}) async-start(), calls=%async_computation.5 | async-start | bytes 4718592 | tf_op jit(solution)/shard_map/all_gather | solution.py:359
  11.3 120.0 %all-gather.8.cloned.1.call-start = ((), (), s32[]{:S(2)}) async-start(), calls=%async_computation.6 | async-start | bytes 4718592 | tf_op jit(solution)/shard_map/all_gather | solution.py:359
  12.1 181.1 %all-gather.10.cloned.1.call-start = ((), (), s32[]{:S(2)}) async-start(), calls=%async_computation.7 | async-start | bytes 4718592 | tf_op jit(solution)/shard_map/all_gather | solution.py:359
  12.8 375.6 %all-gather.12.cloned.1.call-start = ((), (), s32[]{:S(2)}) async-start(), calls=%async_computation.8 | async-start | bytes 6553600 | tf_op jit(solution)/shard_map/all_gather | solution.py:308
  25.1 42.5 %collective-permute-start = (bf16[256,512]{1,0:T(8,128)(2,1)S(1)}, bf16[256,512]{1,0:T(8,128)(2,1)S(1)}, u32[]{:S(2)}, u32[]{:S(2)}) collective-permute-start(bf16[256,512]{1,0:T(8,128)(2,1)S(1)} %copy-done.154), channel_id=1, source_target_pairs={{0,2},{1,3},{2,0},{3,1},{4,6},{5,7},{6,4},{7,5},{8,10},{9,11},{10,... | collective-permute-start | bytes 786440 | tf_op jit(solution)/shard_map/ppermute | solution.py:293
  27.1 42.0 %collective-permute-start.1 = (bf16[256,512]{1,0:T(8,128)(2,1)S(1)}, bf16[256,512]{1,0:T(8,128)(2,1)}, u32[]{:S(2)}, u32[]{:S(2)}) collective-permute-start(bf16[256,512]{1,0:T(8,128)(2,1)S(1)} %copy-done.154), channel_id=1, source_target_pairs={{0,4},{1,5},{2,6},{3,7},{4,0},{5,1},{6,2},{7,3},{8,12},{9,13},{10,... | collective-permute-start | bytes 786440 | tf_op jit(solution)/shard_map/ppermute | solution.py:293
  94.3 346.5 %all-gather.14.cloned.1.call-start = ((), (), s32[]{:S(2)}) async-start(), calls=%async_computation.9 | async-start | bytes 3276800 | tf_op jit(solution)/shard_map/all_gather | solution.py:308
  114.3 44.9 %collective-permute-start.16 = (bf16[384,2048]{1,0:T(8,128)(2,1)}, bf16[384,2048]{1,0:T(8,128)(2,1)}, u32[]{:S(2)}, u32[]{:S(2)}) collective-permute-start(bf16[384,2048]{1,0:T(8,128)(2,1)} %bitcast.23), channel_id=1, source_target_pairs={{0,8},{8,0},{16,24},{24,16},{1,9},{9,1},{17,25},{25,17},{2,10},{10... | collective-permute-start | bytes 4718600 | tf_op jit(solution)/shard_map/ppermute | solution.py:290
  115.8 70.3 %collective-permute-start.17 = (bf16[384,2048]{1,0:T(8,128)(2,1)}, bf16[384,2048]{1,0:T(8,128)(2,1)}, u32[]{:S(2)}, u32[]{:S(2)}) collective-permute-start(bf16[384,2048]{1,0:T(8,128)(2,1)} %bitcast.23), channel_id=1, source_target_pairs={{0,16},{8,24},{16,0},{24,8},{1,17},{9,25},{17,1},{25,9},{2,18},{10... | collective-permute-start | bytes 4718600 | tf_op jit(solution)/shard_map/ppermute | solution.py:290
  117.3 69.8 %collective-permute-start.18 = (bf16[384,2048]{1,0:T(8,128)(2,1)}, bf16[384,2048]{1,0:T(8,128)(2,1)}, u32[]{:S(2)}, u32[]{:S(2)}) collective-permute-start(bf16[384,2048]{1,0:T(8,128)(2,1)} %bitcast.23), channel_id=1, source_target_pairs={{0,24},{8,16},{16,8},{24,0},{1,25},{9,17},{17,9},{25,1},{2,26},{10... | collective-permute-start | bytes 4718600 | tf_op jit(solution)/shard_map/ppermute | solution.py:290
  187.0 371.2 %reduce-scatter.6.cloned.1.call-start = ((), (), s32[]{:S(2)}) async-start(), calls=%async_computation.10 | async-start | bytes 3276800 | tf_op jit(solution)/shard_map/reduce_scatter | solution.py:311
  187.3 45.9 %collective-permute-start.20 = (bf16[1024,512]{1,0:T(8,128)(2,1)}, bf16[1024,512]{1,0:T(8,128)(2,1)}, u32[]{:S(2)}, u32[]{:S(2)}) collective-permute-start(bf16[1024,512]{1,0:T(8,128)(2,1)} %pad_maximum_fusion.19), channel_id=1, source_target_pairs={{0,16},{8,24},{16,0},{24,8},{1,17},{9,25},{17,1},{25,9},{2,18},{10... | collective-permute-start | bytes 3145736 | tf_op jit(solution)/shard_map/ppermute | solution.py:290
  189.2 45.8 %collective-permute-start.21 = (bf16[1024,512]{1,0:T(8,128)(2,1)}, bf16[1024,512]{1,0:T(8,128)(2,1)}, u32[]{:S(2)}, u32[]{:S(2)}) collective-permute-start(bf16[1024,512]{1,0:T(8,128)(2,1)} %pad_maximum_fusion.19), channel_id=1, source_target_pairs={{0,24},{8,16},{16,8},{24,0},{1,25},{9,17},{17,9},{25,1},{2,26},{10... | collective-permute-start | bytes 3145736 | tf_op jit(solution)/shard_map/ppermute | solution.py:290
  238.1 60.3 %collective-permute-start.23 = (bf16[1024,2048]{1,0:T(8,128)(2,1)S(1)}, bf16[1024,2048]{1,0:T(8,128)(2,1)S(1)}, u32[]{:S(2)}, u32[]{:S(2)}) collective-permute-start(bf16[1024,2048]{1,0:T(8,128)(2,1)S(1)} %pad_maximum_fusion), channel_id=1, source_target_pairs={{0,1},{1,0},{2,3},{3,2},{4,5},{5,4},{6,7},{7,6},{8,9},{9,8},{10,11... | collective-permute-start | bytes 12582920 | tf_op jit(solution)/shard_map/ppermute | solution.py:287
  251.0 44.6 %collective-permute-start.30 = (bf16[128,512]{1,0:T(8,128)(2,1)S(1)}, bf16[128,512]{1,0:T(8,128)(2,1)S(1)}, u32[]{:S(2)}, u32[]{:S(2)}) collective-permute-start(bf16[128,512]{1,0:T(8,128)(2,1)S(1)} %get-tuple-element.471), channel_id=1, source_target_pairs={{0,4},{1,5},{2,6},{3,7},{4,0},{5,1},{6,2},{7,3},{8,12},{9,13},{10,... | collective-permute-start | bytes 393224 | tf_op jit(solution)/shard_map/ppermute | solution.py:293
  303.2 47.1 %collective-permute-start.39 = (bf16[128,2048]{1,0:T(8,128)(2,1)S(1)}, bf16[128,2048]{1,0:T(8,128)(2,1)S(1)}, u32[]{:S(2)}, u32[]{:S(2)}) collective-permute-start(bf16[128,2048]{1,0:T(8,128)(2,1)S(1)} %get-tuple-element.503), channel_id=1, source_target_pairs={{0,8},{8,0},{16,24},{24,16},{1,9},{9,1},{17,25},{25,17},{2,10},{10... | collective-permute-start | bytes 1572872 | tf_op jit(solution)/shard_map/ppermute | solution.py:290
  303.2 49.1 %collective-permute-start.40 = (bf16[128,2048]{1,0:T(8,128)(2,1)S(1)}, bf16[128,2048]{1,0:T(8,128)(2,1)S(1)}, u32[]{:S(2)}, u32[]{:S(2)}) collective-permute-start(bf16[128,2048]{1,0:T(8,128)(2,1)S(1)} %get-tuple-element.503), channel_id=1, source_target_pairs={{0,16},{8,24},{16,0},{24,8},{1,17},{9,25},{17,1},{25,9},{2,18},{10... | collective-permute-start | bytes 1572872 | tf_op jit(solution)/shard_map/ppermute | solution.py:290
  305.2 42.2 %collective-permute-start.33 = (bf16[128,2048]{1,0:T(8,128)(2,1)S(1)}, bf16[128,2048]{1,0:T(8,128)(2,1)S(1)}, u32[]{:S(2)}, u32[]{:S(2)}) collective-permute-start(bf16[128,2048]{1,0:T(8,128)(2,1)S(1)} %get-tuple-element.501), channel_id=1, source_target_pairs={{0,16},{8,24},{16,0},{24,8},{1,17},{9,25},{17,1},{25,9},{2,18},{10... | collective-permute-start | bytes 1572872 | tf_op jit(solution)/shard_map/ppermute | solution.py:290
  478.6 344.5 %reduce-scatter.14.cloned.1.call-start = ((), (), s32[]{:S(2)}) async-start(), calls=%async_computation.14 | async-start | bytes 6553600 | tf_op jit(solution)/shard_map/reduce_scatter | solution.py:311
  574.2 345.1 %reduce-scatter.8.cloned.1.call-start = ((), (), s32[]{:S(2)}) async-start(), calls=%async_computation.11 | async-start | bytes 4718592 | tf_op jit(solution)/shard_map/reduce_scatter | solution.py:595
  587.4 52.0 %collective-permute-start.63 = (bf16[1536,2048]{1,0:T(8,128)(2,1)}, bf16[1536,2048]{1,0:T(8,128)(2,1)}, u32[]{:S(2)}, u32[]{:S(2)}) collective-permute-start(bf16[1536,2048]{1,0:T(8,128)(2,1)} %convolution_convert_fusion), channel_id=1, source_target_pairs={{0,1},{1,0},{2,3},{3,2},{4,5},{5,4},{6,7},{7,6},{8,9},{9,8},{10,11... | collective-permute-start | bytes 18874376 | tf_op jit(solution)/shard_map/ppermute | solution.py:287
  622.4 296.9 %reduce-scatter.10.cloned.1.call-start = ((), (), s32[]{:S(2)}) async-start(), calls=%async_computation.12 | async-start | bytes 4718592 | tf_op jit(solution)/shard_map/reduce_scatter | solution.py:595
  648.9 68.1 %collective-permute-start.65 = (bf16[3,128,2048]{2,1,0:T(8,128)(2,1)S(1)}, bf16[3,128,2048]{2,1,0:T(8,128)(2,1)}, u32[]{:S(2)}, u32[]{:S(2)}) collective-permute-start(bf16[3,128,2048]{2,1,0:T(8,128)(2,1)S(1)} %get-tuple-element.327), channel_id=1, source_target_pairs={{0,16},{8,24},{16,0},{24,8},{1,17},{9,25},{17,1},{25,9},{2,18},{10... | collective-permute-start | bytes 4718600 | tf_op jit(solution)/shard_map/ppermute | solution.py:290
  649.6 67.4 %collective-permute-start.66 = (bf16[3,128,2048]{2,1,0:T(8,128)(2,1)S(1)}, bf16[3,128,2048]{2,1,0:T(8,128)(2,1)}, u32[]{:S(2)}, u32[]{:S(2)}) collective-permute-start(bf16[3,128,2048]{2,1,0:T(8,128)(2,1)S(1)} %get-tuple-element.326), channel_id=1, source_target_pairs={{0,24},{8,16},{16,8},{24,0},{1,25},{9,17},{17,9},{25,1},{2,26},{10... | collective-permute-start | bytes 4718600 | tf_op jit(solution)/shard_map/ppermute | solution.py:290
  667.9 64.7 %collective-permute-start.77 = (bf16[1024,2048]{1,0:T(8,128)(2,1)}, bf16[1024,2048]{1,0:T(8,128)(2,1)}, u32[]{:S(2)}, u32[]{:S(2)}) collective-permute-start(bf16[1024,2048]{1,0:T(8,128)(2,1)} %convolution_convert_fusion.1), channel_id=1, source_target_pairs={{0,1},{1,0},{2,3},{3,2},{4,5},{5,4},{6,7},{7,6},{8,9},{9,8},{10,11... | collective-permute-start | bytes 12582920 | tf_op jit(solution)/shard_map/ppermute | solution.py:287
  723.7 195.6 %reduce-scatter.12.cloned.1.call-start = ((), (), s32[]{:S(2)}) async-start(), calls=%async_computation.13 | async-start | bytes 4718592 | tf_op jit(solution)/shard_map/reduce_scatter | solution.py:595
  752.8 44.5 %collective-permute-start.80 = (bf16[1024,512]{1,0:T(8,128)(2,1)S(1)}, bf16[1024,512]{1,0:T(8,128)(2,1)}, u32[]{:S(2)}, u32[]{:S(2)}) collective-permute-start(bf16[1024,512]{1,0:T(8,128)(2,1)S(1)} %get-tuple-element.314), channel_id=1, source_target_pairs={{0,24},{8,16},{16,8},{24,0},{1,25},{9,17},{17,9},{25,1},{2,26},{10... | collective-permute-start | bytes 3145736 | tf_op jit(solution)/shard_map/ppermute | solution.py:290
  814.7 85.1 %collective-permute-start.94 = (bf16[256,512]{1,0:T(8,128)(2,1)}, bf16[256,512]{1,0:T(8,128)(2,1)}, u32[]{:S(2)}, u32[]{:S(2)}) collective-permute-start(bf16[256,512]{1,0:T(8,128)(2,1)} %get-tuple-element.346), channel_id=1, source_target_pairs={{0,2},{1,3},{2,0},{3,1},{4,6},{5,7},{6,4},{7,5},{8,10},{9,11},{10,... | collective-permute-start | bytes 786440 | tf_op jit(solution)/shard_map/ppermute | solution.py:293
  814.7 90.7 %collective-permute-start.95 = (bf16[256,512]{1,0:T(8,128)(2,1)}, bf16[256,512]{1,0:T(8,128)(2,1)}, u32[]{:S(2)}, u32[]{:S(2)}) collective-permute-start(bf16[256,512]{1,0:T(8,128)(2,1)} %get-tuple-element.345), channel_id=1, source_target_pairs={{0,4},{1,5},{2,6},{3,7},{4,0},{5,1},{6,2},{7,3},{8,12},{9,13},{10,... | collective-permute-start | bytes 786440 | tf_op jit(solution)/shard_map/ppermute | solution.py:293
  837.5 71.9 %collective-permute-start.88 = (bf16[512,768]{0,1:T(8,128)(2,1)}, bf16[512,768]{0,1:T(8,128)(2,1)}, u32[]{:S(2)}, u32[]{:S(2)}) collective-permute-start(bf16[512,768]{0,1:T(8,128)(2,1)} %get-tuple-element.325), channel_id=1, source_target_pairs={{0,8},{8,0},{16,24},{24,16},{1,9},{9,1},{17,25},{25,17},{2,10},{10... | collective-permute-start | bytes 2359304 | tf_op jit(solution)/shard_map/ppermute | solution.py:290
  838.4 72.0 %collective-permute-start.89 = (bf16[512,768]{0,1:T(8,128)(2,1)}, bf16[512,768]{0,1:T(8,128)(2,1)}, u32[]{:S(2)}, u32[]{:S(2)}) collective-permute-start(bf16[512,768]{0,1:T(8,128)(2,1)} %get-tuple-element.324), channel_id=1, source_target_pairs={{0,16},{8,24},{16,0},{24,8},{1,17},{9,25},{17,1},{25,9},{2,18},{10... | collective-permute-start | bytes 2359304 | tf_op jit(solution)/shard_map/ppermute | solution.py:290
  839.7 70.6 %collective-permute-start.90 = (bf16[512,768]{0,1:T(8,128)(2,1)}, bf16[512,768]{0,1:T(8,128)(2,1)}, u32[]{:S(2)}, u32[]{:S(2)}) collective-permute-start(bf16[512,768]{0,1:T(8,128)(2,1)} %get-tuple-element.323), channel_id=1, source_target_pairs={{0,24},{8,16},{16,8},{24,0},{1,25},{9,17},{17,9},{25,1},{2,26},{10... | collective-permute-start | bytes 2359304 | tf_op jit(solution)/shard_map/ppermute | solution.py:290
  (290 other events, 3740.3 us)
Sparse Core Ops, SparseCore 0:
  11.4 72.0 all-gather.5
  85.8 45.5 all-gather.7
  133.5 56.9 all-gather.9
  192.5 118.8 all-gather.11
  313.4 52.9 all-gather.13
  478.8 53.3 reduce-scatter.5
  574.3 103.0 reduce-scatter.13
  679.7 51.7 reduce-scatter.7
  733.8 48.3 reduce-scatter.9
  805.0 57.2 reduce-scatter.11

commit v8 on v6

--- a/solution.py
+++ b/solution.py
@@ -539,7 +539,7 @@
             else:
                 grad_pre = after(grad_pre, swapped_in[s - 1], *sums[-1])
             if s == seqs - 1:
-                grad_pre = after(grad_pre, post_z)
+                grad_pre = after(grad_pre, post_z, *moves[0][1:], *sent_in[-1])
             more = tn_dot(grad_pre, norm_two_full[s])
             grad_pre_w = more if grad_pre_w is None else grad_pre_w + more
             if s == seqs - 1:
@@ -594,7 +594,7 @@
             moved = after(moves[s], *gate)
             if s < seqs - 1:
                 moved = after(moved, swapped_in[s + 1])
-            if s == 1:
+            if s == 0:
                 moved = after(moved, *out_blocks)
             if s == seqs - 1:
                 moved = after(moved, *post_moved[1:], *out_give_dp)
@@ -604,12 +604,10 @@
             grad_scores.append(grad_score)
             qkv_grads.append(grad_proj)
             ordered = grad_proj
-            if s == 0:
-                ordered = after(ordered, *sent_in[-1])
             if s == 1:
                 ordered = after(ordered, *out_sent)
             if s == seqs - 1:
-                ordered = after(ordered, *out_moved[1:])
+                ordered = after(ordered, *out_moved[1:], *pre_moved[1:])
             normed_part = nt_dot(ordered, w_qkv).astype(jnp.bfloat16)
             normed_parts.append(normed_part)
             gate = (normed_part,)
@@ -649,7 +647,6 @@
             )
             for k in range(1, zs)
         ]
-        grad_out_sent = [to_z(grad_out_blocks[k - 1], k) for k in range(1, zs)]
         qkv_blocks = [
             lax.dynamic_slice_in_dim(grad_qkv, (dp_at ^ k) * feats, feats, 0).astype(
                 jnp.bfloat16
@@ -657,9 +654,8 @@
             for k in range(1, dp_size)
         ]
         qkv_sent = [to_dp(qkv_blocks[k - 1], k) for k in range(1, dp_size)]
-        bucket_gate = after(
-            buckets_t, *pre_moved[1:], *grad_out_blocks, *qkv_blocks, grad_normed[0]
-        )
+        grad_out_sent = [to_z(grad_out_blocks[k - 1], k) for k in range(1, zs)]
+        bucket_gate = after(buckets_t, *grad_out_blocks, *qkv_blocks, grad_normed[0])
         table_grad = bucket_sums(bucket_gate, grad_scores, bucket_count)
         grad_out = grad_out_keep + sum(
             x.astype(jnp.float32) for x in after(tuple(grad_out_sent), table_grad)

time: 953 us -> 993 us (1.042)
  waiting for transfers between devices: 193 us -> 237 us
    ppermute x54, waiting for transfers between devices: 125 us -> 160 us  [to_dp(): return lax.ppermute(x, 'dp', xor_pairs(dp_size, mask))]
    unnamed x495 -> x445, local copies, waits for them, and re-layouts: 57.3 us -> 62.8 us
  transfers between devices with their start and end apart: 110 -> 110, of which waited for: 25 -> 30; matrix products, arithmetic and copies ran while one was open for 39% -> 39% of each run, Pallas kernels for 19% -> 18%
where the time goes in v8:
time: 993 us; the launch traced here: 985 us
  waiting for transfers between devices  237 us (24%)
  matrix products  237 us (24%)
  Pallas kernels  177 us (18%)
  local copies, waits for them, and re-layouts  118 us (12%)
  starting transfers between devices  105 us (11%)
  other arithmetic  93 us (9%)
  between operations  18 us (2%)
    ppermute x54, waiting for transfers between devices, to_dp(): return lax.ppermute(x, 'dp', xor_pairs(dp_size, mask))  160 us
    dot_general x15, matrix products, nt_dot(): lax.dot_general(left, right, (((1,), (1,)), ((), ())), preferred_element_...  91.9 us
    dot_general x11, matrix products, tn_dot(): lax.dot_general(left, right, (((0,), (0,)), ((), ())), preferred_element_...  77.4 us
    dot_general x14, matrix products, nn_dot(): return jnp.dot(left, right, preferred_element_type=jnp.float32)  67.5 us
    unnamed x445, local copies, waits for them, and re-layouts  62.8 us
    ppermute x54, starting transfers between devices, to_dp(): return lax.ppermute(x, 'dp', xor_pairs(dp_size, mask))  62.6 us
    pallas_call x3, Pallas kernels, attention_backward(): pl.pallas_call(functools.partial(backward_kernel, min(256, length)), grid...  57.9 us
    pallas_call x1, Pallas kernels, bucket_sums(): pl.pallas_call(functools.partial(histogram_kernel, bucket_count, 4), grid...  55.7 us
  transfers between devices with their start and end apart: 110, of which 30 were waited for; matrix products, arithmetic and copies ran while one was open for 39% of the time, Pallas kernels for 18%

profile of v8, /device:TPU:0, one launch (start us, length us, event | category | flops | bytes accessed | tf_op | source)
XLA Modules:
  0.0 984.8 jit_solution(16280065604795697281)
XLA Ops:
  37.6 14.0 %expand_bias.1.bias_ref = bf16[4,1024,1024]{2,1,0:T(8,128)(2,1)} custom-call(s32[1024,1024]{1,0:T(8,128)} %bitcast.326, f32[4,128]{1,0:T(4,128)} %pad_convert_fusion.table_ref), custom_call_target="tpu_custom_call" | custom-call | flops 4096 | bytes 4096 | tf_op jit(solution)/shard_map/expand_bias/pallas_call | solution.py:50
  67.2 16.4 %all-gather.6.cloned.1.call-done = bf16[1024,2048]{1,0:T(8,128)(2,1)} async-done(((bf16[128,2048]{1,0:T(8,128)(2,1)}), bf16[1024,2048]{1,0:T(8,128)(2,1)}) %all-gather.6.cloned.1.call-update) | async-done | bytes 4194320 | tf_op jit(solution)/shard_map/all_gather | solution.py:359
  101.1 16.3 %attention_forward.3 = (bf16[1024,256]{1,0:T(8,128)(2,1)S(1)}, f32[2,2,1024]{2,1,0:T(2,128)S(1)}) custom-call(bf16[1024,768]{1,0:T(8,128)(2,1)S(1)} %convolution_convert_fusion.7.qkv_ref, bf16[4,1024,1024]{2,1,0:T(8,128)(2,1)} %expand_bias.1.bias_ref), custom_call_target="tpu_custom_call" | custom-call | flops 4096 | bytes 4096 | tf_op jit(solution)/shard_map/attention_forward/pallas_call | solution.py:93
  124.5 21.7 %collective-permute-done.17 = bf16[1024,512]{1,0:T(8,128)(2,1)S(1)} collective-permute-done((bf16[1024,512]{1,0:T(8,128)(2,1)S(1)}, bf16[1024,512]{1,0:T(8,128)(2,1)S(1)}, u32[]{:S(2)}, u32[]{:S(2)}) %collective-permute-start.17) | collective-permute-done | bytes 1048608 | tf_op jit(solution)/shard_map/ppermute | solution.py:290
  159.9 17.0 %attention_forward.4 = (bf16[1024,256]{1,0:T(8,128)(2,1)S(1)}, f32[2,2,1024]{2,1,0:T(2,128)S(1)}) custom-call(bf16[1024,768]{1,0:T(8,128)(2,1)S(1)} %convolution_convert_fusion.6.qkv_ref, bf16[4,1024,1024]{2,1,0:T(8,128)(2,1)} %expand_bias.1.bias_ref), custom_call_target="tpu_custom_call" | custom-call | flops 4096 | bytes 4096 | tf_op jit(solution)/shard_map/attention_forward/pallas_call | solution.py:93
  181.6 13.3 %collective-permute-done.21 = bf16[256,2048]{1,0:T(8,128)(2,1)} collective-permute-done((bf16[256,2048]{1,0:T(8,128)(2,1)S(1)}, bf16[256,2048]{1,0:T(8,128)(2,1)}, u32[]{:S(2)}, u32[]{:S(2)}) %collective-permute-start.21) | collective-permute-done | bytes 1048608 | tf_op jit(solution)/shard_map/ppermute | solution.py:290
  236.6 16.5 %attention_forward.5 = (bf16[1024,256]{1,0:T(8,128)(2,1)S(1)}, f32[2,2,1024]{2,1,0:T(2,128)S(1)}) custom-call(bf16[1024,768]{1,0:T(8,128)(2,1)S(1)} %convolution_convert_fusion.5.qkv_ref, bf16[4,1024,1024]{2,1,0:T(8,128)(2,1)} %expand_bias.1.bias_ref), custom_call_target="tpu_custom_call" | custom-call | flops 4096 | bytes 4096 | tf_op jit(solution)/shard_map/attention_forward/pallas_call | solution.py:93
  276.6 11.7 %collective-permute-done.34 = bf16[128,512]{1,0:T(8,128)(2,1)S(1)} collective-permute-done((bf16[128,512]{1,0:T(8,128)(2,1)S(1)}, bf16[128,512]{1,0:T(8,128)(2,1)S(1)}, u32[]{:S(2)}, u32[]{:S(2)}) %collective-permute-start.34) | collective-permute-done | bytes 131104 | tf_op jit(solution)/shard_map/ppermute | solution.py:293
  289.8 12.1 %collective-permute-done.33 = bf16[128,512]{1,0:T(8,128)(2,1)S(1)} collective-permute-done((bf16[128,512]{1,0:T(8,128)(2,1)S(1)}, bf16[128,512]{1,0:T(8,128)(2,1)S(1)}, u32[]{:S(2)}, u32[]{:S(2)}) %collective-permute-start.33) | collective-permute-done | bytes 131104 | tf_op jit(solution)/shard_map/ppermute | solution.py:293
  320.3 10.9 %collective-permute-done.40 = bf16[128,2048]{1,0:T(8,128)(2,1)S(1)} collective-permute-done((bf16[128,2048]{1,0:T(8,128)(2,1)S(1)}, bf16[128,2048]{1,0:T(8,128)(2,1)S(1)}, u32[]{:S(2)}, u32[]{:S(2)}) %collective-permute-start.40) | collective-permute-done | bytes 524320 | tf_op jit(solution)/shard_map/ppermute | solution.py:290
  331.2 10.2 %collective-permute-done.39 = bf16[128,2048]{1,0:T(8,128)(2,1)S(1)} collective-permute-done((bf16[128,2048]{1,0:T(8,128)(2,1)S(1)}, bf16[128,2048]{1,0:T(8,128)(2,1)S(1)}, u32[]{:S(2)}, u32[]{:S(2)}) %collective-permute-start.39) | collective-permute-done | bytes 524320 | tf_op jit(solution)/shard_map/ppermute | solution.py:290
  355.7 9.2 fusion.253
  401.4 9.7 fusion.7
  411.0 7.8 fusion.216
  423.1 8.5 fusion.14
  450.9 7.4 fusion.21
  471.0 10.7 %fusion.256 = f32[1280,2048]{1,0:T(8,128)} fusion(bf16[1024,1280]{1,0:T(8,128)(2,1)S(1)} %copy-done.48, bf16[1024,2048]{1,0:T(8,128)(2,1)} %copy-done.179), kind=kOutput, calls=%fused_computation.619 | convolution fusion | flops 5368709120 | bytes 17301504 | tf_op jit(solution)/shard_map/dot_general | solution.py:272
  504.4 8.3 fusion.257
  540.3 13.5 %add_convert_fusion = bf16[1280,2048]{1,0:T(8,128)(2,1)S(1)} fusion(f32[1280,2048]{1,0:T(8,128)} %fusion.256, f32[1280,2048]{1,0:T(8,128)} %fusion.257, bf16[1024,1280]{1,0:T(8,128)(2,1)} %pad_maximum_fusion.4, bf16[1024,2048]{1,0:T(8,128)(2,1)} %constant_dynamic-update-slice_fusion.5), kind=kOutput, calls=%fused_computation.1 | convolution fusion | flops 5376573440 | bytes 33030144 | tf_op jit(solution)/shard_map/dot_general | solution.py:272
  564.5 9.9 %collective-permute-done.63 = bf16[1536,2048]{1,0:T(8,128)(2,1)S(1)} collective-permute-done((bf16[1536,2048]{1,0:T(8,128)(2,1)S(1)}, bf16[1536,2048]{1,0:T(8,128)(2,1)S(1)}, u32[]{:S(2)}, u32[]{:S(2)}) %collective-permute-start.63) | collective-permute-done | bytes 6291488 | tf_op jit(solution)/shard_map/ppermute | solution.py:287
  585.6 19.4 %attention_backward.3 = (bf16[1024,768]{1,0:T(8,128)(2,1)S(1)}, bf16[4,1024,1024]{2,1,0:T(8,128)(2,1)}) custom-call(bf16[1024,768]{1,0:T(8,128)(2,1)S(1)} %convolution_convert_fusion.7.qkv_ref, bf16[1024,256]{1,0:T(8,128)(2,1)S(1)} %bitcast.321, bf16[4,1024,1024]{2,1,0:T(8,128)(2,1)} %expand_bias.1.bias_ref, f32[2,2,1024]{2,1,0:T(2,128)S(1)} %get-tuple-element.202.lse_ref), custom_call_target="tpu_custom_call" | custom-call | flops 4096 | bytes 4096 | tf_op jit(solution)/shard_map/attention_backward/pallas_call | solution.py:161
  606.2 7.6 convolution_convert_fusion.4
  644.9 11.3 %collective-permute-done.72 = bf16[2,128,256]{2,1,0:T(8,128)(2,1)S(1)} collective-permute-done((bf16[2,128,256]{2,1,0:T(8,128)(2,1)S(1)}, bf16[2,128,256]{2,1,0:T(8,128)(2,1)S(1)}, u32[]{:S(2)}, u32[]{:S(2)}) %collective-permute-start.72) | collective-permute-done | bytes 131104 | tf_op jit(solution)/shard_map/ppermute | solution.py:293
  656.9 19.3 %attention_backward.4 = (bf16[1024,768]{1,0:T(8,128)(2,1)S(1)}, bf16[4,1024,1024]{2,1,0:T(8,128)(2,1)}) custom-call(bf16[1024,768]{1,0:T(8,128)(2,1)S(1)} %copy-done.1, bf16[1024,256]{1,0:T(8,128)(2,1)S(1)} %bitcast.322, bf16[4,1024,1024]{2,1,0:T(8,128)(2,1)} %expand_bias.1.bias_ref, f32[2,2,1024]{2,1,0:T(2,128)S(1)} %get-tuple-element.213.lse_ref), custom_call_target="tpu_custom_call" | custom-call | flops 4096 | bytes 4096 | tf_op jit(solution)/shard_map/attention_backward/pallas_call | solution.py:161
  676.2 23.6 %collective-permute-done.65 = bf16[3,128,2048]{2,1,0:T(8,128)(2,1)S(1)} collective-permute-done((bf16[3,128,2048]{2,1,0:T(8,128)(2,1)S(1)}, bf16[3,128,2048]{2,1,0:T(8,128)(2,1)S(1)}, u32[]{:S(2)}, u32[]{:S(2)}) %collective-permute-start.65) | collective-permute-done | bytes 1572896 | tf_op jit(solution)/shard_map/ppermute | solution.py:290
  745.5 8.6 convolution_add_fusion.1
  757.4 19.3 %attention_backward.5 = (bf16[1024,768]{1,0:T(8,128)(2,1)S(1)}, bf16[4,1024,1024]{2,1,0:T(8,128)(2,1)}) custom-call(bf16[1024,768]{1,0:T(8,128)(2,1)S(1)} %copy-done.3, bf16[1024,256]{1,0:T(8,128)(2,1)S(1)} %bitcast.320, bf16[4,1024,1024]{2,1,0:T(8,128)(2,1)} %expand_bias.1.bias_ref, f32[2,2,1024]{2,1,0:T(2,128)S(1)} %get-tuple-element.227.lse_ref), custom_call_target="tpu_custom_call" | custom-call | flops 4096 | bytes 4096 | tf_op jit(solution)/shard_map/attention_backward/pallas_call | solution.py:161
  776.7 25.9 %collective-permute-done.82 = bf16[320,512]{1,0:T(8,128)(2,1)S(1)} collective-permute-done((bf16[320,512]{1,0:T(8,128)(2,1)S(1)}, bf16[320,512]{1,0:T(8,128)(2,1)S(1)}, u32[]{:S(2)}, u32[]{:S(2)}) %collective-permute-start.82) | collective-permute-done | bytes 327712 | tf_op jit(solution)/shard_map/ppermute | solution.py:290
  805.1 8.1 convolution_convert_fusion.2
  850.0 55.7 %bucket_sums.1 = f32[4,32,8,128]{3,2,1,0:T(8,128)S(1)} custom-call(s32[1024,1024]{1,0:T(8,128)} %bitcast.327, bf16[4,1024,1024]{2,1,0:T(8,128)(2,1)} %get-tuple-element.239.refs_0_, bf16[4,1024,1024]{2,1,0:T(8,128)(2,1)} %get-tuple-element.240.refs_1_, bf16[4,1024,1024]{2,1,0:T(8,128)(2,1)} %get-tuple-element.241.refs_2_), custom_call_target="tpu_custom_call" | custom-call | flops 4096 | bytes 4096 | tf_op jit(solution)/shard_map/bucket_sums/pallas_call | solution.py:223
  912.9 11.5 %collective-permute-done.98 = bf16[8,4]{0,1:T(4,128)(2,1)S(1)} collective-permute-done((bf16[8,4]{0,1:T(4,128)(2,1)S(1)}, bf16[8,4]{0,1:T(4,128)(2,1)S(1)}, u32[]{:S(2)}, u32[]{:S(2)}) %collective-permute-start.98) | collective-permute-done | bytes 96 | tf_op jit(solution)/shard_map/ppermute | solution.py:290
  934.7 10.8 %collective-permute-done.92 = bf16[512,768]{0,1:T(8,128)(2,1)S(1)} collective-permute-done((bf16[512,768]{0,1:T(8,128)(2,1)}, bf16[512,768]{0,1:T(8,128)(2,1)S(1)}, u32[]{:S(2)}, u32[]{:S(2)}) %collective-permute-start.92) | collective-permute-done | bytes 786464 | tf_op jit(solution)/shard_map/ppermute | solution.py:290
  (859 shorter events, 500.6 us)
Async XLA Ops:
  7.2 76.4 %all-gather.6.cloned.1.call-start = ((), (), s32[]{:S(2)}) async-start(), calls=%async_computation.5 | async-start | bytes 4718592 | tf_op jit(solution)/shard_map/all_gather | solution.py:359
  11.4 140.0 %all-gather.8.cloned.1.call-start = ((), (), s32[]{:S(2)}) async-start(), calls=%async_computation.6 | async-start | bytes 4718592 | tf_op jit(solution)/shard_map/all_gather | solution.py:359
  12.1 213.5 %all-gather.12.cloned.1.call-start = ((), (), s32[]{:S(2)}) async-start(), calls=%async_computation.8 | async-start | bytes 4718592 | tf_op jit(solution)/shard_map/all_gather | solution.py:359
  12.9 339.9 %all-gather.10.cloned.1.call-start = ((), (), s32[]{:S(2)}) async-start(), calls=%async_computation.7 | async-start | bytes 6553600 | tf_op jit(solution)/shard_map/all_gather | solution.py:308
  25.2 41.3 %collective-permute-start.1 = (bf16[256,512]{1,0:T(8,128)(2,1)S(1)}, bf16[256,512]{1,0:T(8,128)(2,1)}, u32[]{:S(2)}, u32[]{:S(2)}) collective-permute-start(bf16[256,512]{1,0:T(8,128)(2,1)S(1)} %copy-done.162), channel_id=1, source_target_pairs={{0,4},{1,5},{2,6},{3,7},{4,0},{5,1},{6,2},{7,3},{8,12},{9,13},{10,... | collective-permute-start | bytes 786440 | tf_op jit(solution)/shard_map/ppermute | solution.py:293
  94.0 307.3 %all-gather.14.cloned.1.call-start = ((), (), s32[]{:S(2)}) async-start(), calls=%async_computation.9 | async-start | bytes 3276800 | tf_op jit(solution)/shard_map/all_gather | solution.py:308
  99.8 46.4 %collective-permute-start.17 = (bf16[1024,512]{1,0:T(8,128)(2,1)S(1)}, bf16[1024,512]{1,0:T(8,128)(2,1)S(1)}, u32[]{:S(2)}, u32[]{:S(2)}) collective-permute-start(bf16[1024,512]{1,0:T(8,128)(2,1)S(1)} %pad_maximum_fusion.19), channel_id=1, source_target_pairs={{0,16},{8,24},{16,0},{24,8},{1,17},{9,25},{17,1},{25,9},{2,18},{10... | collective-permute-start | bytes 3145736 | tf_op jit(solution)/shard_map/ppermute | solution.py:290
  100.4 45.8 %collective-permute-start.16 = (bf16[1024,512]{1,0:T(8,128)(2,1)S(1)}, bf16[1024,512]{1,0:T(8,128)(2,1)S(1)}, u32[]{:S(2)}, u32[]{:S(2)}) collective-permute-start(bf16[1024,512]{1,0:T(8,128)(2,1)S(1)} %pad_maximum_fusion.19), channel_id=1, source_target_pairs={{0,8},{8,0},{16,24},{24,16},{1,9},{9,1},{17,25},{25,17},{2,10},{10... | collective-permute-start | bytes 3145736 | tf_op jit(solution)/shard_map/ppermute | solution.py:290
  148.0 46.9 %collective-permute-start.21 = (bf16[256,2048]{1,0:T(8,128)(2,1)S(1)}, bf16[256,2048]{1,0:T(8,128)(2,1)}, u32[]{:S(2)}, u32[]{:S(2)}) collective-permute-start(bf16[256,2048]{1,0:T(8,128)(2,1)S(1)} %pad_maximum_fusion.20), channel_id=1, source_target_pairs={{0,16},{8,24},{16,0},{24,8},{1,17},{9,25},{17,1},{25,9},{2,18},{10... | collective-permute-start | bytes 3145736 | tf_op jit(solution)/shard_map/ppermute | solution.py:290
  149.1 45.8 %collective-permute-start.20 = (bf16[256,2048]{1,0:T(8,128)(2,1)S(1)}, bf16[256,2048]{1,0:T(8,128)(2,1)}, u32[]{:S(2)}, u32[]{:S(2)}) collective-permute-start(bf16[256,2048]{1,0:T(8,128)(2,1)S(1)} %pad_maximum_fusion.20), channel_id=1, source_target_pairs={{0,8},{8,0},{16,24},{24,16},{1,9},{9,1},{17,25},{25,17},{2,10},{10... | collective-permute-start | bytes 3145736 | tf_op jit(solution)/shard_map/ppermute | solution.py:290
  152.2 55.2 %collective-permute-start.12 = (bf16[128,512]{1,0:T(8,128)(2,1)}, bf16[128,512]{1,0:T(8,128)(2,1)}, u32[]{:S(2)}, u32[]{:S(2)}) collective-permute-start(bf16[128,512]{1,0:T(8,128)(2,1)} %get-tuple-element.480), channel_id=1, source_target_pairs={{0,2},{1,3},{2,0},{3,1},{4,6},{5,7},{6,4},{7,5},{8,10},{9,11},{10,... | collective-permute-start | bytes 393224 | tf_op jit(solution)/shard_map/ppermute | solution.py:293
  158.8 48.6 %collective-permute-start.10 = (bf16[128,512]{1,0:T(8,128)(2,1)}, bf16[128,512]{1,0:T(8,128)(2,1)}, u32[]{:S(2)}, u32[]{:S(2)}) collective-permute-start(bf16[128,512]{1,0:T(8,128)(2,1)} %get-tuple-element.481), channel_id=1, source_target_pairs={{0,6},{1,7},{2,4},{3,5},{4,2},{5,3},{6,0},{7,1},{8,14},{9,15},{10,... | collective-permute-start | bytes 393224 | tf_op jit(solution)/shard_map/ppermute | solution.py:293
  206.9 333.4 %reduce-scatter.6.cloned.1.call-start = ((), (), s32[]{:S(2)}) async-start(), calls=%async_computation.10 | async-start | bytes 3276800 | tf_op jit(solution)/shard_map/reduce_scatter | solution.py:311
  222.7 39.1 %collective-permute-start.25 = (bf16[128,2048]{1,0:T(8,128)(2,1)S(1)}, bf16[128,2048]{1,0:T(8,128)(2,1)S(1)}, u32[]{:S(2)}, u32[]{:S(2)}) collective-permute-start(bf16[128,2048]{1,0:T(8,128)(2,1)S(1)} %multiply_convert_fusion.8), channel_id=1, source_target_pairs={{0,24},{8,16},{16,8},{24,0},{1,25},{9,17},{17,9},{25,1},{2,26},{10... | collective-permute-start | bytes 1572872 | tf_op jit(solution)/shard_map/ppermute | solution.py:290
  269.1 39.6 %collective-permute-start.37 = (bf16[256,2048]{1,0:T(8,128)(2,1)S(1)}, bf16[256,2048]{1,0:T(8,128)(2,1)S(1)}, u32[]{:S(2)}, u32[]{:S(2)}) collective-permute-start(bf16[256,2048]{1,0:T(8,128)(2,1)S(1)} %pad_maximum_fusion.21), channel_id=1, source_target_pairs={{0,24},{8,16},{16,8},{24,0},{1,25},{9,17},{17,9},{25,1},{2,26},{10... | collective-permute-start | bytes 3145736 | tf_op jit(solution)/shard_map/ppermute | solution.py:290
  270.6 44.8 %collective-permute-start.36 = (bf16[256,2048]{1,0:T(8,128)(2,1)S(1)}, bf16[256,2048]{1,0:T(8,128)(2,1)S(1)}, u32[]{:S(2)}, u32[]{:S(2)}) collective-permute-start(bf16[256,2048]{1,0:T(8,128)(2,1)S(1)} %pad_maximum_fusion.21), channel_id=1, source_target_pairs={{0,16},{8,24},{16,0},{24,8},{1,17},{9,25},{17,1},{25,9},{2,18},{10... | collective-permute-start | bytes 3145736 | tf_op jit(solution)/shard_map/ppermute | solution.py:290
  289.8 56.6 %collective-permute-start.26 = (bf16[512,2048]{1,0:T(8,128)(2,1)S(1)}, bf16[512,2048]{1,0:T(8,128)(2,1)S(1)}, u32[]{:S(2)}, u32[]{:S(2)}) collective-permute-start(bf16[512,2048]{1,0:T(8,128)(2,1)S(1)} %pad_maximum_fusion.5), channel_id=1, source_target_pairs={{0,1},{1,0},{2,3},{3,2},{4,5},{5,4},{6,7},{7,6},{8,9},{9,8},{10,11... | collective-permute-start | bytes 6291464 | tf_op jit(solution)/shard_map/ppermute | solution.py:287
  401.3 337.4 %reduce-scatter.8.cloned.1.call-start = ((), (), s32[]{:S(2)}) async-start(), calls=%async_computation.11 | async-start | bytes 6553600 | tf_op jit(solution)/shard_map/reduce_scatter | solution.py:311
  556.5 396.9 %reduce-scatter.10.cloned.1.call-start = ((), (), s32[]{:S(2)}) async-start(), calls=%async_computation.12 | async-start | bytes 4718592 | tf_op jit(solution)/shard_map/reduce_scatter | solution.py:615
  613.9 339.5 %reduce-scatter.12.cloned.1.call-start = ((), (), s32[]{:S(2)}) async-start(), calls=%async_computation.13 | async-start | bytes 4718592 | tf_op jit(solution)/shard_map/reduce_scatter | solution.py:615
  629.2 47.0 %collective-permute-start.66 = (bf16[3,128,2048]{2,1,0:T(8,128)(2,1)S(1)}, bf16[3,128,2048]{2,1,0:T(8,128)(2,1)S(1)}, u32[]{:S(2)}, u32[]{:S(2)}) collective-permute-start(bf16[3,128,2048]{2,1,0:T(8,128)(2,1)S(1)} %copy-done.64), channel_id=1, source_target_pairs={{0,24},{8,16},{16,8},{24,0},{1,25},{9,17},{17,9},{25,1},{2,26},{10... | collective-permute-start | bytes 4718600 | tf_op jit(solution)/shard_map/ppermute | solution.py:290
  630.8 69.0 %collective-permute-start.65 = (bf16[3,128,2048]{2,1,0:T(8,128)(2,1)S(1)}, bf16[3,128,2048]{2,1,0:T(8,128)(2,1)S(1)}, u32[]{:S(2)}, u32[]{:S(2)}) collective-permute-start(bf16[3,128,2048]{2,1,0:T(8,128)(2,1)S(1)} %copy-done.63), channel_id=1, source_target_pairs={{0,16},{8,24},{16,0},{24,8},{1,17},{9,25},{17,1},{25,9},{2,18},{10... | collective-permute-start | bytes 4718600 | tf_op jit(solution)/shard_map/ppermute | solution.py:290
  632.4 67.4 %collective-permute-start.64 = (bf16[3,128,2048]{2,1,0:T(8,128)(2,1)S(1)}, bf16[3,128,2048]{2,1,0:T(8,128)(2,1)}, u32[]{:S(2)}, u32[]{:S(2)}) collective-permute-start(bf16[3,128,2048]{2,1,0:T(8,128)(2,1)S(1)} %copy-done.62), channel_id=1, source_target_pairs={{0,8},{8,0},{16,24},{24,16},{1,9},{9,1},{17,25},{25,17},{2,10},{10... | collective-permute-start | bytes 4718600 | tf_op jit(solution)/shard_map/ppermute | solution.py:290
  707.7 245.7 %reduce-scatter.14.cloned.1.call-start = ((), (), s32[]{:S(2)}) async-start(), calls=%async_computation.14 | async-start | bytes 4718592 | tf_op jit(solution)/shard_map/reduce_scatter | solution.py:615
  742.0 62.3 %collective-permute-start.80 = (bf16[1024,512]{1,0:T(8,128)(2,1)}, bf16[1024,512]{1,0:T(8,128)(2,1)}, u32[]{:S(2)}, u32[]{:S(2)}) collective-permute-start(bf16[1024,512]{1,0:T(8,128)(2,1)} %get-tuple-element.318), channel_id=1, source_target_pairs={{0,24},{8,16},{16,8},{24,0},{1,25},{9,17},{17,9},{25,1},{2,26},{10... | collective-permute-start | bytes 3145736 | tf_op jit(solution)/shard_map/ppermute | solution.py:290
  743.4 61.6 %collective-permute-start.79 = (bf16[1024,512]{1,0:T(8,128)(2,1)}, bf16[1024,512]{1,0:T(8,128)(2,1)}, u32[]{:S(2)}, u32[]{:S(2)}) collective-permute-start(bf16[1024,512]{1,0:T(8,128)(2,1)} %get-tuple-element.319), channel_id=1, source_target_pairs={{0,16},{8,24},{16,0},{24,8},{1,17},{9,25},{17,1},{25,9},{2,18},{10... | collective-permute-start | bytes 3145736 | tf_op jit(solution)/shard_map/ppermute | solution.py:290
  744.9 60.2 %collective-permute-start.78 = (bf16[1024,512]{1,0:T(8,128)(2,1)}, bf16[1024,512]{1,0:T(8,128)(2,1)}, u32[]{:S(2)}, u32[]{:S(2)}) collective-permute-start(bf16[1024,512]{1,0:T(8,128)(2,1)} %get-tuple-element.320), channel_id=1, source_target_pairs={{0,8},{8,0},{16,24},{24,16},{1,9},{9,1},{17,25},{25,17},{2,10},{10... | collective-permute-start | bytes 3145736 | tf_op jit(solution)/shard_map/ppermute | solution.py:290
  754.1 48.5 %collective-permute-start.82 = (bf16[320,512]{1,0:T(8,128)(2,1)S(1)}, bf16[320,512]{1,0:T(8,128)(2,1)S(1)}, u32[]{:S(2)}, u32[]{:S(2)}) collective-permute-start(bf16[320,512]{1,0:T(8,128)(2,1)S(1)} %get-tuple-element.383), channel_id=1, source_target_pairs={{0,16},{8,24},{16,0},{24,8},{1,17},{9,25},{17,1},{25,9},{2,18},{10... | collective-permute-start | bytes 983048 | tf_op jit(solution)/shard_map/ppermute | solution.py:290
  755.7 48.7 %collective-permute-start.81 = (bf16[320,512]{1,0:T(8,128)(2,1)S(1)}, bf16[320,512]{1,0:T(8,128)(2,1)S(1)}, u32[]{:S(2)}, u32[]{:S(2)}) collective-permute-start(bf16[320,512]{1,0:T(8,128)(2,1)S(1)} %get-tuple-element.384), channel_id=1, source_target_pairs={{0,8},{8,0},{16,24},{24,16},{1,9},{9,1},{17,25},{25,17},{2,10},{10... | collective-permute-start | bytes 983048 | tf_op jit(solution)/shard_map/ppermute | solution.py:290
  836.2 88.3 %collective-permute-start.96 = (bf16[256,512]{1,0:T(8,128)(2,1)}, bf16[256,512]{1,0:T(8,128)(2,1)}, u32[]{:S(2)}, u32[]{:S(2)}) collective-permute-start(bf16[256,512]{1,0:T(8,128)(2,1)} %get-tuple-element.348), channel_id=1, source_target_pairs={{0,6},{1,7},{2,4},{3,5},{4,2},{5,3},{6,0},{7,1},{8,14},{9,15},{10,... | collective-permute-start | bytes 786440 | tf_op jit(solution)/shard_map/ppermute | solution.py:293
  838.6 93.8 %collective-permute-start.95 = (bf16[256,512]{1,0:T(8,128)(2,1)}, bf16[256,512]{1,0:T(8,128)(2,1)}, u32[]{:S(2)}, u32[]{:S(2)}) collective-permute-start(bf16[256,512]{1,0:T(8,128)(2,1)} %get-tuple-element.349), channel_id=1, source_target_pairs={{0,4},{1,5},{2,6},{3,7},{4,0},{5,1},{6,2},{7,3},{8,12},{9,13},{10,... | collective-permute-start | bytes 786440 | tf_op jit(solution)/shard_map/ppermute | solution.py:293
  838.6 93.8 %collective-permute-start.94 = (bf16[256,512]{1,0:T(8,128)(2,1)S(1)}, bf16[256,512]{1,0:T(8,128)(2,1)}, u32[]{:S(2)}, u32[]{:S(2)}) collective-permute-start(bf16[256,512]{1,0:T(8,128)(2,1)S(1)} %get-tuple-element.350), channel_id=1, source_target_pairs={{0,2},{1,3},{2,0},{3,1},{4,6},{5,7},{6,4},{7,5},{8,10},{9,11},{10,... | collective-permute-start | bytes 786440 | tf_op jit(solution)/shard_map/ppermute | solution.py:293
  (289 other events, 3103.5 us)
Sparse Core Ops, SparseCore 0:
  11.5 72.0 all-gather.5
  85.8 45.5 all-gather.7
  133.5 51.9 all-gather.11
  187.6 121.4 all-gather.9
  311.1 52.9 all-gather.13
  401.4 50.6 reduce-scatter.5
  556.7 101.5 reduce-scatter.7
  660.6 51.7 reduce-scatter.9
  714.7 56.3 reduce-scatter.11
  813.3 65.5 reduce-scatter.13

commit v9 on v6

--- a/solution.py
+++ b/solution.py
@@ -539,7 +539,7 @@
             else:
                 grad_pre = after(grad_pre, swapped_in[s - 1], *sums[-1])
             if s == seqs - 1:
-                grad_pre = after(grad_pre, post_z)
+                grad_pre = after(grad_pre, post_z, *moves[0][1:])
             more = tn_dot(grad_pre, norm_two_full[s])
             grad_pre_w = more if grad_pre_w is None else grad_pre_w + more
             if s == seqs - 1:

time: 953 us -> 928 us (0.974)
  waiting for transfers between devices: 193 us -> 181 us
    unnamed x495 -> x445, local copies, waits for them, and re-layouts: 57.3 us -> 57.6 us
  transfers between devices with their start and end apart: 110 -> 110, of which waited for: 25 -> 26; matrix products, arithmetic and copies ran while one was open for 39% -> 41% of each run, Pallas kernels for 19% -> 19%
where the time goes in v9:
time: 928 us; the launch traced here: 921 us
  matrix products  241 us (26%)
  waiting for transfers between devices  181 us (20%)
  Pallas kernels  176 us (19%)
  local copies, waits for them, and re-layouts  112 us (12%)
  starting transfers between devices  105 us (11%)
  other arithmetic  87 us (9%)
  between operations  18.3 us (2%)
    ppermute x54, waiting for transfers between devices, to_dp(): return lax.ppermute(x, 'dp', xor_pairs(dp_size, mask))  119 us
    dot_general x15, matrix products, nt_dot(): lax.dot_general(left, right, (((1,), (1,)), ((), ())), preferred_element_...  91.3 us
    dot_general x11, matrix products, tn_dot(): lax.dot_general(left, right, (((0,), (0,)), ((), ())), preferred_element_...  77.8 us
    dot_general x14, matrix products, nn_dot(): return jnp.dot(left, right, preferred_element_type=jnp.float32)  71.9 us
    ppermute x54, starting transfers between devices, to_dp(): return lax.ppermute(x, 'dp', xor_pairs(dp_size, mask))  64.7 us
    unnamed x445, local copies, waits for them, and re-layouts  57.6 us
    pallas_call x3, Pallas kernels, attention_backward(): pl.pallas_call(functools.partial(backward_kernel, min(256, length)), grid...  57.2 us
    pallas_call x1, Pallas kernels, bucket_sums(): pl.pallas_call(functools.partial(histogram_kernel, bucket_count, 4), grid...  55.4 us
  transfers between devices with their start and end apart: 110, of which 26 were waited for; matrix products, arithmetic and copies ran while one was open for 41% of the time, Pallas kernels for 19%

profile of v9, /device:TPU:0, one launch (start us, length us, event | category | flops | bytes accessed | tf_op | source)
XLA Modules:
  0.0 920.7 jit_solution(9970816754162507607)
XLA Ops:
  37.6 14.0 %expand_bias.1.bias_ref = bf16[4,1024,1024]{2,1,0:T(8,128)(2,1)} custom-call(s32[1024,1024]{1,0:T(8,128)} %bitcast.326, f32[4,128]{1,0:T(4,128)} %pad_convert_fusion.table_ref), custom_call_target="tpu_custom_call" | custom-call | flops 4096 | bytes 4096 | tf_op jit(solution)/shard_map/expand_bias/pallas_call | solution.py:50
  67.2 16.4 %all-gather.6.cloned.1.call-done = bf16[1024,2048]{1,0:T(8,128)(2,1)} async-done(((bf16[128,2048]{1,0:T(8,128)(2,1)}), bf16[1024,2048]{1,0:T(8,128)(2,1)}) %all-gather.6.cloned.1.call-update) | async-done | bytes 4194320 | tf_op jit(solution)/shard_map/all_gather | solution.py:359
  101.1 16.3 %attention_forward.3 = (bf16[1024,256]{1,0:T(8,128)(2,1)S(1)}, f32[2,2,1024]{2,1,0:T(2,128)S(1)}) custom-call(bf16[1024,768]{1,0:T(8,128)(2,1)S(1)} %convolution_convert_fusion.7.qkv_ref, bf16[4,1024,1024]{2,1,0:T(8,128)(2,1)} %expand_bias.1.bias_ref), custom_call_target="tpu_custom_call" | custom-call | flops 4096 | bytes 4096 | tf_op jit(solution)/shard_map/attention_forward/pallas_call | solution.py:93
  124.5 21.7 %collective-permute-done.17 = bf16[1024,512]{1,0:T(8,128)(2,1)S(1)} collective-permute-done((bf16[1024,512]{1,0:T(8,128)(2,1)S(1)}, bf16[1024,512]{1,0:T(8,128)(2,1)S(1)}, u32[]{:S(2)}, u32[]{:S(2)}) %collective-permute-start.17) | collective-permute-done | bytes 1048608 | tf_op jit(solution)/shard_map/ppermute | solution.py:290
  159.9 17.0 %attention_forward.4 = (bf16[1024,256]{1,0:T(8,128)(2,1)S(1)}, f32[2,2,1024]{2,1,0:T(2,128)S(1)}) custom-call(bf16[1024,768]{1,0:T(8,128)(2,1)S(1)} %convolution_convert_fusion.6.qkv_ref, bf16[4,1024,1024]{2,1,0:T(8,128)(2,1)} %expand_bias.1.bias_ref), custom_call_target="tpu_custom_call" | custom-call | flops 4096 | bytes 4096 | tf_op jit(solution)/shard_map/attention_forward/pallas_call | solution.py:93
  181.8 13.2 %collective-permute-done.21 = bf16[256,2048]{1,0:T(8,128)(2,1)} collective-permute-done((bf16[256,2048]{1,0:T(8,128)(2,1)S(1)}, bf16[256,2048]{1,0:T(8,128)(2,1)}, u32[]{:S(2)}, u32[]{:S(2)}) %collective-permute-start.21) | collective-permute-done | bytes 1048608 | tf_op jit(solution)/shard_map/ppermute | solution.py:290
  236.4 16.5 %attention_forward.5 = (bf16[1024,256]{1,0:T(8,128)(2,1)S(1)}, f32[2,2,1024]{2,1,0:T(2,128)S(1)}) custom-call(bf16[1024,768]{1,0:T(8,128)(2,1)S(1)} %convolution_convert_fusion.5.qkv_ref, bf16[4,1024,1024]{2,1,0:T(8,128)(2,1)} %expand_bias.1.bias_ref), custom_call_target="tpu_custom_call" | custom-call | flops 4096 | bytes 4096 | tf_op jit(solution)/shard_map/attention_forward/pallas_call | solution.py:93
  276.4 11.7 %collective-permute-done.34 = bf16[128,512]{1,0:T(8,128)(2,1)S(1)} collective-permute-done((bf16[128,512]{1,0:T(8,128)(2,1)S(1)}, bf16[128,512]{1,0:T(8,128)(2,1)S(1)}, u32[]{:S(2)}, u32[]{:S(2)}) %collective-permute-start.34) | collective-permute-done | bytes 131104 | tf_op jit(solution)/shard_map/ppermute | solution.py:293
  289.6 12.2 %collective-permute-done.33 = bf16[128,512]{1,0:T(8,128)(2,1)S(1)} collective-permute-done((bf16[128,512]{1,0:T(8,128)(2,1)S(1)}, bf16[128,512]{1,0:T(8,128)(2,1)S(1)}, u32[]{:S(2)}, u32[]{:S(2)}) %collective-permute-start.33) | collective-permute-done | bytes 131104 | tf_op jit(solution)/shard_map/ppermute | solution.py:293
  320.2 10.9 %collective-permute-done.40 = bf16[128,2048]{1,0:T(8,128)(2,1)S(1)} collective-permute-done((bf16[128,2048]{1,0:T(8,128)(2,1)S(1)}, bf16[128,2048]{1,0:T(8,128)(2,1)S(1)}, u32[]{:S(2)}, u32[]{:S(2)}) %collective-permute-start.40) | collective-permute-done | bytes 524320 | tf_op jit(solution)/shard_map/ppermute | solution.py:290
  331.0 10.2 %collective-permute-done.39 = bf16[128,2048]{1,0:T(8,128)(2,1)S(1)} collective-permute-done((bf16[128,2048]{1,0:T(8,128)(2,1)S(1)}, bf16[128,2048]{1,0:T(8,128)(2,1)S(1)}, u32[]{:S(2)}, u32[]{:S(2)}) %collective-permute-start.39) | collective-permute-done | bytes 524320 | tf_op jit(solution)/shard_map/ppermute | solution.py:290
  355.4 9.4 %fusion.253 = f32[1024,1280]{1,0:T(8,128)S(1)} fusion(bf16[1024,2048]{1,0:T(8,128)(2,1)} %constant_dynamic-update-slice_fusion.5, bf16[1280,2048]{1,0:T(8,128)(2,1)S(1)} %bitcast.330), kind=kOutput, calls=%fused_computation.616 | convolution fusion | flops 5368709120 | bytes 14680064 | tf_op jit(solution)/shard_map/dot_general | solution.py:16
  401.3 9.7 %fusion.7 = (bf16[1024,640]{1,0:T(8,128)(2,1)S(1)}, bf16[1024,640]{1,0:T(8,128)(2,1)S(1)}) fusion(f32[1024,1280]{1,0:T(8,128)} %copy-done.37, bf16[1024,2048]{1,0:T(8,128)(2,1)} %constant_dynamic-update-slice_fusion.15, bf16[640,2048]{1,0:T(8,128)(2,1)} %all-gather.14.cloned.1.call-done), kind=kOutput, calls=%fused_computation.33 | convolution fusion | flops 2700083200 | bytes 14680064 | tf_op jit(solution)/shard_map/dot_general | solution.py:16
  411.1 8.3 fusion.216
  423.5 7.6 fusion.14
  448.4 7.6 fusion.21
  469.1 8.4 fusion.256
  499.3 10.5 %fusion.257 = f32[1280,2048]{1,0:T(8,128)} fusion(bf16[1024,1280]{1,0:T(8,128)(2,1)S(1)} %pad_maximum_fusion.3, bf16[1024,2048]{1,0:T(8,128)(2,1)} %copy-done.169), kind=kOutput, calls=%fused_computation.620 | convolution fusion | flops 5368709120 | bytes 17301504 | tf_op jit(solution)/shard_map/dot_general | solution.py:272
  521.1 13.6 %add_convert_fusion = bf16[1280,2048]{1,0:T(8,128)(2,1)S(1)} fusion(f32[1280,2048]{1,0:T(8,128)} %fusion.256, f32[1280,2048]{1,0:T(8,128)} %fusion.257, bf16[1024,1280]{1,0:T(8,128)(2,1)} %pad_maximum_fusion.4, bf16[1024,2048]{1,0:T(8,128)(2,1)} %constant_dynamic-update-slice_fusion.5), kind=kOutput, calls=%fused_computation.1 | convolution fusion | flops 5376573440 | bytes 33030144 | tf_op jit(solution)/shard_map/dot_general | solution.py:272
  543.8 7.0 convolution_convert_fusion
  555.9 19.0 %attention_backward.3 = (bf16[1024,768]{1,0:T(8,128)(2,1)S(1)}, bf16[4,1024,1024]{2,1,0:T(8,128)(2,1)}) custom-call(bf16[1024,768]{1,0:T(8,128)(2,1)S(1)} %convolution_convert_fusion.7.qkv_ref, bf16[1024,256]{1,0:T(8,128)(2,1)S(1)} %bitcast.321, bf16[4,1024,1024]{2,1,0:T(8,128)(2,1)} %expand_bias.1.bias_ref, f32[2,2,1024]{2,1,0:T(2,128)S(1)} %get-tuple-element.199.lse_ref), custom_call_target="tpu_custom_call" | custom-call | flops 4096 | bytes 4096 | tf_op jit(solution)/shard_map/attention_backward/pallas_call | solution.py:161
  578.2 8.0 convolution_convert_fusion.4
  599.2 7.4 convert_add_fusion
  628.9 8.0 collective-permute-done.72
  637.9 19.2 %attention_backward.4 = (bf16[1024,768]{1,0:T(8,128)(2,1)S(1)}, bf16[4,1024,1024]{2,1,0:T(8,128)(2,1)}) custom-call(bf16[1024,768]{1,0:T(8,128)(2,1)S(1)} %copy-done.1, bf16[1024,256]{1,0:T(8,128)(2,1)S(1)} %bitcast.322, bf16[4,1024,1024]{2,1,0:T(8,128)(2,1)} %expand_bias.1.bias_ref, f32[2,2,1024]{2,1,0:T(2,128)S(1)} %get-tuple-element.215.lse_ref), custom_call_target="tpu_custom_call" | custom-call | flops 4096 | bytes 4096 | tf_op jit(solution)/shard_map/attention_backward/pallas_call | solution.py:161
  657.1 21.2 %collective-permute-done.65 = bf16[3,128,2048]{2,1,0:T(8,128)(2,1)S(1)} collective-permute-done((bf16[3,128,2048]{2,1,0:T(8,128)(2,1)S(1)}, bf16[3,128,2048]{2,1,0:T(8,128)(2,1)S(1)}, u32[]{:S(2)}, u32[]{:S(2)}) %collective-permute-start.65) | collective-permute-done | bytes 1572896 | tf_op jit(solution)/shard_map/ppermute | solution.py:290
  717.3 7.4 convolution_add_fusion.1
  726.2 19.0 %attention_backward.5 = (bf16[1024,768]{1,0:T(8,128)(2,1)S(1)}, bf16[4,1024,1024]{2,1,0:T(8,128)(2,1)}) custom-call(bf16[1024,768]{1,0:T(8,128)(2,1)S(1)} %copy-done.3, bf16[1024,256]{1,0:T(8,128)(2,1)S(1)} %bitcast.320, bf16[4,1024,1024]{2,1,0:T(8,128)(2,1)} %expand_bias.1.bias_ref, f32[2,2,1024]{2,1,0:T(2,128)S(1)} %get-tuple-element.229.lse_ref), custom_call_target="tpu_custom_call" | custom-call | flops 4096 | bytes 4096 | tf_op jit(solution)/shard_map/attention_backward/pallas_call | solution.py:161
  745.2 14.8 %collective-permute-done.79 = bf16[1024,512]{1,0:T(8,128)(2,1)} collective-permute-done((bf16[1024,512]{1,0:T(8,128)(2,1)S(1)}, bf16[1024,512]{1,0:T(8,128)(2,1)}, u32[]{:S(2)}, u32[]{:S(2)}) %collective-permute-start.79) | collective-permute-done | bytes 1048608 | tf_op jit(solution)/shard_map/ppermute | solution.py:290
  761.0 7.6 convolution_convert_fusion.2
  781.2 7.6 convolution_add_fusion
  810.8 55.4 %bucket_sums.1 = f32[4,32,8,128]{3,2,1,0:T(8,128)S(1)} custom-call(s32[1024,1024]{1,0:T(8,128)} %bitcast.327, bf16[4,1024,1024]{2,1,0:T(8,128)(2,1)} %get-tuple-element.241.refs_0_, bf16[4,1024,1024]{2,1,0:T(8,128)(2,1)} %get-tuple-element.242.refs_1_, bf16[4,1024,1024]{2,1,0:T(8,128)(2,1)} %get-tuple-element.243.refs_2_), custom_call_target="tpu_custom_call" | custom-call | flops 4096 | bytes 4096 | tf_op jit(solution)/shard_map/bucket_sums/pallas_call | solution.py:223
  (859 shorter events, 465.5 us)
Async XLA Ops:
  7.2 76.4 %all-gather.6.cloned.1.call-start = ((), (), s32[]{:S(2)}) async-start(), calls=%async_computation.5 | async-start | bytes 4718592 | tf_op jit(solution)/shard_map/all_gather | solution.py:359
  11.4 140.0 %all-gather.8.cloned.1.call-start = ((), (), s32[]{:S(2)}) async-start(), calls=%async_computation.6 | async-start | bytes 4718592 | tf_op jit(solution)/shard_map/all_gather | solution.py:359
  12.1 213.3 %all-gather.12.cloned.1.call-start = ((), (), s32[]{:S(2)}) async-start(), calls=%async_computation.8 | async-start | bytes 4718592 | tf_op jit(solution)/shard_map/all_gather | solution.py:359
  12.9 339.6 %all-gather.10.cloned.1.call-start = ((), (), s32[]{:S(2)}) async-start(), calls=%async_computation.7 | async-start | bytes 6553600 | tf_op jit(solution)/shard_map/all_gather | solution.py:308
  25.2 41.4 %collective-permute-start.1 = (bf16[256,512]{1,0:T(8,128)(2,1)S(1)}, bf16[256,512]{1,0:T(8,128)(2,1)}, u32[]{:S(2)}, u32[]{:S(2)}) collective-permute-start(bf16[256,512]{1,0:T(8,128)(2,1)S(1)} %copy-done.164), channel_id=1, source_target_pairs={{0,4},{1,5},{2,6},{3,7},{4,0},{5,1},{6,2},{7,3},{8,12},{9,13},{10,... | collective-permute-start | bytes 786440 | tf_op jit(solution)/shard_map/ppermute | solution.py:293
  94.0 307.3 %all-gather.14.cloned.1.call-start = ((), (), s32[]{:S(2)}) async-start(), calls=%async_computation.9 | async-start | bytes 3276800 | tf_op jit(solution)/shard_map/all_gather | solution.py:308
  99.8 46.4 %collective-permute-start.17 = (bf16[1024,512]{1,0:T(8,128)(2,1)S(1)}, bf16[1024,512]{1,0:T(8,128)(2,1)S(1)}, u32[]{:S(2)}, u32[]{:S(2)}) collective-permute-start(bf16[1024,512]{1,0:T(8,128)(2,1)S(1)} %pad_maximum_fusion.19), channel_id=1, source_target_pairs={{0,16},{8,24},{16,0},{24,8},{1,17},{9,25},{17,1},{25,9},{2,18},{10... | collective-permute-start | bytes 3145736 | tf_op jit(solution)/shard_map/ppermute | solution.py:290
  100.4 45.8 %collective-permute-start.16 = (bf16[1024,512]{1,0:T(8,128)(2,1)S(1)}, bf16[1024,512]{1,0:T(8,128)(2,1)S(1)}, u32[]{:S(2)}, u32[]{:S(2)}) collective-permute-start(bf16[1024,512]{1,0:T(8,128)(2,1)S(1)} %pad_maximum_fusion.19), channel_id=1, source_target_pairs={{0,8},{8,0},{16,24},{24,16},{1,9},{9,1},{17,25},{25,17},{2,10},{10... | collective-permute-start | bytes 3145736 | tf_op jit(solution)/shard_map/ppermute | solution.py:290
  148.0 46.9 %collective-permute-start.21 = (bf16[256,2048]{1,0:T(8,128)(2,1)S(1)}, bf16[256,2048]{1,0:T(8,128)(2,1)}, u32[]{:S(2)}, u32[]{:S(2)}) collective-permute-start(bf16[256,2048]{1,0:T(8,128)(2,1)S(1)} %pad_maximum_fusion.20), channel_id=1, source_target_pairs={{0,16},{8,24},{16,0},{24,8},{1,17},{9,25},{17,1},{25,9},{2,18},{10... | collective-permute-start | bytes 3145736 | tf_op jit(solution)/shard_map/ppermute | solution.py:290
  149.2 45.8 %collective-permute-start.20 = (bf16[256,2048]{1,0:T(8,128)(2,1)S(1)}, bf16[256,2048]{1,0:T(8,128)(2,1)}, u32[]{:S(2)}, u32[]{:S(2)}) collective-permute-start(bf16[256,2048]{1,0:T(8,128)(2,1)S(1)} %pad_maximum_fusion.20), channel_id=1, source_target_pairs={{0,8},{8,0},{16,24},{24,16},{1,9},{9,1},{17,25},{25,17},{2,10},{10... | collective-permute-start | bytes 3145736 | tf_op jit(solution)/shard_map/ppermute | solution.py:290
  152.2 55.0 %collective-permute-start.12 = (bf16[128,512]{1,0:T(8,128)(2,1)}, bf16[128,512]{1,0:T(8,128)(2,1)}, u32[]{:S(2)}, u32[]{:S(2)}) collective-permute-start(bf16[128,512]{1,0:T(8,128)(2,1)} %get-tuple-element.482), channel_id=1, source_target_pairs={{0,2},{1,3},{2,0},{3,1},{4,6},{5,7},{6,4},{7,5},{8,10},{9,11},{10,... | collective-permute-start | bytes 393224 | tf_op jit(solution)/shard_map/ppermute | solution.py:293
  158.8 48.4 %collective-permute-start.10 = (bf16[128,512]{1,0:T(8,128)(2,1)}, bf16[128,512]{1,0:T(8,128)(2,1)}, u32[]{:S(2)}, u32[]{:S(2)}) collective-permute-start(bf16[128,512]{1,0:T(8,128)(2,1)} %get-tuple-element.483), channel_id=1, source_target_pairs={{0,6},{1,7},{2,4},{3,5},{4,2},{5,3},{6,0},{7,1},{8,14},{9,15},{10,... | collective-permute-start | bytes 393224 | tf_op jit(solution)/shard_map/ppermute | solution.py:293
  206.9 314.2 %reduce-scatter.6.cloned.1.call-start = ((), (), s32[]{:S(2)}) async-start(), calls=%async_computation.10 | async-start | bytes 3276800 | tf_op jit(solution)/shard_map/reduce_scatter | solution.py:311
  268.9 39.7 %collective-permute-start.37 = (bf16[256,2048]{1,0:T(8,128)(2,1)S(1)}, bf16[256,2048]{1,0:T(8,128)(2,1)S(1)}, u32[]{:S(2)}, u32[]{:S(2)}) collective-permute-start(bf16[256,2048]{1,0:T(8,128)(2,1)S(1)} %pad_maximum_fusion.21), channel_id=1, source_target_pairs={{0,24},{8,16},{16,8},{24,0},{1,25},{9,17},{17,9},{25,1},{2,26},{10... | collective-permute-start | bytes 3145736 | tf_op jit(solution)/shard_map/ppermute | solution.py:290
  270.4 44.8 %collective-permute-start.36 = (bf16[256,2048]{1,0:T(8,128)(2,1)S(1)}, bf16[256,2048]{1,0:T(8,128)(2,1)S(1)}, u32[]{:S(2)}, u32[]{:S(2)}) collective-permute-start(bf16[256,2048]{1,0:T(8,128)(2,1)S(1)} %pad_maximum_fusion.21), channel_id=1, source_target_pairs={{0,16},{8,24},{16,0},{24,8},{1,17},{9,25},{17,1},{25,9},{2,18},{10... | collective-permute-start | bytes 3145736 | tf_op jit(solution)/shard_map/ppermute | solution.py:290
  289.6 56.6 %collective-permute-start.26 = (bf16[512,2048]{1,0:T(8,128)(2,1)S(1)}, bf16[512,2048]{1,0:T(8,128)(2,1)S(1)}, u32[]{:S(2)}, u32[]{:S(2)}) collective-permute-start(bf16[512,2048]{1,0:T(8,128)(2,1)S(1)} %pad_maximum_fusion.5), channel_id=1, source_target_pairs={{0,1},{1,0},{2,3},{3,2},{4,5},{5,4},{6,7},{7,6},{8,9},{9,8},{10,11... | collective-permute-start | bytes 6291464 | tf_op jit(solution)/shard_map/ppermute | solution.py:287
  401.3 387.6 %reduce-scatter.14.cloned.1.call-start = ((), (), s32[]{:S(2)}) async-start(), calls=%async_computation.14 | async-start | bytes 6553600 | tf_op jit(solution)/shard_map/reduce_scatter | solution.py:311
  537.5 352.2 %reduce-scatter.8.cloned.1.call-start = ((), (), s32[]{:S(2)}) async-start(), calls=%async_computation.11 | async-start | bytes 4718592 | tf_op jit(solution)/shard_map/reduce_scatter | solution.py:617
  550.7 47.2 %collective-permute-start.63 = (bf16[1536,2048]{1,0:T(8,128)(2,1)}, bf16[1536,2048]{1,0:T(8,128)(2,1)}, u32[]{:S(2)}, u32[]{:S(2)}) collective-permute-start(bf16[1536,2048]{1,0:T(8,128)(2,1)} %convolution_convert_fusion), channel_id=1, source_target_pairs={{0,1},{1,0},{2,3},{3,2},{4,5},{5,4},{6,7},{7,6},{8,9},{9,8},{10,11... | collective-permute-start | bytes 18874376 | tf_op jit(solution)/shard_map/ppermute | solution.py:287
  586.3 303.4 %reduce-scatter.10.cloned.1.call-start = ((), (), s32[]{:S(2)}) async-start(), calls=%async_computation.12 | async-start | bytes 4718592 | tf_op jit(solution)/shard_map/reduce_scatter | solution.py:617
  607.5 49.6 %collective-permute-start.66 = (bf16[3,128,2048]{2,1,0:T(8,128)(2,1)S(1)}, bf16[3,128,2048]{2,1,0:T(8,128)(2,1)S(1)}, u32[]{:S(2)}, u32[]{:S(2)}) collective-permute-start(bf16[3,128,2048]{2,1,0:T(8,128)(2,1)S(1)} %get-tuple-element.332), channel_id=1, source_target_pairs={{0,24},{8,16},{16,8},{24,0},{1,25},{9,17},{17,9},{25,1},{2,26},{10... | collective-permute-start | bytes 4718600 | tf_op jit(solution)/shard_map/ppermute | solution.py:290
  608.9 69.4 %collective-permute-start.65 = (bf16[3,128,2048]{2,1,0:T(8,128)(2,1)S(1)}, bf16[3,128,2048]{2,1,0:T(8,128)(2,1)S(1)}, u32[]{:S(2)}, u32[]{:S(2)}) collective-permute-start(bf16[3,128,2048]{2,1,0:T(8,128)(2,1)S(1)} %get-tuple-element.333), channel_id=1, source_target_pairs={{0,16},{8,24},{16,0},{24,8},{1,17},{9,25},{17,1},{25,9},{2,18},{10... | collective-permute-start | bytes 4718600 | tf_op jit(solution)/shard_map/ppermute | solution.py:290
  609.7 68.6 %collective-permute-start.64 = (bf16[3,128,2048]{2,1,0:T(8,128)(2,1)S(1)}, bf16[3,128,2048]{2,1,0:T(8,128)(2,1)}, u32[]{:S(2)}, u32[]{:S(2)}) collective-permute-start(bf16[3,128,2048]{2,1,0:T(8,128)(2,1)S(1)} %get-tuple-element.334), channel_id=1, source_target_pairs={{0,8},{8,0},{16,24},{24,16},{1,9},{9,1},{17,25},{25,17},{2,10},{10... | collective-permute-start | bytes 4718600 | tf_op jit(solution)/shard_map/ppermute | solution.py:290
  637.0 61.0 %collective-permute-start.77 = (bf16[1024,2048]{1,0:T(8,128)(2,1)}, bf16[1024,2048]{1,0:T(8,128)(2,1)}, u32[]{:S(2)}, u32[]{:S(2)}) collective-permute-start(bf16[1024,2048]{1,0:T(8,128)(2,1)} %convolution_convert_fusion.1), channel_id=1, source_target_pairs={{0,1},{1,0},{2,3},{3,2},{4,5},{5,4},{6,7},{7,6},{8,9},{9,8},{10,11... | collective-permute-start | bytes 12582920 | tf_op jit(solution)/shard_map/ppermute | solution.py:287
  686.3 203.4 %reduce-scatter.12.cloned.1.call-start = ((), (), s32[]{:S(2)}) async-start(), calls=%async_computation.13 | async-start | bytes 4718592 | tf_op jit(solution)/shard_map/reduce_scatter | solution.py:617
  714.1 45.9 %collective-permute-start.79 = (bf16[1024,512]{1,0:T(8,128)(2,1)S(1)}, bf16[1024,512]{1,0:T(8,128)(2,1)}, u32[]{:S(2)}, u32[]{:S(2)}) collective-permute-start(bf16[1024,512]{1,0:T(8,128)(2,1)S(1)} %get-tuple-element.321), channel_id=1, source_target_pairs={{0,16},{8,24},{16,0},{24,8},{1,17},{9,25},{17,1},{25,9},{2,18},{10... | collective-permute-start | bytes 3145736 | tf_op jit(solution)/shard_map/ppermute | solution.py:290
  716.0 45.0 %collective-permute-start.78 = (bf16[1024,512]{1,0:T(8,128)(2,1)S(1)}, bf16[1024,512]{1,0:T(8,128)(2,1)}, u32[]{:S(2)}, u32[]{:S(2)}) collective-permute-start(bf16[1024,512]{1,0:T(8,128)(2,1)S(1)} %get-tuple-element.322), channel_id=1, source_target_pairs={{0,8},{8,0},{16,24},{24,16},{1,9},{9,1},{17,25},{25,17},{2,10},{10... | collective-permute-start | bytes 3145736 | tf_op jit(solution)/shard_map/ppermute | solution.py:290
  778.4 89.5 %collective-permute-start.96 = (bf16[256,512]{1,0:T(8,128)(2,1)}, bf16[256,512]{1,0:T(8,128)(2,1)}, u32[]{:S(2)}, u32[]{:S(2)}) collective-permute-start(bf16[256,512]{1,0:T(8,128)(2,1)} %get-tuple-element.350), channel_id=1, source_target_pairs={{0,6},{1,7},{2,4},{3,5},{4,2},{5,3},{6,0},{7,1},{8,14},{9,15},{10,... | collective-permute-start | bytes 786440 | tf_op jit(solution)/shard_map/ppermute | solution.py:293
  781.2 89.8 %collective-permute-start.95 = (bf16[256,512]{1,0:T(8,128)(2,1)}, bf16[256,512]{1,0:T(8,128)(2,1)}, u32[]{:S(2)}, u32[]{:S(2)}) collective-permute-start(bf16[256,512]{1,0:T(8,128)(2,1)} %get-tuple-element.351), channel_id=1, source_target_pairs={{0,4},{1,5},{2,6},{3,7},{4,0},{5,1},{6,2},{7,3},{8,12},{9,13},{10,... | collective-permute-start | bytes 786440 | tf_op jit(solution)/shard_map/ppermute | solution.py:293
  803.3 74.8 %collective-permute-start.90 = (bf16[512,768]{0,1:T(8,128)(2,1)}, bf16[512,768]{0,1:T(8,128)(2,1)}, u32[]{:S(2)}, u32[]{:S(2)}) collective-permute-start(bf16[512,768]{0,1:T(8,128)(2,1)} %get-tuple-element.329), channel_id=1, source_target_pairs={{0,24},{8,16},{16,8},{24,0},{1,25},{9,17},{17,9},{25,1},{2,26},{10... | collective-permute-start | bytes 2359304 | tf_op jit(solution)/shard_map/ppermute | solution.py:290
  807.1 72.2 %collective-permute-start.89 = (bf16[512,768]{0,1:T(8,128)(2,1)}, bf16[512,768]{0,1:T(8,128)(2,1)}, u32[]{:S(2)}, u32[]{:S(2)}) collective-permute-start(bf16[512,768]{0,1:T(8,128)(2,1)} %get-tuple-element.330), channel_id=1, source_target_pairs={{0,16},{8,24},{16,0},{24,8},{1,17},{9,25},{17,1},{25,9},{2,18},{10... | collective-permute-start | bytes 2359304 | tf_op jit(solution)/shard_map/ppermute | solution.py:290
  808.5 70.8 %collective-permute-start.88 = (bf16[512,768]{0,1:T(8,128)(2,1)}, bf16[512,768]{0,1:T(8,128)(2,1)}, u32[]{:S(2)}, u32[]{:S(2)}) collective-permute-start(bf16[512,768]{0,1:T(8,128)(2,1)} %get-tuple-element.331), channel_id=1, source_target_pairs={{0,8},{8,0},{16,24},{24,16},{1,9},{9,1},{17,25},{25,17},{2,10},{10... | collective-permute-start | bytes 2359304 | tf_op jit(solution)/shard_map/ppermute | solution.py:290
  (289 other events, 3087.5 us)
Sparse Core Ops, SparseCore 0:
  11.5 72.0 all-gather.5
  85.8 45.5 all-gather.7
  133.5 51.8 all-gather.11
  187.4 121.6 all-gather.9
  311.1 52.9 all-gather.13
  401.4 50.5 reduce-scatter.5
  537.6 98.9 reduce-scatter.13
  638.9 52.6 reduce-scatter.7
  693.9 52.8 reduce-scatter.9
  768.8 68.5 reduce-scatter.11
